TPU v7x, 256 devices: a whole 4x4x8 slice. The times are simulated.
256 devices in a mesh: batch: 8 (over x, core), hidden: 4 (over z_hi), solver: 8 (over z_lo, y).
Axes of the slice: x: 4, y: 4, z: 8 (z_hi: 4, z_lo: 2; z = z_hi * 2 + z_lo), core: 2. Of those that a mesh axis runs over, the one named last changes fastest.
Arguments:
- activations: bfloat16 [2048, 4096], P('batch', ('hidden', 'solver')), may hold values from -16 to 16, as said below
- cotangent: bfloat16 [8192, 2048], P(('hidden', 'solver'), 'batch'), may hold values from -0.13183594 to 0.13183594
- weight: bfloat16 [4096, 8192], P(('hidden', 'solver'), 'batch'), may hold values from -0.09375 to 0.09375
- left_old: float32 [4, 8, 1024, 1024], P('hidden', 'batch'), may hold values from -0.001953125 to 2.0019531, as said below
- right_old: float32 [4, 8, 1024, 1024], P('hidden', 'batch'), may hold values from -0.001953125 to 2.0019531, as said below
Outputs:
- first_out: bfloat16 [8192, 2048], P(('hidden', 'solver'), 'batch')
- new_left: float32 [4, 8, 1024, 1024], P('hidden', 'batch', 'solver')
- new_right: float32 [4, 8, 1024, 1024], P('hidden', 'batch', 'solver')
- direction: float32 [4096, 8192], P(('hidden', 'solver'), 'batch')
- second_out: bfloat16 [8192, 2048], P(('hidden', 'solver'), 'batch')
Inputs may be any that keep to these rules, and one draw needn't show every extreme that they name: `activations`: in the hidden draw each feature carries its own scale. `left_old`: every block is symmetric, its diagonal is positive and larger than the sum of the magnitudes of the rest of its row. `right_old`: every block is symmetric, its diagonal is positive and larger than the sum of the magnitudes of the rest of its row.
All inputs are finite; a program needn't handle non-finite values. Where the computation divides by a largest or mean magnitude, that divisor is 1e-20 or more.
Results may differ from a plain program's by a relative error of at most 0.017.
Values may be sent and summed in bfloat16 or wider, within the bound.
No kernel may reach another device: no remote copies, remote signals or barrier semaphores. Data moves between devices by JAX's collectives and lax.ppermute only.
A program may use at most 128 MiB of HBM per device.

v0:
```python
import jax
import jax.numpy as jnp
from jax import lax
from jax.sharding import PartitionSpec as P

BLOCK = 1024


STAT_DECAY = 0.8
LEARN_RATE = 0.005
EPSILON = 1e-06


def in_order(blocks, dim):
    blocks = jnp.moveaxis(blocks, 0, dim)
    shape = blocks.shape
    return blocks.reshape(*shape[:dim], shape[dim] * shape[dim + 1], *shape[dim + 2 :])


def sent_to_all(shard, axis):
    copies = jnp.broadcast_to(shard, (lax.axis_size(axis), *shard.shape))
    return lax.all_to_all(copies, axis, split_axis=0, concat_axis=0, tiled=True)


def gather_directly(shard, axis, dim):
    return in_order(sent_to_all(shard, axis), dim)


def cut_along(shard, dim, peers):
    before, after = (shard.shape[:dim], shard.shape[dim + 1 :])
    return jnp.moveaxis(shard.reshape(*before, peers, -1, *after), dim, 0)


def summed_on_arrival(shard, axis, dim):
    blocks = cut_along(shard, dim, lax.axis_size(axis))
    arrived = lax.all_to_all(blocks, axis, split_axis=0, concat_axis=0, tiled=True)
    return arrived.astype(jnp.float32).sum(axis=0)


def taken_together(shard, axis):
    everything = sent_to_all(shard, axis)
    return jnp.sum(everything, axis=0)


def product(left_mat, right_mat):
    return jnp.einsum("bij,bjk->bik", left_mat, right_mat, preferred_element_type=jnp.float32)


def prepare(factor):
    identity = jnp.eye(BLOCK, dtype=jnp.float32)
    scaled = 2.5 / (jnp.max(jnp.sum(jnp.abs(factor), axis=2), axis=1) + EPSILON)
    moment = scaled[:, None, None] * factor
    newton_step = (5.0 * identity - moment) * 0.25
    return (scaled, moment, newton_step)


def transposed_product(weight_cols, acts):
    return lax.dot_general(
        weight_cols, acts, (((0,), (1,)), ((), ())), preferred_element_type=jnp.float32
    )


def body(activations, cotangent, weight, left_old, right_old):
    rows_here = weight.shape[0]
    nblocks = weight.shape[1] // BLOCK
    weight_rows = gather_directly(weight, "batch", 1)
    gathered = lax.all_gather(activations, ("hidden", "solver"), axis=1, tiled=True)
    weight_cols = lax.all_to_all(
        weight_rows, ("hidden", "solver"), split_axis=1, concat_axis=0, tiled=True
    )
    first_sum = transposed_product(weight_cols, gathered)
    first_out = first_sum.astype(jnp.bfloat16)
    cotangent_all = lax.all_gather(cotangent, ("hidden", "solver"), axis=0, tiled=True)
    grad_local = summed_on_arrival(
        jnp.dot(cotangent_all, activations, preferred_element_type=jnp.float32).astype(
            jnp.bfloat16
        ),
        "batch",
        0,
    ).astype(jnp.bfloat16)
    grad_blocks = grad_local.reshape(nblocks, BLOCK, rows_here)
    grad_full = gather_directly(grad_blocks, "solver", 2)
    gram_left = jnp.einsum("bnm,bnk->bmk", grad_full, grad_full, preferred_element_type=jnp.float32)
    gram_right = jnp.einsum(
        "bnm,bkm->bnk", grad_full, grad_full, preferred_element_type=jnp.float32
    )
    left_all = STAT_DECAY * left_old[0] + (1.0 - STAT_DECAY) / BLOCK * gram_left
    right_all = STAT_DECAY * right_old[0] + (1.0 - STAT_DECAY) / BLOCK * gram_right
    first_row = lax.axis_index("solver") * rows_here
    new_left = lax.dynamic_slice_in_dim(left_all, first_row, rows_here, 1)[None]
    new_right = lax.dynamic_slice_in_dim(right_all, first_row, rows_here, 1)[None]
    scale_left, moment_left, step_left = prepare(left_all)
    own_rows = lax.dynamic_slice_in_dim(step_left, first_row, rows_here, 1)
    power_rows = product(
        product(product(product(own_rows, step_left), step_left), step_left), moment_left
    )
    row_index = lax.broadcasted_iota(jnp.int32, (rows_here, BLOCK), 0) + first_row
    col_index = lax.broadcasted_iota(jnp.int32, (rows_here, BLOCK), 1)
    eye_rows = (row_index == col_index).astype(jnp.float32)
    next_rows = (5.0 * eye_rows - power_rows) * 0.25
    root_rows = (scale_left**0.25)[:, None, None] * product(next_rows, step_left)
    grad_float = grad_full.astype(jnp.float32)
    mixed_rows = jnp.einsum(
        "brm,bnm->brn", root_rows, grad_float, preferred_element_type=jnp.float32
    )
    scale_right, moment_right, step_right = prepare(right_all)
    turned = product(mixed_rows, step_right)
    power_right = product(
        product(product(product(product(turned, step_right), step_right), step_right), step_right),
        moment_right,
    )
    update = (scale_right**0.25)[:, None, None] * ((5.0 * turned - power_right) * 0.25)
    squares = taken_together(jnp.sum(update * update, axis=(1, 2)), "solver")
    spread = jnp.sqrt(squares / (BLOCK * BLOCK) + EPSILON)
    scaled_update = update / spread[:, None, None]
    direction = jnp.transpose(scaled_update, (1, 0, 2)).reshape(rows_here, nblocks * BLOCK)
    new_weight = (weight.astype(jnp.float32) - LEARN_RATE * direction).astype(jnp.bfloat16)
    new_rows = gather_directly(new_weight, "batch", 1)
    new_cols = lax.all_to_all(
        new_rows, ("hidden", "solver"), split_axis=1, concat_axis=0, tiled=True
    )
    second_sum = transposed_product(new_cols, gathered)
    second_out = second_sum.astype(jnp.bfloat16)
    return (first_out, new_left, new_right, direction, second_out)


def solution(mesh):
    in_specs = (
        P("batch", ("hidden", "solver")),
        P(("hidden", "solver"), "batch"),
        P(("hidden", "solver"), "batch"),
        P("hidden", "batch", None, None),
        P("hidden", "batch", None, None),
    )
    out_specs = (
        P(("hidden", "solver"), "batch"),
        P("hidden", "batch", "solver", None),
        P("hidden", "batch", "solver", None),
        P(("hidden", "solver"), "batch"),
        P(("hidden", "solver"), "batch"),
    )
    return jax.shard_map(body, mesh=mesh, in_specs=in_specs, out_specs=out_specs, check_vma=False)
```

profile of v0, /device:TPU:7, one launch (start us, length us, event | category | flops | bytes accessed | tf_op | source)
XLA Modules:
  0.0 405.0 jit_solution(7480275849484787042)
XLA Ops:
  7.9 84.8 %all-gather.5.cloned.1.call-done = bf16[8192,256]{1,0:T(8,128)(2,1)} async-done(((bf16[256,256]{1,0:T(8,128)(2,1)}), bf16[8192,256]{1,0:T(8,128)(2,1)}) %all-gather.5.cloned.1.call-update) | async-done | bytes 4194320 | tf_op jit(solution)/shard_map/all_gather | solution.py:73
  92.7 3.4 convolution_convert_fusion
  96.2 32.3 %all_to_all.64 = bf16[8,1024,128]{2,1,0:T(8,128)(2,1)S(1)} all-to-all(bf16[8,1024,128]{2,1,0:T(8,128)(2,1)S(1)} %bitcast.48), channel_id=1, replica_groups=mesh['batch'=8,'hidden'=4,'solver'=8] {'batch'}, dimensions={0} | all-to-all | bytes 4194304 | tf_op jit(solution)/shard_map/all_to_all | solution.py:36
  130.5 3.6 all-to-all-start.3
  134.3 5.4 %copy.43 = f32[1,1,1024,1024]{2,3,1,0:T(8,128)} copy(f32[1,1,1024,1024]{3,2,1,0:T(8,128)} %param.8) | data formatting | bytes 8388608 | tf_op args[3]
  139.7 5.3 %copy.47 = f32[1,1,1024,1024]{2,3,1,0:T(8,128)} copy(f32[1,1,1024,1024]{3,2,1,0:T(8,128)} %param.9) | data formatting | bytes 8388608 | tf_op args[4]
  145.0 15.2 %all-to-all-done.3 = bf16[8,1,1024,128]{3,2,1,0:T(8,128)(2,1)S(1)} async-done(((bf16[8,1,1024,128]{3,2,1,0:T(8,128)(2,1)}), bf16[8,1,1024,128]{3,2,1,0:T(8,128)(2,1)S(1)}, u32[]{:S(2)}, u32[]{:S(2)}) %all-to-all-start.3) | async-done | bytes 2097184 | tf_op jit(solution)/shard_map/all_to_all | solution.py:22
  162.1 6.9 %all-to-all-start = ((bf16[8,128,1024]{1,2,0:T(8,128)(2,1)}), bf16[8,128,1024]{1,2,0:T(8,128)(2,1)}, u32[]{:S(2)}, u32[]{:S(2)}) async-start(bf16[8,128,1024]{1,2,0:T(8,128)(2,1)} %broadcast_in_dim.12), calls=%async_computation | async-start | bytes 4194304 | tf_op jit(solution)/shard_map/all_to_all | solution.py:22
  171.6 8.1 %abs_reduce_fusion.1 = (f32[1024]{0:T(1024)S(1)}, f32[1024,1024]{0,1:T(8,128)}) fusion(bf16[1024,1024]{0,1:T(8,128)(2,1)} %bitcast.51, f32[1,1,1024,1024]{2,3,1,0:T(8,128)} %copy.43), kind=kOutput, calls=%fused_computation.10 | convolution fusion | flops 2152725504 | bytes 10489856 | tf_op jit(solution)/shard_map/bnm,bnk->bmk/dot_general | solution.py:83
  184.5 6.8 %abs_reduce_fusion = (f32[1024]{0:T(1024)S(1)}, f32[1024,1024]{0,1:T(8,128)}) fusion(bf16[8,1,1024,128]{3,2,1,0:T(8,128)(2,1)} %copy-done, f32[1,1,1024,1024]{2,3,1,0:T(8,128)S(1)} %copy-done.1), kind=kOutput, calls=%fused_computation.8 | convolution fusion | flops 2152725504 | bytes 10489856 | tf_op jit(solution)/shard_map/bnm,bkm->bnk/dot_general | solution.py:84
  194.1 5.1 %fusion.29 = bf16[128,1024]{1,0:T(8,128)(2,1)S(1)} fusion(f32[1024,1024]{0,1:T(8,128)} %get-tuple-element.10, f32[]{:T(128)S(6)} %div.20, bf16[128,1024]{1,0:T(8,128)(2,1)S(1)} %fusion.45, s32[128]{0:T(128)S(1)} %iota_add_fusion), kind=kOutput, calls=%fused_computation.23 | convolution fusion | flops 543817728 | bytes 4719108 | tf_op jit(solution)/shard_map/bij,bjk->bik/dot_general | solution.py:46
  199.2 3.3 fusion.48
  205.7 3.0 fusion.41
  208.7 5.0 %fusion.34 = bf16[128,1024]{1,0:T(8,128)(2,1)S(1)} fusion(bf16[128,1024]{1,0:T(8,128)(2,1)S(1)} %fusion.41, f32[1024,1024]{0,1:T(8,128)} %get-tuple-element.8, f32[]{:T(128)S(6)} %div.21), kind=kOutput, calls=%fused_computation.25 | convolution fusion | flops 547356672 | bytes 4718596 | tf_op jit(solution)/shard_map/bij,bjk->bik/dot_general | solution.py:46
  213.7 5.7 %multiply_reduce_fusion = (f32[]{:T(128)}, f32[128,1024]{1,0:T(8,128)S(1)}) fusion(f32[]{:T(128)S(6)} %mul.123, f32[1024,1024]{0,1:T(8,128)} %get-tuple-element.8, f32[]{:T(128)S(6)} %div.21, bf16[128,1024]{1,0:T(8,128)(2,1)S(1)} %fusion.34, f32[128,1024]{1,0:T(8,128)S(1)} %fusion.43), kind=kOutput, calls=%fused_computation.35 | convolution fusion | flops 543817728 | bytes 5505036 | tf_op jit(solution)/shard_map/bij,bjk->bik/dot_general | solution.py:46
  220.0 8.2 %all_to_all.65 = f32[8,1,1]{2,1,0:T(1,128)S(1)} all-to-all(f32[8,1,1]{2,1,0:T(1,128)S(1)} %broadcast_in_dim.30), channel_id=1, replica_groups=mesh['batch'=8,'hidden'=4,'solver'=8] {'solver'}, dimensions={0} | all-to-all | bytes 64 | tf_op jit(solution)/shard_map/all_to_all | solution.py:22
  228.2 5.0 %all-to-all-start.1 = ((bf16[128,32,256]{0,2,1:T(8,128)(2,1)}), bf16[128,32,256]{0,2,1:T(8,128)(2,1)S(1)}, u32[]{:S(2)}, u32[]{:S(2)}) async-start(bf16[128,32,256]{0,2,1:T(8,128)(2,1)} %bitcast.1), calls=%async_computation.1 | async-start | bytes 4194304 | tf_op jit(solution)/shard_map/all_to_all | solution.py:68
  235.5 44.7 %all-to-all-done.1 = bf16[128,32,256]{0,2,1:T(8,128)(2,1)S(1)} async-done(((bf16[128,32,256]{0,2,1:T(8,128)(2,1)}), bf16[128,32,256]{0,2,1:T(8,128)(2,1)S(1)}, u32[]{:S(2)}, u32[]{:S(2)}) %all-to-all-start.1) | async-done | bytes 2097184 | tf_op jit(solution)/shard_map/all_to_all | solution.py:68
  281.8 8.5 %all-to-all-start.5 = ((bf16[8,128,1024]{1,2,0:T(8,128)(2,1)}), bf16[8,128,1024]{1,2,0:T(8,128)(2,1)}, u32[]{:S(2)}, u32[]{:S(2)}) async-start(bf16[8,128,1024]{1,2,0:T(8,128)(2,1)} %broadcast_in_dim.31), calls=%async_computation.5 | async-start | bytes 4194304 | tf_op jit(solution)/shard_map/all_to_all | solution.py:22
  291.0 24.0 %all-to-all-done.5 = bf16[8,128,1024]{1,2,0:T(8,128)(2,1)} async-done(((bf16[8,128,1024]{1,2,0:T(8,128)(2,1)}), bf16[8,128,1024]{1,2,0:T(8,128)(2,1)}, u32[]{:S(2)}, u32[]{:S(2)}) %all-to-all-start.5) | async-done | bytes 2097184 | tf_op jit(solution)/shard_map/all_to_all | solution.py:22
  315.0 5.8 %all-to-all-start.6 = ((bf16[128,32,256]{0,2,1:T(8,128)(2,1)}), bf16[128,32,256]{0,2,1:T(8,128)(2,1)}, u32[]{:S(2)}, u32[]{:S(2)}) async-start(bf16[128,32,256]{0,2,1:T(8,128)(2,1)} %bitcast.16), calls=%async_computation.6 | async-start | bytes 4194304 | tf_op jit(solution)/shard_map/all_to_all | solution.py:119
  323.8 61.3 %all-gather.3.cloned.1.call-done = bf16[256,4096]{1,0:T(8,128)(2,1)} async-done(((bf16[256,128]{1,0:T(8,128)(2,1)}), bf16[256,4096]{1,0:T(8,128)(2,1)}) %all-gather.3.cloned.1.call-update) | async-done | bytes 2097168 | tf_op jit(solution)/shard_map/all_gather | solution.py:67
  385.0 3.6 convolution_convert_fusion.2
  391.9 3.3 copy.51
  (35 shorter events, 30.4 us)
Async XLA Ops:
  7.2 85.6 %all-gather.5.cloned.1.call-start = ((), (), s32[]{:S(2)}) async-start(), calls=%async_computation.8 | async-start | bytes 4325376 | tf_op jit(solution)/shard_map/all_gather | solution.py:73
  128.4 5.7 %copy-start.3 = (bf16[128,1024]{1,0:T(8,128)(2,1)S(1)}, bf16[128,1024]{1,0:T(8,128)(2,1)}, u32[]{:S(2)}) copy-start(bf16[128,1024]{1,0:T(8,128)(2,1)} %param.7) | copy-start | bytes 786436
  130.5 29.8 %all-to-all-start.3 = ((bf16[8,1,1024,128]{3,2,1,0:T(8,128)(2,1)}), bf16[8,1,1024,128]{3,2,1,0:T(8,128)(2,1)S(1)}, u32[]{:S(2)}, u32[]{:S(2)}) async-start(bf16[8,1,1024,128]{3,2,1,0:T(8,128)(2,1)} %broadcast_in_dim.13), calls=%async_computation.3 | async-start | bytes 4194304 | tf_op jit(solution)/shard_map/all_to_all | solution.py:22
  160.2 11.3 %copy-start = (bf16[8,1,1024,128]{3,2,1,0:T(8,128)(2,1)}, bf16[8,1,1024,128]{3,2,1,0:T(8,128)(2,1)S(1)}, u32[]{:S(2)}) copy-start(bf16[8,1,1024,128]{3,2,1,0:T(8,128)(2,1)S(1)} %all-to-all-done.3) | copy-start | bytes 6291460
  162.1 57.3 %all-to-all-start = ((bf16[8,128,1024]{1,2,0:T(8,128)(2,1)}), bf16[8,128,1024]{1,2,0:T(8,128)(2,1)}, u32[]{:S(2)}, u32[]{:S(2)}) async-start(bf16[8,128,1024]{1,2,0:T(8,128)(2,1)} %broadcast_in_dim.12), calls=%async_computation | async-start | bytes 4194304 | tf_op jit(solution)/shard_map/all_to_all | solution.py:22
  181.0 3.5 copy-start.1
  194.1 5.2 %copy-start.2 = (bf16[1,1024,8,128]{1,3,2,0:T(8,128)(2,1)S(1)}, bf16[1,1024,8,128]{1,3,2,0:T(8,128)(2,1)}, u32[]{:S(2)}) copy-start(bf16[1,1024,8,128]{1,3,2,0:T(8,128)(2,1)} %copy.45) | copy-start | bytes 6291460
  228.2 52.0 %all-to-all-start.1 = ((bf16[128,32,256]{0,2,1:T(8,128)(2,1)}), bf16[128,32,256]{0,2,1:T(8,128)(2,1)S(1)}, u32[]{:S(2)}, u32[]{:S(2)}) async-start(bf16[128,32,256]{0,2,1:T(8,128)(2,1)} %bitcast.1), calls=%async_computation.1 | async-start | bytes 4194304 | tf_op jit(solution)/shard_map/all_to_all | solution.py:68
  281.8 33.2 %all-to-all-start.5 = ((bf16[8,128,1024]{1,2,0:T(8,128)(2,1)}), bf16[8,128,1024]{1,2,0:T(8,128)(2,1)}, u32[]{:S(2)}, u32[]{:S(2)}) async-start(bf16[8,128,1024]{1,2,0:T(8,128)(2,1)} %broadcast_in_dim.31), calls=%async_computation.5 | async-start | bytes 4194304 | tf_op jit(solution)/shard_map/all_to_all | solution.py:22
  290.3 94.7 %all-gather.3.cloned.1.call-start = ((), (), s32[]{:S(2)}) async-start(), calls=%async_computation.7 | async-start | bytes 2162688 | tf_op jit(solution)/shard_map/all_gather | solution.py:67
  315.0 76.9 %all-to-all-start.6 = ((bf16[128,32,256]{0,2,1:T(8,128)(2,1)}), bf16[128,32,256]{0,2,1:T(8,128)(2,1)}, u32[]{:S(2)}, u32[]{:S(2)}) async-start(bf16[128,32,256]{0,2,1:T(8,128)(2,1)} %bitcast.16), calls=%async_computation.6 | async-start | bytes 4194304 | tf_op jit(solution)/shard_map/all_to_all | solution.py:119
Sparse Core Ops, SparseCore 0:
  10.6 82.0 all-gather.4
  293.6 91.3 all-gather.2
where the time goes:
time: 408 us; the launch traced here: 405 us
  waiting for transfers between devices  231 us (57%)
  matrix products  51.7 us (13%)
  blocking collectives  40.4 us (10%)
  starting transfers between devices  29.8 us (7%)
  local copies, waits for them, and re-layouts  29.3 us (7%)
  between operations  16.4 us (4%)
  other arithmetic  6.1 us (1%)
    all_gather x1, waiting for transfers between devices, body(): lax.all_gather(cotangent, ('hidden', 'solver'), axis=0, tiled=True)  84.8 us
    all_gather x1, waiting for transfers between devices, body(): lax.all_gather(activations, ('hidden', 'solver'), axis=1, tiled=True)  61.3 us
    all_to_all x1, waiting for transfers between devices, body(): lax.all_to_all(weight_rows, ('hidden', 'solver'), split_axis=1, concat_ax...  44.7 us
    all_to_all x3, waiting for transfers between devices, sent_to_all(): return lax.all_to_all(copies, axis, split_axis=0, concat_axis=0, tiled=True)  39.2 us
    all_to_all x1, blocking collectives, summed_on_arrival(): lax.all_to_all(blocks, axis, split_axis=0, concat_axis=0, tiled=True)  32.3 us
    dot_general x6, matrix products, product(): jnp.einsum('bij,bjk->bik', left_mat, right_mat, preferred_element_type=jn...  23.4 us
    all_to_all x3, starting transfers between devices, sent_to_all(): return lax.all_to_all(copies, axis, split_axis=0, concat_axis=0, tiled=True)  19.1 us
    unnamed x11, local copies, waits for them, and re-layouts  11.3 us
  transfers between devices with their start and end apart: 7, of which 5 were waited for; matrix products, arithmetic and copies ran while one was open for 17% of the time, Pallas kernels for 0%

commit v1 on v0

v1 whole, which is shorter than its diff:
```python
import functools

import jax
import jax.numpy as jnp
from jax import lax
from jax.experimental import pallas as pl
from jax.experimental.pallas import tpu as pltpu
from jax.sharding import Mesh
from jax.sharding import PartitionSpec as P

BLOCK = 1024
STAT_DECAY = 0.8
LEARN_RATE = 0.005
EPSILON = 1e-06

AXES = ("x", "c", "zh", "zl", "y")
BATCH = ("x", "c")
ZAX = ("zh", "zl")
SOLVER = ("zl", "y")
PLANE = ("x", "c", "y")
MIB = 1 << 20

SWAP = [
    ((b * 8 + z) * 4 + y, (z * 8 + b) * 4 + y) for b in range(8) for z in range(8) for y in range(4)
]


def copies_to(shard, axis, count):
    copies = jnp.broadcast_to(shard, (count, *shard.shape))
    return lax.all_to_all(copies, axis, split_axis=0, concat_axis=0, tiled=True)


def swap_batch_z(value):
    return lax.ppermute(value, AXES, SWAP)


def dot(a, b):
    return jnp.dot(a, b, preferred_element_type=jnp.float32)


def vmem_call(body, out_shape, scratch=(), smem_args=0, n_args=0, limit=32, name=None):
    in_specs = [pl.BlockSpec(memory_space=pltpu.SMEM)] * smem_args
    in_specs += [pl.BlockSpec(memory_space=pltpu.VMEM)] * n_args
    return pl.pallas_call(
        body,
        out_shape=out_shape,
        in_specs=in_specs,
        out_specs=jax.tree.map(lambda _: pl.BlockSpec(memory_space=pltpu.VMEM), out_shape),
        scratch_shapes=list(scratch),
        compiler_params=pltpu.CompilerParams(vmem_limit_bytes=limit * MIB),
        name=name,
    )


def acts_of(acts_ref, group):
    return jnp.concatenate([acts_ref[group, q] for q in range(4)], axis=1)


def grad_body(cot_ref, acts_ref, out_ref):
    total = dot(cot_ref[0], acts_of(acts_ref, 0))
    for group in range(1, 8):
        total = total + dot(cot_ref[group], acts_of(acts_ref, group))
    out_ref[...] = total.astype(jnp.bfloat16)


def grad_piece(cot_all, acts_all):
    return vmem_call(
        grad_body, jax.ShapeDtypeStruct((256, 512), jnp.bfloat16), n_args=2, name="grad_piece"
    )(cot_all, acts_all)


def forward_groups(weight_t, acts_ref, out_ref):
    for group in range(8):
        out_ref[group] = lax.dot_general(
            weight_t,
            acts_of(acts_ref, group),
            (((1,), (1,)), ((), ())),
            preferred_element_type=jnp.float32,
        ).astype(jnp.bfloat16)


def first_body(weight_ref, acts_ref, out_ref):
    weight = weight_ref[...].reshape(512, 256)
    forward_groups(weight.T, acts_ref, out_ref)


def second_body(squares_ref, weight_ref, update_ref, acts_ref, out_ref):
    mean = jnp.sum(squares_ref[...], axis=0)[:1, :1] / (BLOCK * BLOCK)
    rate = LEARN_RATE / jnp.sqrt(mean + EPSILON)
    weight = weight_ref[...].reshape(512, 256).astype(jnp.float32)
    update = update_ref[...].reshape(512, 256).astype(jnp.float32)
    new_weight = (weight - rate * update).astype(jnp.bfloat16)
    forward_groups(new_weight.T, acts_ref, out_ref)


PARTIAL = jax.ShapeDtypeStruct((8, 256, 256), jnp.bfloat16)


def first_partial(weight_cols, acts_all):
    return vmem_call(first_body, PARTIAL, n_args=2, name="first_partial")(weight_cols, acts_all)


def second_partial(squares, weight_cols, update_cols, acts_all):
    return vmem_call(second_body, PARTIAL, n_args=4, name="second_partial")(
        squares, weight_cols, update_cols, acts_all
    )


def statistics(lhs_ref, rhs_ref, old_ref, full_ref, off_ref):
    tile = 256
    sums = jnp.zeros((1, BLOCK), jnp.float32)
    diag = jnp.zeros((1, BLOCK), jnp.float32)
    for i in range(BLOCK // tile):
        rows = pl.ds(i * tile, tile)
        gram = dot(lhs_ref[rows, :], rhs_ref[...])
        new = STAT_DECAY * old_ref[rows, :] + (1.0 - STAT_DECAY) / BLOCK * gram
        full_ref[rows, :] = new
        sums = sums + jnp.sum(jnp.abs(new), axis=0, keepdims=True)
        row = lax.broadcasted_iota(jnp.int32, (tile, BLOCK), 0) + i * tile
        col = lax.broadcasted_iota(jnp.int32, (tile, BLOCK), 1)
        on_diag = row == col
        diag = diag + jnp.sum(jnp.where(on_diag, new, 0.0), axis=0, keepdims=True)
        off_ref[rows, :] = jnp.where(on_diag, 0.0, new).astype(jnp.bfloat16)
    scale = 2.5 / (jnp.max(sums, axis=1, keepdims=True) + EPSILON)
    return scale, diag


def times_factor(rows, off_ref, diag):
    return rows * diag + dot(rows.astype(jnp.bfloat16), off_ref[...])


def times_root(start, off_ref, diag, quarter):
    value = start
    for _ in range(4):
        value = 1.25 * value - quarter * times_factor(value, off_ref, diag)
    return 1.25 * start - quarter * times_factor(value, off_ref, diag)


def solver_body(
    place_ref,
    pieces_ref,
    left_old_ref,
    right_old_ref,
    new_left_ref,
    new_right_ref,
    update_ref,
    sent_ref,
    squares_ref,
    grad_ref,
    grad_t_ref,
    full_ref,
    off_left_ref,
    off_right_ref,
):
    first = pl.multiple_of(place_ref[0] * 128, 128)
    own = pl.ds(first, 128)
    for zl in range(2):
        for y in range(4):
            piece = pieces_ref[zl * 4 + y]
            grad_ref[pl.ds(y * 256, 256), pl.ds(zl * 512, 512)] = piece
            grad_t_ref[pl.ds(zl * 512, 512), pl.ds(y * 256, 256)] = piece.T
    scale_left, diag_left = statistics(grad_t_ref, grad_ref, left_old_ref, full_ref, off_left_ref)
    left_rows = full_ref[own, :]
    new_left_ref[...] = left_rows
    scale_right, diag_right = statistics(
        grad_ref, grad_t_ref, right_old_ref, full_ref, off_right_ref
    )
    new_right_ref[...] = full_ref[own, :]
    quarter_left = scale_left * 0.25
    quarter_right = scale_right * 0.25
    row = lax.broadcasted_iota(jnp.int32, (128, BLOCK), 0) + first
    col = lax.broadcasted_iota(jnp.int32, (128, BLOCK), 1)
    start = jnp.where(row == col, 1.25, 0.0) - quarter_left * left_rows
    root = jnp.sqrt(jnp.sqrt(scale_left)) * times_root(start, off_left_ref, diag_left, quarter_left)
    high = root.astype(jnp.bfloat16)
    low = (root - high.astype(jnp.float32)).astype(jnp.bfloat16)
    both = dot(jnp.concatenate([high, low], axis=0), grad_t_ref[...])
    mixed = both[:128] + both[128:]
    turned = 1.25 * mixed - quarter_right * times_factor(mixed, off_right_ref, diag_right)
    update = jnp.sqrt(jnp.sqrt(scale_right)) * times_root(
        turned, off_right_ref, diag_right, quarter_right
    )
    update_ref[...] = update
    for y in range(4):
        sent_ref[y] = update[:, y * 256 : (y + 1) * 256].astype(jnp.bfloat16)
    squares = jnp.sum(jnp.sum(update * update, axis=0, keepdims=True), axis=1, keepdims=True)
    squares_ref[...] = jnp.broadcast_to(squares, (8, 128))


def solve(place, pieces, left_old, right_old):
    shape = jax.ShapeDtypeStruct
    return vmem_call(
        solver_body,
        (
            shape((128, BLOCK), jnp.float32),
            shape((128, BLOCK), jnp.float32),
            shape((128, BLOCK), jnp.float32),
            shape((4, 128, 256), jnp.bfloat16),
            shape((8, 128), jnp.float32),
        ),
        scratch=[
            pltpu.VMEM((BLOCK, BLOCK), jnp.bfloat16),
            pltpu.VMEM((BLOCK, BLOCK), jnp.bfloat16),
            pltpu.VMEM((BLOCK, BLOCK), jnp.float32),
            pltpu.VMEM((BLOCK, BLOCK), jnp.bfloat16),
            pltpu.VMEM((BLOCK, BLOCK), jnp.bfloat16),
        ],
        smem_args=1,
        n_args=3,
        limit=40,
        name="solve",
    )(place, pieces, left_old, right_old)


def finish(partial):
    arrived = lax.all_to_all(partial, ZAX, split_axis=0, concat_axis=0, tiled=True)
    return swap_batch_z(arrived.astype(jnp.float32).sum(axis=0).astype(jnp.bfloat16))


def body(activations, cotangent, weight, left_old, right_old):
    cot_turned = swap_batch_z(cotangent)
    acts_all = copies_to(activations, PLANE, 32).reshape(8, 4, 256, 128)
    cot_all = copies_to(cot_turned, ZAX, 8)
    weight_parts = jnp.transpose(weight.reshape(128, 4, 256), (1, 0, 2))
    weight_cols = lax.all_to_all(weight_parts, "y", split_axis=0, concat_axis=0, tiled=True)
    piece = grad_piece(cot_all, acts_all)
    pieces = copies_to(piece, SOLVER, 8)
    first_out = finish(first_partial(weight_cols, acts_all))
    place = (lax.axis_index("zl") * 4 + lax.axis_index("y")).astype(jnp.int32).reshape(1)
    new_left, new_right, update, sent, squares = solve(
        place, pieces, left_old[0, 0], right_old[0, 0]
    )
    update_cols = lax.all_to_all(sent, "y", split_axis=0, concat_axis=0, tiled=True)
    squares_all = copies_to(squares, SOLVER, 8)
    second_out = finish(second_partial(squares_all, weight_cols, update_cols, acts_all))
    total = jnp.sum(squares_all[:, 0, 0])
    direction = update / jnp.sqrt(total / (BLOCK * BLOCK) + EPSILON)
    return (first_out, new_left[None, None], new_right[None, None], direction, second_out)


def solution(mesh):
    fine = Mesh(mesh.devices.reshape(4, 2, 4, 2, 4), AXES)
    rows = ("zh", "zl", "y")
    in_specs = (
        P(BATCH, rows),
        P(rows, BATCH),
        P(rows, BATCH),
        P("zh", BATCH, None, None),
        P("zh", BATCH, None, None),
    )
    out_specs = (
        P(rows, BATCH),
        P("zh", BATCH, SOLVER, None),
        P("zh", BATCH, SOLVER, None),
        P(rows, BATCH),
        P(rows, BATCH),
    )
    return jax.shard_map(body, mesh=fine, in_specs=in_specs, out_specs=out_specs, check_vma=False)
```

time: 408 us -> 245 us (0.60)
  waiting for transfers between devices: 231 us -> 98.7 us
  matrix products: 51.7 us -> 0 us
  blocking collectives: 40.4 us -> 77.3 us
  local copies, waits for them, and re-layouts: 29.3 us -> 8.74 us
  Pallas kernels: 0 us -> 16.3 us
  between operations: 16.4 us -> 1.47 us
  starting transfers between devices: 29.8 us -> 38.4 us
    all_gather x2 -> x0, waiting for transfers between devices: 146 us -> none  [the longest x1 84.8 us: body(): lax.all_gather(cotangent, ('hidden', 'solver'), axis=0, tiled=True)]
    dot_general x12 -> x0, matrix products: 51.7 us -> none  [the longest x6 23.4 us: product(): jnp.einsum('bij,bjk->bik', left_mat, right_mat, preferred_element_type=jn...]
    ppermute x0 -> x3, waiting for transfers between devices: none -> 45.5 us  [swap_batch_z(): return lax.ppermute(value, AXES, SWAP)]
    all_to_all x2 -> x3, blocking collectives: 40.4 us -> 77.3 us  [copies_to(): return lax.all_to_all(copies, axis, split_axis=0, concat_axis=0, tiled=True)]
    all_to_all x5, waiting for transfers between devices: 83.9 us -> 53.3 us  [the longest x1 25.2 us: copies_to(): return lax.all_to_all(copies, axis, split_axis=0, concat_axis=0, tiled=True)]
    ppermute x0 -> x3, starting transfers between devices: none -> 19.3 us  [swap_batch_z(): return lax.ppermute(value, AXES, SWAP)]
    pallas_call x0 -> x4, Pallas kernels: none -> 16.3 us  [the longest x1 12.1 us: solve(): vmem_call(solver_body, (shape((128, BLOCK), jnp.float32), shape((128, BLO...]
    all_to_all x5, starting transfers between devices: 29.8 us -> 19.1 us  [the longest x2 7.81 us: finish(): lax.all_to_all(partial, ZAX, split_axis=0, concat_axis=0, tiled=True)]
  transfers between devices with their start and end apart: 7 -> 8, of which waited for: 5 -> 6; matrix products, arithmetic and copies ran while one was open for 17% -> 2% of each run, Pallas kernels for 0% -> 6%
where the time goes in v1:
time: 245 us; the launch traced here: 244 us
  waiting for transfers between devices  98.7 us (40%)
  blocking collectives  77.3 us (32%)
  starting transfers between devices  38.4 us (16%)
  Pallas kernels  16.3 us (7%)
  local copies, waits for them, and re-layouts  8.74 us (4%)
  other arithmetic  2.99 us (1%)
    all_to_all x3, blocking collectives, copies_to(): return lax.all_to_all(copies, axis, split_axis=0, concat_axis=0, tiled=True)  77.3 us
    ppermute x3, waiting for transfers between devices, swap_batch_z(): return lax.ppermute(value, AXES, SWAP)  45.5 us
    all_to_all x1, waiting for transfers between devices, copies_to(): return lax.all_to_all(copies, axis, split_axis=0, concat_axis=0, tiled=True)  25.2 us
    all_to_all x2, waiting for transfers between devices, finish(): lax.all_to_all(partial, ZAX, split_axis=0, concat_axis=0, tiled=True)  24.3 us
    ppermute x3, starting transfers between devices, swap_batch_z(): return lax.ppermute(value, AXES, SWAP)  19.3 us
    pallas_call x1, Pallas kernels, solve(): vmem_call(solver_body, (shape((128, BLOCK), jnp.float32), shape((128, BLO...  12.1 us
    all_to_all x2, starting transfers between devices, finish(): lax.all_to_all(partial, ZAX, split_axis=0, concat_axis=0, tiled=True)  7.81 us
    unnamed x11, local copies, waits for them, and re-layouts  5.86 us
  transfers between devices with their start and end apart: 8, of which 6 were waited for; matrix products, arithmetic and copies ran while one was open for 2% of the time, Pallas kernels for 6%

profile of v1, /device:TPU:7, one launch (start us, length us, event | category | flops | bytes accessed | tf_op | source)
XLA Modules:
  0.0 244.0 jit_solution(10310994947792898155)
XLA Ops:
  0.6 8.1 %collective-permute-start.1 = (bf16[256,256]{1,0:T(8,128)(2,1)}, bf16[256,256]{1,0:T(8,128)(2,1)S(1)}, u32[]{:S(2)}, u32[]{:S(2)}) collective-permute-start(bf16[256,256]{1,0:T(8,128)(2,1)} %param.6), channel_id=1, source_target_pairs={{0,0},{1,1},{2,2},{3,3},{4,32},{5,33},{6,34},{7,35},{8,64},{9,65},... | collective-permute-start | bytes 393224 | tf_op jit(solution)/shard_map/ppermute | solution.py:34
  8.7 9.7 %collective-permute-done.1 = bf16[256,256]{1,0:T(8,128)(2,1)S(1)} collective-permute-done((bf16[256,256]{1,0:T(8,128)(2,1)}, bf16[256,256]{1,0:T(8,128)(2,1)S(1)}, u32[]{:S(2)}, u32[]{:S(2)}) %collective-permute-start.1) | collective-permute-done | bytes 131104 | tf_op jit(solution)/shard_map/ppermute | solution.py:34
  18.5 27.2 %all_to_all.40.cot_ref = bf16[8,256,256]{2,1,0:T(8,128)(2,1)S(1)} all-to-all(bf16[8,256,256]{2,1,0:T(8,128)(2,1)S(1)} %broadcast_in_dim.19), channel_id=1, replica_groups=mesh['x'=4,'c'=2,'zh'=4,'zl'=2,'y'=4] {'zh','zl'}, dimensions={0} | all-to-all | bytes 2097152 | tf_op jit(solution)/shard_map/all_to_all | solution.py:30
  46.1 40.1 %all_to_all.41 = bf16[32,256,128]{2,1,0:T(8,128)(2,1)S(1)} all-to-all(bf16[32,256,128]{2,1,0:T(8,128)(2,1)S(1)} %broadcast_in_dim.18), channel_id=1, replica_groups=mesh['x'=4,'c'=2,'zh'=4,'zl'=2,'y'=4] {'x','c','y'}, dimensions={0} | all-to-all | bytes 4194304 | tf_op jit(solution)/shard_map/all_to_all | solution.py:30
  86.9 1.5 broadcast_in_dim.20
  88.4 4.5 %all-to-all-start.4 = ((bf16[8,256,512]{2,1,0:T(8,128)(2,1)}), bf16[8,256,512]{2,1,0:T(8,128)(2,1)}, u32[]{:S(2)}, u32[]{:S(2)}) async-start(bf16[8,256,512]{2,1,0:T(8,128)(2,1)} %broadcast_in_dim.20), calls=%async_computation.4 | async-start | bytes 4194304 | tf_op jit(solution)/shard_map/all_to_all | solution.py:30
  94.0 25.2 %all-to-all-done.4.pieces_ref = bf16[8,256,512]{2,1,0:T(8,128)(2,1)} async-done(((bf16[8,256,512]{2,1,0:T(8,128)(2,1)}), bf16[8,256,512]{2,1,0:T(8,128)(2,1)}, u32[]{:S(2)}, u32[]{:S(2)}) %all-to-all-start.4) | async-done | bytes 2097184 | tf_op jit(solution)/shard_map/all_to_all | solution.py:30
  119.1 3.4 %all-to-all-start = ((bf16[4,128,256]{2,1,0:T(8,128)(2,1)}), bf16[4,128,256]{2,1,0:T(8,128)(2,1)S(1)}, u32[]{:S(2)}, u32[]{:S(2)}) async-start(bf16[4,128,256]{2,1,0:T(8,128)(2,1)} %bitcast.1), calls=%async_computation | async-start | bytes 524288 | tf_op jit(solution)/shard_map/all_to_all | solution.py:225
  122.6 2.2 copy-done
  124.8 2.2 copy-done.1
  126.9 12.1 %solve.1 = (f32[128,1024]{1,0:T(8,128)}, f32[128,1024]{1,0:T(8,128)}, f32[128,1024]{1,0:T(8,128)S(1)}, bf16[4,128,256]{2,1,0:T(8,128)(2,1)}, f32[8,128]{1,0:T(8,128)S(1)}) custom-call(s32[1]{0:T(128)} %bitcast.3.place_ref, bf16[8,256,512]{2,1,0:T(8,128)(2,1)} %all-to-all-done.4.pieces_ref, f32[1024,1024]{1,0:T(8,128)S(1)} %bitcast.11, f32[1024,1024]{1,0:T(8,128)S(1)} %bitcast.12), custom_call_target="tpu_custom_call" | custom-call | tf_op jit(solution)/shard_map/solve/pallas_call | solution.py:192
  139.0 10.0 %all_to_all.42.squares_ref = f32[8,8,128]{2,1,0:T(8,128)S(1)} all-to-all(f32[8,8,128]{2,1,0:T(8,128)S(1)} %broadcast_in_dim.23), channel_id=1, replica_groups=mesh['x'=4,'c'=2,'zh'=4,'zl'=2,'y'=4] {'zl','y'}, dimensions={0} | all-to-all | bytes 65536 | tf_op jit(solution)/shard_map/all_to_all | solution.py:30
  149.1 3.4 %all-to-all-start.6 = ((bf16[4,128,256]{2,1,0:T(8,128)(2,1)}), bf16[4,128,256]{2,1,0:T(8,128)(2,1)S(1)}, u32[]{:S(2)}, u32[]{:S(2)}) async-start(bf16[4,128,256]{2,1,0:T(8,128)(2,1)} %get-tuple-element.14), calls=%async_computation.6 | async-start | bytes 524288 | tf_op jit(solution)/shard_map/all_to_all | solution.py:233
  152.5 1.7 first_partial.1
  154.2 3.8 %all-to-all-done.6.update_ref = bf16[4,128,256]{2,1,0:T(8,128)(2,1)S(1)} async-done(((bf16[4,128,256]{2,1,0:T(8,128)(2,1)}), bf16[4,128,256]{2,1,0:T(8,128)(2,1)S(1)}, u32[]{:S(2)}, u32[]{:S(2)}) %all-to-all-start.6) | async-done | bytes 262176 | tf_op jit(solution)/shard_map/all_to_all | solution.py:233
  158.0 4.3 %all-to-all-start.2 = ((bf16[8,256,256]{2,1,0:T(8,128)(2,1)}), bf16[8,256,256]{2,1,0:T(8,128)(2,1)}, u32[]{:S(2)}, u32[]{:S(2)}) async-start(bf16[8,256,256]{2,1,0:T(8,128)(2,1)} %first_partial.1), calls=%async_computation.2 | async-start | bytes 2097152 | tf_op jit(solution)/shard_map/all_to_all | solution.py:216
  162.2 1.8 second_partial.1
  164.0 24.3 %all-to-all-done.2 = bf16[8,256,256]{2,1,0:T(8,128)(2,1)} async-done(((bf16[8,256,256]{2,1,0:T(8,128)(2,1)}), bf16[8,256,256]{2,1,0:T(8,128)(2,1)}, u32[]{:S(2)}, u32[]{:S(2)}) %all-to-all-start.2) | async-done | bytes 1048608 | tf_op jit(solution)/shard_map/all_to_all | solution.py:216
  188.3 3.6 %all-to-all-start.7 = ((bf16[8,256,256]{2,1,0:T(8,128)(2,1)}), bf16[8,256,256]{2,1,0:T(8,128)(2,1)S(1)}, u32[]{:S(2)}, u32[]{:S(2)}) async-start(bf16[8,256,256]{2,1,0:T(8,128)(2,1)} %second_partial.1), calls=%async_computation.7 | async-start | bytes 2097152 | tf_op jit(solution)/shard_map/all_to_all | solution.py:216
  191.9 1.4 reduce_sum.33
  193.3 9.3 %collective-permute-start = (bf16[256,256]{1,0:T(8,128)(2,1)S(1)}, bf16[256,256]{1,0:T(8,128)(2,1)S(1)}, u32[]{:S(2)}, u32[]{:S(2)}) collective-permute-start(bf16[256,256]{1,0:T(8,128)(2,1)S(1)} %reduce_sum.33), channel_id=1, source_target_pairs={{0,0},{1,1},{2,2},{3,3},{4,32},{5,33},{6,34},{7,35},{8,64},{9,65},... | collective-permute-start | bytes 393224 | tf_op jit(solution)/shard_map/ppermute | solution.py:34
  202.6 24.9 %collective-permute-done = bf16[256,256]{1,0:T(8,128)(2,1)S(1)} collective-permute-done((bf16[256,256]{1,0:T(8,128)(2,1)S(1)}, bf16[256,256]{1,0:T(8,128)(2,1)S(1)}, u32[]{:S(2)}, u32[]{:S(2)}) %collective-permute-start) | collective-permute-done | bytes 131104 | tf_op jit(solution)/shard_map/ppermute | solution.py:34
  229.0 1.9 collective-permute-start.2
  231.8 10.9 %collective-permute-done.2 = bf16[256,256]{1,0:T(8,128)(2,1)S(1)} collective-permute-done((bf16[256,256]{1,0:T(8,128)(2,1)S(1)}, bf16[256,256]{1,0:T(8,128)(2,1)S(1)}, u32[]{:S(2)}, u32[]{:S(2)}) %collective-permute-start.2) | collective-permute-done | bytes 131104 | tf_op jit(solution)/shard_map/ppermute | solution.py:34
  (19 shorter events, 5.2 us)
Async XLA Ops:
  0.6 45.0 %copy-start.3 = (bf16[256,128]{1,0:T(8,128)(2,1)S(1)}, bf16[256,128]{1,0:T(8,128)(2,1)}, u32[]{:S(2)}) copy-start(bf16[256,128]{1,0:T(8,128)(2,1)} %param.5) | copy-start | bytes 196612
  0.6 17.7 %collective-permute-start.1 = (bf16[256,256]{1,0:T(8,128)(2,1)}, bf16[256,256]{1,0:T(8,128)(2,1)S(1)}, u32[]{:S(2)}, u32[]{:S(2)}) collective-permute-start(bf16[256,256]{1,0:T(8,128)(2,1)} %param.6), channel_id=1, source_target_pairs={{0,0},{1,1},{2,2},{3,3},{4,32},{5,33},{6,34},{7,35},{8,64},{9,65},... | collective-permute-start | bytes 393224 | tf_op jit(solution)/shard_map/ppermute | solution.py:34
  88.4 4.5 %copy-start.2 = (bf16[128,1024]{1,0:T(8,128)(2,1)S(1)}, bf16[128,1024]{1,0:T(8,128)(2,1)}, u32[]{:S(2)}) copy-start(bf16[128,1024]{1,0:T(8,128)(2,1)} %param.7) | copy-start | bytes 786436
  88.4 30.7 %all-to-all-start.4 = ((bf16[8,256,512]{2,1,0:T(8,128)(2,1)}), bf16[8,256,512]{2,1,0:T(8,128)(2,1)}, u32[]{:S(2)}, u32[]{:S(2)}) async-start(bf16[8,256,512]{2,1,0:T(8,128)(2,1)} %broadcast_in_dim.20), calls=%async_computation.4 | async-start | bytes 4194304 | tf_op jit(solution)/shard_map/all_to_all | solution.py:30
  119.1 19.9 %all-to-all-start = ((bf16[4,128,256]{2,1,0:T(8,128)(2,1)}), bf16[4,128,256]{2,1,0:T(8,128)(2,1)S(1)}, u32[]{:S(2)}, u32[]{:S(2)}) async-start(bf16[4,128,256]{2,1,0:T(8,128)(2,1)} %bitcast.1), calls=%async_computation | async-start | bytes 524288 | tf_op jit(solution)/shard_map/all_to_all | solution.py:225
  122.6 2.2 copy-start
  124.8 2.2 copy-start.1
  149.1 8.9 %all-to-all-start.6 = ((bf16[4,128,256]{2,1,0:T(8,128)(2,1)}), bf16[4,128,256]{2,1,0:T(8,128)(2,1)S(1)}, u32[]{:S(2)}, u32[]{:S(2)}) async-start(bf16[4,128,256]{2,1,0:T(8,128)(2,1)} %get-tuple-element.14), calls=%async_computation.6 | async-start | bytes 524288 | tf_op jit(solution)/shard_map/all_to_all | solution.py:233
  158.0 30.4 %all-to-all-start.2 = ((bf16[8,256,256]{2,1,0:T(8,128)(2,1)}), bf16[8,256,256]{2,1,0:T(8,128)(2,1)}, u32[]{:S(2)}, u32[]{:S(2)}) async-start(bf16[8,256,256]{2,1,0:T(8,128)(2,1)} %first_partial.1), calls=%async_computation.2 | async-start | bytes 2097152 | tf_op jit(solution)/shard_map/all_to_all | solution.py:216
  188.3 40.5 %all-to-all-start.7 = ((bf16[8,256,256]{2,1,0:T(8,128)(2,1)}), bf16[8,256,256]{2,1,0:T(8,128)(2,1)S(1)}, u32[]{:S(2)}, u32[]{:S(2)}) async-start(bf16[8,256,256]{2,1,0:T(8,128)(2,1)} %second_partial.1), calls=%async_computation.7 | async-start | bytes 2097152 | tf_op jit(solution)/shard_map/all_to_all | solution.py:216
  193.3 34.2 %collective-permute-start = (bf16[256,256]{1,0:T(8,128)(2,1)S(1)}, bf16[256,256]{1,0:T(8,128)(2,1)S(1)}, u32[]{:S(2)}, u32[]{:S(2)}) collective-permute-start(bf16[256,256]{1,0:T(8,128)(2,1)S(1)} %reduce_sum.33), channel_id=1, source_target_pairs={{0,0},{1,1},{2,2},{3,3},{4,32},{5,33},{6,34},{7,35},{8,64},{9,65},... | collective-permute-start | bytes 393224 | tf_op jit(solution)/shard_map/ppermute | solution.py:34
  229.0 13.7 %collective-permute-start.2 = (bf16[256,256]{1,0:T(8,128)(2,1)S(1)}, bf16[256,256]{1,0:T(8,128)(2,1)S(1)}, u32[]{:S(2)}, u32[]{:S(2)}) collective-permute-start(bf16[256,256]{1,0:T(8,128)(2,1)S(1)} %reduce_sum.35), channel_id=1, source_target_pairs={{0,0},{1,1},{2,2},{3,3},{4,32},{5,33},{6,34},{7,35},{8,64},{9,65},... | collective-permute-start | bytes 393224 | tf_op jit(solution)/shard_map/ppermute | solution.py:34

commit v2 on v1

v2 whole, which is shorter than its diff:
```python
import jax
import jax.numpy as jnp
from jax import lax
from jax.experimental import pallas as pl
from jax.experimental.pallas import tpu as pltpu
from jax.sharding import Mesh
from jax.sharding import PartitionSpec as P

BLOCK = 1024
STAT_DECAY = 0.8
LEARN_RATE = 0.005
EPSILON = 1e-06

AXES = ("x", "c", "zh", "zl", "y")
BATCH = ("x", "c")
ZAX = ("zh", "zl")
SOLVER = ("zl", "y")
MIB = 1 << 20
SHAPE = jax.ShapeDtypeStruct
BF16 = jnp.bfloat16
F32 = jnp.float32


def device(x, c, zh, zl, y):
    return (((x * 2 + c) * 4 + zh) * 2 + zl) * 4 + y


EVERY = [
    (x, c, zh, zl, y)
    for x in range(4)
    for c in range(2)
    for zh in range(4)
    for zl in range(2)
    for y in range(4)
]
SWAP = [(device(*d), device(d[2], d[3], d[0], d[1], d[4])) for d in EVERY]
HOME = [
    [(device(*d), device(d[2], d[3] ^ e, d[0], d[1], d[4])) for d in EVERY] for e in range(2)
]
FLIP = [(0, 1), (1, 0)]


def shift(by):
    return [(i, (i + by) % 4) for i in range(4)]


def copies_to(shard, axis, count):
    copies = jnp.broadcast_to(shard, (count, *shard.shape))
    return lax.all_to_all(copies, axis, split_axis=0, concat_axis=0, tiled=True)


def dot(a, b):
    return jnp.dot(a, b, preferred_element_type=F32)


def dot_minor(a, b):
    return lax.dot_general(a, b, (((1,), (1,)), ((), ())), preferred_element_type=F32)


def vmem_call(body, out_shape, n_args, scratch=(), limit=32, name=None):
    in_specs = [pl.BlockSpec(memory_space=pltpu.SMEM)]
    in_specs += [pl.BlockSpec(memory_space=pltpu.VMEM)] * n_args
    return pl.pallas_call(
        body,
        out_shape=out_shape,
        in_specs=in_specs,
        out_specs=jax.tree.map(lambda _: pl.BlockSpec(memory_space=pltpu.VMEM), out_shape),
        scratch_shapes=list(scratch),
        compiler_params=pltpu.CompilerParams(vmem_limit_bytes=limit * MIB),
        name=name,
    )


def wide(slab):
    return jnp.concatenate([slab[q] for q in range(4)], axis=1)


def grad_body(place, cot_ref, *refs):
    own, swapped, out_ref, packed_ref = refs[:4], refs[4:8], refs[8], refs[9]
    x, c = place[0], place[1]
    total = jnp.zeros((256, 512), F32)
    for d in range(4):
        at = ((x - d) & 3) * 2
        mine = own[d][...]
        packed_ref[d] = mine
        total = total + dot(cot_ref[at + c], wide(mine))
        total = total + dot(cot_ref[at + 1 - c], wide(swapped[d][...]))
    piece = total.astype(BF16)
    for s in range(8):
        out_ref[s] = piece


def grad_piece(place, cot_all, own, swapped):
    return vmem_call(
        grad_body,
        (SHAPE((8, 256, 512), BF16), SHAPE((4, 4, 256, 128), BF16)),
        n_args=9,
        name="grad_piece",
    )(place, cot_all, *own, *swapped)


def forward_groups(place, near_t, far_t, near_refs, far_refs, out_ref):
    x, c = place[0], place[1]
    near0, near1 = near_refs
    far0, far1 = far_refs
    for d in range(4):
        at = (x - d) & 3
        out_ref[at, c] = (
            dot_minor(near_t, wide(near0[d])) + dot_minor(far_t, wide(far0[d]))
        ).astype(BF16)
        out_ref[at, 1 - c] = (
            dot_minor(near_t, wide(near1[d][...])) + dot_minor(far_t, wide(far1[d]))
        ).astype(BF16)


def weight_of(place, mixed_ref, far_ref):
    start = pl.multiple_of(256 + place[3] * 128, 128)
    near = jnp.concatenate([mixed_ref[q, pl.ds(start, 128), :] for q in range(4)], axis=0)
    far = jnp.concatenate([far_ref[q] for q in range(4)], axis=0)
    return near, far


def first_body(place, mixed_ref, far_ref, near0, n0, n1, n2, n3, far0, far1, *refs):
    outs, work = refs[:4], refs[4]
    near, far = weight_of(place, mixed_ref, far_ref)
    forward_groups(place, near.T, far.T, (near0, (n0, n1, n2, n3)), (far0, far1), work)
    for e in range(4):
        outs[e][...] = work[(place[2] + e) & 3]


def second_body(
    place, update_ref, mixed_ref, far_ref, near0, n0, n1, n2, n3, far0, far1, out_ref, spread_ref
):
    near, far = weight_of(place, mixed_ref, far_ref)
    squares = jnp.zeros((16, 128), F32)
    for s in range(8):
        squares = squares + update_ref[s, 128:144, :].astype(F32)
    mean = jnp.sum(squares, axis=0, keepdims=True)[:, :1] / (BLOCK * BLOCK)
    spread = jnp.sqrt(mean + EPSILON)
    spread_ref[...] = jnp.broadcast_to(spread, (8, 128))
    rate = LEARN_RATE / spread
    zl = place[3]

    def changed(weight, first):
        update = jnp.concatenate([update_ref[first + q, :128, :] for q in range(4)], axis=0)
        return (weight.astype(F32) - rate * update.astype(F32)).astype(BF16).T

    near_t = changed(near, zl * 4)
    far_t = changed(far, (1 - zl) * 4)
    forward_groups(place, near_t, far_t, (near0, (n0, n1, n2, n3)), (far0, far1), out_ref)


def first_partial(place, weights, acts):
    part = SHAPE((2, 128, 256), BF16)
    return vmem_call(
        first_body,
        (part, part, part, part),
        n_args=9,
        scratch=[pltpu.VMEM((4, 2, 128, 256), BF16)],
        name="first_partial",
    )(place, *weights, *acts)


def second_partial(place, update_cols, weights, acts):
    return vmem_call(
        second_body,
        (SHAPE((4, 2, 128, 256), BF16), SHAPE((8, 128), F32)),
        n_args=10,
        name="second_partial",
    )(place, update_cols, *weights, *acts)


def add_body(place, *refs):
    parts, outs = refs[:-3], refs[-3:]
    zl, work = place[3], outs[2]
    if len(parts) == 1:
        parts = [parts[0].at[i] for i in range(4)]
    total = parts[0][...].astype(F32)
    for part in parts[1:]:
        total = total + part[...].astype(F32)
    work[...] = total.astype(BF16)
    outs[0][...] = work[zl]
    outs[1][...] = work[1 - zl]


def add_up(place, *parts):
    half = SHAPE((128, 256), BF16)
    return vmem_call(
        add_body,
        (half, half),
        n_args=len(parts),
        scratch=[pltpu.VMEM((2, 128, 256), BF16)],
        name="add_up",
    )(place, *parts)


def send_home(halves):
    straight = lax.ppermute(halves[0], AXES, HOME[0])
    crossed = lax.ppermute(halves[1], AXES, HOME[1])
    even = lax.axis_index("c") == 0
    return jnp.concatenate(
        [jnp.where(even, straight, crossed), jnp.where(even, crossed, straight)], axis=0
    )


def statistics(lhs_ref, rhs_ref, old_ref, full_ref, off_ref):
    tile = 256
    sums = jnp.zeros((1, BLOCK), F32)
    diag = jnp.zeros((1, BLOCK), F32)
    for i in range(BLOCK // tile):
        rows = pl.ds(i * tile, tile)
        gram = dot(lhs_ref[rows, :], rhs_ref[...])
        new = STAT_DECAY * old_ref[rows, :] + (1.0 - STAT_DECAY) / BLOCK * gram
        full_ref[rows, :] = new
        sums = sums + jnp.sum(jnp.abs(new), axis=0, keepdims=True)
        row = lax.broadcasted_iota(jnp.int32, (tile, BLOCK), 0) + i * tile
        col = lax.broadcasted_iota(jnp.int32, (tile, BLOCK), 1)
        on_diag = row == col
        diag = diag + jnp.sum(jnp.where(on_diag, new, 0.0), axis=0, keepdims=True)
        off_ref[rows, :] = jnp.where(on_diag, 0.0, new).astype(BF16)
    scale = 2.5 / (jnp.max(sums, axis=1, keepdims=True) + EPSILON)
    return scale, diag


def times_factor(rows, off_ref, diag):
    return rows * diag + dot(rows.astype(BF16), off_ref[...])


def times_root(start, off_ref, diag, quarter):
    value = start
    for _ in range(4):
        value = 1.25 * value - quarter * times_factor(value, off_ref, diag)
    return 1.25 * start - quarter * times_factor(value, off_ref, diag)


def solver_body(
    place,
    pieces_ref,
    left_old_ref,
    right_old_ref,
    new_left_ref,
    new_right_ref,
    update_ref,
    sent_ref,
    grad_ref,
    grad_t_ref,
    full_ref,
    off_left_ref,
    off_right_ref,
):
    first = pl.multiple_of((place[3] * 4 + place[4]) * 128, 128)
    own = pl.ds(first, 128)
    for zl in range(2):
        for y in range(4):
            piece = pieces_ref[zl * 4 + y]
            grad_ref[pl.ds(y * 256, 256), pl.ds(zl * 512, 512)] = piece
            grad_t_ref[pl.ds(zl * 512, 512), pl.ds(y * 256, 256)] = piece.T
    scale_left, diag_left = statistics(grad_t_ref, grad_ref, left_old_ref, full_ref, off_left_ref)
    left_rows = full_ref[own, :]
    new_left_ref[...] = left_rows
    scale_right, diag_right = statistics(
        grad_ref, grad_t_ref, right_old_ref, full_ref, off_right_ref
    )
    new_right_ref[...] = full_ref[own, :]
    quarter_left = scale_left * 0.25
    quarter_right = scale_right * 0.25
    row = lax.broadcasted_iota(jnp.int32, (128, BLOCK), 0) + first
    col = lax.broadcasted_iota(jnp.int32, (128, BLOCK), 1)
    start = jnp.where(row == col, 1.25, 0.0) - quarter_left * left_rows
    root = jnp.sqrt(jnp.sqrt(scale_left)) * times_root(start, off_left_ref, diag_left, quarter_left)
    high = root.astype(BF16)
    low = (root - high.astype(F32)).astype(BF16)
    both = dot(jnp.concatenate([high, low], axis=0), grad_t_ref[...])
    mixed = both[:128] + both[128:]
    turned = 1.25 * mixed - quarter_right * times_factor(mixed, off_right_ref, diag_right)
    update = jnp.sqrt(jnp.sqrt(scale_right)) * times_root(
        turned, off_right_ref, diag_right, quarter_right
    )
    update_ref[...] = update
    squares = jnp.sum(jnp.sum(update * update, axis=0, keepdims=True), axis=1, keepdims=True)
    high = squares.astype(BF16).astype(F32)
    middle = (squares - high).astype(BF16).astype(F32)
    low = squares - high - middle
    row = lax.broadcasted_iota(jnp.int32, (16, 128), 0)
    tail = jnp.where(row == 0, high, jnp.where(row == 1, middle, jnp.where(row == 2, low, 0.0)))
    tail = tail.astype(BF16)
    for zl in range(2):
        for y in range(4):
            at = y * 256 + zl * 128
            sent_ref[zl * 4 + y, :128, :] = update[:, at : at + 128].astype(BF16)
            sent_ref[zl * 4 + y, 128:, :] = tail


def solve(place, pieces, left_old, right_old):
    square = (BLOCK, BLOCK)
    return vmem_call(
        solver_body,
        (
            SHAPE((128, BLOCK), F32),
            SHAPE((128, BLOCK), F32),
            SHAPE((128, BLOCK), F32),
            SHAPE((8, 144, 128), BF16),
        ),
        n_args=3,
        scratch=[pltpu.VMEM(square, kind) for kind in (BF16, BF16, F32, BF16, BF16)],
        limit=40,
        name="solve",
    )(place, pieces, left_old, right_old)


def body(activations, cotangent, weight, left_old, right_old):
    place = jnp.stack([lax.axis_index(a).astype(jnp.int32) for a in AXES])
    cot_turned = lax.ppermute(cotangent, AXES, SWAP)
    acts_copies = jnp.broadcast_to(activations, (4, 256, 128))
    weight_parts = jnp.transpose(weight.reshape(128, 4, 2, 128), (1, 2, 0, 3)).reshape(4, 256, 128)
    mixed = lax.all_to_all(
        jnp.concatenate([acts_copies, weight_parts], axis=1), "y", 0, 0, tiled=True
    )
    own = [mixed[:, :256]]
    own += [lax.ppermute(own[0], "x", shift(d)) for d in range(1, 4)]
    swapped = [lax.ppermute(slab, "c", FLIP) for slab in own]
    leaving = lax.dynamic_slice_in_dim(mixed, 256 + (1 - lax.axis_index("zl")) * 128, 128, 1)
    weight_far = lax.ppermute(leaving, "zl", FLIP)
    cot_all = copies_to(cot_turned, ZAX, 8)
    copies, packed = grad_piece(place, cot_all, own, swapped)
    far = lax.ppermute(packed, "zl", FLIP)
    far_swapped = lax.ppermute(far, "c", FLIP)
    weights = (mixed, weight_far)
    acts = (packed, *swapped, far, far_swapped)

    pieces = lax.all_to_all(copies, SOLVER, 0, 0, tiled=True)
    new_left, new_right, update, sent = solve(place, pieces, left_old[0, 0], right_old[0, 0])
    update_cols = lax.all_to_all(sent, SOLVER, 0, 0, tiled=True)

    parts = first_partial(place, weights, acts)
    parts = [parts[0]] + [lax.ppermute(parts[e], "zh", shift(e)) for e in range(1, 4)]
    first_out = send_home(add_up(place, *parts))

    second, spread = second_partial(place, update_cols, weights, acts)
    arrived = lax.all_to_all(second, "zh", 0, 0, tiled=True)
    second_out = send_home(add_up(place, arrived))
    direction = update / spread[0, 0]
    return (first_out, new_left[None, None], new_right[None, None], direction, second_out)


def solution(mesh):
    fine = Mesh(mesh.devices.reshape(4, 2, 4, 2, 4), AXES)
    rows = ("zh", "zl", "y")
    in_specs = (
        P(BATCH, rows),
        P(rows, BATCH),
        P(rows, BATCH),
        P("zh", BATCH, None, None),
        P("zh", BATCH, None, None),
    )
    out_specs = (
        P(rows, BATCH),
        P("zh", BATCH, SOLVER, None),
        P("zh", BATCH, SOLVER, None),
        P(rows, BATCH),
        P(rows, BATCH),
    )
    return jax.shard_map(body, mesh=fine, in_specs=in_specs, out_specs=out_specs, check_vma=False)
```

time: 245 us -> 212 us (0.87)
  the two profiles are of different devices: /device:TPU:7 before, /device:TPU:70 now
where the time goes in v2:
time: 212 us
  waiting for transfers between devices  95.7 us (45%)
  starting transfers between devices  75.1 us (35%)
  Pallas kernels  21 us (10%)
  local copies, waits for them, and re-layouts  15.3 us (7%)
  other arithmetic  3.68 us (2%)
    ppermute x1, waiting for transfers between devices, body(): far = lax.ppermute(packed, 'zl', FLIP)  41.7 us
    ppermute x2, starting transfers between devices, send_home(): straight = lax.ppermute(halves[0], AXES, HOME[0])  19.5 us
    ppermute x3, waiting for transfers between devices, body(): lax.ppermute(parts[e], 'zh', shift(e))  15.3 us
    unnamed x24, local copies, waits for them, and re-layouts  11.6 us
    pallas_call x1, Pallas kernels, solve(): vmem_call(solver_body, (SHAPE((128, BLOCK), F32), SHAPE((128, BLOCK), F32...  11 us
    all_to_all x1, starting transfers between devices, copies_to(): return lax.all_to_all(copies, axis, split_axis=0, concat_axis=0, tiled=True)  9.6 us
    ppermute x3, waiting for transfers between devices, body(): own += [lax.ppermute(own[0], 'x', shift(d)) for d in range(1, 4)]  9.45 us
    all_to_all x1, starting transfers between devices, body(): arrived = lax.all_to_all(second, 'zh', 0, 0, tiled=True)  8.48 us
  transfers between devices with their start and end apart: 23, of which 12 were waited for; matrix products, arithmetic and copies ran while one was open for 1% of the time, Pallas kernels for 7%

profile of v2, /device:TPU:70, one launch (start us, length us, event | category | flops | bytes accessed | tf_op | source)
XLA Modules:
  0.0 211.6 jit_solution(11434814409167321412)
XLA Ops:
  3.5 4.5 %all-to-all-start = ((bf16[4,512,128]{2,1,0:T(8,128)(2,1)}), bf16[4,512,128]{2,1,0:T(8,128)(2,1)S(1)}, u32[]{:S(2)}, u32[]{:S(2)}) async-start(bf16[4,512,128]{2,1,0:T(8,128)(2,1)} %pad_maximum_fusion), calls=%async_computation | async-start | bytes 1048576 | tf_op jit(solution)/shard_map/all_to_all | solution.py:316
  8.0 8.1 %collective-permute-start.1 = (bf16[256,256]{1,0:T(8,128)(2,1)}, bf16[256,256]{1,0:T(8,128)(2,1)S(1)}, u32[]{:S(2)}, u32[]{:S(2)}) collective-permute-start(bf16[256,256]{1,0:T(8,128)(2,1)} %param.6), channel_id=1, source_target_pairs={{0,0},{1,1},{2,2},{3,3},{4,32},{5,33},{6,34},{7,35},{8,64},{9,65},... | collective-permute-start | bytes 393224 | tf_op jit(solution)/shard_map/ppermute | solution.py:313
  16.1 5.2 %collective-permute-done.1 = bf16[256,256]{1,0:T(8,128)(2,1)S(1)} collective-permute-done((bf16[256,256]{1,0:T(8,128)(2,1)}, bf16[256,256]{1,0:T(8,128)(2,1)S(1)}, u32[]{:S(2)}, u32[]{:S(2)}) %collective-permute-start.1) | collective-permute-done | bytes 131104 | tf_op jit(solution)/shard_map/ppermute | solution.py:313
  22.4 9.6 %all-to-all-start.1 = ((bf16[8,256,256]{2,1,0:T(8,128)(2,1)}), bf16[8,256,256]{2,1,0:T(8,128)(2,1)S(1)}, u32[]{:S(2)}, u32[]{:S(2)}) async-start(bf16[8,256,256]{2,1,0:T(8,128)(2,1)} %broadcast_in_dim.13), calls=%async_computation.1 | async-start | bytes 2097152 | tf_op jit(solution)/shard_map/all_to_all | solution.py:49
  32.1 3.5 %collective-permute-start.3 = (bf16[4,256,128]{2,1,0:T(8,128)(2,1)S(1)}, bf16[4,256,128]{2,1,0:T(8,128)(2,1)S(1)}, u32[]{:S(2)}, u32[]{:S(2)}) collective-permute-start(bf16[4,256,128]{2,1,0:T(8,128)(2,1)S(1)} %slice.8.refs_0_), channel_id=1, source_target_pairs={{0,128},{64,192},{128,0},{192,64},{1,129},{65,193},{129,1},{193,65... | collective-permute-start | bytes 786440 | tf_op jit(solution)/shard_map/ppermute | solution.py:320
  35.8 6.6 %collective-permute-done.4.refs_3_ = bf16[4,256,128]{2,1,0:T(8,128)(2,1)S(1)} collective-permute-done((bf16[4,256,128]{2,1,0:T(8,128)(2,1)S(1)}, bf16[4,256,128]{2,1,0:T(8,128)(2,1)S(1)}, u32[]{:S(2)}, u32[]{:S(2)}) %collective-permute-start.4) | collective-permute-done | bytes 262176 | tf_op jit(solution)/shard_map/ppermute | solution.py:320
  42.5 2.8 %collective-permute-done.3.refs_2_ = bf16[4,256,128]{2,1,0:T(8,128)(2,1)S(1)} collective-permute-done((bf16[4,256,128]{2,1,0:T(8,128)(2,1)S(1)}, bf16[4,256,128]{2,1,0:T(8,128)(2,1)S(1)}, u32[]{:S(2)}, u32[]{:S(2)}) %collective-permute-start.3) | collective-permute-done | bytes 262176 | tf_op jit(solution)/shard_map/ppermute | solution.py:320
  47.4 6.8 %all-to-all-done.1.cot_ref = bf16[8,256,256]{2,1,0:T(8,128)(2,1)S(1)} async-done(((bf16[8,256,256]{2,1,0:T(8,128)(2,1)}), bf16[8,256,256]{2,1,0:T(8,128)(2,1)S(1)}, u32[]{:S(2)}, u32[]{:S(2)}) %all-to-all-start.1) | async-done | bytes 1048608 | tf_op jit(solution)/shard_map/all_to_all | solution.py:49
  58.3 5.4 %all-to-all-start.2 = ((bf16[8,256,512]{2,1,0:T(8,128)(2,1)}), bf16[8,256,512]{2,1,0:T(8,128)(2,1)S(1)}, u32[]{:S(2)}, u32[]{:S(2)}) async-start(bf16[8,256,512]{2,1,0:T(8,128)(2,1)} %copy-done.8), calls=%async_computation.2 | async-start | bytes 4194304 | tf_op jit(solution)/shard_map/all_to_all | solution.py:331
  65.7 41.7 %collective-permute-done.9.far0 = bf16[4,4,256,128]{3,2,1,0:T(8,128)(2,1)} collective-permute-done((bf16[4,4,256,128]{3,2,1,0:T(8,128)(2,1)}, bf16[4,4,256,128]{3,2,1,0:T(8,128)(2,1)}, u32[]{:S(2)}, u32[]{:S(2)}) %collective-permute-start.9) | collective-permute-done | bytes 1048608 | tf_op jit(solution)/shard_map/ppermute | solution.py:326
  109.6 2.2 %copy-done.1 = f32[1,1,1024,1024]{3,2,1,0:T(8,128)S(1)} copy-done((f32[1,1,1024,1024]{3,2,1,0:T(8,128)S(1)}, f32[1,1,1024,1024]{3,2,1,0:T(8,128)}, u32[]{:S(2)}) %copy-start.1) | copy-done | bytes 4194328
  111.8 11.0 %solve.1 = (f32[128,1024]{1,0:T(8,128)}, f32[128,1024]{1,0:T(8,128)}, f32[128,1024]{1,0:T(8,128)S(1)}, bf16[8,144,128]{2,1,0:T(8,128)(2,1)S(1)}) custom-call(s32[5]{0:T(128)S(1)} %stack.23.place, bf16[8,256,512]{2,1,0:T(8,128)(2,1)S(1)} %all-to-all-done.2.pieces_ref, f32[1024,1024]{1,0:T(8,128)S(1)} %bitcast.13, f32[1024,1024]{1,0:T(8,128)S(1)} %bitcast.14), custom_call_target="tpu_custom_call" | custom-call | tf_op jit(solution)/shard_map/solve/pallas_call | solution.py:296
  124.3 4.4 %all-to-all-start.3 = ((bf16[8,144,128]{2,1,0:T(8,128)(2,1)}), bf16[8,144,128]{2,1,0:T(8,128)(2,1)S(1)}, u32[]{:S(2)}, u32[]{:S(2)}) async-start(bf16[8,144,128]{2,1,0:T(8,128)(2,1)} %copy-done.11), calls=%async_computation.3 | async-start | bytes 589824 | tf_op jit(solution)/shard_map/all_to_all | solution.py:333
  130.8 6.9 %collective-permute-done.far_ref = bf16[4,128,128]{2,1,0:T(8,128)(2,1)S(1)} collective-permute-done((bf16[4,128,128]{2,1,0:T(8,128)(2,1)S(1)}, bf16[4,128,128]{2,1,0:T(8,128)(2,1)S(1)}, u32[]{:S(2)}, u32[]{:S(2)}) %collective-permute-start) | collective-permute-done | bytes 131104 | tf_op jit(solution)/shard_map/ppermute | solution.py:323
  139.9 3.9 %second_partial.1 = (bf16[4,2,128,256]{3,2,1,0:T(8,128)(2,1)}, f32[8,128]{1,0:T(8,128)S(1)}) custom-call(s32[5]{0:T(128)S(1)} %stack.23.place, bf16[8,144,128]{2,1,0:T(8,128)(2,1)S(1)} %all-to-all-done.3.update_ref, bf16[4,512,128]{2,1,0:T(8,128)(2,1)S(1)} %all-to-all-done.mixed_ref, bf16[4,128,128]{2,1,0:T(8,128)(2,1)S(1)} %collective-permute-done.far_ref, ...), custom_call_target="tpu_custom_call" | custom-call | tf_op jit(solution)/shard_map/second_partial/pallas_call | solution.py:165
  143.8 8.5 %all-to-all-start.4 = ((bf16[4,2,128,256]{3,2,1,0:T(8,128)(2,1)}), bf16[4,2,128,256]{3,2,1,0:T(8,128)(2,1)S(1)}, u32[]{:S(2)}, u32[]{:S(2)}) async-start(bf16[4,2,128,256]{3,2,1,0:T(8,128)(2,1)} %get-tuple-element.34), calls=%async_computation.4 | async-start | bytes 1048576 | tf_op jit(solution)/shard_map/all_to_all | solution.py:340
  153.5 3.1 %first_partial.1 = (bf16[2,128,256]{2,1,0:T(8,128)(2,1)S(1)}, bf16[2,128,256]{2,1,0:T(8,128)(2,1)S(1)}, bf16[2,128,256]{2,1,0:T(8,128)(2,1)S(1)}, bf16[2,128,256]{2,1,0:T(8,128)(2,1)S(1)}) custom-call(s32[5]{0:T(128)S(1)} %stack.23.place, bf16[4,512,128]{2,1,0:T(8,128)(2,1)S(1)} %all-to-all-done.mixed_ref, ...), custom_call_target="tpu_custom_call" | custom-call | tf_op jit(solution)/shard_map/first_partial/pallas_call | solution.py:155
  156.6 3.7 %collective-permute-start.11 = (bf16[2,128,256]{2,1,0:T(8,128)(2,1)S(1)}, bf16[2,128,256]{2,1,0:T(8,128)(2,1)S(1)}, u32[]{:S(2)}, u32[]{:S(2)}) collective-permute-start(bf16[2,128,256]{2,1,0:T(8,128)(2,1)S(1)} %get-tuple-element.23), channel_id=1, source_target_pairs={{0,8},{8,16},{16,24},{24,0},{1,9},{9,17},{17,25},{25,1},{2,10},{10... | collective-permute-start | bytes 393224 | tf_op jit(solution)/shard_map/ppermute | solution.py:336
  160.6 2.6 %collective-permute-start.13 = (bf16[2,128,256]{2,1,0:T(8,128)(2,1)S(1)}, bf16[2,128,256]{2,1,0:T(8,128)(2,1)S(1)}, u32[]{:S(2)}, u32[]{:S(2)}) collective-permute-start(bf16[2,128,256]{2,1,0:T(8,128)(2,1)S(1)} %get-tuple-element.25), channel_id=1, source_target_pairs={{0,24},{8,0},{16,8},{24,16},{1,25},{9,1},{17,9},{25,17},{2,26},{10... | collective-permute-start | bytes 393224 | tf_op jit(solution)/shard_map/ppermute | solution.py:336
  163.2 9.0 %collective-permute-done.11.refs_1_ = bf16[2,128,256]{2,1,0:T(8,128)(2,1)S(1)} collective-permute-done((bf16[2,128,256]{2,1,0:T(8,128)(2,1)S(1)}, bf16[2,128,256]{2,1,0:T(8,128)(2,1)S(1)}, u32[]{:S(2)}, u32[]{:S(2)}) %collective-permute-start.11) | collective-permute-done | bytes 131104 | tf_op jit(solution)/shard_map/ppermute | solution.py:336
  172.1 6.3 %collective-permute-done.12.refs_2_ = bf16[2,128,256]{2,1,0:T(8,128)(2,1)S(1)} collective-permute-done((bf16[2,128,256]{2,1,0:T(8,128)(2,1)S(1)}, bf16[2,128,256]{2,1,0:T(8,128)(2,1)S(1)}, u32[]{:S(2)}, u32[]{:S(2)}) %collective-permute-start.12) | collective-permute-done | bytes 131104 | tf_op jit(solution)/shard_map/ppermute | solution.py:336
  179.1 9.5 %collective-permute-start.14 = (bf16[128,256]{1,0:T(8,128)(2,1)S(1)}, bf16[128,256]{1,0:T(8,128)(2,1)S(1)}, u32[]{:S(2)}, u32[]{:S(2)}) collective-permute-start(bf16[128,256]{1,0:T(8,128)(2,1)S(1)} %get-tuple-element.26), channel_id=1, source_target_pairs={{0,0},{1,1},{2,2},{3,3},{4,32},{5,33},{6,34},{7,35},{8,64},{9,65},... | collective-permute-start | bytes 196616 | tf_op jit(solution)/shard_map/ppermute | solution.py:198
  189.8 10.0 %collective-permute-start.16 = (bf16[128,256]{1,0:T(8,128)(2,1)S(1)}, bf16[128,256]{1,0:T(8,128)(2,1)S(1)}, u32[]{:S(2)}, u32[]{:S(2)}) collective-permute-start(bf16[128,256]{1,0:T(8,128)(2,1)S(1)} %get-tuple-element.35), channel_id=1, source_target_pairs={{0,0},{1,1},{2,2},{3,3},{4,32},{5,33},{6,34},{7,35},{8,64},{9,65},... | collective-permute-start | bytes 196616 | tf_op jit(solution)/shard_map/ppermute | solution.py:198
  202.3 8.0 %collective-permute-done.17 = bf16[128,256]{1,0:T(8,128)(2,1)S(1)} collective-permute-done((bf16[128,256]{1,0:T(8,128)(2,1)S(1)}, bf16[128,256]{1,0:T(8,128)(2,1)S(1)}, u32[]{:S(2)}, u32[]{:S(2)}) %collective-permute-start.17) | collective-permute-done | bytes 65568 | tf_op jit(solution)/shard_map/ppermute | solution.py:199
  (65 shorter events, 27.7 us)
Async XLA Ops:
  3.5 17.8 %all-to-all-start = ((bf16[4,512,128]{2,1,0:T(8,128)(2,1)}), bf16[4,512,128]{2,1,0:T(8,128)(2,1)S(1)}, u32[]{:S(2)}, u32[]{:S(2)}) async-start(bf16[4,512,128]{2,1,0:T(8,128)(2,1)} %pad_maximum_fusion), calls=%async_computation | async-start | bytes 1048576 | tf_op jit(solution)/shard_map/all_to_all | solution.py:316
  8.0 13.4 %collective-permute-start.1 = (bf16[256,256]{1,0:T(8,128)(2,1)}, bf16[256,256]{1,0:T(8,128)(2,1)S(1)}, u32[]{:S(2)}, u32[]{:S(2)}) collective-permute-start(bf16[256,256]{1,0:T(8,128)(2,1)} %param.6), channel_id=1, source_target_pairs={{0,0},{1,1},{2,2},{3,3},{4,32},{5,33},{6,34},{7,35},{8,64},{9,65},... | collective-permute-start | bytes 393224 | tf_op jit(solution)/shard_map/ppermute | solution.py:313
  22.4 31.7 %all-to-all-start.1 = ((bf16[8,256,256]{2,1,0:T(8,128)(2,1)}), bf16[8,256,256]{2,1,0:T(8,128)(2,1)S(1)}, u32[]{:S(2)}, u32[]{:S(2)}) async-start(bf16[8,256,256]{2,1,0:T(8,128)(2,1)} %broadcast_in_dim.13), calls=%async_computation.1 | async-start | bytes 2097152 | tf_op jit(solution)/shard_map/all_to_all | solution.py:49
  32.1 10.4 %collective-permute-start.4 = (bf16[4,256,128]{2,1,0:T(8,128)(2,1)S(1)}, bf16[4,256,128]{2,1,0:T(8,128)(2,1)S(1)}, u32[]{:S(2)}, u32[]{:S(2)}) collective-permute-start(bf16[4,256,128]{2,1,0:T(8,128)(2,1)S(1)} %slice.8.refs_0_), channel_id=1, source_target_pairs={{0,192},{64,0},{128,64},{192,128},{1,193},{65,1},{129,65},{193,129... | collective-permute-start | bytes 786440 | tf_op jit(solution)/shard_map/ppermute | solution.py:320
  32.1 13.1 %collective-permute-start.3 = (bf16[4,256,128]{2,1,0:T(8,128)(2,1)S(1)}, bf16[4,256,128]{2,1,0:T(8,128)(2,1)S(1)}, u32[]{:S(2)}, u32[]{:S(2)}) collective-permute-start(bf16[4,256,128]{2,1,0:T(8,128)(2,1)S(1)} %slice.8.refs_0_), channel_id=1, source_target_pairs={{0,128},{64,192},{128,0},{192,64},{1,129},{65,193},{129,1},{193,65... | collective-permute-start | bytes 786440 | tf_op jit(solution)/shard_map/ppermute | solution.py:320
  35.6 9.7 %collective-permute-start.2 = (bf16[4,256,128]{2,1,0:T(8,128)(2,1)S(1)}, bf16[4,256,128]{2,1,0:T(8,128)(2,1)}, u32[]{:S(2)}, u32[]{:S(2)}) collective-permute-start(bf16[4,256,128]{2,1,0:T(8,128)(2,1)S(1)} %slice.8.refs_0_), channel_id=1, source_target_pairs={{0,64},{64,128},{128,192},{192,0},{1,65},{65,129},{129,193},{193,1... | collective-permute-start | bytes 786440 | tf_op jit(solution)/shard_map/ppermute | solution.py:320
  35.8 10.1 %collective-permute-start.5 = (bf16[4,256,128]{2,1,0:T(8,128)(2,1)S(1)}, bf16[4,256,128]{2,1,0:T(8,128)(2,1)S(1)}, u32[]{:S(2)}, u32[]{:S(2)}) collective-permute-start(bf16[4,256,128]{2,1,0:T(8,128)(2,1)S(1)} %slice.8.refs_0_), channel_id=1, source_target_pairs={{0,32},{32,0},{1,33},{33,1},{2,34},{34,2},{3,35},{35,3},{4,36},{36... | collective-permute-start | bytes 786440 | tf_op jit(solution)/shard_map/ppermute | solution.py:321
  42.4 3.4 %collective-permute-start.8 = (bf16[4,256,128]{2,1,0:T(8,128)(2,1)S(1)}, bf16[4,256,128]{2,1,0:T(8,128)(2,1)S(1)}, u32[]{:S(2)}, u32[]{:S(2)}) collective-permute-start(bf16[4,256,128]{2,1,0:T(8,128)(2,1)S(1)} %collective-permute-done.4.refs_3_), channel_id=1, source_target_pairs={{0,32},{32,0},{1,33},{33,1},{2,34},{34,2},{3,35},{35,3},{4,36},{36... | collective-permute-start | bytes 786440 | tf_op jit(solution)/shard_map/ppermute | solution.py:321
  45.3 1.8 collective-permute-start.7
  45.3 2.1 collective-permute-start.6
  58.3 49.2 %all-to-all-start.2 = ((bf16[8,256,512]{2,1,0:T(8,128)(2,1)}), bf16[8,256,512]{2,1,0:T(8,128)(2,1)S(1)}, u32[]{:S(2)}, u32[]{:S(2)}) async-start(bf16[8,256,512]{2,1,0:T(8,128)(2,1)} %copy-done.8), calls=%async_computation.2 | async-start | bytes 4194304 | tf_op jit(solution)/shard_map/all_to_all | solution.py:331
  63.7 43.7 %collective-permute-start.9 = (bf16[4,4,256,128]{3,2,1,0:T(8,128)(2,1)}, bf16[4,4,256,128]{3,2,1,0:T(8,128)(2,1)}, u32[]{:S(2)}, u32[]{:S(2)}) collective-permute-start(bf16[4,4,256,128]{3,2,1,0:T(8,128)(2,1)} %copy-done.2), channel_id=1, source_target_pairs={{0,4},{4,0},{1,5},{5,1},{2,6},{6,2},{3,7},{7,3},{8,12},{12,8},{9,1... | collective-permute-start | bytes 3145736 | tf_op jit(solution)/shard_map/ppermute | solution.py:326
  107.4 30.3 %collective-permute-start.10 = (bf16[4,4,256,128]{3,2,1,0:T(8,128)(2,1)}, bf16[4,4,256,128]{3,2,1,0:T(8,128)(2,1)}, u32[]{:S(2)}, u32[]{:S(2)}) collective-permute-start(bf16[4,4,256,128]{3,2,1,0:T(8,128)(2,1)} %collective-permute-done.9.far0), channel_id=1, source_target_pairs={{0,32},{32,0},{1,33},{33,1},{2,34},{34,2},{3,35},{35,3},{4,36},{36... | collective-permute-start | bytes 3145736 | tf_op jit(solution)/shard_map/ppermute | solution.py:327
  124.3 13.4 %all-to-all-start.3 = ((bf16[8,144,128]{2,1,0:T(8,128)(2,1)}), bf16[8,144,128]{2,1,0:T(8,128)(2,1)S(1)}, u32[]{:S(2)}, u32[]{:S(2)}) async-start(bf16[8,144,128]{2,1,0:T(8,128)(2,1)} %copy-done.11), calls=%async_computation.3 | async-start | bytes 589824 | tf_op jit(solution)/shard_map/all_to_all | solution.py:333
  128.7 9.0 %collective-permute-start = (bf16[4,128,128]{2,1,0:T(8,128)(2,1)S(1)}, bf16[4,128,128]{2,1,0:T(8,128)(2,1)S(1)}, u32[]{:S(2)}, u32[]{:S(2)}) collective-permute-start(bf16[4,128,128]{2,1,0:T(8,128)(2,1)S(1)} %constant_dynamic-slice_fusion), channel_id=1, source_target_pairs={{0,4},{4,0},{1,5},{5,1},{2,6},{6,2},{3,7},{7,3},{8,12},{12,8},{9,1... | collective-permute-start | bytes 393224 | tf_op jit(solution)/shard_map/ppermute | solution.py:323
  143.8 56.2 %copy-start.10 = (f32[128,1024]{1,0:T(8,128)S(1)}, f32[128,1024]{1,0:T(8,128)}, u32[]{:S(2)}) copy-start(f32[128,1024]{1,0:T(8,128)} %copy-done.9) | copy-start | bytes 1572868
  143.8 45.4 %all-to-all-start.4 = ((bf16[4,2,128,256]{3,2,1,0:T(8,128)(2,1)}), bf16[4,2,128,256]{3,2,1,0:T(8,128)(2,1)S(1)}, u32[]{:S(2)}, u32[]{:S(2)}) async-start(bf16[4,2,128,256]{3,2,1,0:T(8,128)(2,1)} %get-tuple-element.34), calls=%async_computation.4 | async-start | bytes 1048576 | tf_op jit(solution)/shard_map/all_to_all | solution.py:340
  156.6 15.5 %collective-permute-start.11 = (bf16[2,128,256]{2,1,0:T(8,128)(2,1)S(1)}, bf16[2,128,256]{2,1,0:T(8,128)(2,1)S(1)}, u32[]{:S(2)}, u32[]{:S(2)}) collective-permute-start(bf16[2,128,256]{2,1,0:T(8,128)(2,1)S(1)} %get-tuple-element.23), channel_id=1, source_target_pairs={{0,8},{8,16},{16,24},{24,0},{1,9},{9,17},{17,25},{25,1},{2,10},{10... | collective-permute-start | bytes 393224 | tf_op jit(solution)/shard_map/ppermute | solution.py:336
  160.2 18.2 %collective-permute-start.12 = (bf16[2,128,256]{2,1,0:T(8,128)(2,1)S(1)}, bf16[2,128,256]{2,1,0:T(8,128)(2,1)S(1)}, u32[]{:S(2)}, u32[]{:S(2)}) collective-permute-start(bf16[2,128,256]{2,1,0:T(8,128)(2,1)S(1)} %get-tuple-element.24), channel_id=1, source_target_pairs={{0,16},{8,24},{16,0},{24,8},{1,17},{9,25},{17,1},{25,9},{2,18},{10... | collective-permute-start | bytes 393224 | tf_op jit(solution)/shard_map/ppermute | solution.py:336
  160.6 17.9 %collective-permute-start.13 = (bf16[2,128,256]{2,1,0:T(8,128)(2,1)S(1)}, bf16[2,128,256]{2,1,0:T(8,128)(2,1)S(1)}, u32[]{:S(2)}, u32[]{:S(2)}) collective-permute-start(bf16[2,128,256]{2,1,0:T(8,128)(2,1)S(1)} %get-tuple-element.25), channel_id=1, source_target_pairs={{0,24},{8,0},{16,8},{24,16},{1,25},{9,1},{17,9},{25,17},{2,26},{10... | collective-permute-start | bytes 393224 | tf_op jit(solution)/shard_map/ppermute | solution.py:336
  179.1 22.4 %collective-permute-start.14 = (bf16[128,256]{1,0:T(8,128)(2,1)S(1)}, bf16[128,256]{1,0:T(8,128)(2,1)S(1)}, u32[]{:S(2)}, u32[]{:S(2)}) collective-permute-start(bf16[128,256]{1,0:T(8,128)(2,1)S(1)} %get-tuple-element.26), channel_id=1, source_target_pairs={{0,0},{1,1},{2,2},{3,3},{4,32},{5,33},{6,34},{7,35},{8,64},{9,65},... | collective-permute-start | bytes 196616 | tf_op jit(solution)/shard_map/ppermute | solution.py:198
  188.6 12.9 %collective-permute-start.15 = (bf16[128,256]{1,0:T(8,128)(2,1)S(1)}, bf16[128,256]{1,0:T(8,128)(2,1)S(1)}, u32[]{:S(2)}, u32[]{:S(2)}) collective-permute-start(bf16[128,256]{1,0:T(8,128)(2,1)S(1)} %get-tuple-element.27), channel_id=1, source_target_pairs={{0,32},{1,33},{2,34},{3,35},{4,0},{5,1},{6,2},{7,3},{8,96},{9,97},... | collective-permute-start | bytes 196616 | tf_op jit(solution)/shard_map/ppermute | solution.py:199
  189.8 12.5 %collective-permute-start.16 = (bf16[128,256]{1,0:T(8,128)(2,1)S(1)}, bf16[128,256]{1,0:T(8,128)(2,1)S(1)}, u32[]{:S(2)}, u32[]{:S(2)}) collective-permute-start(bf16[128,256]{1,0:T(8,128)(2,1)S(1)} %get-tuple-element.35), channel_id=1, source_target_pairs={{0,0},{1,1},{2,2},{3,3},{4,32},{5,33},{6,34},{7,35},{8,64},{9,65},... | collective-permute-start | bytes 196616 | tf_op jit(solution)/shard_map/ppermute | solution.py:198
  199.9 10.4 %collective-permute-start.17 = (bf16[128,256]{1,0:T(8,128)(2,1)S(1)}, bf16[128,256]{1,0:T(8,128)(2,1)S(1)}, u32[]{:S(2)}, u32[]{:S(2)}) collective-permute-start(bf16[128,256]{1,0:T(8,128)(2,1)S(1)} %get-tuple-element.36), channel_id=1, source_target_pairs={{0,32},{1,33},{2,34},{3,35},{4,0},{5,1},{6,2},{7,3},{8,96},{9,97},... | collective-permute-start | bytes 196616 | tf_op jit(solution)/shard_map/ppermute | solution.py:199
  (11 other events, 50.5 us)

commit v3 on v2

v3 whole, which is shorter than its diff:
```python
import jax
import jax.numpy as jnp
from jax import lax
from jax.experimental import pallas as pl
from jax.experimental.pallas import tpu as pltpu
from jax.sharding import Mesh
from jax.sharding import PartitionSpec as P

BLOCK = 1024
STAT_DECAY = 0.8
LEARN_RATE = 0.005
EPSILON = 1e-06

AXES = ("x", "c", "zh", "zl", "y")
BATCH = ("x", "c")
ZAX = ("zh", "zl")
SOLVER = ("zl", "y")
MIB = 1 << 20
SHAPE = jax.ShapeDtypeStruct
BF16 = jnp.bfloat16
F32 = jnp.float32


def device(x, c, zh, zl, y):
    return (((x * 2 + c) * 4 + zh) * 2 + zl) * 4 + y


EVERY = [
    (x, c, zh, zl, y)
    for x in range(4)
    for c in range(2)
    for zh in range(4)
    for zl in range(2)
    for y in range(4)
]
SWAP = [(device(*d), device(d[2], d[3], d[0], d[1], d[4])) for d in EVERY]
FLIP = [(0, 1), (1, 0)]


def shift(by):
    return [(i, (i + by) % 4) for i in range(4)]


def copies_to(shard, axis, count):
    copies = jnp.broadcast_to(shard, (count, *shard.shape))
    return lax.all_to_all(copies, axis, split_axis=0, concat_axis=0, tiled=True)


def dot(a, b):
    return jnp.dot(a, b, preferred_element_type=F32)


def dot_minor(a, b):
    return lax.dot_general(a, b, (((1,), (1,)), ((), ())), preferred_element_type=F32)


VMEM = pl.BlockSpec(memory_space=pltpu.VMEM)
HBM = pl.BlockSpec(memory_space=pltpu.HBM)


def call(body, in_specs, out_specs, out_shape, scratch=(), limit=24, name=None):
    return pl.pallas_call(
        body,
        out_shape=out_shape,
        in_specs=[pl.BlockSpec(memory_space=pltpu.SMEM), *in_specs],
        out_specs=out_specs,
        scratch_shapes=list(scratch),
        compiler_params=pltpu.CompilerParams(vmem_limit_bytes=limit * MIB),
        name=name,
    )


def wide(slab):
    return jnp.concatenate([slab[q] for q in range(4)], axis=1)


def order_body(place, *refs):
    for d in range(4):
        refs[4][(place[4] - d) & 3] = refs[d][...]


def in_order(place, parts):
    shape = SHAPE((4, *parts[0].shape), BF16)
    return call(order_body, [VMEM] * 4, VMEM, shape, limit=8, name="in_order")(place, *parts)


def columns_body(place, weight_ref, *refs):
    outs, work = refs[:4], refs[4]
    for q in range(4):
        work[q] = weight_ref[:, q * 256 : (q + 1) * 256]
    for d in range(4):
        outs[d][...] = work[(place[4] + d) & 3]


def columns(place, weight):
    part = SHAPE((128, 256), BF16)
    return call(
        columns_body,
        [VMEM],
        [VMEM] * 4,
        [part] * 4,
        scratch=[pltpu.VMEM((4, 128, 256), BF16)],
        limit=8,
        name="columns",
    )(place, weight)


def grad_body(place, cot_ref, *refs):
    own, swapped = refs[:4], refs[4:8]
    copies_ref, near_ref, away_ref, piece_ref, near_buf, away_buf, sems = refs[8:]
    x, c, zl = place[0], place[1], place[3]
    total = jnp.zeros((256, 512), F32)
    for d in range(4):
        at = (x - d) & 3
        mine, theirs = own[d][...], swapped[d][...]
        near_buf[at] = jnp.where(c == zl, mine, theirs)
        away_buf[at] = jnp.where(c == zl, theirs, mine)
        total = total + dot(cot_ref[at * 2 + c], wide(mine))
        total = total + dot(cot_ref[at * 2 + 1 - c], wide(theirs))
    piece_ref[...] = total.astype(BF16)
    sends = [
        pltpu.make_async_copy(piece_ref, copies_ref.at[s], sems.at[s]) for s in range(8)
    ]
    sends.append(pltpu.make_async_copy(near_buf, near_ref, sems.at[8]))
    sends.append(pltpu.make_async_copy(away_buf.at[pl.ds(c * 2, 2)], away_ref, sems.at[9]))
    for send in sends:
        send.start()
    for send in sends:
        send.wait()


def grad_piece(place, cot_all, own, swapped):
    return call(
        grad_body,
        [VMEM] * 9,
        [HBM] * 3,
        [
            pltpu.HBM((8, 256, 512), BF16),
            pltpu.HBM((4, 4, 256, 128), BF16),
            pltpu.HBM((2, 4, 256, 128), BF16),
        ],
        scratch=[
            pltpu.VMEM((256, 512), BF16),
            pltpu.VMEM((4, 4, 256, 128), BF16),
            pltpu.VMEM((4, 4, 256, 128), BF16),
            pltpu.SemaphoreType.DMA((10,)),
        ],
        limit=10,
        name="grad_piece",
    )(place, cot_all, *own, *swapped)


def forward_groups(place, near_t, far_t, near_ref, far_refs, out_ref):
    c = place[1]
    for i in range(2):
        for j in range(2):
            at = (c * 2 if i == 0 else 2 - c * 2) + j
            total = dot_minor(near_t, wide(near_ref.at[at]))
            total = total + dot_minor(far_t, wide(far_refs[i].at[j]))
            out_ref[at] = total.astype(BF16)


def first_body(place, near_w, far_w, near_ref, far0, far1, *refs):
    outs, work = refs[:4], refs[4]
    near_t = near_w[...].reshape(512, 256).T
    far_t = far_w[...].reshape(512, 256).T
    forward_groups(place, near_t, far_t, near_ref, (far0, far1), work)
    for e in range(4):
        outs[e][...] = work[(place[2] + e) & 3]


def second_body(place, update_ref, near_w, far_w, near_ref, far0, far1, out_ref, spread_ref):
    squares = jnp.zeros((16, 128), F32)
    for s in range(8):
        squares = squares + update_ref[s, 128:144, :128].astype(F32)
    mean = jnp.sum(squares, axis=0, keepdims=True)[:, :1] / (BLOCK * BLOCK)
    spread = jnp.sqrt(mean + EPSILON)
    spread_ref[...] = jnp.broadcast_to(spread, (8, 128))
    rate = LEARN_RATE / spread
    zl = place[3]

    def changed(weight, first):
        update = jnp.concatenate([update_ref[first + q, :128, :] for q in range(4)], axis=0)
        weight = weight[...].reshape(512, 256)
        return (weight.astype(F32) - rate * update.astype(F32)).astype(BF16).T

    near_t = changed(near_w, zl * 4)
    far_t = changed(far_w, 4 - zl * 4)
    forward_groups(place, near_t, far_t, near_ref, (far0, far1), out_ref)


def first_partial(place, weights, acts):
    part = SHAPE((256, 256), BF16)
    return call(
        first_body,
        [VMEM] * 5,
        [VMEM] * 4,
        [part] * 4,
        scratch=[pltpu.VMEM((4, 256, 256), BF16)],
        limit=12,
        name="first_partial",
    )(place, *weights, *acts)


def second_partial(place, update_cols, weights, acts):
    return call(
        second_body,
        [VMEM] * 6,
        [VMEM] * 2,
        [SHAPE((4, 256, 256), BF16), SHAPE((8, 128), F32)],
        limit=12,
        name="second_partial",
    )(place, update_cols, *weights, *acts)


def add_body(place, *refs):
    parts = refs[:-1]
    if len(parts) == 1:
        parts = [parts[0].at[i] for i in range(4)]
    total = parts[0][...].astype(F32)
    for part in parts[1:]:
        total = total + part[...].astype(F32)
    refs[-1][...] = total.astype(BF16)


def add_up(place, *parts):
    return call(
        add_body, [VMEM] * len(parts), VMEM, SHAPE((256, 256), BF16), limit=8, name="add_up"
    )(place, *parts)


def statistics(lhs_ref, rhs_ref, old_ref, full_ref, off_ref):
    tile = 256
    sums = jnp.zeros((1, BLOCK), F32)
    diag = jnp.zeros((1, BLOCK), F32)
    for i in range(BLOCK // tile):
        rows = pl.ds(i * tile, tile)
        gram = dot(lhs_ref[rows, :], rhs_ref[...])
        new = STAT_DECAY * old_ref[rows, :] + (1.0 - STAT_DECAY) / BLOCK * gram
        full_ref[rows, :] = new
        sums = sums + jnp.sum(jnp.abs(new), axis=0, keepdims=True)
        row = lax.broadcasted_iota(jnp.int32, (tile, BLOCK), 0) + i * tile
        col = lax.broadcasted_iota(jnp.int32, (tile, BLOCK), 1)
        on_diag = row == col
        diag = diag + jnp.sum(jnp.where(on_diag, new, 0.0), axis=0, keepdims=True)
        off_ref[rows, :] = jnp.where(on_diag, 0.0, new).astype(BF16)
    scale = 2.5 / (jnp.max(sums, axis=1, keepdims=True) + EPSILON)
    return scale, diag


def times_factor(rows, off_ref, diag):
    return rows * diag + dot(rows.astype(BF16), off_ref[...])


def times_root(start, off_ref, diag, quarter):
    value = start
    for _ in range(4):
        value = 1.25 * value - quarter * times_factor(value, off_ref, diag)
    return 1.25 * start - quarter * times_factor(value, off_ref, diag)


def solver_body(
    place,
    pieces_ref,
    left_old_ref,
    right_old_ref,
    new_left_ref,
    new_right_ref,
    update_ref,
    sent_ref,
    left_buf,
    right_buf,
    grad_ref,
    grad_t_ref,
    full_ref,
    off_left_ref,
    off_right_ref,
    rows_buf,
    update_buf,
    sent_buf,
    sems,
):
    load_left = pltpu.make_async_copy(left_old_ref, left_buf, sems.at[0])
    load_right = pltpu.make_async_copy(right_old_ref, right_buf, sems.at[1])
    load_left.start()
    load_right.start()
    first = pl.multiple_of((place[3] * 4 + place[4]) * 128, 128)
    own = pl.ds(first, 128)
    for zl in range(2):
        for y in range(4):
            piece = pieces_ref[zl * 4 + y]
            grad_ref[pl.ds(y * 256, 256), pl.ds(zl * 512, 512)] = piece
            grad_t_ref[pl.ds(zl * 512, 512), pl.ds(y * 256, 256)] = piece.T
    load_left.wait()
    scale_left, diag_left = statistics(grad_t_ref, grad_ref, left_buf, full_ref, off_left_ref)
    left_rows = full_ref[own, :]
    rows_buf[...] = left_rows
    store_left = pltpu.make_async_copy(rows_buf, new_left_ref, sems.at[2])
    store_left.start()
    load_right.wait()
    scale_right, diag_right = statistics(
        grad_ref, grad_t_ref, right_buf, full_ref, off_right_ref
    )
    store_right = pltpu.make_async_copy(full_ref.at[own, :], new_right_ref, sems.at[3])
    store_right.start()
    quarter_left = scale_left * 0.25
    quarter_right = scale_right * 0.25
    row = lax.broadcasted_iota(jnp.int32, (128, BLOCK), 0) + first
    col = lax.broadcasted_iota(jnp.int32, (128, BLOCK), 1)
    start = jnp.where(row == col, 1.25, 0.0) - quarter_left * left_rows
    root = jnp.sqrt(jnp.sqrt(scale_left)) * times_root(start, off_left_ref, diag_left, quarter_left)
    high = root.astype(BF16)
    low = (root - high.astype(F32)).astype(BF16)
    both = dot(jnp.concatenate([high, low], axis=0), grad_t_ref[...])
    mixed = both[:128] + both[128:]
    turned = 1.25 * mixed - quarter_right * times_factor(mixed, off_right_ref, diag_right)
    update = jnp.sqrt(jnp.sqrt(scale_right)) * times_root(
        turned, off_right_ref, diag_right, quarter_right
    )
    squares = jnp.sum(jnp.sum(update * update, axis=0, keepdims=True), axis=1, keepdims=True)
    high = squares.astype(BF16).astype(F32)
    middle = (squares - high).astype(BF16).astype(F32)
    low = squares - high - middle
    row = lax.broadcasted_iota(jnp.int32, (16, 256), 0)
    tail = jnp.where(row == 0, high, jnp.where(row == 1, middle, jnp.where(row == 2, low, 0.0)))
    tail = tail.astype(BF16)
    for y in range(4):
        sent_buf[y, :128, :] = update[:, y * 256 : (y + 1) * 256].astype(BF16)
        sent_buf[y, 128:, :] = tail
    stores = [
        pltpu.make_async_copy(sent_buf, sent_ref.at[pl.ds(zl * 4, 4)], sems.at[4 + zl])
        for zl in range(2)
    ]
    for store in stores:
        store.start()
    update_buf[...] = update
    stores.append(pltpu.make_async_copy(update_buf, update_ref, sems.at[6]))
    stores[-1].start()
    for store in [store_left, store_right, *stores]:
        store.wait()


def solve(place, pieces, left_old, right_old):
    square = (BLOCK, BLOCK)
    rows = pltpu.HBM((128, BLOCK), F32)
    return call(
        solver_body,
        [VMEM, HBM, HBM],
        [HBM] * 4,
        [rows, rows, rows, pltpu.HBM((8, 144, 256), BF16)],
        scratch=[
            *[pltpu.VMEM(square, kind) for kind in (F32, F32, BF16, BF16, F32, BF16, BF16)],
            pltpu.VMEM((128, BLOCK), F32),
            pltpu.VMEM((128, BLOCK), F32),
            pltpu.VMEM((4, 144, 256), BF16),
            pltpu.SemaphoreType.DMA((7,)),
        ],
        limit=30,
        name="solve",
    )(place, pieces, left_old, right_old)


def body(activations, cotangent, weight, left_old, right_old):
    place = jnp.stack([lax.axis_index(a).astype(jnp.int32) for a in AXES])
    cot_turned = lax.ppermute(cotangent, AXES, SWAP)
    slab = in_order(
        place, [activations] + [lax.ppermute(activations, "y", shift(d)) for d in range(1, 4)]
    )
    cot_all = copies_to(cot_turned, ZAX, 8)
    own = [slab] + [lax.ppermute(slab, "x", shift(d)) for d in range(1, 4)]
    swapped = [lax.ppermute(part, "c", FLIP) for part in own]
    weight, _ = lax.optimization_barrier((weight, slab))
    cols = columns(place, weight)
    near_w = in_order(
        place, [cols[0]] + [lax.ppermute(cols[d], "y", shift(d)) for d in range(1, 4)]
    )
    far_w = lax.ppermute(near_w, "zl", FLIP)
    copies, near, away = grad_piece(place, cot_all, own, swapped)
    pieces = lax.all_to_all(copies, SOLVER, 0, 0, tiled=True)
    pieces, away, near_w, far_w = lax.optimization_barrier((pieces, away, near_w, far_w))
    far = lax.ppermute(away, "zl", FLIP)
    left_old = pltpu.with_memory_space_constraint(left_old[0, 0], pltpu.HBM)
    right_old = pltpu.with_memory_space_constraint(right_old[0, 0], pltpu.HBM)
    new_left, new_right, update, sent = solve(place, pieces, left_old, right_old)
    update_cols = lax.all_to_all(sent, SOLVER, 0, 0, tiled=True)
    far, sent = lax.optimization_barrier((far, sent))
    far_swapped = lax.ppermute(far, "c", FLIP)
    weights = (near_w, far_w)
    acts = (near, far, far_swapped)

    parts = first_partial(place, weights, acts)
    update_cols, _ = lax.optimization_barrier((update_cols, parts[0]))
    parts = [parts[0]] + [lax.ppermute(parts[e], "zh", shift(e)) for e in range(1, 4)]
    first_out = lax.ppermute(add_up(place, *parts), AXES, SWAP)

    second, spread = second_partial(place, update_cols, weights, acts)
    arrived = lax.all_to_all(second, "zh", 0, 0, tiled=True)
    second_out = lax.ppermute(add_up(place, arrived), AXES, SWAP)
    direction = update / spread[0, 0]
    return (first_out, new_left[None, None], new_right[None, None], direction, second_out)


def solution(mesh):
    fine = Mesh(mesh.devices.reshape(4, 2, 4, 2, 4), AXES)
    rows = ("zh", "zl", "y")
    in_specs = (
        P(BATCH, rows),
        P(rows, BATCH),
        P(rows, BATCH),
        P("zh", BATCH, None, None),
        P("zh", BATCH, None, None),
    )
    out_specs = (
        P(rows, BATCH),
        P("zh", BATCH, SOLVER, None),
        P("zh", BATCH, SOLVER, None),
        P(rows, BATCH),
        P(rows, BATCH),
    )
    return jax.shard_map(body, mesh=fine, in_specs=in_specs, out_specs=out_specs, check_vma=False)
```

time: 212 us -> 186 us (0.88)
  the two profiles are of different devices: /device:TPU:70 before, /device:TPU:7 now
where the time goes in v3:
time: 186 us; the launch traced here: 184 us
  starting transfers between devices  76.9 us (41%)
  waiting for transfers between devices  73.3 us (39%)
  Pallas kernels  24.4 us (13%)
  local copies, waits for them, and re-layouts  6.39 us (3%)
  other arithmetic  2.54 us (1%)
    ppermute x3, waiting for transfers between devices, body(): lax.ppermute(cols[d], 'y', shift(d))  22.5 us
    ppermute x3, waiting for transfers between devices, body(): lax.ppermute(parts[e], 'zh', shift(e))  17.1 us
    pallas_call x1, Pallas kernels, solve(): call(solver_body, [VMEM, HBM, HBM], [HBM] * 4, [rows, rows, rows, pltpu.H...  13.6 us
    ppermute x4, starting transfers between devices, body(): swapped = [lax.ppermute(part, 'c', FLIP) for part in own]  11.4 us
    ppermute x1, waiting for transfers between devices, body(): first_out = lax.ppermute(add_up(place, *parts), AXES, SWAP)  10.2 us
    ppermute x1, waiting for transfers between devices, body(): cot_turned = lax.ppermute(cotangent, AXES, SWAP)  9.65 us
    ppermute x3, starting transfers between devices, body(): lax.ppermute(parts[e], 'zh', shift(e))  8.95 us
    ppermute x1, starting transfers between devices, body(): first_out = lax.ppermute(add_up(place, *parts), AXES, SWAP)  8.16 us
  transfers between devices with their start and end apart: 26, of which 14 were waited for; matrix products, arithmetic and copies ran while one was open for 2% of the time, Pallas kernels for 10%

profile of v3, /device:TPU:7, one launch (start us, length us, event | category | flops | bytes accessed | tf_op | source)
XLA Modules:
  0.0 184.3 jit_solution(8444659820896148195)
XLA Ops:
  0.6 8.0 %collective-permute-start = (bf16[256,256]{1,0:T(8,128)(2,1)}, bf16[256,256]{1,0:T(8,128)(2,1)S(1)}, u32[]{:S(2)}, u32[]{:S(2)}) collective-permute-start(bf16[256,256]{1,0:T(8,128)(2,1)} %param.6), channel_id=1, source_target_pairs={{0,0},{1,1},{2,2},{3,3},{4,32},{5,33},{6,34},{7,35},{8,64},{9,65},... | collective-permute-start | bytes 393224 | tf_op jit(solution)/shard_map/ppermute | solution.py:365
  8.6 9.7 %collective-permute-done = bf16[256,256]{1,0:T(8,128)(2,1)S(1)} collective-permute-done((bf16[256,256]{1,0:T(8,128)(2,1)}, bf16[256,256]{1,0:T(8,128)(2,1)S(1)}, u32[]{:S(2)}, u32[]{:S(2)}) %collective-permute-start) | collective-permute-done | bytes 131104 | tf_op jit(solution)/shard_map/ppermute | solution.py:365
  19.3 3.6 %all-to-all-start = ((bf16[8,256,256]{2,1,0:T(8,128)(2,1)}), bf16[8,256,256]{2,1,0:T(8,128)(2,1)S(1)}, u32[]{:S(2)}, u32[]{:S(2)}) async-start(bf16[8,256,256]{2,1,0:T(8,128)(2,1)} %broadcast_in_dim.9), calls=%async_computation | async-start | bytes 2097152 | tf_op jit(solution)/shard_map/all_to_all | solution.py:46
  24.2 2.6 %collective-permute-start.2 = (bf16[256,128]{1,0:T(8,128)(2,1)}, bf16[256,128]{1,0:T(8,128)(2,1)S(1)}, u32[]{:S(2)}, u32[]{:S(2)}) collective-permute-start(bf16[256,128]{1,0:T(8,128)(2,1)} %refs_0_.1), channel_id=1, source_target_pairs={{0,2},{1,3},{2,0},{3,1},{4,6},{5,7},{6,4},{7,5},{8,10},{9,11},{10,... | collective-permute-start | bytes 196616 | tf_op jit(solution)/shard_map/ppermute | solution.py:367
  34.7 2.7 %collective-permute-start.5 = (bf16[4,256,128]{2,1,0:T(8,128)(2,1)S(1)}, bf16[4,256,128]{2,1,0:T(8,128)(2,1)S(1)}, u32[]{:S(2)}, u32[]{:S(2)}) collective-permute-start(bf16[4,256,128]{2,1,0:T(8,128)(2,1)S(1)} %in_order.2.refs_0_), channel_id=1, source_target_pairs={{0,128},{64,192},{128,0},{192,64},{1,129},{65,193},{129,1},{193,65... | collective-permute-start | bytes 786440 | tf_op jit(solution)/shard_map/ppermute | solution.py:370
  39.7 6.3 %collective-permute-start.10 = (bf16[4,256,128]{2,1,0:T(8,128)(2,1)S(1)}, bf16[4,256,128]{2,1,0:T(8,128)(2,1)S(1)}, u32[]{:S(2)}, u32[]{:S(2)}) collective-permute-start(bf16[4,256,128]{2,1,0:T(8,128)(2,1)S(1)} %collective-permute-done.6.refs_3_), channel_id=1, source_target_pairs={{0,32},{32,0},{1,33},{33,1},{2,34},{34,2},{3,35},{35,3},{4,36},{36... | collective-permute-start | bytes 786440 | tf_op jit(solution)/shard_map/ppermute | solution.py:371
  50.0 3.3 %grad_piece.1 = (bf16[8,256,512]{2,1,0:T(8,128)(2,1)}, bf16[4,4,256,128]{3,2,1,0:T(8,128)(2,1)}, bf16[2,4,256,128]{3,2,1,0:T(8,128)(2,1)}) custom-call(s32[5]{0:T(128)S(1)} %stack.23.place, bf16[8,256,256]{2,1,0:T(8,128)(2,1)S(1)} %all-to-all-done.cot_ref, bf16[4,256,128]{2,1,0:T(8,128)(2,1)S(1)} %in_order.2.refs_0_, ...), custom_call_target="tpu_custom_call" | custom-call | tf_op jit(solution)/shard_map/grad_piece/pallas_call | solution.py:133
  53.3 4.4 %all-to-all-start.1 = ((bf16[8,256,512]{2,1,0:T(8,128)(2,1)}), bf16[8,256,512]{2,1,0:T(8,128)(2,1)S(1)}, u32[]{:S(2)}, u32[]{:S(2)}) async-start(bf16[8,256,512]{2,1,0:T(8,128)(2,1)} %get-tuple-element.29), calls=%async_computation.1 | async-start | bytes 4194304 | tf_op jit(solution)/shard_map/all_to_all | solution.py:379
  59.8 2.4 %collective-permute-start.12 = (bf16[128,256]{1,0:T(8,128)(2,1)S(1)}, bf16[128,256]{1,0:T(8,128)(2,1)S(1)}, u32[]{:S(2)}, u32[]{:S(2)}) collective-permute-start(bf16[128,256]{1,0:T(8,128)(2,1)S(1)} %get-tuple-element.34), channel_id=1, source_target_pairs={{0,2},{1,3},{2,0},{3,1},{4,6},{5,7},{6,4},{7,5},{8,10},{9,11},{10,... | collective-permute-start | bytes 196616 | tf_op jit(solution)/shard_map/ppermute | solution.py:375
  63.3 22.5 %collective-permute-done.11.refs_1_ = bf16[128,256]{1,0:T(8,128)(2,1)S(1)} collective-permute-done((bf16[128,256]{1,0:T(8,128)(2,1)S(1)}, bf16[128,256]{1,0:T(8,128)(2,1)S(1)}, u32[]{:S(2)}, u32[]{:S(2)}) %collective-permute-start.11) | collective-permute-done | bytes 65568 | tf_op jit(solution)/shard_map/ppermute | solution.py:375
  87.7 4.7 %collective-permute-done.14.far_w = bf16[4,128,256]{2,1,0:T(8,128)(2,1)S(1)} collective-permute-done((bf16[4,128,256]{2,1,0:T(8,128)(2,1)S(1)}, bf16[4,128,256]{2,1,0:T(8,128)(2,1)S(1)}, u32[]{:S(2)}, u32[]{:S(2)}) %collective-permute-start.14) | collective-permute-done | bytes 262176 | tf_op jit(solution)/shard_map/ppermute | solution.py:377
  94.3 13.6 %solve.1 = (f32[128,1024]{1,0:T(8,128)}, f32[128,1024]{1,0:T(8,128)}, f32[128,1024]{1,0:T(8,128)}, bf16[8,144,256]{2,1,0:T(8,128)(2,1)}) custom-call(s32[5]{0:T(128)S(1)} %stack.23.place, bf16[8,256,512]{2,1,0:T(8,128)(2,1)S(1)} %all-to-all-done.1.pieces_ref, f32[1024,1024]{1,0:T(8,128)} %bitcast.10, f32[1024,1024]{1,0:T(8,128)} %bitcast.11), custom_call_target="tpu_custom_call" | custom-call | tf_op jit(solution)/shard_map/solve/pallas_call | solution.py:346
  108.0 5.0 %all-to-all-start.2 = ((bf16[8,144,256]{2,1,0:T(8,128)(2,1)}), bf16[8,144,256]{2,1,0:T(8,128)(2,1)S(1)}, u32[]{:S(2)}, u32[]{:S(2)}) async-start(bf16[8,144,256]{2,1,0:T(8,128)(2,1)} %get-tuple-element.41), calls=%async_computation.2 | async-start | bytes 1179648 | tf_op jit(solution)/shard_map/all_to_all | solution.py:385
  121.5 2.7 %second_partial.1 = (bf16[4,256,256]{2,1,0:T(8,128)(2,1)}, f32[8,128]{1,0:T(8,128)S(1)}) custom-call(s32[5]{0:T(128)S(1)} %stack.23.place, bf16[8,144,256]{2,1,0:T(8,128)(2,1)S(1)} %all-to-all-done.2.update_ref, bf16[4,128,256]{2,1,0:T(8,128)(2,1)S(1)} %in_order.3.near_w, bf16[4,128,256]{2,1,0:T(8,128)(2,1)S(1)} %copy-done.3, ...), custom_call_target="tpu_custom_call" | custom-call | tf_op jit(solution)/shard_map/second_partial/pallas_call | solution.py:206
  124.2 5.5 %all-to-all-start.3 = ((bf16[4,256,256]{2,1,0:T(8,128)(2,1)}), bf16[4,256,256]{2,1,0:T(8,128)(2,1)S(1)}, u32[]{:S(2)}, u32[]{:S(2)}) async-start(bf16[4,256,256]{2,1,0:T(8,128)(2,1)} %get-tuple-element.52), calls=%async_computation.3 | async-start | bytes 1048576 | tf_op jit(solution)/shard_map/all_to_all | solution.py:397
  129.6 2.4 %collective-permute-start.17 = (bf16[256,256]{1,0:T(8,128)(2,1)S(1)}, bf16[256,256]{1,0:T(8,128)(2,1)S(1)}, u32[]{:S(2)}, u32[]{:S(2)}) collective-permute-start(bf16[256,256]{1,0:T(8,128)(2,1)S(1)} %get-tuple-element.44), channel_id=1, source_target_pairs={{0,8},{8,16},{16,24},{24,0},{1,9},{9,17},{17,25},{25,1},{2,10},{10... | collective-permute-start | bytes 393224 | tf_op jit(solution)/shard_map/ppermute | solution.py:393
  132.0 3.3 %collective-permute-start.18 = (bf16[256,256]{1,0:T(8,128)(2,1)S(1)}, bf16[256,256]{1,0:T(8,128)(2,1)S(1)}, u32[]{:S(2)}, u32[]{:S(2)}) collective-permute-start(bf16[256,256]{1,0:T(8,128)(2,1)S(1)} %get-tuple-element.45), channel_id=1, source_target_pairs={{0,16},{8,24},{16,0},{24,8},{1,17},{9,25},{17,1},{25,9},{2,18},{10... | collective-permute-start | bytes 393224 | tf_op jit(solution)/shard_map/ppermute | solution.py:393
  135.3 3.3 %collective-permute-start.19 = (bf16[256,256]{1,0:T(8,128)(2,1)S(1)}, bf16[256,256]{1,0:T(8,128)(2,1)S(1)}, u32[]{:S(2)}, u32[]{:S(2)}) collective-permute-start(bf16[256,256]{1,0:T(8,128)(2,1)S(1)} %get-tuple-element.46), channel_id=1, source_target_pairs={{0,24},{8,0},{16,8},{24,16},{1,25},{9,1},{17,9},{25,17},{2,26},{10... | collective-permute-start | bytes 393224 | tf_op jit(solution)/shard_map/ppermute | solution.py:393
  141.3 4.9 %collective-permute-done.18.refs_2_ = bf16[256,256]{1,0:T(8,128)(2,1)S(1)} collective-permute-done((bf16[256,256]{1,0:T(8,128)(2,1)S(1)}, bf16[256,256]{1,0:T(8,128)(2,1)S(1)}, u32[]{:S(2)}, u32[]{:S(2)}) %collective-permute-start.18) | collective-permute-done | bytes 131104 | tf_op jit(solution)/shard_map/ppermute | solution.py:393
  146.2 10.0 %collective-permute-done.19.refs_3_ = bf16[256,256]{1,0:T(8,128)(2,1)S(1)} collective-permute-done((bf16[256,256]{1,0:T(8,128)(2,1)S(1)}, bf16[256,256]{1,0:T(8,128)(2,1)S(1)}, u32[]{:S(2)}, u32[]{:S(2)}) %collective-permute-start.19) | collective-permute-done | bytes 131104 | tf_op jit(solution)/shard_map/ppermute | solution.py:393
  156.8 8.2 %collective-permute-start.20 = (bf16[256,256]{1,0:T(8,128)(2,1)S(1)}, bf16[256,256]{1,0:T(8,128)(2,1)S(1)}, u32[]{:S(2)}, u32[]{:S(2)}) collective-permute-start(bf16[256,256]{1,0:T(8,128)(2,1)S(1)} %add_up.2), channel_id=1, source_target_pairs={{0,0},{1,1},{2,2},{3,3},{4,32},{5,33},{6,34},{7,35},{8,64},{9,65},... | collective-permute-start | bytes 393224 | tf_op jit(solution)/shard_map/ppermute | solution.py:394
  167.6 2.5 %broadcast_divide_fusion = f32[128,1024]{1,0:T(8,128)} fusion(f32[128,1024]{1,0:T(8,128)} %get-tuple-element.49, f32[]{:T(128)} %bitcast.9), kind=kLoop, calls=%fused_computation | loop fusion | flops 131072 | bytes 1048580 | tf_op jit(solution)/shard_map/div | solution.py:399
  170.1 10.2 %collective-permute-done.20 = bf16[256,256]{1,0:T(8,128)(2,1)S(1)} collective-permute-done((bf16[256,256]{1,0:T(8,128)(2,1)S(1)}, bf16[256,256]{1,0:T(8,128)(2,1)S(1)}, u32[]{:S(2)}, u32[]{:S(2)}) %collective-permute-start.20) | collective-permute-done | bytes 131104 | tf_op jit(solution)/shard_map/ppermute | solution.py:394
  180.3 2.7 %collective-permute-done.21 = bf16[256,256]{1,0:T(8,128)(2,1)S(1)} collective-permute-done((bf16[256,256]{1,0:T(8,128)(2,1)S(1)}, bf16[256,256]{1,0:T(8,128)(2,1)S(1)}, u32[]{:S(2)}, u32[]{:S(2)}) %collective-permute-start.21) | collective-permute-done | bytes 131104 | tf_op jit(solution)/shard_map/ppermute | solution.py:398
  (55 shorter events, 39.1 us)
Async XLA Ops:
  0.6 17.6 %collective-permute-start = (bf16[256,256]{1,0:T(8,128)(2,1)}, bf16[256,256]{1,0:T(8,128)(2,1)S(1)}, u32[]{:S(2)}, u32[]{:S(2)}) collective-permute-start(bf16[256,256]{1,0:T(8,128)(2,1)} %param.6), channel_id=1, source_target_pairs={{0,0},{1,1},{2,2},{3,3},{4,32},{5,33},{6,34},{7,35},{8,64},{9,65},... | collective-permute-start | bytes 393224 | tf_op jit(solution)/shard_map/ppermute | solution.py:365
  19.3 30.7 %all-to-all-start = ((bf16[8,256,256]{2,1,0:T(8,128)(2,1)}), bf16[8,256,256]{2,1,0:T(8,128)(2,1)S(1)}, u32[]{:S(2)}, u32[]{:S(2)}) async-start(bf16[8,256,256]{2,1,0:T(8,128)(2,1)} %broadcast_in_dim.9), calls=%async_computation | async-start | bytes 2097152 | tf_op jit(solution)/shard_map/all_to_all | solution.py:46
  22.9 5.2 %collective-permute-start.1 = (bf16[256,128]{1,0:T(8,128)(2,1)}, bf16[256,128]{1,0:T(8,128)(2,1)S(1)}, u32[]{:S(2)}, u32[]{:S(2)}) collective-permute-start(bf16[256,128]{1,0:T(8,128)(2,1)} %refs_0_.1), channel_id=1, source_target_pairs={{0,1},{1,2},{2,3},{3,0},{4,5},{5,6},{6,7},{7,4},{8,9},{9,10},{10,1... | collective-permute-start | bytes 196616 | tf_op jit(solution)/shard_map/ppermute | solution.py:367
  24.2 5.2 %collective-permute-start.2 = (bf16[256,128]{1,0:T(8,128)(2,1)}, bf16[256,128]{1,0:T(8,128)(2,1)S(1)}, u32[]{:S(2)}, u32[]{:S(2)}) collective-permute-start(bf16[256,128]{1,0:T(8,128)(2,1)} %refs_0_.1), channel_id=1, source_target_pairs={{0,2},{1,3},{2,0},{3,1},{4,6},{5,7},{6,4},{7,5},{8,10},{9,11},{10,... | collective-permute-start | bytes 196616 | tf_op jit(solution)/shard_map/ppermute | solution.py:367
  26.9 3.6 %collective-permute-start.3 = (bf16[256,128]{1,0:T(8,128)(2,1)}, bf16[256,128]{1,0:T(8,128)(2,1)S(1)}, u32[]{:S(2)}, u32[]{:S(2)}) collective-permute-start(bf16[256,128]{1,0:T(8,128)(2,1)} %refs_0_.1), channel_id=1, source_target_pairs={{0,3},{1,0},{2,1},{3,2},{4,7},{5,4},{6,5},{7,6},{8,11},{9,8},{10,9... | collective-permute-start | bytes 196616 | tf_op jit(solution)/shard_map/ppermute | solution.py:367
  31.9 7.8 %collective-permute-start.6 = (bf16[4,256,128]{2,1,0:T(8,128)(2,1)S(1)}, bf16[4,256,128]{2,1,0:T(8,128)(2,1)S(1)}, u32[]{:S(2)}, u32[]{:S(2)}) collective-permute-start(bf16[4,256,128]{2,1,0:T(8,128)(2,1)S(1)} %in_order.2.refs_0_), channel_id=1, source_target_pairs={{0,192},{64,0},{128,64},{192,128},{1,193},{65,1},{129,65},{193,129... | collective-permute-start | bytes 786440 | tf_op jit(solution)/shard_map/ppermute | solution.py:370
  32.9 13.1 %collective-permute-start.4 = (bf16[4,256,128]{2,1,0:T(8,128)(2,1)S(1)}, bf16[4,256,128]{2,1,0:T(8,128)(2,1)S(1)}, u32[]{:S(2)}, u32[]{:S(2)}) collective-permute-start(bf16[4,256,128]{2,1,0:T(8,128)(2,1)S(1)} %in_order.2.refs_0_), channel_id=1, source_target_pairs={{0,64},{64,128},{128,192},{192,0},{1,65},{65,129},{129,193},{193,1... | collective-permute-start | bytes 786440 | tf_op jit(solution)/shard_map/ppermute | solution.py:370
  34.7 13.6 %collective-permute-start.5 = (bf16[4,256,128]{2,1,0:T(8,128)(2,1)S(1)}, bf16[4,256,128]{2,1,0:T(8,128)(2,1)S(1)}, u32[]{:S(2)}, u32[]{:S(2)}) collective-permute-start(bf16[4,256,128]{2,1,0:T(8,128)(2,1)S(1)} %in_order.2.refs_0_), channel_id=1, source_target_pairs={{0,128},{64,192},{128,0},{192,64},{1,129},{65,193},{129,1},{193,65... | collective-permute-start | bytes 786440 | tf_op jit(solution)/shard_map/ppermute | solution.py:370
  37.4 11.4 %collective-permute-start.7 = (bf16[4,256,128]{2,1,0:T(8,128)(2,1)S(1)}, bf16[4,256,128]{2,1,0:T(8,128)(2,1)S(1)}, u32[]{:S(2)}, u32[]{:S(2)}) collective-permute-start(bf16[4,256,128]{2,1,0:T(8,128)(2,1)S(1)} %in_order.2.refs_0_), channel_id=1, source_target_pairs={{0,32},{32,0},{1,33},{33,1},{2,34},{34,2},{3,35},{35,3},{4,36},{36... | collective-permute-start | bytes 786440 | tf_op jit(solution)/shard_map/ppermute | solution.py:371
  39.7 9.1 %collective-permute-start.10 = (bf16[4,256,128]{2,1,0:T(8,128)(2,1)S(1)}, bf16[4,256,128]{2,1,0:T(8,128)(2,1)S(1)}, u32[]{:S(2)}, u32[]{:S(2)}) collective-permute-start(bf16[4,256,128]{2,1,0:T(8,128)(2,1)S(1)} %collective-permute-done.6.refs_3_), channel_id=1, source_target_pairs={{0,32},{32,0},{1,33},{33,1},{2,34},{34,2},{3,35},{35,3},{4,36},{36... | collective-permute-start | bytes 786440 | tf_op jit(solution)/shard_map/ppermute | solution.py:371
  53.3 39.9 %all-to-all-start.1 = ((bf16[8,256,512]{2,1,0:T(8,128)(2,1)}), bf16[8,256,512]{2,1,0:T(8,128)(2,1)S(1)}, u32[]{:S(2)}, u32[]{:S(2)}) async-start(bf16[8,256,512]{2,1,0:T(8,128)(2,1)} %get-tuple-element.29), calls=%async_computation.1 | async-start | bytes 4194304 | tf_op jit(solution)/shard_map/all_to_all | solution.py:379
  58.2 27.7 %collective-permute-start.11 = (bf16[128,256]{1,0:T(8,128)(2,1)S(1)}, bf16[128,256]{1,0:T(8,128)(2,1)S(1)}, u32[]{:S(2)}, u32[]{:S(2)}) collective-permute-start(bf16[128,256]{1,0:T(8,128)(2,1)S(1)} %get-tuple-element.33), channel_id=1, source_target_pairs={{0,1},{1,2},{2,3},{3,0},{4,5},{5,6},{6,7},{7,4},{8,9},{9,10},{10,1... | collective-permute-start | bytes 196616 | tf_op jit(solution)/shard_map/ppermute | solution.py:375
  59.8 26.1 %collective-permute-start.12 = (bf16[128,256]{1,0:T(8,128)(2,1)S(1)}, bf16[128,256]{1,0:T(8,128)(2,1)S(1)}, u32[]{:S(2)}, u32[]{:S(2)}) collective-permute-start(bf16[128,256]{1,0:T(8,128)(2,1)S(1)} %get-tuple-element.34), channel_id=1, source_target_pairs={{0,2},{1,3},{2,0},{3,1},{4,6},{5,7},{6,4},{7,5},{8,10},{9,11},{10,... | collective-permute-start | bytes 196616 | tf_op jit(solution)/shard_map/ppermute | solution.py:375
  62.2 23.7 %collective-permute-start.13 = (bf16[128,256]{1,0:T(8,128)(2,1)S(1)}, bf16[128,256]{1,0:T(8,128)(2,1)S(1)}, u32[]{:S(2)}, u32[]{:S(2)}) collective-permute-start(bf16[128,256]{1,0:T(8,128)(2,1)S(1)} %get-tuple-element.35), channel_id=1, source_target_pairs={{0,3},{1,0},{2,1},{3,2},{4,7},{5,4},{6,5},{7,6},{8,11},{9,8},{10,9... | collective-permute-start | bytes 196616 | tf_op jit(solution)/shard_map/ppermute | solution.py:375
  86.5 6.0 %collective-permute-start.14 = (bf16[4,128,256]{2,1,0:T(8,128)(2,1)S(1)}, bf16[4,128,256]{2,1,0:T(8,128)(2,1)S(1)}, u32[]{:S(2)}, u32[]{:S(2)}) collective-permute-start(bf16[4,128,256]{2,1,0:T(8,128)(2,1)S(1)} %in_order.3.near_w), channel_id=1, source_target_pairs={{0,4},{4,0},{1,5},{5,1},{2,6},{6,2},{3,7},{7,3},{8,12},{12,8},{9,1... | collective-permute-start | bytes 786440 | tf_op jit(solution)/shard_map/ppermute | solution.py:377
  93.2 19.9 %collective-permute-start.15 = (bf16[2,4,256,128]{3,2,1,0:T(8,128)(2,1)}, bf16[2,4,256,128]{3,2,1,0:T(8,128)(2,1)}, u32[]{:S(2)}, u32[]{:S(2)}) collective-permute-start(bf16[2,4,256,128]{3,2,1,0:T(8,128)(2,1)} %get-tuple-element.39), channel_id=1, source_target_pairs={{0,4},{4,0},{1,5},{5,1},{2,6},{6,2},{3,7},{7,3},{8,12},{12,8},{9,1... | collective-permute-start | bytes 1572872 | tf_op jit(solution)/shard_map/ppermute | solution.py:381
  108.0 12.5 %all-to-all-start.2 = ((bf16[8,144,256]{2,1,0:T(8,128)(2,1)}), bf16[8,144,256]{2,1,0:T(8,128)(2,1)S(1)}, u32[]{:S(2)}, u32[]{:S(2)}) async-start(bf16[8,144,256]{2,1,0:T(8,128)(2,1)} %get-tuple-element.41), calls=%async_computation.2 | async-start | bytes 1179648 | tf_op jit(solution)/shard_map/all_to_all | solution.py:385
  113.1 3.7 %collective-permute-start.16 = (bf16[2,4,256,128]{3,2,1,0:T(8,128)(2,1)}, bf16[2,4,256,128]{3,2,1,0:T(8,128)(2,1)S(1)}, u32[]{:S(2)}, u32[]{:S(2)}) collective-permute-start(bf16[2,4,256,128]{3,2,1,0:T(8,128)(2,1)} %collective-permute-done.15.far0), channel_id=1, source_target_pairs={{0,32},{32,0},{1,33},{33,1},{2,34},{34,2},{3,35},{35,3},{4,36},{36... | collective-permute-start | bytes 1572872 | tf_op jit(solution)/shard_map/ppermute | solution.py:387
  124.2 40.8 %all-to-all-start.3 = ((bf16[4,256,256]{2,1,0:T(8,128)(2,1)}), bf16[4,256,256]{2,1,0:T(8,128)(2,1)S(1)}, u32[]{:S(2)}, u32[]{:S(2)}) async-start(bf16[4,256,256]{2,1,0:T(8,128)(2,1)} %get-tuple-element.52), calls=%async_computation.3 | async-start | bytes 1048576 | tf_op jit(solution)/shard_map/all_to_all | solution.py:397
  129.6 11.7 %collective-permute-start.17 = (bf16[256,256]{1,0:T(8,128)(2,1)S(1)}, bf16[256,256]{1,0:T(8,128)(2,1)S(1)}, u32[]{:S(2)}, u32[]{:S(2)}) collective-permute-start(bf16[256,256]{1,0:T(8,128)(2,1)S(1)} %get-tuple-element.44), channel_id=1, source_target_pairs={{0,8},{8,16},{16,24},{24,0},{1,9},{9,17},{17,25},{25,1},{2,10},{10... | collective-permute-start | bytes 393224 | tf_op jit(solution)/shard_map/ppermute | solution.py:393
  132.0 14.2 %collective-permute-start.18 = (bf16[256,256]{1,0:T(8,128)(2,1)S(1)}, bf16[256,256]{1,0:T(8,128)(2,1)S(1)}, u32[]{:S(2)}, u32[]{:S(2)}) collective-permute-start(bf16[256,256]{1,0:T(8,128)(2,1)S(1)} %get-tuple-element.45), channel_id=1, source_target_pairs={{0,16},{8,24},{16,0},{24,8},{1,17},{9,25},{17,1},{25,9},{2,18},{10... | collective-permute-start | bytes 393224 | tf_op jit(solution)/shard_map/ppermute | solution.py:393
  135.3 20.9 %collective-permute-start.19 = (bf16[256,256]{1,0:T(8,128)(2,1)S(1)}, bf16[256,256]{1,0:T(8,128)(2,1)S(1)}, u32[]{:S(2)}, u32[]{:S(2)}) collective-permute-start(bf16[256,256]{1,0:T(8,128)(2,1)S(1)} %get-tuple-element.46), channel_id=1, source_target_pairs={{0,24},{8,0},{16,8},{24,16},{1,25},{9,1},{17,9},{25,17},{2,26},{10... | collective-permute-start | bytes 393224 | tf_op jit(solution)/shard_map/ppermute | solution.py:393
  156.8 23.4 %collective-permute-start.20 = (bf16[256,256]{1,0:T(8,128)(2,1)S(1)}, bf16[256,256]{1,0:T(8,128)(2,1)S(1)}, u32[]{:S(2)}, u32[]{:S(2)}) collective-permute-start(bf16[256,256]{1,0:T(8,128)(2,1)S(1)} %add_up.2), channel_id=1, source_target_pairs={{0,0},{1,1},{2,2},{3,3},{4,32},{5,33},{6,34},{7,35},{8,64},{9,65},... | collective-permute-start | bytes 393224 | tf_op jit(solution)/shard_map/ppermute | solution.py:394
  165.6 17.4 %collective-permute-start.21 = (bf16[256,256]{1,0:T(8,128)(2,1)S(1)}, bf16[256,256]{1,0:T(8,128)(2,1)S(1)}, u32[]{:S(2)}, u32[]{:S(2)}) collective-permute-start(bf16[256,256]{1,0:T(8,128)(2,1)S(1)} %add_up.3), channel_id=1, source_target_pairs={{0,0},{1,1},{2,2},{3,3},{4,32},{5,33},{6,34},{7,35},{8,64},{9,65},... | collective-permute-start | bytes 393224 | tf_op jit(solution)/shard_map/ppermute | solution.py:398
  (8 other events, 65.8 us)

commit v4 on v3

--- a/solution.py
+++ b/solution.py
@@ -115,16 +115,21 @@
         mine, theirs = own[d][...], swapped[d][...]
         near_buf[at] = jnp.where(c == zl, mine, theirs)
         away_buf[at] = jnp.where(c == zl, theirs, mine)
-        total = total + dot(cot_ref[at * 2 + c], wide(mine))
-        total = total + dot(cot_ref[at * 2 + 1 - c], wide(theirs))
-    piece_ref[...] = total.astype(BF16)
     sends = [
-        pltpu.make_async_copy(piece_ref, copies_ref.at[s], sems.at[s]) for s in range(8)
+        pltpu.make_async_copy(near_buf, near_ref, sems.at[8]),
+        pltpu.make_async_copy(away_buf.at[pl.ds(c * 2, 2)], away_ref, sems.at[9]),
     ]
-    sends.append(pltpu.make_async_copy(near_buf, near_ref, sems.at[8]))
-    sends.append(pltpu.make_async_copy(away_buf.at[pl.ds(c * 2, 2)], away_ref, sems.at[9]))
     for send in sends:
         send.start()
+    for d in range(4):
+        at = (x - d) & 3
+        total = total + dot(cot_ref[at * 2 + c], wide(own[d]))
+        total = total + dot(cot_ref[at * 2 + 1 - c], wide(swapped[d]))
+    piece_ref[...] = total.astype(BF16)
+    for s in range(8):
+        send = pltpu.make_async_copy(piece_ref, copies_ref.at[s], sems.at[s])
+        send.start()
+        sends.append(send)
     for send in sends:
         send.wait()
 
@@ -363,10 +368,10 @@
 def body(activations, cotangent, weight, left_old, right_old):
     place = jnp.stack([lax.axis_index(a).astype(jnp.int32) for a in AXES])
     cot_turned = lax.ppermute(cotangent, AXES, SWAP)
-    slab = in_order(
-        place, [activations] + [lax.ppermute(activations, "y", shift(d)) for d in range(1, 4)]
-    )
+    crossed = [lax.ppermute(activations, "y", shift(d)) for d in range(1, 4)]
+    cot_turned, *crossed = lax.optimization_barrier((cot_turned, *crossed))
     cot_all = copies_to(cot_turned, ZAX, 8)
+    slab = in_order(place, [activations, *crossed])
     own = [slab] + [lax.ppermute(slab, "x", shift(d)) for d in range(1, 4)]
     swapped = [lax.ppermute(part, "c", FLIP) for part in own]
     weight, _ = lax.optimization_barrier((weight, slab))
@@ -374,27 +379,28 @@
     near_w = in_order(
         place, [cols[0]] + [lax.ppermute(cols[d], "y", shift(d)) for d in range(1, 4)]
     )
-    far_w = lax.ppermute(near_w, "zl", FLIP)
+    cot_all, near_w = lax.optimization_barrier((cot_all, near_w))
     copies, near, away = grad_piece(place, cot_all, own, swapped)
+
     pieces = lax.all_to_all(copies, SOLVER, 0, 0, tiled=True)
-    pieces, away, near_w, far_w = lax.optimization_barrier((pieces, away, near_w, far_w))
+    pieces, away, leaving_w = lax.optimization_barrier((pieces, away, near_w))
     far = lax.ppermute(away, "zl", FLIP)
+    far_w = lax.ppermute(leaving_w, "zl", FLIP)
     left_old = pltpu.with_memory_space_constraint(left_old[0, 0], pltpu.HBM)
     right_old = pltpu.with_memory_space_constraint(right_old[0, 0], pltpu.HBM)
     new_left, new_right, update, sent = solve(place, pieces, left_old, right_old)
     update_cols = lax.all_to_all(sent, SOLVER, 0, 0, tiled=True)
-    far, sent = lax.optimization_barrier((far, sent))
+    far, far_w, sent = lax.optimization_barrier((far, far_w, sent))
     far_swapped = lax.ppermute(far, "c", FLIP)
     weights = (near_w, far_w)
     acts = (near, far, far_swapped)
 
     parts = first_partial(place, weights, acts)
-    update_cols, _ = lax.optimization_barrier((update_cols, parts[0]))
     parts = [parts[0]] + [lax.ppermute(parts[e], "zh", shift(e)) for e in range(1, 4)]
-    first_out = lax.ppermute(add_up(place, *parts), AXES, SWAP)
-
+    update_cols, *parts = lax.optimization_barrier((update_cols, *parts))
     second, spread = second_partial(place, update_cols, weights, acts)
     arrived = lax.all_to_all(second, "zh", 0, 0, tiled=True)
+    first_out = lax.ppermute(add_up(place, *parts), AXES, SWAP)
     second_out = lax.ppermute(add_up(place, arrived), AXES, SWAP)
     direction = update / spread[0, 0]
     return (first_out, new_left[None, None], new_right[None, None], direction, second_out)

time: 186 us -> 185 us (level)
  blocking collectives: 0 us -> 28.5 us
  waiting for transfers between devices: 73.3 us -> 50 us
  starting transfers between devices: 76.9 us -> 70.4 us
    all_to_all x0 -> x1, blocking collectives: none -> 28.5 us  [body(): pieces = lax.all_to_all(copies, SOLVER, 0, 0, tiled=True)]
    ppermute x3, waiting for transfers between devices: 22.5 us -> 8.02 us  [body(): lax.ppermute(cols[d], 'y', shift(d))]
    ppermute x1, waiting for transfers between devices: 9.65 us -> 2.11 us  [body(): cot_turned = lax.ppermute(cotangent, AXES, SWAP)]
    all_to_all x1, waiting for transfers between devices: 0.01 us -> 6.86 us  [body(): arrived = lax.all_to_all(second, 'zh', 0, 0, tiled=True)]
    ppermute x3, waiting for transfers between devices: 17.1 us -> 10.3 us  [body(): lax.ppermute(parts[e], 'zh', shift(e))]
    ppermute x1, starting transfers between devices: 1.98 us -> 7.28 us  [body(): far_swapped = lax.ppermute(far, 'c', FLIP)]
    all_to_all x1 -> x0, starting transfers between devices: 4.36 us -> none  [body(): pieces = lax.all_to_all(copies, SOLVER, 0, 0, tiled=True)]
    ppermute x1, starting transfers between devices: 8.16 us -> 5.19 us  [body(): first_out = lax.ppermute(add_up(place, *parts), AXES, SWAP)]
  transfers between devices with their start and end apart: 26 -> 25, of which waited for: 14 -> 14; matrix products, arithmetic and copies ran while one was open for 2% -> 2% of each run, Pallas kernels for 10% -> 10%
where the time goes in v4:
time: 185 us; the launch traced here: 182 us
  starting transfers between devices  70.4 us (38%)
  waiting for transfers between devices  50 us (27%)
  blocking collectives  28.5 us (15%)
  Pallas kernels  24.1 us (13%)
  local copies, waits for them, and re-layouts  6.17 us (3%)
  other arithmetic  2.54 us (1%)
    all_to_all x1, blocking collectives, body(): pieces = lax.all_to_all(copies, SOLVER, 0, 0, tiled=True)  28.5 us
    pallas_call x1, Pallas kernels, solve(): call(solver_body, [VMEM, HBM, HBM], [HBM] * 4, [rows, rows, rows, pltpu.H...  13.6 us
    ppermute x3, waiting for transfers between devices, body(): lax.ppermute(parts[e], 'zh', shift(e))  10.3 us
    ppermute x4, starting transfers between devices, body(): swapped = [lax.ppermute(part, 'c', FLIP) for part in own]  9.86 us
    ppermute x1, waiting for transfers between devices, body(): first_out = lax.ppermute(add_up(place, *parts), AXES, SWAP)  8.29 us
    ppermute x3, waiting for transfers between devices, body(): lax.ppermute(cols[d], 'y', shift(d))  8.02 us
    ppermute x1, starting transfers between devices, body(): cot_turned = lax.ppermute(cotangent, AXES, SWAP)  7.96 us
    ppermute x3, starting transfers between devices, body(): lax.ppermute(parts[e], 'zh', shift(e))  7.55 us
  transfers between devices with their start and end apart: 25, of which 14 were waited for; matrix products, arithmetic and copies ran while one was open for 2% of the time, Pallas kernels for 10%

profile of v4, /device:TPU:7, one launch (start us, length us, event | category | flops | bytes accessed | tf_op | source)
XLA Modules:
  0.0 182.5 jit_solution(17697116475114755959)
XLA Ops:
  0.6 8.0 %collective-permute-start = (bf16[256,256]{1,0:T(8,128)(2,1)}, bf16[256,256]{1,0:T(8,128)(2,1)S(1)}, u32[]{:S(2)}, u32[]{:S(2)}) collective-permute-start(bf16[256,256]{1,0:T(8,128)(2,1)} %param.6), channel_id=1, source_target_pairs={{0,0},{1,1},{2,2},{3,3},{4,32},{5,33},{6,34},{7,35},{8,64},{9,65},... | collective-permute-start | bytes 393224 | tf_op jit(solution)/shard_map/ppermute | solution.py:370
  8.6 3.0 %collective-permute-start.2 = (bf16[256,128]{1,0:T(8,128)(2,1)}, bf16[256,128]{1,0:T(8,128)(2,1)S(1)}, u32[]{:S(2)}, u32[]{:S(2)}) collective-permute-start(bf16[256,128]{1,0:T(8,128)(2,1)} %refs_0_.1), channel_id=1, source_target_pairs={{0,2},{1,3},{2,0},{3,1},{4,6},{5,7},{6,4},{7,5},{8,10},{9,11},{10,... | collective-permute-start | bytes 196616 | tf_op jit(solution)/shard_map/ppermute | solution.py:371
  19.3 3.6 %all-to-all-start = ((bf16[8,256,256]{2,1,0:T(8,128)(2,1)}), bf16[8,256,256]{2,1,0:T(8,128)(2,1)S(1)}, u32[]{:S(2)}, u32[]{:S(2)}) async-start(bf16[8,256,256]{2,1,0:T(8,128)(2,1)} %broadcast_in_dim.9), calls=%async_computation | async-start | bytes 2097152 | tf_op jit(solution)/shard_map/all_to_all | solution.py:46
  25.4 2.8 %collective-permute-start.8 = (bf16[4,256,128]{2,1,0:T(8,128)(2,1)S(1)}, bf16[4,256,128]{2,1,0:T(8,128)(2,1)S(1)}, u32[]{:S(2)}, u32[]{:S(2)}) collective-permute-start(bf16[4,256,128]{2,1,0:T(8,128)(2,1)S(1)} %in_order.2.refs_0_), channel_id=1, source_target_pairs={{0,128},{64,192},{128,0},{192,64},{1,129},{65,193},{129,1},{193,65... | collective-permute-start | bytes 786440 | tf_op jit(solution)/shard_map/ppermute | solution.py:375
  30.9 6.0 %collective-permute-start.13 = (bf16[4,256,128]{2,1,0:T(8,128)(2,1)S(1)}, bf16[4,256,128]{2,1,0:T(8,128)(2,1)S(1)}, u32[]{:S(2)}, u32[]{:S(2)}) collective-permute-start(bf16[4,256,128]{2,1,0:T(8,128)(2,1)S(1)} %collective-permute-done.9.refs_3_), channel_id=1, source_target_pairs={{0,32},{32,0},{1,33},{33,1},{2,34},{34,2},{3,35},{35,3},{4,36},{36... | collective-permute-start | bytes 786440 | tf_op jit(solution)/shard_map/ppermute | solution.py:376
  37.9 3.0 %collective-permute-start.12 = (bf16[4,256,128]{2,1,0:T(8,128)(2,1)S(1)}, bf16[4,256,128]{2,1,0:T(8,128)(2,1)S(1)}, u32[]{:S(2)}, u32[]{:S(2)}) collective-permute-start(bf16[4,256,128]{2,1,0:T(8,128)(2,1)S(1)} %collective-permute-done.8.refs_2_), channel_id=1, source_target_pairs={{0,32},{32,0},{1,33},{33,1},{2,34},{34,2},{3,35},{35,3},{4,36},{36... | collective-permute-start | bytes 786440 | tf_op jit(solution)/shard_map/ppermute | solution.py:376
  43.9 3.1 %collective-permute-done.4.refs_1_ = bf16[128,256]{1,0:T(8,128)(2,1)S(1)} collective-permute-done((bf16[128,256]{1,0:T(8,128)(2,1)S(1)}, bf16[128,256]{1,0:T(8,128)(2,1)S(1)}, u32[]{:S(2)}, u32[]{:S(2)}) %collective-permute-start.4) | collective-permute-done | bytes 65568 | tf_op jit(solution)/shard_map/ppermute | solution.py:380
  48.6 3.3 %collective-permute-done.5.refs_2_ = bf16[128,256]{1,0:T(8,128)(2,1)S(1)} collective-permute-done((bf16[128,256]{1,0:T(8,128)(2,1)S(1)}, bf16[128,256]{1,0:T(8,128)(2,1)S(1)}, u32[]{:S(2)}, u32[]{:S(2)}) %collective-permute-start.5) | collective-permute-done | bytes 65568 | tf_op jit(solution)/shard_map/ppermute | solution.py:380
  55.6 3.6 %grad_piece.1 = (bf16[8,256,512]{2,1,0:T(8,128)(2,1)}, bf16[4,4,256,128]{3,2,1,0:T(8,128)(2,1)}, bf16[2,4,256,128]{3,2,1,0:T(8,128)(2,1)}) custom-call(s32[5]{0:T(128)S(1)} %stack.23.place, bf16[8,256,256]{2,1,0:T(8,128)(2,1)S(1)} %all-to-all-done.cot_ref, bf16[4,256,128]{2,1,0:T(8,128)(2,1)S(1)} %in_order.2.refs_0_, ...), custom_call_target="tpu_custom_call" | custom-call | tf_op jit(solution)/shard_map/grad_piece/pallas_call | solution.py:138
  59.2 28.5 %all_to_all.20.pieces_ref = bf16[8,256,512]{2,1,0:T(8,128)(2,1)S(1)} all-to-all(bf16[8,256,512]{2,1,0:T(8,128)(2,1)} %get-tuple-element.49), channel_id=1, replica_groups=mesh['x'=4,'c'=2,'zh'=4,'zl'=2,'y'=4] {'zl','y'}, dimensions={0} | all-to-all | bytes 4194304 | tf_op jit(solution)/shard_map/all_to_all | solution.py:385
  88.3 13.6 %solve.1 = (f32[128,1024]{1,0:T(8,128)}, f32[128,1024]{1,0:T(8,128)}, f32[128,1024]{1,0:T(8,128)}, bf16[8,144,256]{2,1,0:T(8,128)(2,1)}) custom-call(s32[5]{0:T(128)S(1)} %stack.23.place, bf16[8,256,512]{2,1,0:T(8,128)(2,1)S(1)} %all_to_all.20.pieces_ref, f32[1024,1024]{1,0:T(8,128)} %bitcast.10, f32[1024,1024]{1,0:T(8,128)} %bitcast.11), custom_call_target="tpu_custom_call" | custom-call | tf_op jit(solution)/shard_map/solve/pallas_call | solution.py:351
  101.9 3.5 %all-to-all-start.2 = ((bf16[8,144,256]{2,1,0:T(8,128)(2,1)}), bf16[8,144,256]{2,1,0:T(8,128)(2,1)S(1)}, u32[]{:S(2)}, u32[]{:S(2)}) async-start(bf16[8,144,256]{2,1,0:T(8,128)(2,1)} %get-tuple-element.53), calls=%async_computation.2 | async-start | bytes 1179648 | tf_op jit(solution)/shard_map/all_to_all | solution.py:392
  106.9 7.1 %collective-permute-done.15.far_w = bf16[4,128,256]{2,1,0:T(8,128)(2,1)S(1)} collective-permute-done((bf16[4,128,256]{2,1,0:T(8,128)(2,1)S(1)}, bf16[4,128,256]{2,1,0:T(8,128)(2,1)S(1)}, u32[]{:S(2)}, u32[]{:S(2)}) %collective-permute-start.15) | collective-permute-done | bytes 262176 | tf_op jit(solution)/shard_map/ppermute | solution.py:388
  114.0 7.3 %collective-permute-start.16 = (bf16[2,4,256,128]{3,2,1,0:T(8,128)(2,1)S(1)}, bf16[2,4,256,128]{3,2,1,0:T(8,128)(2,1)S(1)}, u32[]{:S(2)}, u32[]{:S(2)}) collective-permute-start(bf16[2,4,256,128]{3,2,1,0:T(8,128)(2,1)S(1)} %collective-permute-done.14.far0), channel_id=1, source_target_pairs={{0,32},{32,0},{1,33},{33,1},{2,34},{34,2},{3,35},{35,3},{4,36},{36... | collective-permute-start | bytes 1572872 | tf_op jit(solution)/shard_map/ppermute | solution.py:394
  129.8 3.3 %collective-permute-start.19 = (bf16[256,256]{1,0:T(8,128)(2,1)}, bf16[256,256]{1,0:T(8,128)(2,1)}, u32[]{:S(2)}, u32[]{:S(2)}) collective-permute-start(bf16[256,256]{1,0:T(8,128)(2,1)} %get-tuple-element.62), channel_id=1, source_target_pairs={{0,24},{8,0},{16,8},{24,16},{1,25},{9,1},{17,9},{25,17},{2,26},{10... | collective-permute-start | bytes 393224 | tf_op jit(solution)/shard_map/ppermute | solution.py:399
  133.1 2.4 %collective-permute-done.17.refs_1_ = bf16[256,256]{1,0:T(8,128)(2,1)} collective-permute-done((bf16[256,256]{1,0:T(8,128)(2,1)}, bf16[256,256]{1,0:T(8,128)(2,1)}, u32[]{:S(2)}, u32[]{:S(2)}) %collective-permute-start.17) | collective-permute-done | bytes 131104 | tf_op jit(solution)/shard_map/ppermute | solution.py:399
  135.5 4.7 %collective-permute-done.18.refs_2_ = bf16[256,256]{1,0:T(8,128)(2,1)} collective-permute-done((bf16[256,256]{1,0:T(8,128)(2,1)}, bf16[256,256]{1,0:T(8,128)(2,1)}, u32[]{:S(2)}, u32[]{:S(2)}) %collective-permute-start.18) | collective-permute-done | bytes 131104 | tf_op jit(solution)/shard_map/ppermute | solution.py:399
  140.2 3.2 %collective-permute-done.19.refs_3_ = bf16[256,256]{1,0:T(8,128)(2,1)} collective-permute-done((bf16[256,256]{1,0:T(8,128)(2,1)}, bf16[256,256]{1,0:T(8,128)(2,1)}, u32[]{:S(2)}, u32[]{:S(2)}) %collective-permute-start.19) | collective-permute-done | bytes 131104 | tf_op jit(solution)/shard_map/ppermute | solution.py:399
  145.6 5.2 %all-to-all-start.3 = ((bf16[4,256,256]{2,1,0:T(8,128)(2,1)}), bf16[4,256,256]{2,1,0:T(8,128)(2,1)S(1)}, u32[]{:S(2)}, u32[]{:S(2)}) async-start(bf16[4,256,256]{2,1,0:T(8,128)(2,1)} %copy-done.1), calls=%async_computation.3 | async-start | bytes 1048576 | tf_op jit(solution)/shard_map/all_to_all | solution.py:402
  152.4 5.2 %collective-permute-start.20 = (bf16[256,256]{1,0:T(8,128)(2,1)S(1)}, bf16[256,256]{1,0:T(8,128)(2,1)S(1)}, u32[]{:S(2)}, u32[]{:S(2)}) collective-permute-start(bf16[256,256]{1,0:T(8,128)(2,1)S(1)} %add_up.2), channel_id=1, source_target_pairs={{0,0},{1,1},{2,2},{3,3},{4,32},{5,33},{6,34},{7,35},{8,64},{9,65},... | collective-permute-start | bytes 393224 | tf_op jit(solution)/shard_map/ppermute | solution.py:403
  157.6 6.9 %all-to-all-done.3.refs_0_ = bf16[4,256,256]{2,1,0:T(8,128)(2,1)S(1)} async-done(((bf16[4,256,256]{2,1,0:T(8,128)(2,1)}), bf16[4,256,256]{2,1,0:T(8,128)(2,1)S(1)}, u32[]{:S(2)}, u32[]{:S(2)}) %all-to-all-start.3) | async-done | bytes 524320 | tf_op jit(solution)/shard_map/all_to_all | solution.py:402
  167.4 2.5 %broadcast_divide_fusion = f32[128,1024]{1,0:T(8,128)} fusion(f32[128,1024]{1,0:T(8,128)} %get-tuple-element.69, f32[]{:T(128)} %bitcast.9), kind=kLoop, calls=%fused_computation | loop fusion | flops 131072 | bytes 1048580 | tf_op jit(solution)/shard_map/div | solution.py:405
  170.0 8.3 %collective-permute-done.20 = bf16[256,256]{1,0:T(8,128)(2,1)S(1)} collective-permute-done((bf16[256,256]{1,0:T(8,128)(2,1)S(1)}, bf16[256,256]{1,0:T(8,128)(2,1)S(1)}, u32[]{:S(2)}, u32[]{:S(2)}) %collective-permute-start.20) | collective-permute-done | bytes 131104 | tf_op jit(solution)/shard_map/ppermute | solution.py:403
  178.3 2.9 %collective-permute-done.21 = bf16[256,256]{1,0:T(8,128)(2,1)S(1)} collective-permute-done((bf16[256,256]{1,0:T(8,128)(2,1)S(1)}, bf16[256,256]{1,0:T(8,128)(2,1)S(1)}, u32[]{:S(2)}, u32[]{:S(2)}) %collective-permute-start.21) | collective-permute-done | bytes 131104 | tf_op jit(solution)/shard_map/ppermute | solution.py:404
  (56 shorter events, 40.7 us)
Async XLA Ops:
  0.6 17.6 %collective-permute-start = (bf16[256,256]{1,0:T(8,128)(2,1)}, bf16[256,256]{1,0:T(8,128)(2,1)S(1)}, u32[]{:S(2)}, u32[]{:S(2)}) collective-permute-start(bf16[256,256]{1,0:T(8,128)(2,1)} %param.6), channel_id=1, source_target_pairs={{0,0},{1,1},{2,2},{3,3},{4,32},{5,33},{6,34},{7,35},{8,64},{9,65},... | collective-permute-start | bytes 393224 | tf_op jit(solution)/shard_map/ppermute | solution.py:370
  8.6 5.7 %collective-permute-start.2 = (bf16[256,128]{1,0:T(8,128)(2,1)}, bf16[256,128]{1,0:T(8,128)(2,1)S(1)}, u32[]{:S(2)}, u32[]{:S(2)}) collective-permute-start(bf16[256,128]{1,0:T(8,128)(2,1)} %refs_0_.1), channel_id=1, source_target_pairs={{0,2},{1,3},{2,0},{3,1},{4,6},{5,7},{6,4},{7,5},{8,10},{9,11},{10,... | collective-permute-start | bytes 196616 | tf_op jit(solution)/shard_map/ppermute | solution.py:371
  11.6 4.5 %collective-permute-start.1 = (bf16[256,128]{1,0:T(8,128)(2,1)}, bf16[256,128]{1,0:T(8,128)(2,1)S(1)}, u32[]{:S(2)}, u32[]{:S(2)}) collective-permute-start(bf16[256,128]{1,0:T(8,128)(2,1)} %refs_0_.1), channel_id=1, source_target_pairs={{0,1},{1,2},{2,3},{3,0},{4,5},{5,6},{6,7},{7,4},{8,9},{9,10},{10,1... | collective-permute-start | bytes 196616 | tf_op jit(solution)/shard_map/ppermute | solution.py:371
  12.0 4.1 %collective-permute-start.3 = (bf16[256,128]{1,0:T(8,128)(2,1)}, bf16[256,128]{1,0:T(8,128)(2,1)S(1)}, u32[]{:S(2)}, u32[]{:S(2)}) collective-permute-start(bf16[256,128]{1,0:T(8,128)(2,1)} %refs_0_.1), channel_id=1, source_target_pairs={{0,3},{1,0},{2,1},{3,2},{4,7},{5,4},{6,5},{7,6},{8,11},{9,8},{10,9... | collective-permute-start | bytes 196616 | tf_op jit(solution)/shard_map/ppermute | solution.py:371
  19.3 36.3 %all-to-all-start = ((bf16[8,256,256]{2,1,0:T(8,128)(2,1)}), bf16[8,256,256]{2,1,0:T(8,128)(2,1)S(1)}, u32[]{:S(2)}, u32[]{:S(2)}) async-start(bf16[8,256,256]{2,1,0:T(8,128)(2,1)} %broadcast_in_dim.9), calls=%async_computation | async-start | bytes 2097152 | tf_op jit(solution)/shard_map/all_to_all | solution.py:46
  24.4 6.6 %collective-permute-start.9 = (bf16[4,256,128]{2,1,0:T(8,128)(2,1)S(1)}, bf16[4,256,128]{2,1,0:T(8,128)(2,1)S(1)}, u32[]{:S(2)}, u32[]{:S(2)}) collective-permute-start(bf16[4,256,128]{2,1,0:T(8,128)(2,1)S(1)} %in_order.2.refs_0_), channel_id=1, source_target_pairs={{0,192},{64,0},{128,64},{192,128},{1,193},{65,1},{129,65},{193,129... | collective-permute-start | bytes 786440 | tf_op jit(solution)/shard_map/ppermute | solution.py:375
  25.4 12.5 %collective-permute-start.8 = (bf16[4,256,128]{2,1,0:T(8,128)(2,1)S(1)}, bf16[4,256,128]{2,1,0:T(8,128)(2,1)S(1)}, u32[]{:S(2)}, u32[]{:S(2)}) collective-permute-start(bf16[4,256,128]{2,1,0:T(8,128)(2,1)S(1)} %in_order.2.refs_0_), channel_id=1, source_target_pairs={{0,128},{64,192},{128,0},{192,64},{1,129},{65,193},{129,1},{193,65... | collective-permute-start | bytes 786440 | tf_op jit(solution)/shard_map/ppermute | solution.py:375
  28.2 12.8 %collective-permute-start.7 = (bf16[4,256,128]{2,1,0:T(8,128)(2,1)S(1)}, bf16[4,256,128]{2,1,0:T(8,128)(2,1)S(1)}, u32[]{:S(2)}, u32[]{:S(2)}) collective-permute-start(bf16[4,256,128]{2,1,0:T(8,128)(2,1)S(1)} %in_order.2.refs_0_), channel_id=1, source_target_pairs={{0,64},{64,128},{128,192},{192,0},{1,65},{65,129},{129,193},{193,1... | collective-permute-start | bytes 786440 | tf_op jit(solution)/shard_map/ppermute | solution.py:375
  30.1 25.4 %collective-permute-start.10 = (bf16[4,256,128]{2,1,0:T(8,128)(2,1)S(1)}, bf16[4,256,128]{2,1,0:T(8,128)(2,1)S(1)}, u32[]{:S(2)}, u32[]{:S(2)}) collective-permute-start(bf16[4,256,128]{2,1,0:T(8,128)(2,1)S(1)} %in_order.2.refs_0_), channel_id=1, source_target_pairs={{0,32},{32,0},{1,33},{33,1},{2,34},{34,2},{3,35},{35,3},{4,36},{36... | collective-permute-start | bytes 786440 | tf_op jit(solution)/shard_map/ppermute | solution.py:376
  30.9 24.6 %collective-permute-start.13 = (bf16[4,256,128]{2,1,0:T(8,128)(2,1)S(1)}, bf16[4,256,128]{2,1,0:T(8,128)(2,1)S(1)}, u32[]{:S(2)}, u32[]{:S(2)}) collective-permute-start(bf16[4,256,128]{2,1,0:T(8,128)(2,1)S(1)} %collective-permute-done.9.refs_3_), channel_id=1, source_target_pairs={{0,32},{32,0},{1,33},{33,1},{2,34},{34,2},{3,35},{35,3},{4,36},{36... | collective-permute-start | bytes 786440 | tf_op jit(solution)/shard_map/ppermute | solution.py:376
  37.9 17.7 %collective-permute-start.12 = (bf16[4,256,128]{2,1,0:T(8,128)(2,1)S(1)}, bf16[4,256,128]{2,1,0:T(8,128)(2,1)S(1)}, u32[]{:S(2)}, u32[]{:S(2)}) collective-permute-start(bf16[4,256,128]{2,1,0:T(8,128)(2,1)S(1)} %collective-permute-done.8.refs_2_), channel_id=1, source_target_pairs={{0,32},{32,0},{1,33},{33,1},{2,34},{34,2},{3,35},{35,3},{4,36},{36... | collective-permute-start | bytes 786440 | tf_op jit(solution)/shard_map/ppermute | solution.py:376
  41.0 14.7 %collective-permute-start.11 = (bf16[4,256,128]{2,1,0:T(8,128)(2,1)S(1)}, bf16[4,256,128]{2,1,0:T(8,128)(2,1)S(1)}, u32[]{:S(2)}, u32[]{:S(2)}) collective-permute-start(bf16[4,256,128]{2,1,0:T(8,128)(2,1)S(1)} %collective-permute-done.7.refs_1_), channel_id=1, source_target_pairs={{0,32},{32,0},{1,33},{33,1},{2,34},{34,2},{3,35},{35,3},{4,36},{36... | collective-permute-start | bytes 786440 | tf_op jit(solution)/shard_map/ppermute | solution.py:376
  42.5 4.5 %collective-permute-start.4 = (bf16[128,256]{1,0:T(8,128)(2,1)S(1)}, bf16[128,256]{1,0:T(8,128)(2,1)S(1)}, u32[]{:S(2)}, u32[]{:S(2)}) collective-permute-start(bf16[128,256]{1,0:T(8,128)(2,1)S(1)} %get-tuple-element.45), channel_id=1, source_target_pairs={{0,1},{1,2},{2,3},{3,0},{4,5},{5,6},{6,7},{7,4},{8,9},{9,10},{10,1... | collective-permute-start | bytes 196616 | tf_op jit(solution)/shard_map/ppermute | solution.py:380
  47.0 4.9 %collective-permute-start.5 = (bf16[128,256]{1,0:T(8,128)(2,1)S(1)}, bf16[128,256]{1,0:T(8,128)(2,1)S(1)}, u32[]{:S(2)}, u32[]{:S(2)}) collective-permute-start(bf16[128,256]{1,0:T(8,128)(2,1)S(1)} %get-tuple-element.46), channel_id=1, source_target_pairs={{0,2},{1,3},{2,0},{3,1},{4,6},{5,7},{6,4},{7,5},{8,10},{9,11},{10,... | collective-permute-start | bytes 196616 | tf_op jit(solution)/shard_map/ppermute | solution.py:380
  87.7 26.3 %collective-permute-start.14 = (bf16[2,4,256,128]{3,2,1,0:T(8,128)(2,1)S(1)}, bf16[2,4,256,128]{3,2,1,0:T(8,128)(2,1)S(1)}, u32[]{:S(2)}, u32[]{:S(2)}) collective-permute-start(bf16[2,4,256,128]{3,2,1,0:T(8,128)(2,1)S(1)} %copy-done.6), channel_id=1, source_target_pairs={{0,4},{4,0},{1,5},{5,1},{2,6},{6,2},{3,7},{7,3},{8,12},{12,8},{9,1... | collective-permute-start | bytes 1572872 | tf_op jit(solution)/shard_map/ppermute | solution.py:387
  101.9 31.1 %all-to-all-start.2 = ((bf16[8,144,256]{2,1,0:T(8,128)(2,1)}), bf16[8,144,256]{2,1,0:T(8,128)(2,1)S(1)}, u32[]{:S(2)}, u32[]{:S(2)}) async-start(bf16[8,144,256]{2,1,0:T(8,128)(2,1)} %get-tuple-element.53), calls=%async_computation.2 | async-start | bytes 1179648 | tf_op jit(solution)/shard_map/all_to_all | solution.py:392
  105.5 8.5 %collective-permute-start.15 = (bf16[4,128,256]{2,1,0:T(8,128)(2,1)S(1)}, bf16[4,128,256]{2,1,0:T(8,128)(2,1)S(1)}, u32[]{:S(2)}, u32[]{:S(2)}) collective-permute-start(bf16[4,128,256]{2,1,0:T(8,128)(2,1)S(1)} %in_order.3.near_w), channel_id=1, source_target_pairs={{0,4},{4,0},{1,5},{5,1},{2,6},{6,2},{3,7},{7,3},{8,12},{12,8},{9,1... | collective-permute-start | bytes 786440 | tf_op jit(solution)/shard_map/ppermute | solution.py:388
  114.0 8.8 %collective-permute-start.16 = (bf16[2,4,256,128]{3,2,1,0:T(8,128)(2,1)S(1)}, bf16[2,4,256,128]{3,2,1,0:T(8,128)(2,1)S(1)}, u32[]{:S(2)}, u32[]{:S(2)}) collective-permute-start(bf16[2,4,256,128]{3,2,1,0:T(8,128)(2,1)S(1)} %collective-permute-done.14.far0), channel_id=1, source_target_pairs={{0,32},{32,0},{1,33},{33,1},{2,34},{34,2},{3,35},{35,3},{4,36},{36... | collective-permute-start | bytes 1572872 | tf_op jit(solution)/shard_map/ppermute | solution.py:394
  125.5 10.0 %collective-permute-start.17 = (bf16[256,256]{1,0:T(8,128)(2,1)}, bf16[256,256]{1,0:T(8,128)(2,1)}, u32[]{:S(2)}, u32[]{:S(2)}) collective-permute-start(bf16[256,256]{1,0:T(8,128)(2,1)} %get-tuple-element.60), channel_id=1, source_target_pairs={{0,8},{8,16},{16,24},{24,0},{1,9},{9,17},{17,25},{25,1},{2,10},{10... | collective-permute-start | bytes 393224 | tf_op jit(solution)/shard_map/ppermute | solution.py:399
  127.4 12.9 %collective-permute-start.18 = (bf16[256,256]{1,0:T(8,128)(2,1)}, bf16[256,256]{1,0:T(8,128)(2,1)}, u32[]{:S(2)}, u32[]{:S(2)}) collective-permute-start(bf16[256,256]{1,0:T(8,128)(2,1)} %get-tuple-element.61), channel_id=1, source_target_pairs={{0,16},{8,24},{16,0},{24,8},{1,17},{9,25},{17,1},{25,9},{2,18},{10... | collective-permute-start | bytes 393224 | tf_op jit(solution)/shard_map/ppermute | solution.py:399
  129.8 13.6 %collective-permute-start.19 = (bf16[256,256]{1,0:T(8,128)(2,1)}, bf16[256,256]{1,0:T(8,128)(2,1)}, u32[]{:S(2)}, u32[]{:S(2)}) collective-permute-start(bf16[256,256]{1,0:T(8,128)(2,1)} %get-tuple-element.62), channel_id=1, source_target_pairs={{0,24},{8,0},{16,8},{24,16},{1,25},{9,1},{17,9},{25,17},{2,26},{10... | collective-permute-start | bytes 393224 | tf_op jit(solution)/shard_map/ppermute | solution.py:399
  145.6 18.9 %all-to-all-start.3 = ((bf16[4,256,256]{2,1,0:T(8,128)(2,1)}), bf16[4,256,256]{2,1,0:T(8,128)(2,1)S(1)}, u32[]{:S(2)}, u32[]{:S(2)}) async-start(bf16[4,256,256]{2,1,0:T(8,128)(2,1)} %copy-done.1), calls=%async_computation.3 | async-start | bytes 1048576 | tf_op jit(solution)/shard_map/all_to_all | solution.py:402
  152.4 25.8 %collective-permute-start.20 = (bf16[256,256]{1,0:T(8,128)(2,1)S(1)}, bf16[256,256]{1,0:T(8,128)(2,1)S(1)}, u32[]{:S(2)}, u32[]{:S(2)}) collective-permute-start(bf16[256,256]{1,0:T(8,128)(2,1)S(1)} %add_up.2), channel_id=1, source_target_pairs={{0,0},{1,1},{2,2},{3,3},{4,32},{5,33},{6,34},{7,35},{8,64},{9,65},... | collective-permute-start | bytes 393224 | tf_op jit(solution)/shard_map/ppermute | solution.py:403
  165.1 16.1 %collective-permute-start.21 = (bf16[256,256]{1,0:T(8,128)(2,1)S(1)}, bf16[256,256]{1,0:T(8,128)(2,1)S(1)}, u32[]{:S(2)}, u32[]{:S(2)}) collective-permute-start(bf16[256,256]{1,0:T(8,128)(2,1)S(1)} %add_up.3), channel_id=1, source_target_pairs={{0,0},{1,1},{2,2},{3,3},{4,32},{5,33},{6,34},{7,35},{8,64},{9,65},... | collective-permute-start | bytes 393224 | tf_op jit(solution)/shard_map/ppermute | solution.py:404
  (8 other events, 95.2 us)

commit v5 on v4

--- a/solution.py
+++ b/solution.py
@@ -74,107 +74,132 @@
     return jnp.concatenate([slab[q] for q in range(4)], axis=1)
 
 
-def order_body(place, *refs):
-    for d in range(4):
-        refs[4][(place[4] - d) & 3] = refs[d][...]
-
-
-def in_order(place, parts):
-    shape = SHAPE((4, *parts[0].shape), BF16)
-    return call(order_body, [VMEM] * 4, VMEM, shape, limit=8, name="in_order")(place, *parts)
-
-
-def columns_body(place, weight_ref, *refs):
+def pack_body(place, acts_ref, weight_ref, *refs):
     outs, work = refs[:4], refs[4]
     for q in range(4):
-        work[q] = weight_ref[:, q * 256 : (q + 1) * 256]
+        for half in range(2):
+            at = q * 256 + half * 128
+            work[q, half * 128 : (half + 1) * 128, :] = weight_ref[:, at : at + 128]
+    acts = acts_ref[...]
     for d in range(4):
-        outs[d][...] = work[(place[4] + d) & 3]
-
-
-def columns(place, weight):
-    part = SHAPE((128, 256), BF16)
+        outs[d][:256, :] = acts
+        outs[d][256:, :] = work[(place[4] + d) & 3]
+
+
+def pack(place, acts, weight):
+    part = SHAPE((512, 128), BF16)
     return call(
-        columns_body,
-        [VMEM],
+        pack_body,
+        [VMEM] * 2,
         [VMEM] * 4,
         [part] * 4,
-        scratch=[pltpu.VMEM((4, 128, 256), BF16)],
+        scratch=[pltpu.VMEM((4, 256, 128), BF16)],
         limit=8,
-        name="columns",
-    )(place, weight)
-
-
-def grad_body(place, cot_ref, *refs):
+        name="pack",
+    )(place, acts, weight)
+
+
+def unpack_body(place, *refs):
+    for d in range(4):
+        at = (place[4] - d) & 3
+        refs[4][at] = refs[d][:256, :]
+        refs[5][at] = refs[d][256:, :]
+
+
+def unpack(place, parts):
+    shape = SHAPE((4, 256, 128), BF16)
+    return call(unpack_body, [VMEM] * 4, [VMEM] * 2, [shape] * 2, limit=8, name="unpack")(
+        place, *parts
+    )
+
+
+def weight_of(parts):
+    rows = [jnp.concatenate([parts[q, :128, :], parts[q, 128:, :]], axis=1) for q in range(4)]
+    return jnp.concatenate(rows, axis=0)
+
+
+def grad_body(place, cot_ref, weight_ref, *refs):
     own, swapped = refs[:4], refs[4:8]
-    copies_ref, near_ref, away_ref, piece_ref, near_buf, away_buf, sems = refs[8:]
+    piece_ref, near_ref, away_ref, near_buf, away_buf, sems = refs[8:]
     x, c, zl = place[0], place[1], place[3]
-    total = jnp.zeros((256, 512), F32)
     for d in range(4):
         at = (x - d) & 3
         mine, theirs = own[d][...], swapped[d][...]
         near_buf[at] = jnp.where(c == zl, mine, theirs)
         away_buf[at] = jnp.where(c == zl, theirs, mine)
     sends = [
-        pltpu.make_async_copy(near_buf, near_ref, sems.at[8]),
-        pltpu.make_async_copy(away_buf.at[pl.ds(c * 2, 2)], away_ref, sems.at[9]),
+        pltpu.make_async_copy(near_buf, near_ref, sems.at[0]),
+        pltpu.make_async_copy(
+            away_buf.at[pl.ds(c * 2, 2)], away_ref.at[pl.ds(0, 2)], sems.at[1]
+        ),
+        pltpu.make_async_copy(weight_ref, away_ref.at[2], sems.at[2]),
     ]
     for send in sends:
         send.start()
+    total = jnp.zeros((256, 512), F32)
     for d in range(4):
         at = (x - d) & 3
         total = total + dot(cot_ref[at * 2 + c], wide(own[d]))
         total = total + dot(cot_ref[at * 2 + 1 - c], wide(swapped[d]))
     piece_ref[...] = total.astype(BF16)
-    for s in range(8):
-        send = pltpu.make_async_copy(piece_ref, copies_ref.at[s], sems.at[s])
-        send.start()
-        sends.append(send)
     for send in sends:
         send.wait()
 
 
-def grad_piece(place, cot_all, own, swapped):
+def grad_piece(place, cot_all, near_w, own, swapped):
     return call(
         grad_body,
-        [VMEM] * 9,
-        [HBM] * 3,
+        [VMEM] * 10,
+        [VMEM, HBM, HBM],
         [
-            pltpu.HBM((8, 256, 512), BF16),
+            SHAPE((256, 512), BF16),
             pltpu.HBM((4, 4, 256, 128), BF16),
-            pltpu.HBM((2, 4, 256, 128), BF16),
+            pltpu.HBM((3, 4, 256, 128), BF16),
         ],
         scratch=[
-            pltpu.VMEM((256, 512), BF16),
             pltpu.VMEM((4, 4, 256, 128), BF16),
             pltpu.VMEM((4, 4, 256, 128), BF16),
-            pltpu.SemaphoreType.DMA((10,)),
+            pltpu.SemaphoreType.DMA((3,)),
         ],
         limit=10,
         name="grad_piece",
-    )(place, cot_all, *own, *swapped)
-
-
-def forward_groups(place, near_t, far_t, near_ref, far_refs, out_ref):
-    c = place[1]
-    for i in range(2):
-        for j in range(2):
-            at = (c * 2 if i == 0 else 2 - c * 2) + j
-            total = dot_minor(near_t, wide(near_ref.at[at]))
-            total = total + dot_minor(far_t, wide(far_refs[i].at[j]))
-            out_ref[at] = total.astype(BF16)
-
-
-def first_body(place, near_w, far_w, near_ref, far0, far1, *refs):
-    outs, work = refs[:4], refs[4]
-    near_t = near_w[...].reshape(512, 256).T
-    far_t = far_w[...].reshape(512, 256).T
-    forward_groups(place, near_t, far_t, near_ref, (far0, far1), work)
-    for e in range(4):
-        outs[e][...] = work[(place[2] + e) & 3]
-
-
-def second_body(place, update_ref, near_w, far_w, near_ref, far0, far1, out_ref, spread_ref):
+    )(place, cot_all, near_w, *own, *swapped)
+
+
+def first_body(place, weight_ref, *refs):
+    own, swapped = refs[:4], refs[4:8]
+    out_ref, work, sems = refs[8:]
+    weight_t = weight_of(weight_ref).T
+    sends = []
+    for d in range(4):
+        at = ((place[0] - d) & 3) * 2
+        for i, (slab, group) in enumerate(
+            ((own[d], at + place[1]), (swapped[d], at + 1 - place[1]))
+        ):
+            work[d * 2 + i] = dot_minor(weight_t, wide(slab)).astype(BF16)
+            sends.append(
+                pltpu.make_async_copy(work.at[d * 2 + i], out_ref.at[group], sems.at[d * 2 + i])
+            )
+            sends[-1].start()
+    for send in sends:
+        send.wait()
+
+
+def first_partial(place, near_w, own, swapped):
+    return call(
+        first_body,
+        [VMEM] * 9,
+        HBM,
+        pltpu.HBM((8, 256, 256), BF16),
+        scratch=[pltpu.VMEM((8, 256, 256), BF16), pltpu.SemaphoreType.DMA((8,))],
+        limit=12,
+        name="first_partial",
+    )(place, near_w, *own, *swapped)
+
+
+def second_body(
+    place, update_ref, near_w, near_ref, far_ref, swap_ref, out_ref, spread_ref, work, sems
+):
     squares = jnp.zeros((16, 128), F32)
     for s in range(8):
         squares = squares + update_ref[s, 128:144, :128].astype(F32)
@@ -182,56 +207,52 @@
     spread = jnp.sqrt(mean + EPSILON)
     spread_ref[...] = jnp.broadcast_to(spread, (8, 128))
     rate = LEARN_RATE / spread
-    zl = place[3]
+    c, zl = place[1], place[3]
 
     def changed(weight, first):
         update = jnp.concatenate([update_ref[first + q, :128, :] for q in range(4)], axis=0)
-        weight = weight[...].reshape(512, 256)
-        return (weight.astype(F32) - rate * update.astype(F32)).astype(BF16).T
+        return (weight_of(weight).astype(F32) - rate * update.astype(F32)).astype(BF16).T
 
     near_t = changed(near_w, zl * 4)
-    far_t = changed(far_w, 4 - zl * 4)
-    forward_groups(place, near_t, far_t, near_ref, (far0, far1), out_ref)
-
-
-def first_partial(place, weights, acts):
-    part = SHAPE((256, 256), BF16)
-    return call(
-        first_body,
-        [VMEM] * 5,
-        [VMEM] * 4,
-        [part] * 4,
-        scratch=[pltpu.VMEM((4, 256, 256), BF16)],
-        limit=12,
-        name="first_partial",
-    )(place, *weights, *acts)
-
-
-def second_partial(place, update_cols, weights, acts):
+    far_t = changed(far_ref.at[2], 4 - zl * 4)
+    sends = []
+    for i in range(2):
+        for j in range(2):
+            at = (c * 2 if i == 0 else 2 - c * 2) + j
+            total = dot_minor(near_t, wide(near_ref.at[at]))
+            total = total + dot_minor(far_t, wide((far_ref, swap_ref)[i].at[j]))
+            work[i * 2 + j] = total.astype(BF16)
+            sends.append(
+                pltpu.make_async_copy(work.at[i * 2 + j], out_ref.at[at], sems.at[i * 2 + j])
+            )
+            sends[-1].start()
+    for send in sends:
+        send.wait()
+
+
+def second_partial(place, update_cols, near_w, near, far, far_swapped):
     return call(
         second_body,
-        [VMEM] * 6,
-        [VMEM] * 2,
-        [SHAPE((4, 256, 256), BF16), SHAPE((8, 128), F32)],
+        [VMEM] * 5,
+        [HBM, VMEM],
+        [pltpu.HBM((4, 256, 256), BF16), SHAPE((8, 128), F32)],
+        scratch=[pltpu.VMEM((4, 256, 256), BF16), pltpu.SemaphoreType.DMA((4,))],
         limit=12,
         name="second_partial",
-    )(place, update_cols, *weights, *acts)
-
-
-def add_body(place, *refs):
-    parts = refs[:-1]
-    if len(parts) == 1:
-        parts = [parts[0].at[i] for i in range(4)]
-    total = parts[0][...].astype(F32)
-    for part in parts[1:]:
-        total = total + part[...].astype(F32)
-    refs[-1][...] = total.astype(BF16)
-
-
-def add_up(place, *parts):
-    return call(
-        add_body, [VMEM] * len(parts), VMEM, SHAPE((256, 256), BF16), limit=8, name="add_up"
-    )(place, *parts)
+    )(place, update_cols, near_w, near, far, far_swapped)
+
+
+def add_body(place, parts_ref, out_ref):
+    total = parts_ref[0].astype(F32)
+    for i in range(1, parts_ref.shape[0]):
+        total = total + parts_ref[i].astype(F32)
+    out_ref[...] = total.astype(BF16)
+
+
+def add_up(place, parts):
+    return call(add_body, [VMEM], VMEM, SHAPE((256, 256), BF16), limit=8, name="add_up")(
+        place, parts
+    )
 
 
 def statistics(lhs_ref, rhs_ref, old_ref, full_ref, off_ref):
@@ -266,13 +287,21 @@
 
 def solver_body(
     place,
-    pieces_ref,
+    near0,
+    near1,
+    near2,
+    near3,
+    far0,
+    far1,
+    far2,
+    far3,
     left_old_ref,
     right_old_ref,
     new_left_ref,
     new_right_ref,
     update_ref,
     sent_ref,
+    pieces_ref,
     left_buf,
     right_buf,
     grad_ref,
@@ -291,6 +320,10 @@
     load_right.start()
     first = pl.multiple_of((place[3] * 4 + place[4]) * 128, 128)
     own = pl.ds(first, 128)
+    for d, (near, far) in enumerate(((near0, far0), (near1, far1), (near2, far2), (near3, far3))):
+        at = (place[4] - d) & 3
+        pieces_ref[place[3] * 4 + at] = near[...]
+        pieces_ref[4 - place[3] * 4 + at] = far[...]
     for zl in range(2):
         for y in range(4):
             piece = pieces_ref[zl * 4 + y]
@@ -350,57 +383,54 @@
     rows = pltpu.HBM((128, BLOCK), F32)
     return call(
         solver_body,
-        [VMEM, HBM, HBM],
+        [*[VMEM] * 8, HBM, HBM],
         [HBM] * 4,
         [rows, rows, rows, pltpu.HBM((8, 144, 256), BF16)],
         scratch=[
+            pltpu.VMEM((8, 256, 512), BF16),
             *[pltpu.VMEM(square, kind) for kind in (F32, F32, BF16, BF16, F32, BF16, BF16)],
             pltpu.VMEM((128, BLOCK), F32),
             pltpu.VMEM((128, BLOCK), F32),
             pltpu.VMEM((4, 144, 256), BF16),
             pltpu.SemaphoreType.DMA((7,)),
         ],
-        limit=30,
+        limit=27,
         name="solve",
-    )(place, pieces, left_old, right_old)
+    )(place, *pieces, left_old, right_old)
 
 
 def body(activations, cotangent, weight, left_old, right_old):
     place = jnp.stack([lax.axis_index(a).astype(jnp.int32) for a in AXES])
     cot_turned = lax.ppermute(cotangent, AXES, SWAP)
-    crossed = [lax.ppermute(activations, "y", shift(d)) for d in range(1, 4)]
+    packed = pack(place, activations, weight)
+    crossed = [lax.ppermute(packed[d], "y", shift(d)) for d in range(1, 4)]
     cot_turned, *crossed = lax.optimization_barrier((cot_turned, *crossed))
     cot_all = copies_to(cot_turned, ZAX, 8)
-    slab = in_order(place, [activations, *crossed])
+    slab, near_w = unpack(place, [packed[0], *crossed])
     own = [slab] + [lax.ppermute(slab, "x", shift(d)) for d in range(1, 4)]
     swapped = [lax.ppermute(part, "c", FLIP) for part in own]
-    weight, _ = lax.optimization_barrier((weight, slab))
-    cols = columns(place, weight)
-    near_w = in_order(
-        place, [cols[0]] + [lax.ppermute(cols[d], "y", shift(d)) for d in range(1, 4)]
-    )
-    cot_all, near_w = lax.optimization_barrier((cot_all, near_w))
-    copies, near, away = grad_piece(place, cot_all, own, swapped)
-
-    pieces = lax.all_to_all(copies, SOLVER, 0, 0, tiled=True)
-    pieces, away, leaving_w = lax.optimization_barrier((pieces, away, near_w))
+    first = first_partial(place, near_w, own, swapped)
+    cot_all, first = lax.optimization_barrier((cot_all, first))
+    piece, near, away = grad_piece(place, cot_all, near_w, own, swapped)
+
+    beside = lax.ppermute(piece, "zl", FLIP)
+    pieces = [piece] + [lax.ppermute(piece, "y", shift(d)) for d in range(1, 4)]
+    pieces += [beside] + [lax.ppermute(beside, "y", shift(d)) for d in range(1, 4)]
+    first, *_ = lax.optimization_barrier((first, beside, pieces[1], pieces[3]))
+    first_parts = lax.all_to_all(first, ZAX, 0, 0, tiled=True)
+    away, first, *pieces = lax.optimization_barrier((away, first, *pieces))
     far = lax.ppermute(away, "zl", FLIP)
-    far_w = lax.ppermute(leaving_w, "zl", FLIP)
     left_old = pltpu.with_memory_space_constraint(left_old[0, 0], pltpu.HBM)
     right_old = pltpu.with_memory_space_constraint(right_old[0, 0], pltpu.HBM)
     new_left, new_right, update, sent = solve(place, pieces, left_old, right_old)
+    sent, first_parts = lax.optimization_barrier((sent, first_parts))
     update_cols = lax.all_to_all(sent, SOLVER, 0, 0, tiled=True)
-    far, far_w, sent = lax.optimization_barrier((far, far_w, sent))
+    far, sent = lax.optimization_barrier((far, sent))
     far_swapped = lax.ppermute(far, "c", FLIP)
-    weights = (near_w, far_w)
-    acts = (near, far, far_swapped)
-
-    parts = first_partial(place, weights, acts)
-    parts = [parts[0]] + [lax.ppermute(parts[e], "zh", shift(e)) for e in range(1, 4)]
-    update_cols, *parts = lax.optimization_barrier((update_cols, *parts))
-    second, spread = second_partial(place, update_cols, weights, acts)
+    first_out = lax.ppermute(add_up(place, first_parts), AXES, SWAP)
+
+    second, spread = second_partial(place, update_cols, near_w, near, far, far_swapped)
     arrived = lax.all_to_all(second, "zh", 0, 0, tiled=True)
-    first_out = lax.ppermute(add_up(place, *parts), AXES, SWAP)
     second_out = lax.ppermute(add_up(place, arrived), AXES, SWAP)
     direction = update / spread[0, 0]
     return (first_out, new_left[None, None], new_right[None, None], direction, second_out)

time: 185 us -> 174 us (0.941); the launches traced: 182 us -> 174 us
  waiting for transfers between devices: 50 us -> 78.6 us
  blocking collectives: 28.5 us -> 0 us
  starting transfers between devices: 70.4 us -> 59.9 us
    all_to_all x1 -> x0, blocking collectives: 28.5 us -> none  [body(): pieces = lax.all_to_all(copies, SOLVER, 0, 0, tiled=True)]
    all_to_all x1, waiting for transfers between devices: 0.01 us -> 8.99 us  [copies_to(): return lax.all_to_all(copies, axis, split_axis=0, concat_axis=0, tiled=True)]
    ppermute x3, waiting for transfers between devices: 0.95 us -> 9.16 us  [body(): own = [slab] + [lax.ppermute(slab, 'x', shift(d)) for d in range(1, 4)]]
    ppermute x11, waiting for transfers between devices: 35.6 us -> 43.3 us  [the longest x1 15.3 us: body(): first_out = lax.ppermute(add_up(place, first_parts), AXES, SWAP)]
    all_to_all x1, waiting for transfers between devices: 6.86 us -> 0.01 us  [body(): arrived = lax.all_to_all(second, 'zh', 0, 0, tiled=True)]
    ppermute x1, starting transfers between devices: 7.28 us -> 0.65 us  [body(): far_swapped = lax.ppermute(far, 'c', FLIP)]
    ppermute x4, starting transfers between devices: 9.86 us -> 4.32 us  [body(): swapped = [lax.ppermute(part, 'c', FLIP) for part in own]]
    ppermute x11, starting transfers between devices: 24.3 us -> 18.8 us  [the longest x1 7.73 us: body(): first_out = lax.ppermute(add_up(place, first_parts), AXES, SWAP)]
  transfers between devices with their start and end apart: 25 -> 26, of which waited for: 14 -> 17; matrix products, arithmetic and copies ran while one was open for 2% -> 2% of each run, Pallas kernels for 10% -> 10%
where the time goes in v5:
time: 174 us
  waiting for transfers between devices  78.6 us (45%)
  starting transfers between devices  59.9 us (34%)
  Pallas kernels  24 us (14%)
  local copies, waits for them, and re-layouts  7.72 us (4%)
  other arithmetic  2.54 us (1%)
    ppermute x1, waiting for transfers between devices, body(): first_out = lax.ppermute(add_up(place, first_parts), AXES, SWAP)  15.3 us
    pallas_call x1, Pallas kernels, solve(): call(solver_body, [*[VMEM] * 8, HBM, HBM], [HBM] * 4, [rows, rows, rows,...  13.8 us
    ppermute x3, waiting for transfers between devices, body(): lax.ppermute(beside, 'y', shift(d))  13.3 us
    ppermute x3, waiting for transfers between devices, body(): pieces = [piece] + [lax.ppermute(piece, 'y', shift(d)) for d in range(1, 4)]  12.3 us
    ppermute x3, waiting for transfers between devices, body(): own = [slab] + [lax.ppermute(slab, 'x', shift(d)) for d in range(1, 4)]  9.16 us
    all_to_all x1, waiting for transfers between devices, copies_to(): return lax.all_to_all(copies, axis, split_axis=0, concat_axis=0, tiled=True)  8.99 us
    ppermute x1, starting transfers between devices, body(): cot_turned = lax.ppermute(cotangent, AXES, SWAP)  7.96 us
    ppermute x1, starting transfers between devices, body(): first_out = lax.ppermute(add_up(place, first_parts), AXES, SWAP)  7.73 us
  transfers between devices with their start and end apart: 26, of which 17 were waited for; matrix products, arithmetic and copies ran while one was open for 2% of the time, Pallas kernels for 10%

profile of v5, /device:TPU:7, one launch (start us, length us, event | category | flops | bytes accessed | tf_op | source)
XLA Modules:
  0.0 173.6 jit_solution(14020233084778421278)
XLA Ops:
  0.6 8.0 %collective-permute-start = (bf16[256,256]{1,0:T(8,128)(2,1)}, bf16[256,256]{1,0:T(8,128)(2,1)S(1)}, u32[]{:S(2)}, u32[]{:S(2)}) collective-permute-start(bf16[256,256]{1,0:T(8,128)(2,1)} %param.6), channel_id=1, source_target_pairs={{0,0},{1,1},{2,2},{3,3},{4,32},{5,33},{6,34},{7,35},{8,64},{9,65},... | collective-permute-start | bytes 393224 | tf_op jit(solution)/shard_map/ppermute | solution.py:404
  12.5 2.6 %collective-permute-start.2 = (bf16[512,128]{1,0:T(8,128)(2,1)S(1)}, bf16[512,128]{1,0:T(8,128)(2,1)S(1)}, u32[]{:S(2)}, u32[]{:S(2)}) collective-permute-start(bf16[512,128]{1,0:T(8,128)(2,1)S(1)} %get-tuple-element.40), channel_id=1, source_target_pairs={{0,2},{1,3},{2,0},{3,1},{4,6},{5,7},{6,4},{7,5},{8,10},{9,11},{10,... | collective-permute-start | bytes 393224 | tf_op jit(solution)/shard_map/ppermute | solution.py:406
  18.3 2.4 %collective-permute-done.2.refs_2_ = bf16[512,128]{1,0:T(8,128)(2,1)S(1)} collective-permute-done((bf16[512,128]{1,0:T(8,128)(2,1)S(1)}, bf16[512,128]{1,0:T(8,128)(2,1)S(1)}, u32[]{:S(2)}, u32[]{:S(2)}) %collective-permute-start.2) | collective-permute-done | bytes 131104 | tf_op jit(solution)/shard_map/ppermute | solution.py:406
  21.7 5.6 %all-to-all-start = ((bf16[8,256,256]{2,1,0:T(8,128)(2,1)}), bf16[8,256,256]{2,1,0:T(8,128)(2,1)S(1)}, u32[]{:S(2)}, u32[]{:S(2)}) async-start(bf16[8,256,256]{2,1,0:T(8,128)(2,1)} %broadcast_in_dim.9), calls=%async_computation | async-start | bytes 2097152 | tf_op jit(solution)/shard_map/all_to_all | solution.py:46
  32.5 9.2 %collective-permute-done.6.refs_3_ = bf16[4,256,128]{2,1,0:T(8,128)(2,1)S(1)} collective-permute-done((bf16[4,256,128]{2,1,0:T(8,128)(2,1)S(1)}, bf16[4,256,128]{2,1,0:T(8,128)(2,1)S(1)}, u32[]{:S(2)}, u32[]{:S(2)}) %collective-permute-start.6) | collective-permute-done | bytes 262176 | tf_op jit(solution)/shard_map/ppermute | solution.py:410
  47.6 9.0 %all-to-all-done.cot_ref = bf16[8,256,256]{2,1,0:T(8,128)(2,1)S(1)} async-done(((bf16[8,256,256]{2,1,0:T(8,128)(2,1)}), bf16[8,256,256]{2,1,0:T(8,128)(2,1)S(1)}, u32[]{:S(2)}, u32[]{:S(2)}) %all-to-all-start) | async-done | bytes 1048608 | tf_op jit(solution)/shard_map/all_to_all | solution.py:46
  56.5 2.9 %grad_piece.1 = (bf16[256,512]{1,0:T(8,128)(2,1)S(1)}, bf16[4,4,256,128]{3,2,1,0:T(8,128)(2,1)}, bf16[3,4,256,128]{3,2,1,0:T(8,128)(2,1)}) custom-call(s32[5]{0:T(128)S(1)} %stack.23.place, bf16[8,256,256]{2,1,0:T(8,128)(2,1)S(1)} %all-to-all-done.cot_ref, bf16[4,256,128]{2,1,0:T(8,128)(2,1)S(1)} %get-tuple-element.47.weight_ref.near_w, ...), custom_call_target="tpu_custom_call" | custom-call | tf_op jit(solution)/shard_map/grad_piece/pallas_call | solution.py:150
  61.6 5.4 %collective-permute-done.13.near3 = bf16[256,512]{1,0:T(8,128)(2,1)S(1)} collective-permute-done((bf16[256,512]{1,0:T(8,128)(2,1)S(1)}, bf16[256,512]{1,0:T(8,128)(2,1)S(1)}, u32[]{:S(2)}, u32[]{:S(2)}) %collective-permute-start.13) | collective-permute-done | bytes 262176 | tf_op jit(solution)/shard_map/ppermute | solution.py:417
  67.0 2.9 %collective-permute-done.12.near1 = bf16[256,512]{1,0:T(8,128)(2,1)S(1)} collective-permute-done((bf16[256,512]{1,0:T(8,128)(2,1)S(1)}, bf16[256,512]{1,0:T(8,128)(2,1)S(1)}, u32[]{:S(2)}, u32[]{:S(2)}) %collective-permute-start.12) | collective-permute-done | bytes 262176 | tf_op jit(solution)/shard_map/ppermute | solution.py:417
  69.8 3.6 %all-to-all-start.1 = ((bf16[8,256,256]{2,1,0:T(8,128)(2,1)}), bf16[8,256,256]{2,1,0:T(8,128)(2,1)S(1)}, u32[]{:S(2)}, u32[]{:S(2)}) async-start(bf16[8,256,256]{2,1,0:T(8,128)(2,1)} %first_partial.1), calls=%async_computation.1 | async-start | bytes 2097152 | tf_op jit(solution)/shard_map/all_to_all | solution.py:420
  77.3 4.0 %collective-permute-done.14.near2 = bf16[256,512]{1,0:T(8,128)(2,1)S(1)} collective-permute-done((bf16[256,512]{1,0:T(8,128)(2,1)}, bf16[256,512]{1,0:T(8,128)(2,1)S(1)}, u32[]{:S(2)}, u32[]{:S(2)}) %collective-permute-start.14) | collective-permute-done | bytes 262176 | tf_op jit(solution)/shard_map/ppermute | solution.py:417
  81.3 6.7 %collective-permute-done.17.far3 = bf16[256,512]{1,0:T(8,128)(2,1)S(1)} collective-permute-done((bf16[256,512]{1,0:T(8,128)(2,1)S(1)}, bf16[256,512]{1,0:T(8,128)(2,1)S(1)}, u32[]{:S(2)}, u32[]{:S(2)}) %collective-permute-start.17) | collective-permute-done | bytes 262176 | tf_op jit(solution)/shard_map/ppermute | solution.py:418
  88.0 6.6 %collective-permute-done.15.far1 = bf16[256,512]{1,0:T(8,128)(2,1)S(1)} collective-permute-done((bf16[256,512]{1,0:T(8,128)(2,1)S(1)}, bf16[256,512]{1,0:T(8,128)(2,1)S(1)}, u32[]{:S(2)}, u32[]{:S(2)}) %collective-permute-start.15) | collective-permute-done | bytes 262176 | tf_op jit(solution)/shard_map/ppermute | solution.py:418
  96.9 13.8 %solve.1 = (f32[128,1024]{1,0:T(8,128)}, f32[128,1024]{1,0:T(8,128)}, f32[128,1024]{1,0:T(8,128)}, bf16[8,144,256]{2,1,0:T(8,128)(2,1)}) custom-call(s32[5]{0:T(128)S(1)} %stack.23.place, bf16[256,512]{1,0:T(8,128)(2,1)S(1)} %copy-done.5, bf16[256,512]{1,0:T(8,128)(2,1)S(1)} %collective-permute-done.12.near1, ...), custom_call_target="tpu_custom_call" | custom-call | tf_op jit(solution)/shard_map/solve/pallas_call | solution.py:384
  110.7 3.5 %all-to-all-start.2 = ((bf16[8,144,256]{2,1,0:T(8,128)(2,1)}), bf16[8,144,256]{2,1,0:T(8,128)(2,1)S(1)}, u32[]{:S(2)}, u32[]{:S(2)}) async-start(bf16[8,144,256]{2,1,0:T(8,128)(2,1)} %get-tuple-element.67), calls=%async_computation.2 | async-start | bytes 1179648 | tf_op jit(solution)/shard_map/all_to_all | solution.py:427
  116.0 2.1 %collective-permute-done.20.swap_ref = bf16[3,4,256,128]{3,2,1,0:T(8,128)(2,1)S(1)} collective-permute-done((bf16[3,4,256,128]{3,2,1,0:T(8,128)(2,1)}, bf16[3,4,256,128]{3,2,1,0:T(8,128)(2,1)S(1)}, u32[]{:S(2)}, u32[]{:S(2)}) %collective-permute-start.20) | collective-permute-done | bytes 786464 | tf_op jit(solution)/shard_map/ppermute | solution.py:429
  119.0 3.7 %all-to-all-done.2.update_ref = bf16[8,144,256]{2,1,0:T(8,128)(2,1)S(1)} async-done(((bf16[8,144,256]{2,1,0:T(8,128)(2,1)}), bf16[8,144,256]{2,1,0:T(8,128)(2,1)S(1)}, u32[]{:S(2)}, u32[]{:S(2)}) %all-to-all-start.2) | async-done | bytes 589856 | tf_op jit(solution)/shard_map/all_to_all | solution.py:427
  123.9 2.8 %second_partial.1 = (bf16[4,256,256]{2,1,0:T(8,128)(2,1)}, f32[8,128]{1,0:T(8,128)S(1)}) custom-call(s32[5]{0:T(128)S(1)} %stack.23.place, bf16[8,144,256]{2,1,0:T(8,128)(2,1)S(1)} %all-to-all-done.2.update_ref, bf16[4,256,128]{2,1,0:T(8,128)(2,1)S(1)} %get-tuple-element.47.weight_ref.near_w, bf16[4,4,256,128]{3,2,1,0:T(8,128)(2,1)S(1)} %copy-done, ...), custom_call_target="tpu_custom_call" | custom-call | tf_op jit(solution)/shard_map/second_partial/pallas_call | solution.py:234
  126.7 5.3 %all-to-all-start.3 = ((bf16[4,256,256]{2,1,0:T(8,128)(2,1)}), bf16[4,256,256]{2,1,0:T(8,128)(2,1)S(1)}, u32[]{:S(2)}, u32[]{:S(2)}) async-start(bf16[4,256,256]{2,1,0:T(8,128)(2,1)} %get-tuple-element.72), calls=%async_computation.3 | async-start | bytes 1048576 | tf_op jit(solution)/shard_map/all_to_all | solution.py:433
  132.7 7.7 %collective-permute-start.18 = (bf16[256,256]{1,0:T(8,128)(2,1)S(1)}, bf16[256,256]{1,0:T(8,128)(2,1)S(1)}, u32[]{:S(2)}, u32[]{:S(2)}) collective-permute-start(bf16[256,256]{1,0:T(8,128)(2,1)S(1)} %add_up.2), channel_id=1, source_target_pairs={{0,0},{1,1},{2,2},{3,3},{4,32},{5,33},{6,34},{7,35},{8,64},{9,65},... | collective-permute-start | bytes 393224 | tf_op jit(solution)/shard_map/ppermute | solution.py:430
  140.4 15.3 %collective-permute-done.18 = bf16[256,256]{1,0:T(8,128)(2,1)S(1)} collective-permute-done((bf16[256,256]{1,0:T(8,128)(2,1)S(1)}, bf16[256,256]{1,0:T(8,128)(2,1)S(1)}, u32[]{:S(2)}, u32[]{:S(2)}) %collective-permute-start.18) | collective-permute-done | bytes 131104 | tf_op jit(solution)/shard_map/ppermute | solution.py:430
  156.9 6.1 %collective-permute-start.21 = (bf16[256,256]{1,0:T(8,128)(2,1)S(1)}, bf16[256,256]{1,0:T(8,128)(2,1)S(1)}, u32[]{:S(2)}, u32[]{:S(2)}) collective-permute-start(bf16[256,256]{1,0:T(8,128)(2,1)S(1)} %add_up.3), channel_id=1, source_target_pairs={{0,0},{1,1},{2,2},{3,3},{4,32},{5,33},{6,34},{7,35},{8,64},{9,65},... | collective-permute-start | bytes 393224 | tf_op jit(solution)/shard_map/ppermute | solution.py:434
  163.0 2.5 %broadcast_divide_fusion = f32[128,1024]{1,0:T(8,128)} fusion(f32[128,1024]{1,0:T(8,128)} %get-tuple-element.66, f32[]{:T(128)} %bitcast.9), kind=kLoop, calls=%fused_computation | loop fusion | flops 131072 | bytes 1048580 | tf_op jit(solution)/shard_map/div | solution.py:435
  165.5 6.8 %collective-permute-done.21 = bf16[256,256]{1,0:T(8,128)(2,1)S(1)} collective-permute-done((bf16[256,256]{1,0:T(8,128)(2,1)S(1)}, bf16[256,256]{1,0:T(8,128)(2,1)S(1)}, u32[]{:S(2)}, u32[]{:S(2)}) %collective-permute-start.21) | collective-permute-done | bytes 131104 | tf_op jit(solution)/shard_map/ppermute | solution.py:434
  (56 shorter events, 34.2 us)
Async XLA Ops:
  0.6 17.6 %collective-permute-start = (bf16[256,256]{1,0:T(8,128)(2,1)}, bf16[256,256]{1,0:T(8,128)(2,1)S(1)}, u32[]{:S(2)}, u32[]{:S(2)}) collective-permute-start(bf16[256,256]{1,0:T(8,128)(2,1)} %param.6), channel_id=1, source_target_pairs={{0,0},{1,1},{2,2},{3,3},{4,32},{5,33},{6,34},{7,35},{8,64},{9,65},... | collective-permute-start | bytes 393224 | tf_op jit(solution)/shard_map/ppermute | solution.py:404
  11.1 7.1 %collective-permute-start.1 = (bf16[512,128]{1,0:T(8,128)(2,1)S(1)}, bf16[512,128]{1,0:T(8,128)(2,1)S(1)}, u32[]{:S(2)}, u32[]{:S(2)}) collective-permute-start(bf16[512,128]{1,0:T(8,128)(2,1)S(1)} %get-tuple-element.39), channel_id=1, source_target_pairs={{0,1},{1,2},{2,3},{3,0},{4,5},{5,6},{6,7},{7,4},{8,9},{9,10},{10,1... | collective-permute-start | bytes 393224 | tf_op jit(solution)/shard_map/ppermute | solution.py:406
  12.5 8.1 %collective-permute-start.2 = (bf16[512,128]{1,0:T(8,128)(2,1)S(1)}, bf16[512,128]{1,0:T(8,128)(2,1)S(1)}, u32[]{:S(2)}, u32[]{:S(2)}) collective-permute-start(bf16[512,128]{1,0:T(8,128)(2,1)S(1)} %get-tuple-element.40), channel_id=1, source_target_pairs={{0,2},{1,3},{2,0},{3,1},{4,6},{5,7},{6,4},{7,5},{8,10},{9,11},{10,... | collective-permute-start | bytes 393224 | tf_op jit(solution)/shard_map/ppermute | solution.py:406
  15.1 5.5 %collective-permute-start.3 = (bf16[512,128]{1,0:T(8,128)(2,1)S(1)}, bf16[512,128]{1,0:T(8,128)(2,1)S(1)}, u32[]{:S(2)}, u32[]{:S(2)}) collective-permute-start(bf16[512,128]{1,0:T(8,128)(2,1)S(1)} %get-tuple-element.41), channel_id=1, source_target_pairs={{0,3},{1,0},{2,1},{3,2},{4,7},{5,4},{6,5},{7,6},{8,11},{9,8},{10,9... | collective-permute-start | bytes 393224 | tf_op jit(solution)/shard_map/ppermute | solution.py:406
  21.7 34.8 %all-to-all-start = ((bf16[8,256,256]{2,1,0:T(8,128)(2,1)}), bf16[8,256,256]{2,1,0:T(8,128)(2,1)S(1)}, u32[]{:S(2)}, u32[]{:S(2)}) async-start(bf16[8,256,256]{2,1,0:T(8,128)(2,1)} %broadcast_in_dim.9), calls=%async_computation | async-start | bytes 2097152 | tf_op jit(solution)/shard_map/all_to_all | solution.py:46
  27.9 13.7 %collective-permute-start.6 = (bf16[4,256,128]{2,1,0:T(8,128)(2,1)S(1)}, bf16[4,256,128]{2,1,0:T(8,128)(2,1)S(1)}, u32[]{:S(2)}, u32[]{:S(2)}) collective-permute-start(bf16[4,256,128]{2,1,0:T(8,128)(2,1)S(1)} %get-tuple-element.48.refs_0_), channel_id=1, source_target_pairs={{0,192},{64,0},{128,64},{192,128},{1,193},{65,1},{129,65},{193,129... | collective-permute-start | bytes 786440 | tf_op jit(solution)/shard_map/ppermute | solution.py:410
  28.0 15.5 %collective-permute-start.5 = (bf16[4,256,128]{2,1,0:T(8,128)(2,1)S(1)}, bf16[4,256,128]{2,1,0:T(8,128)(2,1)S(1)}, u32[]{:S(2)}, u32[]{:S(2)}) collective-permute-start(bf16[4,256,128]{2,1,0:T(8,128)(2,1)S(1)} %get-tuple-element.48.refs_0_), channel_id=1, source_target_pairs={{0,128},{64,192},{128,0},{192,64},{1,129},{65,193},{129,1},{193,65... | collective-permute-start | bytes 786440 | tf_op jit(solution)/shard_map/ppermute | solution.py:410
  28.8 14.7 %collective-permute-start.4 = (bf16[4,256,128]{2,1,0:T(8,128)(2,1)S(1)}, bf16[4,256,128]{2,1,0:T(8,128)(2,1)S(1)}, u32[]{:S(2)}, u32[]{:S(2)}) collective-permute-start(bf16[4,256,128]{2,1,0:T(8,128)(2,1)S(1)} %get-tuple-element.48.refs_0_), channel_id=1, source_target_pairs={{0,64},{64,128},{128,192},{192,0},{1,65},{65,129},{129,193},{193,1... | collective-permute-start | bytes 786440 | tf_op jit(solution)/shard_map/ppermute | solution.py:410
  30.7 13.5 %collective-permute-start.7 = (bf16[4,256,128]{2,1,0:T(8,128)(2,1)S(1)}, bf16[4,256,128]{2,1,0:T(8,128)(2,1)S(1)}, u32[]{:S(2)}, u32[]{:S(2)}) collective-permute-start(bf16[4,256,128]{2,1,0:T(8,128)(2,1)S(1)} %get-tuple-element.48.refs_0_), channel_id=1, source_target_pairs={{0,32},{32,0},{1,33},{33,1},{2,34},{34,2},{3,35},{35,3},{4,36},{36... | collective-permute-start | bytes 786440 | tf_op jit(solution)/shard_map/ppermute | solution.py:411
  41.7 3.1 %collective-permute-start.10 = (bf16[4,256,128]{2,1,0:T(8,128)(2,1)S(1)}, bf16[4,256,128]{2,1,0:T(8,128)(2,1)S(1)}, u32[]{:S(2)}, u32[]{:S(2)}) collective-permute-start(bf16[4,256,128]{2,1,0:T(8,128)(2,1)S(1)} %collective-permute-done.6.refs_3_), channel_id=1, source_target_pairs={{0,32},{32,0},{1,33},{33,1},{2,34},{34,2},{3,35},{35,3},{4,36},{36... | collective-permute-start | bytes 786440 | tf_op jit(solution)/shard_map/ppermute | solution.py:411
  59.5 7.5 %collective-permute-start.13 = (bf16[256,512]{1,0:T(8,128)(2,1)S(1)}, bf16[256,512]{1,0:T(8,128)(2,1)S(1)}, u32[]{:S(2)}, u32[]{:S(2)}) collective-permute-start(bf16[256,512]{1,0:T(8,128)(2,1)S(1)} %get-tuple-element.54.near0), channel_id=1, source_target_pairs={{0,3},{1,0},{2,1},{3,2},{4,7},{5,4},{6,5},{7,6},{8,11},{9,8},{10,9... | collective-permute-start | bytes 786440 | tf_op jit(solution)/shard_map/ppermute | solution.py:417
  61.6 8.3 %collective-permute-start.12 = (bf16[256,512]{1,0:T(8,128)(2,1)S(1)}, bf16[256,512]{1,0:T(8,128)(2,1)S(1)}, u32[]{:S(2)}, u32[]{:S(2)}) collective-permute-start(bf16[256,512]{1,0:T(8,128)(2,1)S(1)} %get-tuple-element.54.near0), channel_id=1, source_target_pairs={{0,1},{1,2},{2,3},{3,0},{4,5},{5,6},{6,7},{7,4},{8,9},{9,10},{10,1... | collective-permute-start | bytes 786440 | tf_op jit(solution)/shard_map/ppermute | solution.py:417
  61.6 8.3 %collective-permute-start.11 = (bf16[256,512]{1,0:T(8,128)(2,1)S(1)}, bf16[256,512]{1,0:T(8,128)(2,1)S(1)}, u32[]{:S(2)}, u32[]{:S(2)}) collective-permute-start(bf16[256,512]{1,0:T(8,128)(2,1)S(1)} %get-tuple-element.54.near0), channel_id=1, source_target_pairs={{0,4},{4,0},{1,5},{5,1},{2,6},{6,2},{3,7},{7,3},{8,12},{12,8},{9,1... | collective-permute-start | bytes 786440 | tf_op jit(solution)/shard_map/ppermute | solution.py:416
  69.8 40.8 %all-to-all-start.1 = ((bf16[8,256,256]{2,1,0:T(8,128)(2,1)}), bf16[8,256,256]{2,1,0:T(8,128)(2,1)S(1)}, u32[]{:S(2)}, u32[]{:S(2)}) async-start(bf16[8,256,256]{2,1,0:T(8,128)(2,1)} %first_partial.1), calls=%async_computation.1 | async-start | bytes 2097152 | tf_op jit(solution)/shard_map/all_to_all | solution.py:420
  73.4 7.9 %collective-permute-start.14 = (bf16[256,512]{1,0:T(8,128)(2,1)}, bf16[256,512]{1,0:T(8,128)(2,1)S(1)}, u32[]{:S(2)}, u32[]{:S(2)}) collective-permute-start(bf16[256,512]{1,0:T(8,128)(2,1)} %copy-done.4), channel_id=1, source_target_pairs={{0,2},{1,3},{2,0},{3,1},{4,6},{5,7},{6,4},{7,5},{8,10},{9,11},{10,... | collective-permute-start | bytes 786440 | tf_op jit(solution)/shard_map/ppermute | solution.py:417
  73.5 14.5 %collective-permute-start.17 = (bf16[256,512]{1,0:T(8,128)(2,1)S(1)}, bf16[256,512]{1,0:T(8,128)(2,1)S(1)}, u32[]{:S(2)}, u32[]{:S(2)}) collective-permute-start(bf16[256,512]{1,0:T(8,128)(2,1)S(1)} %collective-permute-done.11.far0), channel_id=1, source_target_pairs={{0,3},{1,0},{2,1},{3,2},{4,7},{5,4},{6,5},{7,6},{8,11},{9,8},{10,9... | collective-permute-start | bytes 786440 | tf_op jit(solution)/shard_map/ppermute | solution.py:418
  75.0 13.0 %collective-permute-start.16 = (bf16[256,512]{1,0:T(8,128)(2,1)S(1)}, bf16[256,512]{1,0:T(8,128)(2,1)S(1)}, u32[]{:S(2)}, u32[]{:S(2)}) collective-permute-start(bf16[256,512]{1,0:T(8,128)(2,1)S(1)} %collective-permute-done.11.far0), channel_id=1, source_target_pairs={{0,2},{1,3},{2,0},{3,1},{4,6},{5,7},{6,4},{7,5},{8,10},{9,11},{10,... | collective-permute-start | bytes 786440 | tf_op jit(solution)/shard_map/ppermute | solution.py:418
  77.0 17.7 %collective-permute-start.15 = (bf16[256,512]{1,0:T(8,128)(2,1)S(1)}, bf16[256,512]{1,0:T(8,128)(2,1)S(1)}, u32[]{:S(2)}, u32[]{:S(2)}) collective-permute-start(bf16[256,512]{1,0:T(8,128)(2,1)S(1)} %collective-permute-done.11.far0), channel_id=1, source_target_pairs={{0,1},{1,2},{2,3},{3,0},{4,5},{5,6},{6,7},{7,4},{8,9},{9,10},{10,1... | collective-permute-start | bytes 786440 | tf_op jit(solution)/shard_map/ppermute | solution.py:418
  94.7 20.7 %collective-permute-start.19 = (bf16[3,4,256,128]{3,2,1,0:T(8,128)(2,1)}, bf16[3,4,256,128]{3,2,1,0:T(8,128)(2,1)}, u32[]{:S(2)}, u32[]{:S(2)}) collective-permute-start(bf16[3,4,256,128]{3,2,1,0:T(8,128)(2,1)} %get-tuple-element.69), channel_id=1, source_target_pairs={{0,4},{4,0},{1,5},{5,1},{2,6},{6,2},{3,7},{7,3},{8,12},{12,8},{9,1... | collective-permute-start | bytes 2359304 | tf_op jit(solution)/shard_map/ppermute | solution.py:422
  110.7 12.1 %all-to-all-start.2 = ((bf16[8,144,256]{2,1,0:T(8,128)(2,1)}), bf16[8,144,256]{2,1,0:T(8,128)(2,1)S(1)}, u32[]{:S(2)}, u32[]{:S(2)}) async-start(bf16[8,144,256]{2,1,0:T(8,128)(2,1)} %get-tuple-element.67), calls=%async_computation.2 | async-start | bytes 1179648 | tf_op jit(solution)/shard_map/all_to_all | solution.py:427
  115.4 2.8 %collective-permute-start.20 = (bf16[3,4,256,128]{3,2,1,0:T(8,128)(2,1)}, bf16[3,4,256,128]{3,2,1,0:T(8,128)(2,1)S(1)}, u32[]{:S(2)}, u32[]{:S(2)}) collective-permute-start(bf16[3,4,256,128]{3,2,1,0:T(8,128)(2,1)} %collective-permute-done.19.far_ref), channel_id=1, source_target_pairs={{0,32},{32,0},{1,33},{33,1},{2,34},{34,2},{3,35},{35,3},{4,36},{36... | collective-permute-start | bytes 2359304 | tf_op jit(solution)/shard_map/ppermute | solution.py:429
  126.7 29.6 %all-to-all-start.3 = ((bf16[4,256,256]{2,1,0:T(8,128)(2,1)}), bf16[4,256,256]{2,1,0:T(8,128)(2,1)S(1)}, u32[]{:S(2)}, u32[]{:S(2)}) async-start(bf16[4,256,256]{2,1,0:T(8,128)(2,1)} %get-tuple-element.72), calls=%async_computation.3 | async-start | bytes 1048576 | tf_op jit(solution)/shard_map/all_to_all | solution.py:433
  132.7 23.1 %collective-permute-start.18 = (bf16[256,256]{1,0:T(8,128)(2,1)S(1)}, bf16[256,256]{1,0:T(8,128)(2,1)S(1)}, u32[]{:S(2)}, u32[]{:S(2)}) collective-permute-start(bf16[256,256]{1,0:T(8,128)(2,1)S(1)} %add_up.2), channel_id=1, source_target_pairs={{0,0},{1,1},{2,2},{3,3},{4,32},{5,33},{6,34},{7,35},{8,64},{9,65},... | collective-permute-start | bytes 393224 | tf_op jit(solution)/shard_map/ppermute | solution.py:430
  156.9 15.5 %collective-permute-start.21 = (bf16[256,256]{1,0:T(8,128)(2,1)S(1)}, bf16[256,256]{1,0:T(8,128)(2,1)S(1)}, u32[]{:S(2)}, u32[]{:S(2)}) collective-permute-start(bf16[256,256]{1,0:T(8,128)(2,1)S(1)} %add_up.3), channel_id=1, source_target_pairs={{0,0},{1,1},{2,2},{3,3},{4,32},{5,33},{6,34},{7,35},{8,64},{9,65},... | collective-permute-start | bytes 393224 | tf_op jit(solution)/shard_map/ppermute | solution.py:434
  (9 other events, 36.1 us)

commit v6 on v5

--- a/solution.py
+++ b/solution.py
@@ -70,12 +70,24 @@
     )
 
 
+def in_hbm(value):
+    return pltpu.with_memory_space_constraint(value, pltpu.HBM)
+
+
 def wide(slab):
     return jnp.concatenate([slab[q] for q in range(4)], axis=1)
 
 
-def pack_body(place, acts_ref, weight_ref, *refs):
-    outs, work = refs[:4], refs[4]
+def pack_body(place, acts_hbm, weight_hbm, *refs):
+    outs, (acts_ref, weight_ref, work, sems) = refs[:4], refs[4:]
+    loads = [
+        pltpu.make_async_copy(weight_hbm, weight_ref, sems.at[0]),
+        pltpu.make_async_copy(acts_hbm, acts_ref, sems.at[1]),
+    ]
+    for load in loads:
+        load.start()
+    for load in loads:
+        load.wait()
     for q in range(4):
         for half in range(2):
             at = q * 256 + half * 128
@@ -90,13 +102,18 @@
     part = SHAPE((512, 128), BF16)
     return call(
         pack_body,
-        [VMEM] * 2,
+        [HBM] * 2,
         [VMEM] * 4,
         [part] * 4,
-        scratch=[pltpu.VMEM((4, 256, 128), BF16)],
+        scratch=[
+            pltpu.VMEM((256, 128), BF16),
+            pltpu.VMEM((128, 1024), BF16),
+            pltpu.VMEM((4, 256, 128), BF16),
+            pltpu.SemaphoreType.DMA((2,)),
+        ],
         limit=8,
         name="pack",
-    )(place, acts, weight)
+    )(place, in_hbm(acts), in_hbm(weight))
 
 
 def unpack_body(place, *refs):
@@ -118,64 +135,58 @@
     return jnp.concatenate(rows, axis=0)
 
 
-def grad_body(place, cot_ref, weight_ref, *refs):
+def grad_body(place, cot_ref, *refs):
     own, swapped = refs[:4], refs[4:8]
-    piece_ref, near_ref, away_ref, near_buf, away_buf, sems = refs[8:]
-    x, c, zl = place[0], place[1], place[3]
-    for d in range(4):
-        at = (x - d) & 3
-        mine, theirs = own[d][...], swapped[d][...]
-        near_buf[at] = jnp.where(c == zl, mine, theirs)
-        away_buf[at] = jnp.where(c == zl, theirs, mine)
-    sends = [
-        pltpu.make_async_copy(near_buf, near_ref, sems.at[0]),
-        pltpu.make_async_copy(
-            away_buf.at[pl.ds(c * 2, 2)], away_ref.at[pl.ds(0, 2)], sems.at[1]
-        ),
-        pltpu.make_async_copy(weight_ref, away_ref.at[2], sems.at[2]),
-    ]
-    for send in sends:
-        send.start()
+    piece_ref, kept_ref, sem = refs[8:]
+    x, c = place[0], place[1]
     total = jnp.zeros((256, 512), F32)
     for d in range(4):
         at = (x - d) & 3
         total = total + dot(cot_ref[at * 2 + c], wide(own[d]))
         total = total + dot(cot_ref[at * 2 + 1 - c], wide(swapped[d]))
     piece_ref[...] = total.astype(BF16)
-    for send in sends:
-        send.wait()
-
-
-def grad_piece(place, cot_all, near_w, own, swapped):
+    keep = pltpu.make_async_copy(piece_ref, kept_ref, sem)
+    keep.start()
+    keep.wait()
+
+
+def grad_piece(place, cot_all, own, swapped):
     return call(
         grad_body,
-        [VMEM] * 10,
-        [VMEM, HBM, HBM],
-        [
-            SHAPE((256, 512), BF16),
-            pltpu.HBM((4, 4, 256, 128), BF16),
-            pltpu.HBM((3, 4, 256, 128), BF16),
-        ],
-        scratch=[
-            pltpu.VMEM((4, 4, 256, 128), BF16),
-            pltpu.VMEM((4, 4, 256, 128), BF16),
-            pltpu.SemaphoreType.DMA((3,)),
-        ],
+        [VMEM] * 9,
+        [VMEM, HBM],
+        [SHAPE((256, 512), BF16), pltpu.HBM((256, 512), BF16)],
+        scratch=[pltpu.SemaphoreType.DMA],
         limit=10,
         name="grad_piece",
-    )(place, cot_all, near_w, *own, *swapped)
+    )(place, cot_all, *own, *swapped)
 
 
 def first_body(place, weight_ref, *refs):
     own, swapped = refs[:4], refs[4:8]
-    out_ref, work, sems = refs[8:]
+    out_ref, near_ref, away_ref, work, sems = refs[8:]
+    x, c, zl = place[0], place[1], place[3]
+
+    def slabs_move(step):
+        step(pltpu.make_async_copy(weight_ref, away_ref.at[2], sems.at[16]))
+        for mine, theirs, here in ((own, swapped, c == zl), (swapped, own, c != zl)):
+            for d in range(4):
+                at = (x - d) & 3
+
+                @pl.when(here)
+                def _(mine=mine, d=d, at=at):
+                    step(pltpu.make_async_copy(mine[d], near_ref.at[at], sems.at[8 + d]))
+
+                @pl.when(here & (at // 2 == c))
+                def _(theirs=theirs, d=d, at=at):
+                    step(pltpu.make_async_copy(theirs[d], away_ref.at[at & 1], sems.at[12 + d]))
+
+    slabs_move(lambda copy: copy.start())
     weight_t = weight_of(weight_ref).T
     sends = []
     for d in range(4):
-        at = ((place[0] - d) & 3) * 2
-        for i, (slab, group) in enumerate(
-            ((own[d], at + place[1]), (swapped[d], at + 1 - place[1]))
-        ):
+        at = ((x - d) & 3) * 2
+        for i, (slab, group) in enumerate(((own[d], at + c), (swapped[d], at + 1 - c))):
             work[d * 2 + i] = dot_minor(weight_t, wide(slab)).astype(BF16)
             sends.append(
                 pltpu.make_async_copy(work.at[d * 2 + i], out_ref.at[group], sems.at[d * 2 + i])
@@ -183,23 +194,47 @@
             sends[-1].start()
     for send in sends:
         send.wait()
+    slabs_move(lambda copy: copy.wait())
 
 
 def first_partial(place, near_w, own, swapped):
     return call(
         first_body,
         [VMEM] * 9,
-        HBM,
-        pltpu.HBM((8, 256, 256), BF16),
-        scratch=[pltpu.VMEM((8, 256, 256), BF16), pltpu.SemaphoreType.DMA((8,))],
+        [HBM] * 3,
+        [
+            pltpu.HBM((8, 256, 256), BF16),
+            pltpu.HBM((4, 4, 256, 128), BF16),
+            pltpu.HBM((3, 4, 256, 128), BF16),
+        ],
+        scratch=[pltpu.VMEM((8, 256, 256), BF16), pltpu.SemaphoreType.DMA((17,))],
         limit=12,
         name="first_partial",
     )(place, near_w, *own, *swapped)
 
 
 def second_body(
-    place, update_ref, near_w, near_ref, far_ref, swap_ref, out_ref, spread_ref, work, sems
+    place,
+    update_ref,
+    near_w,
+    near_hbm,
+    far_hbm,
+    swap_hbm,
+    out_ref,
+    spread_ref,
+    near_ref,
+    far_ref,
+    swap_ref,
+    work,
+    sems,
 ):
+    loads = [
+        pltpu.make_async_copy(far_hbm, far_ref, sems.at[4]),
+        pltpu.make_async_copy(near_hbm, near_ref, sems.at[5]),
+        pltpu.make_async_copy(swap_hbm, swap_ref, sems.at[6]),
+    ]
+    for load in loads:
+        load.start()
     squares = jnp.zeros((16, 128), F32)
     for s in range(8):
         squares = squares + update_ref[s, 128:144, :128].astype(F32)
@@ -214,8 +249,11 @@
         return (weight_of(weight).astype(F32) - rate * update.astype(F32)).astype(BF16).T
 
     near_t = changed(near_w, zl * 4)
+    loads[0].wait()
     far_t = changed(far_ref.at[2], 4 - zl * 4)
     sends = []
+    for load in loads[1:]:
+        load.wait()
     for i in range(2):
         for j in range(2):
             at = (c * 2 if i == 0 else 2 - c * 2) + j
@@ -233,13 +271,19 @@
 def second_partial(place, update_cols, near_w, near, far, far_swapped):
     return call(
         second_body,
-        [VMEM] * 5,
+        [VMEM, VMEM, HBM, HBM, HBM],
         [HBM, VMEM],
         [pltpu.HBM((4, 256, 256), BF16), SHAPE((8, 128), F32)],
-        scratch=[pltpu.VMEM((4, 256, 256), BF16), pltpu.SemaphoreType.DMA((4,))],
-        limit=12,
+        scratch=[
+            pltpu.VMEM((4, 4, 256, 128), BF16),
+            pltpu.VMEM((3, 4, 256, 128), BF16),
+            pltpu.VMEM((3, 4, 256, 128), BF16),
+            pltpu.VMEM((4, 256, 256), BF16),
+            pltpu.SemaphoreType.DMA((7,)),
+        ],
+        limit=14,
         name="second_partial",
-    )(place, update_cols, near_w, near, far, far_swapped)
+    )(place, update_cols, near_w, in_hbm(near), in_hbm(far), in_hbm(far_swapped))
 
 
 def add_body(place, parts_ref, out_ref):
@@ -316,14 +360,20 @@
 ):
     load_left = pltpu.make_async_copy(left_old_ref, left_buf, sems.at[0])
     load_right = pltpu.make_async_copy(right_old_ref, right_buf, sems.at[1])
+    load_own = pltpu.make_async_copy(
+        near0, pieces_ref.at[place[3] * 4 + place[4]], sems.at[7]
+    )
+    load_own.start()
     load_left.start()
     load_right.start()
     first = pl.multiple_of((place[3] * 4 + place[4]) * 128, 128)
     own = pl.ds(first, 128)
     for d, (near, far) in enumerate(((near0, far0), (near1, far1), (near2, far2), (near3, far3))):
         at = (place[4] - d) & 3
-        pieces_ref[place[3] * 4 + at] = near[...]
+        if d > 0:
+            pieces_ref[place[3] * 4 + at] = near[...]
         pieces_ref[4 - place[3] * 4 + at] = far[...]
+    load_own.wait()
     for zl in range(2):
         for y in range(4):
             piece = pieces_ref[zl * 4 + y]
@@ -383,7 +433,7 @@
     rows = pltpu.HBM((128, BLOCK), F32)
     return call(
         solver_body,
-        [*[VMEM] * 8, HBM, HBM],
+        [HBM, *[VMEM] * 7, HBM, HBM],
         [HBM] * 4,
         [rows, rows, rows, pltpu.HBM((8, 144, 256), BF16)],
         scratch=[
@@ -392,7 +442,7 @@
             pltpu.VMEM((128, BLOCK), F32),
             pltpu.VMEM((128, BLOCK), F32),
             pltpu.VMEM((4, 144, 256), BF16),
-            pltpu.SemaphoreType.DMA((7,)),
+            pltpu.SemaphoreType.DMA((8,)),
         ],
         limit=27,
         name="solve",
@@ -404,30 +454,32 @@
     cot_turned = lax.ppermute(cotangent, AXES, SWAP)
     packed = pack(place, activations, weight)
     crossed = [lax.ppermute(packed[d], "y", shift(d)) for d in range(1, 4)]
-    cot_turned, *crossed = lax.optimization_barrier((cot_turned, *crossed))
+    cot_turned, crossed[0], crossed[2] = lax.optimization_barrier(
+        (cot_turned, crossed[0], crossed[2])
+    )
     cot_all = copies_to(cot_turned, ZAX, 8)
     slab, near_w = unpack(place, [packed[0], *crossed])
     own = [slab] + [lax.ppermute(slab, "x", shift(d)) for d in range(1, 4)]
     swapped = [lax.ppermute(part, "c", FLIP) for part in own]
-    first = first_partial(place, near_w, own, swapped)
+    first, near, away = first_partial(place, near_w, own, swapped)
     cot_all, first = lax.optimization_barrier((cot_all, first))
-    piece, near, away = grad_piece(place, cot_all, near_w, own, swapped)
+    first_parts = lax.all_to_all(first, ZAX, 0, 0, tiled=True)
+    piece, kept = grad_piece(place, cot_all, own, swapped)
 
     beside = lax.ppermute(piece, "zl", FLIP)
-    pieces = [piece] + [lax.ppermute(piece, "y", shift(d)) for d in range(1, 4)]
+    pieces = [in_hbm(kept)] + [lax.ppermute(piece, "y", shift(d)) for d in range(1, 4)]
     pieces += [beside] + [lax.ppermute(beside, "y", shift(d)) for d in range(1, 4)]
-    first, *_ = lax.optimization_barrier((first, beside, pieces[1], pieces[3]))
-    first_parts = lax.all_to_all(first, ZAX, 0, 0, tiled=True)
-    away, first, *pieces = lax.optimization_barrier((away, first, *pieces))
+    away, *pieces = lax.optimization_barrier((away, *pieces))
     far = lax.ppermute(away, "zl", FLIP)
-    left_old = pltpu.with_memory_space_constraint(left_old[0, 0], pltpu.HBM)
-    right_old = pltpu.with_memory_space_constraint(right_old[0, 0], pltpu.HBM)
-    new_left, new_right, update, sent = solve(place, pieces, left_old, right_old)
+    new_left, new_right, update, sent = solve(
+        place, pieces, in_hbm(left_old[0, 0]), in_hbm(right_old[0, 0])
+    )
     sent, first_parts = lax.optimization_barrier((sent, first_parts))
     update_cols = lax.all_to_all(sent, SOLVER, 0, 0, tiled=True)
     far, sent = lax.optimization_barrier((far, sent))
     far_swapped = lax.ppermute(far, "c", FLIP)
-    first_out = lax.ppermute(add_up(place, first_parts), AXES, SWAP)
+    first_sum = add_up(place, first_parts)
+    near_w, first_out = lax.optimization_barrier((near_w, lax.ppermute(first_sum, AXES, SWAP)))
 
     second, spread = second_partial(place, update_cols, near_w, near, far, far_swapped)
     arrived = lax.all_to_all(second, "zh", 0, 0, tiled=True)

time: 174 us -> 187 us (1.075)
  the two profiles are of different devices: /device:TPU:7 before, /device:TPU:65 now
where the time goes in v6:
time: 187 us
  waiting for transfers between devices  77.8 us (42%)
  starting transfers between devices  69.6 us (37%)
  Pallas kernels  25.4 us (14%)
  local copies, waits for them, and re-layouts  10.4 us (6%)
  other arithmetic  2.54 us (1%)
    ppermute x1, waiting for transfers between devices, body(): beside = lax.ppermute(piece, 'zl', FLIP)  19 us
    all_to_all x1, waiting for transfers between devices, body(): arrived = lax.all_to_all(second, 'zh', 0, 0, tiled=True)  14.9 us
    ppermute x3, waiting for transfers between devices, body(): lax.ppermute(beside, 'y', shift(d))  14.3 us
    pallas_call x1, Pallas kernels, solve(): call(solver_body, [HBM, *[VMEM] * 7, HBM, HBM], [HBM] * 4, [rows, rows, r...  13.7 us
    ppermute x1, waiting for transfers between devices, body(): lax.ppermute(first_sum, AXES, SWAP)  11.7 us
    ppermute x4, starting transfers between devices, body(): swapped = [lax.ppermute(part, 'c', FLIP) for part in own]  11.5 us
    unnamed x22, local copies, waits for them, and re-layouts  8.78 us
    all_to_all x1, starting transfers between devices, copies_to(): return lax.all_to_all(copies, axis, split_axis=0, concat_axis=0, tiled=True)  8.07 us
  transfers between devices with their start and end apart: 26, of which 13 were waited for; matrix products, arithmetic and copies ran while one was open for 2% of the time, Pallas kernels for 11%

profile of v6, /device:TPU:65, one launch (start us, length us, event | category | flops | bytes accessed | tf_op | source)
XLA Modules:
  0.0 186.6 jit_solution(3307756116267273609)
XLA Ops:
  0.6 3.2 %collective-permute-start = (bf16[256,256]{1,0:T(8,128)(2,1)}, bf16[256,256]{1,0:T(8,128)(2,1)S(1)}, u32[]{:S(2)}, u32[]{:S(2)}) collective-permute-start(bf16[256,256]{1,0:T(8,128)(2,1)} %param.6), channel_id=1, source_target_pairs={{0,0},{1,1},{2,2},{3,3},{4,32},{5,33},{6,34},{7,35},{8,64},{9,65},... | collective-permute-start | bytes 393224 | tf_op jit(solution)/shard_map/ppermute | solution.py:454
  8.5 5.8 %collective-permute-done = bf16[256,256]{1,0:T(8,128)(2,1)S(1)} collective-permute-done((bf16[256,256]{1,0:T(8,128)(2,1)}, bf16[256,256]{1,0:T(8,128)(2,1)S(1)}, u32[]{:S(2)}, u32[]{:S(2)}) %collective-permute-start) | collective-permute-done | bytes 131104 | tf_op jit(solution)/shard_map/ppermute | solution.py:454
  15.3 8.1 %all-to-all-start = ((bf16[8,256,256]{2,1,0:T(8,128)(2,1)}), bf16[8,256,256]{2,1,0:T(8,128)(2,1)S(1)}, u32[]{:S(2)}, u32[]{:S(2)}) async-start(bf16[8,256,256]{2,1,0:T(8,128)(2,1)} %broadcast_in_dim.9), calls=%async_computation | async-start | bytes 2097152 | tf_op jit(solution)/shard_map/all_to_all | solution.py:46
  23.4 2.9 %collective-permute-start.3 = (bf16[512,128]{1,0:T(8,128)(2,1)S(1)}, bf16[512,128]{1,0:T(8,128)(2,1)S(1)}, u32[]{:S(2)}, u32[]{:S(2)}) collective-permute-start(bf16[512,128]{1,0:T(8,128)(2,1)S(1)} %get-tuple-element.45), channel_id=1, source_target_pairs={{0,2},{1,3},{2,0},{3,1},{4,6},{5,7},{6,4},{7,5},{8,10},{9,11},{10,... | collective-permute-start | bytes 393224 | tf_op jit(solution)/shard_map/ppermute | solution.py:456
  30.6 4.2 %collective-permute-start.5 = (bf16[4,256,128]{2,1,0:T(8,128)(2,1)S(1)}, bf16[4,256,128]{2,1,0:T(8,128)(2,1)S(1)}, u32[]{:S(2)}, u32[]{:S(2)}) collective-permute-start(bf16[4,256,128]{2,1,0:T(8,128)(2,1)S(1)} %get-tuple-element.48.refs_0_), channel_id=1, source_target_pairs={{0,128},{64,192},{128,0},{192,64},{1,129},{65,193},{129,1},{193,65... | collective-permute-start | bytes 786440 | tf_op jit(solution)/shard_map/ppermute | solution.py:462
  37.0 6.0 %collective-permute-start.10 = (bf16[4,256,128]{2,1,0:T(8,128)(2,1)S(1)}, bf16[4,256,128]{2,1,0:T(8,128)(2,1)S(1)}, u32[]{:S(2)}, u32[]{:S(2)}) collective-permute-start(bf16[4,256,128]{2,1,0:T(8,128)(2,1)S(1)} %collective-permute-done.6.refs_3_), channel_id=1, source_target_pairs={{0,32},{32,0},{1,33},{33,1},{2,34},{34,2},{3,35},{35,3},{4,36},{36... | collective-permute-start | bytes 786440 | tf_op jit(solution)/shard_map/ppermute | solution.py:463
  48.8 2.5 %first_partial.1 = (bf16[8,256,256]{2,1,0:T(8,128)(2,1)}, bf16[4,4,256,128]{3,2,1,0:T(8,128)(2,1)}, bf16[3,4,256,128]{3,2,1,0:T(8,128)(2,1)}) custom-call(s32[5]{0:T(128)S(1)} %stack.23.place, bf16[4,256,128]{2,1,0:T(8,128)(2,1)S(1)} %get-tuple-element.71.weight_ref.near_w, bf16[4,256,128]{2,1,0:T(8,128)(2,1)S(1)} %get-tuple-element.48.refs_0_, ...), custom_call_target="tpu_custom_call" | custom-call | tf_op jit(solution)/shard_map/first_partial/pallas_call | solution.py:201
  54.1 6.6 %all-to-all-start.1 = ((bf16[8,256,256]{2,1,0:T(8,128)(2,1)}), bf16[8,256,256]{2,1,0:T(8,128)(2,1)S(1)}, u32[]{:S(2)}, u32[]{:S(2)}) async-start(bf16[8,256,256]{2,1,0:T(8,128)(2,1)} %get-tuple-element.64), calls=%async_computation.1 | async-start | bytes 2097152 | tf_op jit(solution)/shard_map/all_to_all | solution.py:466
  67.8 2.7 %collective-permute-start.13 = (bf16[256,512]{1,0:T(8,128)(2,1)S(1)}, bf16[256,512]{1,0:T(8,128)(2,1)S(1)}, u32[]{:S(2)}, u32[]{:S(2)}) collective-permute-start(bf16[256,512]{1,0:T(8,128)(2,1)S(1)} %get-tuple-element.54), channel_id=1, source_target_pairs={{0,3},{1,0},{2,1},{3,2},{4,7},{5,4},{6,5},{7,6},{8,11},{9,8},{10,9... | collective-permute-start | bytes 786440 | tf_op jit(solution)/shard_map/ppermute | solution.py:470
  71.6 19.0 %collective-permute-done.14.far0 = bf16[256,512]{1,0:T(8,128)(2,1)S(1)} collective-permute-done((bf16[256,512]{1,0:T(8,128)(2,1)S(1)}, bf16[256,512]{1,0:T(8,128)(2,1)S(1)}, u32[]{:S(2)}, u32[]{:S(2)}) %collective-permute-start.14) | collective-permute-done | bytes 262176 | tf_op jit(solution)/shard_map/ppermute | solution.py:469
  90.6 2.7 %collective-permute-start.17 = (bf16[256,512]{1,0:T(8,128)(2,1)S(1)}, bf16[256,512]{1,0:T(8,128)(2,1)S(1)}, u32[]{:S(2)}, u32[]{:S(2)}) collective-permute-start(bf16[256,512]{1,0:T(8,128)(2,1)S(1)} %collective-permute-done.14.far0), channel_id=1, source_target_pairs={{0,3},{1,0},{2,1},{3,2},{4,7},{5,4},{6,5},{7,6},{8,11},{9,8},{10,9... | collective-permute-start | bytes 786440 | tf_op jit(solution)/shard_map/ppermute | solution.py:471
  94.4 4.3 %collective-permute-done.17.far3 = bf16[256,512]{1,0:T(8,128)(2,1)S(1)} collective-permute-done((bf16[256,512]{1,0:T(8,128)(2,1)S(1)}, bf16[256,512]{1,0:T(8,128)(2,1)S(1)}, u32[]{:S(2)}, u32[]{:S(2)}) %collective-permute-start.17) | collective-permute-done | bytes 262176 | tf_op jit(solution)/shard_map/ppermute | solution.py:471
  98.7 2.5 %collective-permute-done.16.far2 = bf16[256,512]{1,0:T(8,128)(2,1)S(1)} collective-permute-done((bf16[256,512]{1,0:T(8,128)(2,1)S(1)}, bf16[256,512]{1,0:T(8,128)(2,1)S(1)}, u32[]{:S(2)}, u32[]{:S(2)}) %collective-permute-start.16) | collective-permute-done | bytes 262176 | tf_op jit(solution)/shard_map/ppermute | solution.py:471
  101.2 7.5 %collective-permute-done.15.far1 = bf16[256,512]{1,0:T(8,128)(2,1)S(1)} collective-permute-done((bf16[256,512]{1,0:T(8,128)(2,1)S(1)}, bf16[256,512]{1,0:T(8,128)(2,1)S(1)}, u32[]{:S(2)}, u32[]{:S(2)}) %collective-permute-start.15) | collective-permute-done | bytes 262176 | tf_op jit(solution)/shard_map/ppermute | solution.py:471
  109.5 13.7 %solve.1 = (f32[128,1024]{1,0:T(8,128)}, f32[128,1024]{1,0:T(8,128)}, f32[128,1024]{1,0:T(8,128)}, bf16[8,144,256]{2,1,0:T(8,128)(2,1)}) custom-call(s32[5]{0:T(128)S(1)} %stack.23.place, bf16[256,512]{1,0:T(8,128)(2,1)} %get-tuple-element.55.near0, bf16[256,512]{1,0:T(8,128)(2,1)S(1)} %collective-permute-done.11.near1, ...), custom_call_target="tpu_custom_call" | custom-call | tf_op jit(solution)/shard_map/solve/pallas_call | solution.py:434
  123.3 3.5 %all-to-all-start.2 = ((bf16[8,144,256]{2,1,0:T(8,128)(2,1)}), bf16[8,144,256]{2,1,0:T(8,128)(2,1)S(1)}, u32[]{:S(2)}, u32[]{:S(2)}) async-start(bf16[8,144,256]{2,1,0:T(8,128)(2,1)} %get-tuple-element.70), calls=%async_computation.2 | async-start | bytes 1179648 | tf_op jit(solution)/shard_map/all_to_all | solution.py:478
  129.6 2.5 %collective-permute-start.18 = (bf16[256,256]{1,0:T(8,128)(2,1)S(1)}, bf16[256,256]{1,0:T(8,128)(2,1)S(1)}, u32[]{:S(2)}, u32[]{:S(2)}) collective-permute-start(bf16[256,256]{1,0:T(8,128)(2,1)S(1)} %add_up.2), channel_id=1, source_target_pairs={{0,0},{1,1},{2,2},{3,3},{4,32},{5,33},{6,34},{7,35},{8,64},{9,65},... | collective-permute-start | bytes 393224 | tf_op jit(solution)/shard_map/ppermute | solution.py:482
  132.1 11.7 %collective-permute-done.18 = bf16[256,256]{1,0:T(8,128)(2,1)S(1)} collective-permute-done((bf16[256,256]{1,0:T(8,128)(2,1)S(1)}, bf16[256,256]{1,0:T(8,128)(2,1)S(1)}, u32[]{:S(2)}, u32[]{:S(2)}) %collective-permute-start.18) | collective-permute-done | bytes 131104 | tf_op jit(solution)/shard_map/ppermute | solution.py:482
  144.6 3.8 %second_partial.1 = (bf16[4,256,256]{2,1,0:T(8,128)(2,1)}, f32[8,128]{1,0:T(8,128)S(1)}) custom-call(s32[5]{0:T(128)S(1)} %stack.23.place, bf16[8,144,256]{2,1,0:T(8,128)(2,1)S(1)} %all-to-all-done.2.update_ref, bf16[4,256,128]{2,1,0:T(8,128)(2,1)S(1)} %get-tuple-element.71.weight_ref.near_w, bf16[4,4,256,128]{3,2,1,0:T(8,128)(2,1)} %get-tuple-element.72.near_hbm, ...), custom_call_target="tpu_custom_call" | custom-call | tf_op jit(solution)/shard_map/second_partial/pallas_call | solution.py:272
  148.4 5.8 %all-to-all-start.3 = ((bf16[4,256,256]{2,1,0:T(8,128)(2,1)}), bf16[4,256,256]{2,1,0:T(8,128)(2,1)S(1)}, u32[]{:S(2)}, u32[]{:S(2)}) async-start(bf16[4,256,256]{2,1,0:T(8,128)(2,1)} %get-tuple-element.76), calls=%async_computation.3 | async-start | bytes 1048576 | tf_op jit(solution)/shard_map/all_to_all | solution.py:485
  154.7 14.9 %all-to-all-done.3.parts_ref = bf16[4,256,256]{2,1,0:T(8,128)(2,1)S(1)} async-done(((bf16[4,256,256]{2,1,0:T(8,128)(2,1)}), bf16[4,256,256]{2,1,0:T(8,128)(2,1)S(1)}, u32[]{:S(2)}, u32[]{:S(2)}) %all-to-all-start.3) | async-done | bytes 524320 | tf_op jit(solution)/shard_map/all_to_all | solution.py:485
  170.2 6.1 %collective-permute-start.21 = (bf16[256,256]{1,0:T(8,128)(2,1)S(1)}, bf16[256,256]{1,0:T(8,128)(2,1)S(1)}, u32[]{:S(2)}, u32[]{:S(2)}) collective-permute-start(bf16[256,256]{1,0:T(8,128)(2,1)S(1)} %add_up.3), channel_id=1, source_target_pairs={{0,0},{1,1},{2,2},{3,3},{4,32},{5,33},{6,34},{7,35},{8,64},{9,65},... | collective-permute-start | bytes 393224 | tf_op jit(solution)/shard_map/ppermute | solution.py:486
  176.3 2.5 %broadcast_divide_fusion = f32[128,1024]{1,0:T(8,128)} fusion(f32[128,1024]{1,0:T(8,128)} %get-tuple-element.69, f32[]{:T(128)} %bitcast.9), kind=kLoop, calls=%fused_computation | loop fusion | flops 131072 | bytes 1048580 | tf_op jit(solution)/shard_map/div | solution.py:487
  178.8 6.5 %collective-permute-done.21 = bf16[256,256]{1,0:T(8,128)(2,1)S(1)} collective-permute-done((bf16[256,256]{1,0:T(8,128)(2,1)S(1)}, bf16[256,256]{1,0:T(8,128)(2,1)S(1)}, u32[]{:S(2)}, u32[]{:S(2)}) %collective-permute-start.21) | collective-permute-done | bytes 131104 | tf_op jit(solution)/shard_map/ppermute | solution.py:486
  (62 shorter events, 36.6 us)
Async XLA Ops:
  0.6 13.7 %collective-permute-start = (bf16[256,256]{1,0:T(8,128)(2,1)}, bf16[256,256]{1,0:T(8,128)(2,1)S(1)}, u32[]{:S(2)}, u32[]{:S(2)}) collective-permute-start(bf16[256,256]{1,0:T(8,128)(2,1)} %param.6), channel_id=1, source_target_pairs={{0,0},{1,1},{2,2},{3,3},{4,32},{5,33},{6,34},{7,35},{8,64},{9,65},... | collective-permute-start | bytes 393224 | tf_op jit(solution)/shard_map/ppermute | solution.py:454
  5.6 8.7 %collective-permute-start.1 = (bf16[512,128]{1,0:T(8,128)(2,1)S(1)}, bf16[512,128]{1,0:T(8,128)(2,1)S(1)}, u32[]{:S(2)}, u32[]{:S(2)}) collective-permute-start(bf16[512,128]{1,0:T(8,128)(2,1)S(1)} %get-tuple-element.42), channel_id=1, source_target_pairs={{0,1},{1,2},{2,3},{3,0},{4,5},{5,6},{6,7},{7,4},{8,9},{9,10},{10,1... | collective-permute-start | bytes 393224 | tf_op jit(solution)/shard_map/ppermute | solution.py:456
  6.9 7.4 %collective-permute-start.2 = (bf16[512,128]{1,0:T(8,128)(2,1)S(1)}, bf16[512,128]{1,0:T(8,128)(2,1)S(1)}, u32[]{:S(2)}, u32[]{:S(2)}) collective-permute-start(bf16[512,128]{1,0:T(8,128)(2,1)S(1)} %get-tuple-element.43), channel_id=1, source_target_pairs={{0,3},{1,0},{2,1},{3,2},{4,7},{5,4},{6,5},{7,6},{8,11},{9,8},{10,9... | collective-permute-start | bytes 393224 | tf_op jit(solution)/shard_map/ppermute | solution.py:456
  15.3 38.8 %all-to-all-start = ((bf16[8,256,256]{2,1,0:T(8,128)(2,1)}), bf16[8,256,256]{2,1,0:T(8,128)(2,1)S(1)}, u32[]{:S(2)}, u32[]{:S(2)}) async-start(bf16[8,256,256]{2,1,0:T(8,128)(2,1)} %broadcast_in_dim.9), calls=%async_computation | async-start | bytes 2097152 | tf_op jit(solution)/shard_map/all_to_all | solution.py:46
  23.4 5.3 %collective-permute-start.3 = (bf16[512,128]{1,0:T(8,128)(2,1)S(1)}, bf16[512,128]{1,0:T(8,128)(2,1)S(1)}, u32[]{:S(2)}, u32[]{:S(2)}) collective-permute-start(bf16[512,128]{1,0:T(8,128)(2,1)S(1)} %get-tuple-element.45), channel_id=1, source_target_pairs={{0,2},{1,3},{2,0},{3,1},{4,6},{5,7},{6,4},{7,5},{8,10},{9,11},{10,... | collective-permute-start | bytes 393224 | tf_op jit(solution)/shard_map/ppermute | solution.py:456
  29.3 7.7 %collective-permute-start.6 = (bf16[4,256,128]{2,1,0:T(8,128)(2,1)S(1)}, bf16[4,256,128]{2,1,0:T(8,128)(2,1)S(1)}, u32[]{:S(2)}, u32[]{:S(2)}) collective-permute-start(bf16[4,256,128]{2,1,0:T(8,128)(2,1)S(1)} %get-tuple-element.48.refs_0_), channel_id=1, source_target_pairs={{0,192},{64,0},{128,64},{192,128},{1,193},{65,1},{129,65},{193,129... | collective-permute-start | bytes 786440 | tf_op jit(solution)/shard_map/ppermute | solution.py:462
  30.6 12.5 %collective-permute-start.5 = (bf16[4,256,128]{2,1,0:T(8,128)(2,1)S(1)}, bf16[4,256,128]{2,1,0:T(8,128)(2,1)S(1)}, u32[]{:S(2)}, u32[]{:S(2)}) collective-permute-start(bf16[4,256,128]{2,1,0:T(8,128)(2,1)S(1)} %get-tuple-element.48.refs_0_), channel_id=1, source_target_pairs={{0,128},{64,192},{128,0},{192,64},{1,129},{65,193},{129,1},{193,65... | collective-permute-start | bytes 786440 | tf_op jit(solution)/shard_map/ppermute | solution.py:462
  34.8 10.9 %collective-permute-start.4 = (bf16[4,256,128]{2,1,0:T(8,128)(2,1)S(1)}, bf16[4,256,128]{2,1,0:T(8,128)(2,1)S(1)}, u32[]{:S(2)}, u32[]{:S(2)}) collective-permute-start(bf16[4,256,128]{2,1,0:T(8,128)(2,1)S(1)} %get-tuple-element.48.refs_0_), channel_id=1, source_target_pairs={{0,64},{64,128},{128,192},{192,0},{1,65},{65,129},{129,193},{193,1... | collective-permute-start | bytes 786440 | tf_op jit(solution)/shard_map/ppermute | solution.py:462
  34.8 12.9 %collective-permute-start.7 = (bf16[4,256,128]{2,1,0:T(8,128)(2,1)S(1)}, bf16[4,256,128]{2,1,0:T(8,128)(2,1)S(1)}, u32[]{:S(2)}, u32[]{:S(2)}) collective-permute-start(bf16[4,256,128]{2,1,0:T(8,128)(2,1)S(1)} %get-tuple-element.48.refs_0_), channel_id=1, source_target_pairs={{0,32},{32,0},{1,33},{33,1},{2,34},{34,2},{3,35},{35,3},{4,36},{36... | collective-permute-start | bytes 786440 | tf_op jit(solution)/shard_map/ppermute | solution.py:463
  37.0 10.6 %collective-permute-start.10 = (bf16[4,256,128]{2,1,0:T(8,128)(2,1)S(1)}, bf16[4,256,128]{2,1,0:T(8,128)(2,1)S(1)}, u32[]{:S(2)}, u32[]{:S(2)}) collective-permute-start(bf16[4,256,128]{2,1,0:T(8,128)(2,1)S(1)} %collective-permute-done.6.refs_3_), channel_id=1, source_target_pairs={{0,32},{32,0},{1,33},{33,1},{2,34},{34,2},{3,35},{35,3},{4,36},{36... | collective-permute-start | bytes 786440 | tf_op jit(solution)/shard_map/ppermute | solution.py:463
  54.1 69.2 %all-to-all-start.1 = ((bf16[8,256,256]{2,1,0:T(8,128)(2,1)}), bf16[8,256,256]{2,1,0:T(8,128)(2,1)S(1)}, u32[]{:S(2)}, u32[]{:S(2)}) async-start(bf16[8,256,256]{2,1,0:T(8,128)(2,1)} %get-tuple-element.64), calls=%async_computation.1 | async-start | bytes 2097152 | tf_op jit(solution)/shard_map/all_to_all | solution.py:466
  66.5 24.1 %collective-permute-start.14 = (bf16[256,512]{1,0:T(8,128)(2,1)S(1)}, bf16[256,512]{1,0:T(8,128)(2,1)S(1)}, u32[]{:S(2)}, u32[]{:S(2)}) collective-permute-start(bf16[256,512]{1,0:T(8,128)(2,1)S(1)} %get-tuple-element.54), channel_id=1, source_target_pairs={{0,4},{4,0},{1,5},{5,1},{2,6},{6,2},{3,7},{7,3},{8,12},{12,8},{9,1... | collective-permute-start | bytes 786440 | tf_op jit(solution)/shard_map/ppermute | solution.py:469
  67.8 25.9 %collective-permute-start.13 = (bf16[256,512]{1,0:T(8,128)(2,1)S(1)}, bf16[256,512]{1,0:T(8,128)(2,1)S(1)}, u32[]{:S(2)}, u32[]{:S(2)}) collective-permute-start(bf16[256,512]{1,0:T(8,128)(2,1)S(1)} %get-tuple-element.54), channel_id=1, source_target_pairs={{0,3},{1,0},{2,1},{3,2},{4,7},{5,4},{6,5},{7,6},{8,11},{9,8},{10,9... | collective-permute-start | bytes 786440 | tf_op jit(solution)/shard_map/ppermute | solution.py:470
  70.5 23.9 %collective-permute-start.12 = (bf16[256,512]{1,0:T(8,128)(2,1)S(1)}, bf16[256,512]{1,0:T(8,128)(2,1)S(1)}, u32[]{:S(2)}, u32[]{:S(2)}) collective-permute-start(bf16[256,512]{1,0:T(8,128)(2,1)S(1)} %get-tuple-element.54), channel_id=1, source_target_pairs={{0,2},{1,3},{2,0},{3,1},{4,6},{5,7},{6,4},{7,5},{8,10},{9,11},{10,... | collective-permute-start | bytes 786440 | tf_op jit(solution)/shard_map/ppermute | solution.py:470
  70.9 23.5 %collective-permute-start.11 = (bf16[256,512]{1,0:T(8,128)(2,1)S(1)}, bf16[256,512]{1,0:T(8,128)(2,1)S(1)}, u32[]{:S(2)}, u32[]{:S(2)}) collective-permute-start(bf16[256,512]{1,0:T(8,128)(2,1)S(1)} %get-tuple-element.54), channel_id=1, source_target_pairs={{0,1},{1,2},{2,3},{3,0},{4,5},{5,6},{6,7},{7,4},{8,9},{9,10},{10,1... | collective-permute-start | bytes 786440 | tf_op jit(solution)/shard_map/ppermute | solution.py:470
  90.6 8.1 %collective-permute-start.17 = (bf16[256,512]{1,0:T(8,128)(2,1)S(1)}, bf16[256,512]{1,0:T(8,128)(2,1)S(1)}, u32[]{:S(2)}, u32[]{:S(2)}) collective-permute-start(bf16[256,512]{1,0:T(8,128)(2,1)S(1)} %collective-permute-done.14.far0), channel_id=1, source_target_pairs={{0,3},{1,0},{2,1},{3,2},{4,7},{5,4},{6,5},{7,6},{8,11},{9,8},{10,9... | collective-permute-start | bytes 786440 | tf_op jit(solution)/shard_map/ppermute | solution.py:471
  93.4 7.8 %collective-permute-start.16 = (bf16[256,512]{1,0:T(8,128)(2,1)S(1)}, bf16[256,512]{1,0:T(8,128)(2,1)S(1)}, u32[]{:S(2)}, u32[]{:S(2)}) collective-permute-start(bf16[256,512]{1,0:T(8,128)(2,1)S(1)} %collective-permute-done.14.far0), channel_id=1, source_target_pairs={{0,2},{1,3},{2,0},{3,1},{4,6},{5,7},{6,4},{7,5},{8,10},{9,11},{10,... | collective-permute-start | bytes 786440 | tf_op jit(solution)/shard_map/ppermute | solution.py:471
  93.7 15.0 %collective-permute-start.15 = (bf16[256,512]{1,0:T(8,128)(2,1)S(1)}, bf16[256,512]{1,0:T(8,128)(2,1)S(1)}, u32[]{:S(2)}, u32[]{:S(2)}) collective-permute-start(bf16[256,512]{1,0:T(8,128)(2,1)S(1)} %collective-permute-done.14.far0), channel_id=1, source_target_pairs={{0,1},{1,2},{2,3},{3,0},{4,5},{5,6},{6,7},{7,4},{8,9},{9,10},{10,1... | collective-permute-start | bytes 786440 | tf_op jit(solution)/shard_map/ppermute | solution.py:471
  108.7 18.8 %collective-permute-start.19 = (bf16[3,4,256,128]{3,2,1,0:T(8,128)(2,1)}, bf16[3,4,256,128]{3,2,1,0:T(8,128)(2,1)S(1)}, u32[]{:S(2)}, u32[]{:S(2)}) collective-permute-start(bf16[3,4,256,128]{3,2,1,0:T(8,128)(2,1)} %get-tuple-element.73), channel_id=1, source_target_pairs={{0,4},{4,0},{1,5},{5,1},{2,6},{6,2},{3,7},{7,3},{8,12},{12,8},{9,1... | collective-permute-start | bytes 2359304 | tf_op jit(solution)/shard_map/ppermute | solution.py:473
  123.3 20.4 %all-to-all-start.2 = ((bf16[8,144,256]{2,1,0:T(8,128)(2,1)}), bf16[8,144,256]{2,1,0:T(8,128)(2,1)S(1)}, u32[]{:S(2)}, u32[]{:S(2)}) async-start(bf16[8,144,256]{2,1,0:T(8,128)(2,1)} %get-tuple-element.70), calls=%async_computation.2 | async-start | bytes 1179648 | tf_op jit(solution)/shard_map/all_to_all | solution.py:478
  127.5 16.2 %collective-permute-start.20 = (bf16[3,4,256,128]{3,2,1,0:T(8,128)(2,1)S(1)}, bf16[3,4,256,128]{3,2,1,0:T(8,128)(2,1)S(1)}, u32[]{:S(2)}, u32[]{:S(2)}) collective-permute-start(bf16[3,4,256,128]{3,2,1,0:T(8,128)(2,1)S(1)} %collective-permute-done.19.far_hbm), channel_id=1, source_target_pairs={{0,32},{32,0},{1,33},{33,1},{2,34},{34,2},{3,35},{35,3},{4,36},{36... | collective-permute-start | bytes 2359304 | tf_op jit(solution)/shard_map/ppermute | solution.py:480
  129.6 14.2 %collective-permute-start.18 = (bf16[256,256]{1,0:T(8,128)(2,1)S(1)}, bf16[256,256]{1,0:T(8,128)(2,1)S(1)}, u32[]{:S(2)}, u32[]{:S(2)}) collective-permute-start(bf16[256,256]{1,0:T(8,128)(2,1)S(1)} %add_up.2), channel_id=1, source_target_pairs={{0,0},{1,1},{2,2},{3,3},{4,32},{5,33},{6,34},{7,35},{8,64},{9,65},... | collective-permute-start | bytes 393224 | tf_op jit(solution)/shard_map/ppermute | solution.py:482
  148.4 21.2 %all-to-all-start.3 = ((bf16[4,256,256]{2,1,0:T(8,128)(2,1)}), bf16[4,256,256]{2,1,0:T(8,128)(2,1)S(1)}, u32[]{:S(2)}, u32[]{:S(2)}) async-start(bf16[4,256,256]{2,1,0:T(8,128)(2,1)} %get-tuple-element.76), calls=%async_computation.3 | async-start | bytes 1048576 | tf_op jit(solution)/shard_map/all_to_all | solution.py:485
  170.2 15.1 %collective-permute-start.21 = (bf16[256,256]{1,0:T(8,128)(2,1)S(1)}, bf16[256,256]{1,0:T(8,128)(2,1)S(1)}, u32[]{:S(2)}, u32[]{:S(2)}) collective-permute-start(bf16[256,256]{1,0:T(8,128)(2,1)S(1)} %add_up.3), channel_id=1, source_target_pairs={{0,0},{1,1},{2,2},{3,3},{4,32},{5,33},{6,34},{7,35},{8,64},{9,65},... | collective-permute-start | bytes 393224 | tf_op jit(solution)/shard_map/ppermute | solution.py:486
  (12 other events, 31.5 us)

commit v7 on v5

v7 whole, which is shorter than its diff:
```python
import jax
import jax.numpy as jnp
from jax import lax
from jax.experimental import pallas as pl
from jax.experimental.pallas import tpu as pltpu
from jax.sharding import Mesh
from jax.sharding import PartitionSpec as P

BLOCK = 1024
STAT_DECAY = 0.8
LEARN_RATE = 0.005
EPSILON = 1e-06

AXES = ("x", "c", "zh", "zl", "y")
BATCH = ("x", "c")
ZAX = ("zh", "zl")
SOLVER = ("zl", "y")
MIB = 1 << 20
SHAPE = jax.ShapeDtypeStruct
BF16 = jnp.bfloat16
F32 = jnp.float32


def device(x, c, zh, zl, y):
    return (((x * 2 + c) * 4 + zh) * 2 + zl) * 4 + y


EVERY = [
    (x, c, zh, zl, y)
    for x in range(4)
    for c in range(2)
    for zh in range(4)
    for zl in range(2)
    for y in range(4)
]
SWAP = [(device(*d), device(d[2], d[3], d[0], d[1], d[4])) for d in EVERY]
FLIP = [(0, 1), (1, 0)]


def shift(by):
    return [(i, (i + by) % 4) for i in range(4)]


def copies_to(shard, axis, count):
    copies = jnp.broadcast_to(shard, (count, *shard.shape))
    return lax.all_to_all(copies, axis, split_axis=0, concat_axis=0, tiled=True)


def dot(a, b):
    return jnp.dot(a, b, preferred_element_type=F32)


def dot_minor(a, b):
    return lax.dot_general(a, b, (((1,), (1,)), ((), ())), preferred_element_type=F32)


VMEM = pl.BlockSpec(memory_space=pltpu.VMEM)
HBM = pl.BlockSpec(memory_space=pltpu.HBM)


def call(body, in_specs, out_specs, out_shape, scratch=(), limit=24, name=None):
    return pl.pallas_call(
        body,
        out_shape=out_shape,
        in_specs=[pl.BlockSpec(memory_space=pltpu.SMEM), *in_specs],
        out_specs=out_specs,
        scratch_shapes=list(scratch),
        compiler_params=pltpu.CompilerParams(vmem_limit_bytes=limit * MIB),
        name=name,
    )


def in_hbm(value):
    return pltpu.with_memory_space_constraint(value, pltpu.HBM)


def wide(slab):
    return jnp.concatenate([slab[q] for q in range(4)], axis=1)


def pack_body(place, acts_hbm, weight_hbm, *refs):
    outs, (acts_ref, weight_ref, work, sems) = refs[:4], refs[4:]
    loads = [
        pltpu.make_async_copy(weight_hbm, weight_ref, sems.at[0]),
        pltpu.make_async_copy(acts_hbm, acts_ref, sems.at[1]),
    ]
    for load in loads:
        load.start()
    for load in loads:
        load.wait()
    for q in range(4):
        for half in range(2):
            at = q * 256 + half * 128
            work[q, half * 128 : (half + 1) * 128, :] = weight_ref[:, at : at + 128]
    acts = acts_ref[...]
    for d in range(4):
        outs[d][:256, :] = acts
        outs[d][256:, :] = work[(place[4] + d) & 3]


def pack(place, acts, weight):
    part = SHAPE((512, 128), BF16)
    return call(
        pack_body,
        [HBM] * 2,
        [VMEM] * 4,
        [part] * 4,
        scratch=[
            pltpu.VMEM((256, 128), BF16),
            pltpu.VMEM((128, 1024), BF16),
            pltpu.VMEM((4, 256, 128), BF16),
            pltpu.SemaphoreType.DMA((2,)),
        ],
        limit=8,
        name="pack",
    )(place, in_hbm(acts), in_hbm(weight))


def unpack_body(place, *refs):
    for d in range(4):
        at = (place[4] - d) & 3
        refs[4][at] = refs[d][:256, :]
        refs[5][at] = refs[d][256:, :]


def unpack(place, parts):
    shape = SHAPE((4, 256, 128), BF16)
    return call(unpack_body, [VMEM] * 4, [VMEM] * 2, [shape] * 2, limit=8, name="unpack")(
        place, *parts
    )


def weight_of(parts):
    rows = [jnp.concatenate([parts[q, :128, :], parts[q, 128:, :]], axis=1) for q in range(4)]
    return jnp.concatenate(rows, axis=0)


def grad_body(place, cot_ref, *refs):
    own, swapped = refs[:4], refs[4:8]
    copies_ref, acts_ref, piece_ref, sems = refs[8:]
    x, c = place[0], place[1]
    sends = []
    for d in range(4):
        at = ((x - d) & 3) * 2
        sends.append(pltpu.make_async_copy(own[d], acts_ref.at[at + c], sems.at[d]))
        sends.append(pltpu.make_async_copy(swapped[d], acts_ref.at[at + 1 - c], sems.at[4 + d]))
    for send in sends:
        send.start()
    total = jnp.zeros((256, 512), F32)
    for d in range(4):
        at = ((x - d) & 3) * 2
        total = total + dot(cot_ref[at + c], wide(own[d]))
        total = total + dot(cot_ref[at + 1 - c], wide(swapped[d]))
    piece_ref[...] = total.astype(BF16)
    for s in range(8):
        sends.append(pltpu.make_async_copy(piece_ref, copies_ref.at[s], sems.at[8 + s]))
        sends[-1].start()
    for send in sends:
        send.wait()


def grad_piece(place, cot_all, own, swapped):
    return call(
        grad_body,
        [VMEM] * 9,
        [HBM, HBM],
        [pltpu.HBM((8, 256, 512), BF16), pltpu.HBM((8, 4, 256, 128), BF16)],
        scratch=[pltpu.VMEM((256, 512), BF16), pltpu.SemaphoreType.DMA((16,))],
        limit=10,
        name="grad_piece",
    )(place, cot_all, *own, *swapped)


def first_body(place, weight_ref, acts_ref, out_ref, work, sems):
    weight_t = weight_of(weight_ref).T
    sends = []
    for group in range(8):
        work[group] = dot_minor(weight_t, wide(acts_ref.at[group])).astype(BF16)
        sends.append(pltpu.make_async_copy(work.at[group], out_ref.at[group], sems.at[group]))
        sends[-1].start()
    for send in sends:
        send.wait()


def first_partial(place, near_w, acts):
    return call(
        first_body,
        [VMEM] * 2,
        HBM,
        pltpu.HBM((8, 256, 256), BF16),
        scratch=[pltpu.VMEM((8, 256, 256), BF16), pltpu.SemaphoreType.DMA((8,))],
        limit=12,
        name="first_partial",
    )(place, near_w, acts)


def as_rows(value):
    high = value.astype(BF16).astype(F32)
    middle = (value - high).astype(BF16).astype(F32)
    low = value - high - middle
    row = lax.broadcasted_iota(jnp.int32, (16, 256), 0)
    rows = jnp.where(row == 0, high, jnp.where(row == 1, middle, jnp.where(row == 2, low, 0.0)))
    return rows.astype(BF16)


def from_rows(rows):
    return jnp.sum(rows.astype(F32), axis=0, keepdims=True)[:, :1]


def second_body(place, u0, u1, u2, u3, acts_ref, out_ref, squares_ref, update_ref, work, sems):
    squares = jnp.zeros((1, 1), F32)
    for d, piece in enumerate((u0, u1, u2, u3)):
        update_ref[(place[4] - d) & 3] = piece[:128, :]
        squares = squares + from_rows(piece[128:, :])
    squares_ref[...] = jnp.broadcast_to(squares, (8, 128))
    tail = as_rows(squares)
    update_t = update_ref[...].reshape(512, 256).T
    sends = []
    for group in range(8):
        work[group, :256, :] = dot_minor(update_t, wide(acts_ref.at[group])).astype(BF16)
        work[group, 256:, :] = tail
        sends.append(pltpu.make_async_copy(work.at[group], out_ref.at[group], sems.at[group]))
        sends[-1].start()
    for send in sends:
        send.wait()


def second_partial(place, update_parts, acts):
    return call(
        second_body,
        [VMEM] * 5,
        [HBM, VMEM],
        [pltpu.HBM((8, 272, 256), BF16), SHAPE((8, 128), F32)],
        scratch=[
            pltpu.VMEM((4, 128, 256), BF16),
            pltpu.VMEM((8, 272, 256), BF16),
            pltpu.SemaphoreType.DMA((8,)),
        ],
        limit=12,
        name="second_partial",
    )(place, *update_parts, acts)


def first_add_body(place, parts_ref, total_ref, out_ref):
    total = parts_ref[0].astype(F32)
    for i in range(1, 8):
        total = total + parts_ref[i].astype(F32)
    total_ref[...] = total
    out_ref[...] = total.astype(BF16)


def first_add(place, parts):
    shape = (256, 256)
    return call(
        first_add_body,
        [VMEM],
        [VMEM] * 2,
        [SHAPE(shape, F32), SHAPE(shape, BF16)],
        limit=8,
        name="first_add",
    )(place, parts)


def second_add_body(place, total_ref, parts_ref, out_ref):
    total = total_ref[...]
    for h in range(4):
        squares = from_rows(parts_ref[2 * h, 256:, :]) + from_rows(parts_ref[2 * h + 1, 256:, :])
        rate = LEARN_RATE / jnp.sqrt(squares / (BLOCK * BLOCK) + EPSILON)
        change = parts_ref[2 * h, :256, :].astype(F32) + parts_ref[2 * h + 1, :256, :].astype(F32)
        total = total - rate * change
    out_ref[...] = total.astype(BF16)


def second_add(place, total, parts):
    return call(
        second_add_body,
        [VMEM] * 2,
        VMEM,
        SHAPE((256, 256), BF16),
        limit=8,
        name="second_add",
    )(place, total, parts)


def statistics(lhs_ref, rhs_ref, old_ref, full_ref, off_ref):
    tile = 256
    sums = jnp.zeros((1, BLOCK), F32)
    diag = jnp.zeros((1, BLOCK), F32)
    for i in range(BLOCK // tile):
        rows = pl.ds(i * tile, tile)
        gram = dot(lhs_ref[rows, :], rhs_ref[...])
        new = STAT_DECAY * old_ref[rows, :] + (1.0 - STAT_DECAY) / BLOCK * gram
        full_ref[rows, :] = new
        sums = sums + jnp.sum(jnp.abs(new), axis=0, keepdims=True)
        row = lax.broadcasted_iota(jnp.int32, (tile, BLOCK), 0) + i * tile
        col = lax.broadcasted_iota(jnp.int32, (tile, BLOCK), 1)
        on_diag = row == col
        diag = diag + jnp.sum(jnp.where(on_diag, new, 0.0), axis=0, keepdims=True)
        off_ref[rows, :] = jnp.where(on_diag, 0.0, new).astype(BF16)
    scale = 2.5 / (jnp.max(sums, axis=1, keepdims=True) + EPSILON)
    return scale, diag


def times_factor(rows, off_ref, diag):
    return rows * diag + dot(rows.astype(BF16), off_ref[...])


def times_root(start, off_ref, diag, quarter):
    value = start
    for _ in range(4):
        value = 1.25 * value - quarter * times_factor(value, off_ref, diag)
    return 1.25 * start - quarter * times_factor(value, off_ref, diag)


def solver_body(
    place,
    pieces_ref,
    left_old_ref,
    right_old_ref,
    new_left_ref,
    new_right_ref,
    update_ref,
    sent0,
    sent1,
    sent2,
    sent3,
    left_buf,
    right_buf,
    grad_ref,
    grad_t_ref,
    full_ref,
    off_left_ref,
    off_right_ref,
    rows_buf,
    update_buf,
    sent_buf,
    sems,
):
    load_left = pltpu.make_async_copy(left_old_ref, left_buf, sems.at[0])
    load_right = pltpu.make_async_copy(right_old_ref, right_buf, sems.at[1])
    load_left.start()
    load_right.start()
    first = pl.multiple_of((place[3] * 4 + place[4]) * 128, 128)
    own = pl.ds(first, 128)
    for zl in range(2):
        for y in range(4):
            piece = pieces_ref[zl * 4 + y]
            grad_ref[pl.ds(y * 256, 256), pl.ds(zl * 512, 512)] = piece
            grad_t_ref[pl.ds(zl * 512, 512), pl.ds(y * 256, 256)] = piece.T
    load_left.wait()
    scale_left, diag_left = statistics(grad_t_ref, grad_ref, left_buf, full_ref, off_left_ref)
    left_rows = full_ref[own, :]
    rows_buf[...] = left_rows
    store_left = pltpu.make_async_copy(rows_buf, new_left_ref, sems.at[2])
    store_left.start()
    load_right.wait()
    scale_right, diag_right = statistics(
        grad_ref, grad_t_ref, right_buf, full_ref, off_right_ref
    )
    store_right = pltpu.make_async_copy(full_ref.at[own, :], new_right_ref, sems.at[3])
    store_right.start()
    quarter_left = scale_left * 0.25
    quarter_right = scale_right * 0.25
    row = lax.broadcasted_iota(jnp.int32, (128, BLOCK), 0) + first
    col = lax.broadcasted_iota(jnp.int32, (128, BLOCK), 1)
    start = jnp.where(row == col, 1.25, 0.0) - quarter_left * left_rows
    root = jnp.sqrt(jnp.sqrt(scale_left)) * times_root(start, off_left_ref, diag_left, quarter_left)
    high = root.astype(BF16)
    low = (root - high.astype(F32)).astype(BF16)
    both = dot(jnp.concatenate([high, low], axis=0), grad_t_ref[...])
    mixed = both[:128] + both[128:]
    turned = 1.25 * mixed - quarter_right * times_factor(mixed, off_right_ref, diag_right)
    update = jnp.sqrt(jnp.sqrt(scale_right)) * times_root(
        turned, off_right_ref, diag_right, quarter_right
    )
    squares = jnp.sum(jnp.sum(update * update, axis=0, keepdims=True), axis=1, keepdims=True)
    tail = as_rows(squares)
    for y in range(4):
        sent_buf[y, :128, :] = update[:, y * 256 : (y + 1) * 256].astype(BF16)
        sent_buf[y, 128:, :] = tail
    stores = [
        pltpu.make_async_copy(sent_buf.at[(place[4] + d) & 3], sent, sems.at[4 + d])
        for d, sent in enumerate((sent0, sent1, sent2, sent3))
    ]
    for store in stores:
        store.start()
    update_buf[...] = update
    stores.append(pltpu.make_async_copy(update_buf, update_ref, sems.at[8]))
    stores[-1].start()
    for store in [store_left, store_right, *stores]:
        store.wait()


def solve(place, pieces, left_old, right_old):
    square = (BLOCK, BLOCK)
    rows = pltpu.HBM((128, BLOCK), F32)
    return call(
        solver_body,
        [VMEM, HBM, HBM],
        [HBM] * 7,
        [rows, rows, rows, *[pltpu.HBM((144, 256), BF16)] * 4],
        scratch=[
            *[pltpu.VMEM(square, kind) for kind in (F32, F32, BF16, BF16, F32, BF16, BF16)],
            pltpu.VMEM((128, BLOCK), F32),
            pltpu.VMEM((128, BLOCK), F32),
            pltpu.VMEM((4, 144, 256), BF16),
            pltpu.SemaphoreType.DMA((9,)),
        ],
        limit=27,
        name="solve",
    )(place, pieces, left_old, right_old)


def body(activations, cotangent, weight, left_old, right_old):
    place = jnp.stack([lax.axis_index(a).astype(jnp.int32) for a in AXES])
    cot_turned = lax.ppermute(cotangent, AXES, SWAP)
    packed = pack(place, activations, weight)
    crossed = [lax.ppermute(packed[d], "y", shift(d)) for d in range(1, 4)]
    cot_turned, crossed[0], crossed[2] = lax.optimization_barrier(
        (cot_turned, crossed[0], crossed[2])
    )
    cot_all = copies_to(cot_turned, ZAX, 8)
    slab, near_w = unpack(place, [packed[0], *crossed])
    own = [slab] + [lax.ppermute(slab, "x", shift(d)) for d in range(1, 4)]
    swapped = [lax.ppermute(part, "c", FLIP) for part in own]
    copies, acts = grad_piece(place, cot_all, own, swapped)

    pieces = lax.all_to_all(copies, SOLVER, 0, 0, tiled=True)
    first = first_partial(place, near_w, acts)
    pieces, first = lax.optimization_barrier((pieces, first))
    first_parts = lax.all_to_all(first, ZAX, 0, 0, tiled=True)
    new_left, new_right, update, *sent = solve(
        place, pieces, in_hbm(left_old[0, 0]), in_hbm(right_old[0, 0])
    )
    update_parts = [sent[0]] + [lax.ppermute(sent[d], "y", shift(d)) for d in range(1, 4)]
    second, squares = second_partial(place, update_parts, acts)
    second, first_parts = lax.optimization_barrier((second, first_parts))
    arrived = lax.all_to_all(second, ZAX, 0, 0, tiled=True)
    first_total, first_sum = first_add(place, first_parts)
    first_out = lax.ppermute(first_sum, AXES, SWAP)
    second_out = lax.ppermute(second_add(place, first_total, arrived), AXES, SWAP)
    total = squares[0, 0] + lax.ppermute(squares, "zl", FLIP)[0, 0]
    direction = update / jnp.sqrt(total / (BLOCK * BLOCK) + EPSILON)
    return (first_out, new_left[None, None], new_right[None, None], direction, second_out)


def solution(mesh):
    fine = Mesh(mesh.devices.reshape(4, 2, 4, 2, 4), AXES)
    rows = ("zh", "zl", "y")
    in_specs = (
        P(BATCH, rows),
        P(rows, BATCH),
        P(rows, BATCH),
        P("zh", BATCH, None, None),
        P("zh", BATCH, None, None),
    )
    out_specs = (
        P(rows, BATCH),
        P("zh", BATCH, SOLVER, None),
        P("zh", BATCH, SOLVER, None),
        P(rows, BATCH),
        P(rows, BATCH),
    )
    return jax.shard_map(body, mesh=fine, in_specs=in_specs, out_specs=out_specs, check_vma=False)
```

time: 174 us -> 176 us (1.011)
  local copies, waits for them, and re-layouts: 7.72 us -> 4.35 us
  starting transfers between devices: 59.9 us -> 62.3 us
    all_to_all x2, waiting for transfers between devices: 3.72 us -> 24.1 us  [the longest x1 24.1 us: body(): pieces = lax.all_to_all(copies, SOLVER, 0, 0, tiled=True)]
    ppermute x11 -> x6, waiting for transfers between devices: 51 us -> 37.9 us  [the longest x1 21.7 us: body(): total = squares[0, 0] + lax.ppermute(squares, 'zl', FLIP)[0, 0]]
    all_to_all x1, waiting for transfers between devices: 8.99 us -> 1.57 us  [copies_to(): return lax.all_to_all(copies, axis, split_axis=0, concat_axis=0, tiled=True)]
    ppermute x3, waiting for transfers between devices: 9.16 us -> 1.78 us  [body(): own = [slab] + [lax.ppermute(slab, 'x', shift(d)) for d in range(1, 4)]]
    ppermute x11 -> x6, starting transfers between devices: 21.7 us -> 15.6 us  [the longest x1 9.21 us: body(): first_out = lax.ppermute(first_sum, AXES, SWAP)]
    all_to_all x1, waiting for transfers between devices: 0.01 us -> 5.18 us  [body(): first_parts = lax.all_to_all(first, ZAX, 0, 0, tiled=True)]
    ppermute x4, starting transfers between devices: 4.32 us -> 9.03 us  [body(): swapped = [lax.ppermute(part, 'c', FLIP) for part in own]]
    ppermute x3, starting transfers between devices: 2.75 us -> 7.06 us  [body(): own = [slab] + [lax.ppermute(slab, 'x', shift(d)) for d in range(1, 4)]]
  transfers between devices with their start and end apart: 26 -> 21, of which waited for: 17 -> 14; matrix products, arithmetic and copies ran while one was open for 2% -> 1% of each run, Pallas kernels for 10% -> 13%
where the time goes in v7:
time: 176 us; the launch traced here: 175 us
  waiting for transfers between devices  79.6 us (45%)
  starting transfers between devices  62.3 us (35%)
  Pallas kernels  25.7 us (15%)
  local copies, waits for them, and re-layouts  4.35 us (2%)
  between operations  2.15 us (1%)
    all_to_all x1, waiting for transfers between devices, body(): pieces = lax.all_to_all(copies, SOLVER, 0, 0, tiled=True)  24.1 us
    ppermute x1, waiting for transfers between devices, body(): total = squares[0, 0] + lax.ppermute(squares, 'zl', FLIP)[0, 0]  21.7 us
    pallas_call x1, Pallas kernels, solve(): call(solver_body, [VMEM, HBM, HBM], [HBM] * 7, [rows, rows, rows, *[pltpu...  14.6 us
    ppermute x1, starting transfers between devices, body(): first_out = lax.ppermute(first_sum, AXES, SWAP)  9.21 us
    ppermute x4, starting transfers between devices, body(): swapped = [lax.ppermute(part, 'c', FLIP) for part in own]  9.03 us
    ppermute x1, waiting for transfers between devices, body(): first_out = lax.ppermute(first_sum, AXES, SWAP)  8.01 us
    ppermute x1, starting transfers between devices, body(): cot_turned = lax.ppermute(cotangent, AXES, SWAP)  7.96 us
    ppermute x3, starting transfers between devices, body(): own = [slab] + [lax.ppermute(slab, 'x', shift(d)) for d in range(1, 4)]  7.06 us
  transfers between devices with their start and end apart: 21, of which 14 were waited for; matrix products, arithmetic and copies ran while one was open for 1% of the time, Pallas kernels for 13%

profile of v7, /device:TPU:7, one launch (start us, length us, event | category | flops | bytes accessed | tf_op | source)
XLA Modules:
  0.0 174.9 jit_solution(7400084393513851856)
XLA Ops:
  0.6 8.0 %collective-permute-start = (bf16[256,256]{1,0:T(8,128)(2,1)}, bf16[256,256]{1,0:T(8,128)(2,1)S(1)}, u32[]{:S(2)}, u32[]{:S(2)}) collective-permute-start(bf16[256,256]{1,0:T(8,128)(2,1)} %param.6), channel_id=1, source_target_pairs={{0,0},{1,1},{2,2},{3,3},{4,32},{5,33},{6,34},{7,35},{8,64},{9,65},... | collective-permute-start | bytes 393224 | tf_op jit(solution)/shard_map/ppermute | solution.py:416
  13.2 5.0 %collective-permute-done = bf16[256,256]{1,0:T(8,128)(2,1)S(1)} collective-permute-done((bf16[256,256]{1,0:T(8,128)(2,1)}, bf16[256,256]{1,0:T(8,128)(2,1)S(1)}, u32[]{:S(2)}, u32[]{:S(2)}) %collective-permute-start) | collective-permute-done | bytes 131104 | tf_op jit(solution)/shard_map/ppermute | solution.py:416
  19.3 3.6 %all-to-all-start = ((bf16[8,256,256]{2,1,0:T(8,128)(2,1)}), bf16[8,256,256]{2,1,0:T(8,128)(2,1)S(1)}, u32[]{:S(2)}, u32[]{:S(2)}) async-start(bf16[8,256,256]{2,1,0:T(8,128)(2,1)} %broadcast_in_dim.9), calls=%async_computation | async-start | bytes 2097152 | tf_op jit(solution)/shard_map/all_to_all | solution.py:46
  22.9 3.0 %collective-permute-start.3 = (bf16[512,128]{1,0:T(8,128)(2,1)S(1)}, bf16[512,128]{1,0:T(8,128)(2,1)S(1)}, u32[]{:S(2)}, u32[]{:S(2)}) collective-permute-start(bf16[512,128]{1,0:T(8,128)(2,1)S(1)} %get-tuple-element.36), channel_id=1, source_target_pairs={{0,2},{1,3},{2,0},{3,1},{4,6},{5,7},{6,4},{7,5},{8,10},{9,11},{10,... | collective-permute-start | bytes 393224 | tf_op jit(solution)/shard_map/ppermute | solution.py:418
  25.9 2.4 %collective-permute-done.3.refs_2_ = bf16[512,128]{1,0:T(8,128)(2,1)S(1)} collective-permute-done((bf16[512,128]{1,0:T(8,128)(2,1)S(1)}, bf16[512,128]{1,0:T(8,128)(2,1)S(1)}, u32[]{:S(2)}, u32[]{:S(2)}) %collective-permute-start.3) | collective-permute-done | bytes 131104 | tf_op jit(solution)/shard_map/ppermute | solution.py:418
  30.4 3.5 %collective-permute-start.5 = (bf16[4,256,128]{2,1,0:T(8,128)(2,1)S(1)}, bf16[4,256,128]{2,1,0:T(8,128)(2,1)S(1)}, u32[]{:S(2)}, u32[]{:S(2)}) collective-permute-start(bf16[4,256,128]{2,1,0:T(8,128)(2,1)S(1)} %get-tuple-element.38.refs_0_), channel_id=1, source_target_pairs={{0,128},{64,192},{128,0},{192,64},{1,129},{65,193},{129,1},{193,65... | collective-permute-start | bytes 786440 | tf_op jit(solution)/shard_map/ppermute | solution.py:424
  33.9 2.0 %collective-permute-start.4 = (bf16[4,256,128]{2,1,0:T(8,128)(2,1)S(1)}, bf16[4,256,128]{2,1,0:T(8,128)(2,1)S(1)}, u32[]{:S(2)}, u32[]{:S(2)}) collective-permute-start(bf16[4,256,128]{2,1,0:T(8,128)(2,1)S(1)} %get-tuple-element.38.refs_0_), channel_id=1, source_target_pairs={{0,64},{64,128},{128,192},{192,0},{1,65},{65,129},{129,193},{193,1... | collective-permute-start | bytes 786440 | tf_op jit(solution)/shard_map/ppermute | solution.py:424
  37.5 4.6 %collective-permute-start.10 = (bf16[4,256,128]{2,1,0:T(8,128)(2,1)S(1)}, bf16[4,256,128]{2,1,0:T(8,128)(2,1)S(1)}, u32[]{:S(2)}, u32[]{:S(2)}) collective-permute-start(bf16[4,256,128]{2,1,0:T(8,128)(2,1)S(1)} %collective-permute-done.6.refs_3_), channel_id=1, source_target_pairs={{0,32},{32,0},{1,33},{33,1},{2,34},{34,2},{3,35},{35,3},{4,36},{36... | collective-permute-start | bytes 786440 | tf_op jit(solution)/shard_map/ppermute | solution.py:425
  43.9 2.8 %collective-permute-start.9 = (bf16[4,256,128]{2,1,0:T(8,128)(2,1)S(1)}, bf16[4,256,128]{2,1,0:T(8,128)(2,1)S(1)}, u32[]{:S(2)}, u32[]{:S(2)}) collective-permute-start(bf16[4,256,128]{2,1,0:T(8,128)(2,1)S(1)} %collective-permute-done.5.refs_2_), channel_id=1, source_target_pairs={{0,32},{32,0},{1,33},{33,1},{2,34},{34,2},{3,35},{35,3},{4,36},{36... | collective-permute-start | bytes 786440 | tf_op jit(solution)/shard_map/ppermute | solution.py:425
  49.8 3.1 %grad_piece.1 = (bf16[8,256,512]{2,1,0:T(8,128)(2,1)}, bf16[8,4,256,128]{3,2,1,0:T(8,128)(2,1)}) custom-call(s32[5]{0:T(128)S(1)} %stack.23.place, bf16[8,256,256]{2,1,0:T(8,128)(2,1)S(1)} %all-to-all-done.cot_ref, bf16[4,256,128]{2,1,0:T(8,128)(2,1)S(1)} %get-tuple-element.38.refs_0_, bf16[4,256,128]{2,1,0:T(8,128)(2,1)S(1)} %collective-permute-done.4.refs_1_, ...), custom_call_target="tpu_custom_call" | custom-call | tf_op jit(solution)/shard_map/grad_piece/pallas_call | solution.py:163
  53.0 4.5 %all-to-all-start.1 = ((bf16[8,256,512]{2,1,0:T(8,128)(2,1)}), bf16[8,256,512]{2,1,0:T(8,128)(2,1)}, u32[]{:S(2)}, u32[]{:S(2)}) async-start(bf16[8,256,512]{2,1,0:T(8,128)(2,1)} %get-tuple-element.39), calls=%async_computation.1 | async-start | bytes 4194304 | tf_op jit(solution)/shard_map/all_to_all | solution.py:428
  57.5 2.1 %first_partial.1 = bf16[8,256,256]{2,1,0:T(8,128)(2,1)} custom-call(s32[5]{0:T(128)S(1)} %stack.23.place, bf16[4,256,128]{2,1,0:T(8,128)(2,1)S(1)} %get-tuple-element.40.weight_ref, bf16[8,4,256,128]{3,2,1,0:T(8,128)(2,1)S(1)} %copy-done), custom_call_target="tpu_custom_call" | custom-call | tf_op jit(solution)/shard_map/first_partial/pallas_call | solution.py:186
  59.6 24.1 %all-to-all-done.1.pieces_ref = bf16[8,256,512]{2,1,0:T(8,128)(2,1)} async-done(((bf16[8,256,512]{2,1,0:T(8,128)(2,1)}), bf16[8,256,512]{2,1,0:T(8,128)(2,1)}, u32[]{:S(2)}, u32[]{:S(2)}) %all-to-all-start.1) | async-done | bytes 2097184 | tf_op jit(solution)/shard_map/all_to_all | solution.py:428
  83.7 5.0 %all-to-all-start.2 = ((bf16[8,256,256]{2,1,0:T(8,128)(2,1)}), bf16[8,256,256]{2,1,0:T(8,128)(2,1)S(1)}, u32[]{:S(2)}, u32[]{:S(2)}) async-start(bf16[8,256,256]{2,1,0:T(8,128)(2,1)} %first_partial.1), calls=%async_computation.2 | async-start | bytes 2097152 | tf_op jit(solution)/shard_map/all_to_all | solution.py:431
  88.7 14.6 %solve.1 = (f32[128,1024]{1,0:T(8,128)}, f32[128,1024]{1,0:T(8,128)}, f32[128,1024]{1,0:T(8,128)}, bf16[144,256]{1,0:T(8,128)(2,1)}, bf16[144,256]{1,0:T(8,128)(...) custom-call(s32[5]{0:T(128)S(1)} %stack.23.place, bf16[8,256,512]{2,1,0:T(8,128)(2,1)} %all-to-all-done.1.pieces_ref, ...), custom_call_target="tpu_custom_call" | custom-call | tf_op jit(solution)/shard_map/solve/pallas_call | solution.py:397
  106.5 1.9 %collective-permute-done.11.u1 = bf16[144,256]{1,0:T(8,128)(2,1)S(1)} collective-permute-done((bf16[144,256]{1,0:T(8,128)(2,1)}, bf16[144,256]{1,0:T(8,128)(2,1)S(1)}, u32[]{:S(2)}, u32[]{:S(2)}) %collective-permute-start.11) | collective-permute-done | bytes 73760 | tf_op jit(solution)/shard_map/ppermute | solution.py:435
  110.6 2.1 %second_partial.1 = (bf16[8,272,256]{2,1,0:T(8,128)(2,1)}, f32[8,128]{1,0:T(8,128)S(1)}) custom-call(s32[5]{0:T(128)S(1)} %stack.23.place, bf16[144,256]{1,0:T(8,128)(2,1)S(1)} %copy-done.1, bf16[144,256]{1,0:T(8,128)(2,1)S(1)} %collective-permute-done.11.u1, bf16[144,256]{1,0:T(8,128)(2,1)S(1)} %collective-permute-done.12.u2, ...), custom_call_target="tpu_custom_call" | custom-call | tf_op jit(solution)/shard_map/second_partial/pallas_call | solution.py:229
  112.7 5.2 %all-to-all-done.2.parts_ref = bf16[8,256,256]{2,1,0:T(8,128)(2,1)S(1)} async-done(((bf16[8,256,256]{2,1,0:T(8,128)(2,1)}), bf16[8,256,256]{2,1,0:T(8,128)(2,1)S(1)}, u32[]{:S(2)}, u32[]{:S(2)}) %all-to-all-start.2) | async-done | bytes 1048608 | tf_op jit(solution)/shard_map/all_to_all | solution.py:431
  117.9 3.7 %all-to-all-start.3 = ((bf16[8,272,256]{2,1,0:T(8,128)(2,1)}), bf16[8,272,256]{2,1,0:T(8,128)(2,1)S(1)}, u32[]{:S(2)}, u32[]{:S(2)}) async-start(bf16[8,272,256]{2,1,0:T(8,128)(2,1)} %get-tuple-element.56), calls=%async_computation.3 | async-start | bytes 2228224 | tf_op jit(solution)/shard_map/all_to_all | solution.py:438
  123.5 21.7 %collective-permute-done.15 = f32[8,128]{1,0:T(8,128)S(1)} collective-permute-done((f32[8,128]{1,0:T(8,128)S(1)}, f32[8,128]{1,0:T(8,128)S(1)}, u32[]{:S(2)}, u32[]{:S(2)}) %collective-permute-start.15) | collective-permute-done | bytes 4128 | tf_op jit(solution)/shard_map/ppermute | solution.py:442
  147.7 9.2 %collective-permute-start.14 = (bf16[256,256]{1,0:T(8,128)(2,1)S(1)}, bf16[256,256]{1,0:T(8,128)(2,1)S(1)}, u32[]{:S(2)}, u32[]{:S(2)}) collective-permute-start(bf16[256,256]{1,0:T(8,128)(2,1)S(1)} %get-tuple-element.50), channel_id=1, source_target_pairs={{0,0},{1,1},{2,2},{3,3},{4,32},{5,33},{6,34},{7,35},{8,64},{9,65},... | collective-permute-start | bytes 393224 | tf_op jit(solution)/shard_map/ppermute | solution.py:440
  157.8 1.9 %collective-permute-start.16 = (bf16[256,256]{1,0:T(8,128)(2,1)S(1)}, bf16[256,256]{1,0:T(8,128)(2,1)S(1)}, u32[]{:S(2)}, u32[]{:S(2)}) collective-permute-start(bf16[256,256]{1,0:T(8,128)(2,1)S(1)} %second_add.1), channel_id=1, source_target_pairs={{0,0},{1,1},{2,2},{3,3},{4,32},{5,33},{6,34},{7,35},{8,64},{9,65},... | collective-permute-start | bytes 393224 | tf_op jit(solution)/shard_map/ppermute | solution.py:441
  160.5 8.0 %collective-permute-done.14 = bf16[256,256]{1,0:T(8,128)(2,1)S(1)} collective-permute-done((bf16[256,256]{1,0:T(8,128)(2,1)S(1)}, bf16[256,256]{1,0:T(8,128)(2,1)S(1)}, u32[]{:S(2)}, u32[]{:S(2)}) %collective-permute-start.14) | collective-permute-done | bytes 131104 | tf_op jit(solution)/shard_map/ppermute | solution.py:440
  168.6 5.0 %collective-permute-done.16 = bf16[256,256]{1,0:T(8,128)(2,1)S(1)} collective-permute-done((bf16[256,256]{1,0:T(8,128)(2,1)S(1)}, bf16[256,256]{1,0:T(8,128)(2,1)S(1)}, u32[]{:S(2)}, u32[]{:S(2)}) %collective-permute-start.16) | collective-permute-done | bytes 131104 | tf_op jit(solution)/shard_map/ppermute | solution.py:441
  (39 shorter events, 25.7 us)
Async XLA Ops:
  0.6 17.6 %collective-permute-start = (bf16[256,256]{1,0:T(8,128)(2,1)}, bf16[256,256]{1,0:T(8,128)(2,1)S(1)}, u32[]{:S(2)}, u32[]{:S(2)}) collective-permute-start(bf16[256,256]{1,0:T(8,128)(2,1)} %param.6), channel_id=1, source_target_pairs={{0,0},{1,1},{2,2},{3,3},{4,32},{5,33},{6,34},{7,35},{8,64},{9,65},... | collective-permute-start | bytes 393224 | tf_op jit(solution)/shard_map/ppermute | solution.py:416
  10.3 7.9 %collective-permute-start.1 = (bf16[512,128]{1,0:T(8,128)(2,1)S(1)}, bf16[512,128]{1,0:T(8,128)(2,1)S(1)}, u32[]{:S(2)}, u32[]{:S(2)}) collective-permute-start(bf16[512,128]{1,0:T(8,128)(2,1)S(1)} %get-tuple-element.31), channel_id=1, source_target_pairs={{0,1},{1,2},{2,3},{3,0},{4,5},{5,6},{6,7},{7,4},{8,9},{9,10},{10,1... | collective-permute-start | bytes 393224 | tf_op jit(solution)/shard_map/ppermute | solution.py:418
  11.7 6.6 %collective-permute-start.2 = (bf16[512,128]{1,0:T(8,128)(2,1)S(1)}, bf16[512,128]{1,0:T(8,128)(2,1)S(1)}, u32[]{:S(2)}, u32[]{:S(2)}) collective-permute-start(bf16[512,128]{1,0:T(8,128)(2,1)S(1)} %get-tuple-element.32), channel_id=1, source_target_pairs={{0,3},{1,0},{2,1},{3,2},{4,7},{5,4},{6,5},{7,6},{8,11},{9,8},{10,9... | collective-permute-start | bytes 393224 | tf_op jit(solution)/shard_map/ppermute | solution.py:418
  19.3 30.5 %all-to-all-start = ((bf16[8,256,256]{2,1,0:T(8,128)(2,1)}), bf16[8,256,256]{2,1,0:T(8,128)(2,1)S(1)}, u32[]{:S(2)}, u32[]{:S(2)}) async-start(bf16[8,256,256]{2,1,0:T(8,128)(2,1)} %broadcast_in_dim.9), calls=%async_computation | async-start | bytes 2097152 | tf_op jit(solution)/shard_map/all_to_all | solution.py:46
  22.9 5.4 %collective-permute-start.3 = (bf16[512,128]{1,0:T(8,128)(2,1)S(1)}, bf16[512,128]{1,0:T(8,128)(2,1)S(1)}, u32[]{:S(2)}, u32[]{:S(2)}) collective-permute-start(bf16[512,128]{1,0:T(8,128)(2,1)S(1)} %get-tuple-element.36), channel_id=1, source_target_pairs={{0,2},{1,3},{2,0},{3,1},{4,6},{5,7},{6,4},{7,5},{8,10},{9,11},{10,... | collective-permute-start | bytes 393224 | tf_op jit(solution)/shard_map/ppermute | solution.py:418
  28.9 8.6 %collective-permute-start.6 = (bf16[4,256,128]{2,1,0:T(8,128)(2,1)S(1)}, bf16[4,256,128]{2,1,0:T(8,128)(2,1)S(1)}, u32[]{:S(2)}, u32[]{:S(2)}) collective-permute-start(bf16[4,256,128]{2,1,0:T(8,128)(2,1)S(1)} %get-tuple-element.38.refs_0_), channel_id=1, source_target_pairs={{0,192},{64,0},{128,64},{192,128},{1,193},{65,1},{129,65},{193,129... | collective-permute-start | bytes 786440 | tf_op jit(solution)/shard_map/ppermute | solution.py:424
  30.4 13.5 %collective-permute-start.5 = (bf16[4,256,128]{2,1,0:T(8,128)(2,1)S(1)}, bf16[4,256,128]{2,1,0:T(8,128)(2,1)S(1)}, u32[]{:S(2)}, u32[]{:S(2)}) collective-permute-start(bf16[4,256,128]{2,1,0:T(8,128)(2,1)S(1)} %get-tuple-element.38.refs_0_), channel_id=1, source_target_pairs={{0,128},{64,192},{128,0},{192,64},{1,129},{65,193},{129,1},{193,65... | collective-permute-start | bytes 786440 | tf_op jit(solution)/shard_map/ppermute | solution.py:424
  33.9 12.8 %collective-permute-start.4 = (bf16[4,256,128]{2,1,0:T(8,128)(2,1)S(1)}, bf16[4,256,128]{2,1,0:T(8,128)(2,1)S(1)}, u32[]{:S(2)}, u32[]{:S(2)}) collective-permute-start(bf16[4,256,128]{2,1,0:T(8,128)(2,1)S(1)} %get-tuple-element.38.refs_0_), channel_id=1, source_target_pairs={{0,64},{64,128},{128,192},{192,0},{1,65},{65,129},{129,193},{193,1... | collective-permute-start | bytes 786440 | tf_op jit(solution)/shard_map/ppermute | solution.py:424
  35.9 10.8 %collective-permute-start.7 = (bf16[4,256,128]{2,1,0:T(8,128)(2,1)S(1)}, bf16[4,256,128]{2,1,0:T(8,128)(2,1)S(1)}, u32[]{:S(2)}, u32[]{:S(2)}) collective-permute-start(bf16[4,256,128]{2,1,0:T(8,128)(2,1)S(1)} %get-tuple-element.38.refs_0_), channel_id=1, source_target_pairs={{0,32},{32,0},{1,33},{33,1},{2,34},{34,2},{3,35},{35,3},{4,36},{36... | collective-permute-start | bytes 786440 | tf_op jit(solution)/shard_map/ppermute | solution.py:425
  37.5 9.2 %collective-permute-start.10 = (bf16[4,256,128]{2,1,0:T(8,128)(2,1)S(1)}, bf16[4,256,128]{2,1,0:T(8,128)(2,1)S(1)}, u32[]{:S(2)}, u32[]{:S(2)}) collective-permute-start(bf16[4,256,128]{2,1,0:T(8,128)(2,1)S(1)} %collective-permute-done.6.refs_3_), channel_id=1, source_target_pairs={{0,32},{32,0},{1,33},{33,1},{2,34},{34,2},{3,35},{35,3},{4,36},{36... | collective-permute-start | bytes 786440 | tf_op jit(solution)/shard_map/ppermute | solution.py:425
  43.9 4.0 %collective-permute-start.9 = (bf16[4,256,128]{2,1,0:T(8,128)(2,1)S(1)}, bf16[4,256,128]{2,1,0:T(8,128)(2,1)S(1)}, u32[]{:S(2)}, u32[]{:S(2)}) collective-permute-start(bf16[4,256,128]{2,1,0:T(8,128)(2,1)S(1)} %collective-permute-done.5.refs_2_), channel_id=1, source_target_pairs={{0,32},{32,0},{1,33},{33,1},{2,34},{34,2},{3,35},{35,3},{4,36},{36... | collective-permute-start | bytes 786440 | tf_op jit(solution)/shard_map/ppermute | solution.py:425
  46.7 1.5 collective-permute-start.8
  53.0 4.5 %copy-start = (bf16[8,4,256,128]{3,2,1,0:T(8,128)(2,1)S(1)}, bf16[8,4,256,128]{3,2,1,0:T(8,128)(2,1)}, u32[]{:S(2)}) copy-start(bf16[8,4,256,128]{3,2,1,0:T(8,128)(2,1)} %get-tuple-element.41.acts_ref) | copy-start | bytes 6291460
  53.0 30.7 %all-to-all-start.1 = ((bf16[8,256,512]{2,1,0:T(8,128)(2,1)}), bf16[8,256,512]{2,1,0:T(8,128)(2,1)}, u32[]{:S(2)}, u32[]{:S(2)}) async-start(bf16[8,256,512]{2,1,0:T(8,128)(2,1)} %get-tuple-element.39), calls=%async_computation.1 | async-start | bytes 4194304 | tf_op jit(solution)/shard_map/all_to_all | solution.py:428
  83.7 34.2 %all-to-all-start.2 = ((bf16[8,256,256]{2,1,0:T(8,128)(2,1)}), bf16[8,256,256]{2,1,0:T(8,128)(2,1)S(1)}, u32[]{:S(2)}, u32[]{:S(2)}) async-start(bf16[8,256,256]{2,1,0:T(8,128)(2,1)} %first_partial.1), calls=%async_computation.2 | async-start | bytes 2097152 | tf_op jit(solution)/shard_map/all_to_all | solution.py:431
  103.3 5.0 %collective-permute-start.11 = (bf16[144,256]{1,0:T(8,128)(2,1)}, bf16[144,256]{1,0:T(8,128)(2,1)S(1)}, u32[]{:S(2)}, u32[]{:S(2)}) collective-permute-start(bf16[144,256]{1,0:T(8,128)(2,1)} %get-tuple-element.44), channel_id=1, source_target_pairs={{0,1},{1,2},{2,3},{3,0},{4,5},{5,6},{6,7},{7,4},{8,9},{9,10},{10,1... | collective-permute-start | bytes 221192 | tf_op jit(solution)/shard_map/ppermute | solution.py:435
  104.0 5.4 %collective-permute-start.12 = (bf16[144,256]{1,0:T(8,128)(2,1)}, bf16[144,256]{1,0:T(8,128)(2,1)S(1)}, u32[]{:S(2)}, u32[]{:S(2)}) collective-permute-start(bf16[144,256]{1,0:T(8,128)(2,1)} %get-tuple-element.45), channel_id=1, source_target_pairs={{0,2},{1,3},{2,0},{3,1},{4,6},{5,7},{6,4},{7,5},{8,10},{9,11},{10,... | collective-permute-start | bytes 221192 | tf_op jit(solution)/shard_map/ppermute | solution.py:435
  105.8 3.9 %collective-permute-start.13 = (bf16[144,256]{1,0:T(8,128)(2,1)}, bf16[144,256]{1,0:T(8,128)(2,1)S(1)}, u32[]{:S(2)}, u32[]{:S(2)}) collective-permute-start(bf16[144,256]{1,0:T(8,128)(2,1)} %get-tuple-element.46), channel_id=1, source_target_pairs={{0,3},{1,0},{2,1},{3,2},{4,7},{5,4},{6,5},{7,6},{8,11},{9,8},{10,9... | collective-permute-start | bytes 221192 | tf_op jit(solution)/shard_map/ppermute | solution.py:435
  109.7 0.9 copy-start.1
  117.9 41.8 %copy-start.2 = (f32[128,1024]{1,0:T(8,128)S(1)}, f32[128,1024]{1,0:T(8,128)}, u32[]{:S(2)}) copy-start(f32[128,1024]{1,0:T(8,128)} %get-tuple-element.53) | copy-start | bytes 1572868
  117.9 39.0 %all-to-all-start.3 = ((bf16[8,272,256]{2,1,0:T(8,128)(2,1)}), bf16[8,272,256]{2,1,0:T(8,128)(2,1)S(1)}, u32[]{:S(2)}, u32[]{:S(2)}) async-start(bf16[8,272,256]{2,1,0:T(8,128)(2,1)} %get-tuple-element.56), calls=%async_computation.3 | async-start | bytes 2228224 | tf_op jit(solution)/shard_map/all_to_all | solution.py:438
  121.6 23.6 %collective-permute-start.15 = (f32[8,128]{1,0:T(8,128)S(1)}, f32[8,128]{1,0:T(8,128)S(1)}, u32[]{:S(2)}, u32[]{:S(2)}) collective-permute-start(f32[8,128]{1,0:T(8,128)S(1)} %get-tuple-element.54), channel_id=1, source_target_pairs={{0,4},{4,0},{1,5},{5,1},{2,6},{6,2},{3,7},{7,3},{8,12},{12,8},{9,1... | collective-permute-start | bytes 12296 | tf_op jit(solution)/shard_map/ppermute | solution.py:442
  147.7 20.9 %collective-permute-start.14 = (bf16[256,256]{1,0:T(8,128)(2,1)S(1)}, bf16[256,256]{1,0:T(8,128)(2,1)S(1)}, u32[]{:S(2)}, u32[]{:S(2)}) collective-permute-start(bf16[256,256]{1,0:T(8,128)(2,1)S(1)} %get-tuple-element.50), channel_id=1, source_target_pairs={{0,0},{1,1},{2,2},{3,3},{4,32},{5,33},{6,34},{7,35},{8,64},{9,65},... | collective-permute-start | bytes 393224 | tf_op jit(solution)/shard_map/ppermute | solution.py:440
  157.8 15.8 %collective-permute-start.16 = (bf16[256,256]{1,0:T(8,128)(2,1)S(1)}, bf16[256,256]{1,0:T(8,128)(2,1)S(1)}, u32[]{:S(2)}, u32[]{:S(2)}) collective-permute-start(bf16[256,256]{1,0:T(8,128)(2,1)S(1)} %second_add.1), channel_id=1, source_target_pairs={{0,0},{1,1},{2,2},{3,3},{4,32},{5,33},{6,34},{7,35},{8,64},{9,65},... | collective-permute-start | bytes 393224 | tf_op jit(solution)/shard_map/ppermute | solution.py:441

commit v8 on v7

--- a/solution.py
+++ b/solution.py
@@ -171,10 +171,17 @@
     )(place, cot_all, *own, *swapped)
 
 
-def first_body(place, weight_ref, acts_ref, out_ref, work, sems):
+def first_body(place, weight_ref, acts_hbm, out_ref, acts_ref, work, sems):
+    loads = [
+        pltpu.make_async_copy(acts_hbm.at[group], acts_ref.at[group], sems.at[8 + group])
+        for group in range(8)
+    ]
+    for load in loads:
+        load.start()
     weight_t = weight_of(weight_ref).T
     sends = []
     for group in range(8):
+        loads[group].wait()
         work[group] = dot_minor(weight_t, wide(acts_ref.at[group])).astype(BF16)
         sends.append(pltpu.make_async_copy(work.at[group], out_ref.at[group], sems.at[group]))
         sends[-1].start()
@@ -185,13 +192,17 @@
 def first_partial(place, near_w, acts):
     return call(
         first_body,
-        [VMEM] * 2,
+        [VMEM, HBM],
         HBM,
         pltpu.HBM((8, 256, 256), BF16),
-        scratch=[pltpu.VMEM((8, 256, 256), BF16), pltpu.SemaphoreType.DMA((8,))],
+        scratch=[
+            pltpu.VMEM((8, 4, 256, 128), BF16),
+            pltpu.VMEM((8, 256, 256), BF16),
+            pltpu.SemaphoreType.DMA((16,)),
+        ],
         limit=12,
         name="first_partial",
-    )(place, near_w, acts)
+    )(place, near_w, in_hbm(acts))
 
 
 def as_rows(value):
@@ -207,12 +218,15 @@
     return jnp.sum(rows.astype(F32), axis=0, keepdims=True)[:, :1]
 
 
-def second_body(place, u0, u1, u2, u3, acts_ref, out_ref, squares_ref, update_ref, work, sems):
+def second_body(place, own_hbm, u1, u2, u3, acts_ref, out_ref, own_ref, update_ref, work, sems):
+    load = pltpu.make_async_copy(own_hbm, own_ref, sems.at[8])
+    load.start()
     squares = jnp.zeros((1, 1), F32)
-    for d, piece in enumerate((u0, u1, u2, u3)):
+    for d, piece in ((1, u1), (2, u2), (3, u3), (0, own_ref)):
+        if d == 0:
+            load.wait()
         update_ref[(place[4] - d) & 3] = piece[:128, :]
         squares = squares + from_rows(piece[128:, :])
-    squares_ref[...] = jnp.broadcast_to(squares, (8, 128))
     tail = as_rows(squares)
     update_t = update_ref[...].reshape(512, 256).T
     sends = []
@@ -228,13 +242,14 @@
 def second_partial(place, update_parts, acts):
     return call(
         second_body,
-        [VMEM] * 5,
-        [HBM, VMEM],
-        [pltpu.HBM((8, 272, 256), BF16), SHAPE((8, 128), F32)],
+        [HBM, *[VMEM] * 4],
+        HBM,
+        pltpu.HBM((8, 272, 256), BF16),
         scratch=[
+            pltpu.VMEM((144, 256), BF16),
             pltpu.VMEM((4, 128, 256), BF16),
             pltpu.VMEM((8, 272, 256), BF16),
-            pltpu.SemaphoreType.DMA((8,)),
+            pltpu.SemaphoreType.DMA((9,)),
         ],
         limit=12,
         name="second_partial",
@@ -261,22 +276,26 @@
     )(place, parts)
 
 
-def second_add_body(place, total_ref, parts_ref, out_ref):
+def second_add_body(place, total_ref, parts_ref, out_ref, spread_ref):
     total = total_ref[...]
+    own = jnp.zeros((1, 1), F32)
     for h in range(4):
         squares = from_rows(parts_ref[2 * h, 256:, :]) + from_rows(parts_ref[2 * h + 1, 256:, :])
-        rate = LEARN_RATE / jnp.sqrt(squares / (BLOCK * BLOCK) + EPSILON)
+        spread = jnp.sqrt(squares / (BLOCK * BLOCK) + EPSILON)
+        own = jnp.where(place[2] == h, spread, own)
+        rate = LEARN_RATE / spread
         change = parts_ref[2 * h, :256, :].astype(F32) + parts_ref[2 * h + 1, :256, :].astype(F32)
         total = total - rate * change
     out_ref[...] = total.astype(BF16)
+    spread_ref[...] = jnp.broadcast_to(own, (8, 128))
 
 
 def second_add(place, total, parts):
     return call(
         second_add_body,
         [VMEM] * 2,
-        VMEM,
-        SHAPE((256, 256), BF16),
+        [VMEM] * 2,
+        [SHAPE((256, 256), BF16), SHAPE((8, 128), F32)],
         limit=8,
         name="second_add",
     )(place, total, parts)
@@ -324,6 +343,7 @@
     sent1,
     sent2,
     sent3,
+    pieces_buf,
     left_buf,
     right_buf,
     grad_ref,
@@ -338,13 +358,19 @@
 ):
     load_left = pltpu.make_async_copy(left_old_ref, left_buf, sems.at[0])
     load_right = pltpu.make_async_copy(right_old_ref, right_buf, sems.at[1])
+    loads = [
+        pltpu.make_async_copy(pieces_ref.at[s], pieces_buf.at[s], sems.at[9 + s]) for s in range(8)
+    ]
+    for load in loads:
+        load.start()
     load_left.start()
     load_right.start()
     first = pl.multiple_of((place[3] * 4 + place[4]) * 128, 128)
     own = pl.ds(first, 128)
     for zl in range(2):
         for y in range(4):
-            piece = pieces_ref[zl * 4 + y]
+            loads[zl * 4 + y].wait()
+            piece = pieces_buf[zl * 4 + y]
             grad_ref[pl.ds(y * 256, 256), pl.ds(zl * 512, 512)] = piece
             grad_t_ref[pl.ds(zl * 512, 512), pl.ds(y * 256, 256)] = piece.T
     load_left.wait()
@@ -396,17 +422,18 @@
     rows = pltpu.HBM((128, BLOCK), F32)
     return call(
         solver_body,
-        [VMEM, HBM, HBM],
+        [HBM] * 3,
         [HBM] * 7,
         [rows, rows, rows, *[pltpu.HBM((144, 256), BF16)] * 4],
         scratch=[
+            pltpu.VMEM((8, 256, 512), BF16),
             *[pltpu.VMEM(square, kind) for kind in (F32, F32, BF16, BF16, F32, BF16, BF16)],
             pltpu.VMEM((128, BLOCK), F32),
             pltpu.VMEM((128, BLOCK), F32),
             pltpu.VMEM((4, 144, 256), BF16),
-            pltpu.SemaphoreType.DMA((9,)),
+            pltpu.SemaphoreType.DMA((17,)),
         ],
-        limit=27,
+        limit=28,
         name="solve",
     )(place, pieces, left_old, right_old)
 
@@ -426,21 +453,21 @@
     copies, acts = grad_piece(place, cot_all, own, swapped)
 
     pieces = lax.all_to_all(copies, SOLVER, 0, 0, tiled=True)
+    pieces, near_w = lax.optimization_barrier((pieces, near_w))
     first = first_partial(place, near_w, acts)
-    pieces, first = lax.optimization_barrier((pieces, first))
     first_parts = lax.all_to_all(first, ZAX, 0, 0, tiled=True)
     new_left, new_right, update, *sent = solve(
-        place, pieces, in_hbm(left_old[0, 0]), in_hbm(right_old[0, 0])
-    )
-    update_parts = [sent[0]] + [lax.ppermute(sent[d], "y", shift(d)) for d in range(1, 4)]
-    second, squares = second_partial(place, update_parts, acts)
+        place, in_hbm(pieces), in_hbm(left_old[0, 0]), in_hbm(right_old[0, 0])
+    )
+    update_parts = [in_hbm(sent[0])] + [lax.ppermute(sent[d], "y", shift(d)) for d in range(1, 4)]
+    second = second_partial(place, update_parts, acts)
     second, first_parts = lax.optimization_barrier((second, first_parts))
     arrived = lax.all_to_all(second, ZAX, 0, 0, tiled=True)
     first_total, first_sum = first_add(place, first_parts)
     first_out = lax.ppermute(first_sum, AXES, SWAP)
-    second_out = lax.ppermute(second_add(place, first_total, arrived), AXES, SWAP)
-    total = squares[0, 0] + lax.ppermute(squares, "zl", FLIP)[0, 0]
-    direction = update / jnp.sqrt(total / (BLOCK * BLOCK) + EPSILON)
+    second_sum, spread = second_add(place, first_total, arrived)
+    second_out = lax.ppermute(second_sum, AXES, SWAP)
+    direction = update / spread[0, 0]
     return (first_out, new_left[None, None], new_right[None, None], direction, second_out)
 
 

time: 176 us -> 181 us (1.028); the launches traced: 175 us -> 178 us
  blocking collectives: 0 us -> 27.7 us
  waiting for transfers between devices: 79.6 us -> 55.1 us
  Pallas kernels: 25.7 us -> 28.9 us
    all_to_all x0 -> x1, blocking collectives: none -> 27.7 us  [body(): pieces = lax.all_to_all(copies, SOLVER, 0, 0, tiled=True)]
    all_to_all x1 -> x0, waiting for transfers between devices: 24.1 us -> none  [body(): pieces = lax.all_to_all(copies, SOLVER, 0, 0, tiled=True)]
    ppermute x1, waiting for transfers between devices: 8.01 us -> 27 us  [body(): first_out = lax.ppermute(first_sum, AXES, SWAP)]
    ppermute x2 -> x1, waiting for transfers between devices: 26.7 us -> 9.12 us  [body(): second_out = lax.ppermute(second_sum, AXES, SWAP)]
    all_to_all x1 -> x0, starting transfers between devices: 4.48 us -> none  [body(): pieces = lax.all_to_all(copies, SOLVER, 0, 0, tiled=True)]
    pallas_call x4, Pallas kernels: 19.7 us -> 22.9 us  [the longest x1 14.3 us: solve(): call(solver_body, [HBM] * 3, [HBM] * 7, [rows, rows, rows, *[pltpu.HBM((1...]
    all_to_all x1, starting transfers between devices: 5.01 us -> 7.08 us  [body(): first_parts = lax.all_to_all(first, ZAX, 0, 0, tiled=True)]
  transfers between devices with their start and end apart: 21 -> 19, of which waited for: 14 -> 12; matrix products, arithmetic and copies ran while one was open for 1% -> 1% of each run, Pallas kernels for 13% -> 11%
where the time goes in v8:
time: 181 us; the launch traced here: 178 us
  starting transfers between devices  60.5 us (33%)
  waiting for transfers between devices  55.1 us (30%)
  Pallas kernels  28.9 us (16%)
  blocking collectives  27.7 us (15%)
  local copies, waits for them, and re-layouts  2.98 us (2%)
    all_to_all x1, blocking collectives, body(): pieces = lax.all_to_all(copies, SOLVER, 0, 0, tiled=True)  27.7 us
    ppermute x1, waiting for transfers between devices, body(): first_out = lax.ppermute(first_sum, AXES, SWAP)  27 us
    pallas_call x1, Pallas kernels, solve(): call(solver_body, [HBM] * 3, [HBM] * 7, [rows, rows, rows, *[pltpu.HBM((1...  14.3 us
    ppermute x1, starting transfers between devices, body(): first_out = lax.ppermute(first_sum, AXES, SWAP)  9.78 us
    ppermute x1, waiting for transfers between devices, body(): second_out = lax.ppermute(second_sum, AXES, SWAP)  9.12 us
    ppermute x4, starting transfers between devices, body(): swapped = [lax.ppermute(part, 'c', FLIP) for part in own]  9.03 us
    ppermute x1, starting transfers between devices, body(): cot_turned = lax.ppermute(cotangent, AXES, SWAP)  7.96 us
    all_to_all x1, starting transfers between devices, body(): first_parts = lax.all_to_all(first, ZAX, 0, 0, tiled=True)  7.08 us
  transfers between devices with their start and end apart: 19, of which 12 were waited for; matrix products, arithmetic and copies ran while one was open for 1% of the time, Pallas kernels for 11%

profile of v8, /device:TPU:7, one launch (start us, length us, event | category | flops | bytes accessed | tf_op | source)
XLA Modules:
  0.0 177.5 jit_solution(4600514593288891942)
XLA Ops:
  0.6 8.0 %collective-permute-start = (bf16[256,256]{1,0:T(8,128)(2,1)}, bf16[256,256]{1,0:T(8,128)(2,1)S(1)}, u32[]{:S(2)}, u32[]{:S(2)}) collective-permute-start(bf16[256,256]{1,0:T(8,128)(2,1)} %param.6), channel_id=1, source_target_pairs={{0,0},{1,1},{2,2},{3,3},{4,32},{5,33},{6,34},{7,35},{8,64},{9,65},... | collective-permute-start | bytes 393224 | tf_op jit(solution)/shard_map/ppermute | solution.py:443
  8.7 1.6 pack.1
  13.2 5.0 %collective-permute-done = bf16[256,256]{1,0:T(8,128)(2,1)S(1)} collective-permute-done((bf16[256,256]{1,0:T(8,128)(2,1)}, bf16[256,256]{1,0:T(8,128)(2,1)S(1)}, u32[]{:S(2)}, u32[]{:S(2)}) %collective-permute-start) | collective-permute-done | bytes 131104 | tf_op jit(solution)/shard_map/ppermute | solution.py:443
  19.3 3.6 %all-to-all-start = ((bf16[8,256,256]{2,1,0:T(8,128)(2,1)}), bf16[8,256,256]{2,1,0:T(8,128)(2,1)S(1)}, u32[]{:S(2)}, u32[]{:S(2)}) async-start(bf16[8,256,256]{2,1,0:T(8,128)(2,1)} %broadcast_in_dim.9), calls=%async_computation | async-start | bytes 2097152 | tf_op jit(solution)/shard_map/all_to_all | solution.py:46
  22.9 3.0 %collective-permute-start.3 = (bf16[512,128]{1,0:T(8,128)(2,1)S(1)}, bf16[512,128]{1,0:T(8,128)(2,1)S(1)}, u32[]{:S(2)}, u32[]{:S(2)}) collective-permute-start(bf16[512,128]{1,0:T(8,128)(2,1)S(1)} %get-tuple-element.36), channel_id=1, source_target_pairs={{0,2},{1,3},{2,0},{3,1},{4,6},{5,7},{6,4},{7,5},{8,10},{9,11},{10,... | collective-permute-start | bytes 393224 | tf_op jit(solution)/shard_map/ppermute | solution.py:445
  25.9 2.4 %collective-permute-done.3.refs_2_ = bf16[512,128]{1,0:T(8,128)(2,1)S(1)} collective-permute-done((bf16[512,128]{1,0:T(8,128)(2,1)S(1)}, bf16[512,128]{1,0:T(8,128)(2,1)S(1)}, u32[]{:S(2)}, u32[]{:S(2)}) %collective-permute-start.3) | collective-permute-done | bytes 131104 | tf_op jit(solution)/shard_map/ppermute | solution.py:445
  30.4 3.5 %collective-permute-start.5 = (bf16[4,256,128]{2,1,0:T(8,128)(2,1)S(1)}, bf16[4,256,128]{2,1,0:T(8,128)(2,1)S(1)}, u32[]{:S(2)}, u32[]{:S(2)}) collective-permute-start(bf16[4,256,128]{2,1,0:T(8,128)(2,1)S(1)} %get-tuple-element.38.refs_0_), channel_id=1, source_target_pairs={{0,128},{64,192},{128,0},{192,64},{1,129},{65,193},{129,1},{193,65... | collective-permute-start | bytes 786440 | tf_op jit(solution)/shard_map/ppermute | solution.py:451
  34.0 2.0 %collective-permute-start.4 = (bf16[4,256,128]{2,1,0:T(8,128)(2,1)S(1)}, bf16[4,256,128]{2,1,0:T(8,128)(2,1)S(1)}, u32[]{:S(2)}, u32[]{:S(2)}) collective-permute-start(bf16[4,256,128]{2,1,0:T(8,128)(2,1)S(1)} %get-tuple-element.38.refs_0_), channel_id=1, source_target_pairs={{0,64},{64,128},{128,192},{192,0},{1,65},{65,129},{129,193},{193,1... | collective-permute-start | bytes 786440 | tf_op jit(solution)/shard_map/ppermute | solution.py:451
  37.5 4.6 %collective-permute-start.10 = (bf16[4,256,128]{2,1,0:T(8,128)(2,1)S(1)}, bf16[4,256,128]{2,1,0:T(8,128)(2,1)S(1)}, u32[]{:S(2)}, u32[]{:S(2)}) collective-permute-start(bf16[4,256,128]{2,1,0:T(8,128)(2,1)S(1)} %collective-permute-done.6.refs_3_), channel_id=1, source_target_pairs={{0,32},{32,0},{1,33},{33,1},{2,34},{34,2},{3,35},{35,3},{4,36},{36... | collective-permute-start | bytes 786440 | tf_op jit(solution)/shard_map/ppermute | solution.py:452
  42.1 1.8 %collective-permute-done.5.refs_2_ = bf16[4,256,128]{2,1,0:T(8,128)(2,1)S(1)} collective-permute-done((bf16[4,256,128]{2,1,0:T(8,128)(2,1)S(1)}, bf16[4,256,128]{2,1,0:T(8,128)(2,1)S(1)}, u32[]{:S(2)}, u32[]{:S(2)}) %collective-permute-start.5) | collective-permute-done | bytes 262176 | tf_op jit(solution)/shard_map/ppermute | solution.py:451
  43.9 2.8 %collective-permute-start.9 = (bf16[4,256,128]{2,1,0:T(8,128)(2,1)S(1)}, bf16[4,256,128]{2,1,0:T(8,128)(2,1)S(1)}, u32[]{:S(2)}, u32[]{:S(2)}) collective-permute-start(bf16[4,256,128]{2,1,0:T(8,128)(2,1)S(1)} %collective-permute-done.5.refs_2_), channel_id=1, source_target_pairs={{0,32},{32,0},{1,33},{33,1},{2,34},{34,2},{3,35},{35,3},{4,36},{36... | collective-permute-start | bytes 786440 | tf_op jit(solution)/shard_map/ppermute | solution.py:452
  49.9 3.1 %grad_piece.1 = (bf16[8,256,512]{2,1,0:T(8,128)(2,1)}, bf16[8,4,256,128]{3,2,1,0:T(8,128)(2,1)}) custom-call(s32[5]{0:T(128)S(1)} %stack.23.place, bf16[8,256,256]{2,1,0:T(8,128)(2,1)S(1)} %all-to-all-done.cot_ref, bf16[4,256,128]{2,1,0:T(8,128)(2,1)S(1)} %get-tuple-element.38.refs_0_, bf16[4,256,128]{2,1,0:T(8,128)(2,1)S(1)} %collective-permute-done.4.refs_1_, ...), custom_call_target="tpu_custom_call" | custom-call | tf_op jit(solution)/shard_map/grad_piece/pallas_call | solution.py:163
  53.0 27.7 %all_to_all.20.pieces_ref = bf16[8,256,512]{2,1,0:T(8,128)(2,1)} all-to-all(bf16[8,256,512]{2,1,0:T(8,128)(2,1)} %get-tuple-element.39), channel_id=1, replica_groups=mesh['x'=4,'c'=2,'zh'=4,'zl'=2,'y'=4] {'zl','y'}, dimensions={0} | all-to-all | bytes 4194304 | tf_op jit(solution)/shard_map/all_to_all | solution.py:455
  80.7 4.8 %first_partial.1 = bf16[8,256,256]{2,1,0:T(8,128)(2,1)} custom-call(s32[5]{0:T(128)S(1)} %stack.23.place, bf16[4,256,128]{2,1,0:T(8,128)(2,1)S(1)} %get-tuple-element.47.weight_ref, bf16[8,4,256,128]{3,2,1,0:T(8,128)(2,1)} %get-tuple-element.46.acts_ref.acts_hbm), custom_call_target="tpu_custom_call" | custom-call | tf_op jit(solution)/shard_map/first_partial/pallas_call | solution.py:193
  85.5 7.1 %all-to-all-start.2 = ((bf16[8,256,256]{2,1,0:T(8,128)(2,1)}), bf16[8,256,256]{2,1,0:T(8,128)(2,1)S(1)}, u32[]{:S(2)}, u32[]{:S(2)}) async-start(bf16[8,256,256]{2,1,0:T(8,128)(2,1)} %first_partial.1), calls=%async_computation.2 | async-start | bytes 2097152 | tf_op jit(solution)/shard_map/all_to_all | solution.py:458
  92.6 14.3 %solve.1 = (f32[128,1024]{1,0:T(8,128)}, f32[128,1024]{1,0:T(8,128)}, f32[128,1024]{1,0:T(8,128)}, bf16[144,256]{1,0:T(8,128)(2,1)}, bf16[144,256]{1,0:T(8,128)(...) custom-call(s32[5]{0:T(128)S(1)} %stack.23.place, bf16[8,256,512]{2,1,0:T(8,128)(2,1)} %all_to_all.20.pieces_ref, ...), custom_call_target="tpu_custom_call" | custom-call | tf_op jit(solution)/shard_map/solve/pallas_call | solution.py:423
  107.9 1.7 collective-permute-start.12
  113.3 3.0 %second_partial.1 = bf16[8,272,256]{2,1,0:T(8,128)(2,1)} custom-call(s32[5]{0:T(128)S(1)} %stack.23.place, bf16[144,256]{1,0:T(8,128)(2,1)} %get-tuple-element.42.own_hbm, bf16[144,256]{1,0:T(8,128)(2,1)S(1)} %collective-permute-done.11.u1, bf16[144,256]{1,0:T(8,128)(2,1)S(1)} %collective-permute-done.12.u2, ...), custom_call_target="tpu_custom_call" | custom-call | tf_op jit(solution)/shard_map/second_partial/pallas_call | solution.py:243
  116.3 3.7 %all-to-all-done.2.parts_ref = bf16[8,256,256]{2,1,0:T(8,128)(2,1)S(1)} async-done(((bf16[8,256,256]{2,1,0:T(8,128)(2,1)}), bf16[8,256,256]{2,1,0:T(8,128)(2,1)S(1)}, u32[]{:S(2)}, u32[]{:S(2)}) %all-to-all-start.2) | async-done | bytes 1048608 | tf_op jit(solution)/shard_map/all_to_all | solution.py:458
  120.0 3.6 %all-to-all-start.3 = ((bf16[8,272,256]{2,1,0:T(8,128)(2,1)}), bf16[8,272,256]{2,1,0:T(8,128)(2,1)S(1)}, u32[]{:S(2)}, u32[]{:S(2)}) async-start(bf16[8,272,256]{2,1,0:T(8,128)(2,1)} %second_partial.1), calls=%async_computation.3 | async-start | bytes 2228224 | tf_op jit(solution)/shard_map/all_to_all | solution.py:465
  124.3 9.8 %collective-permute-start.14 = (bf16[256,256]{1,0:T(8,128)(2,1)S(1)}, bf16[256,256]{1,0:T(8,128)(2,1)S(1)}, u32[]{:S(2)}, u32[]{:S(2)}) collective-permute-start(bf16[256,256]{1,0:T(8,128)(2,1)S(1)} %get-tuple-element.49), channel_id=1, source_target_pairs={{0,0},{1,1},{2,2},{3,3},{4,32},{5,33},{6,34},{7,35},{8,64},{9,65},... | collective-permute-start | bytes 393224 | tf_op jit(solution)/shard_map/ppermute | solution.py:467
  134.1 27.0 %collective-permute-done.14 = bf16[256,256]{1,0:T(8,128)(2,1)S(1)} collective-permute-done((bf16[256,256]{1,0:T(8,128)(2,1)S(1)}, bf16[256,256]{1,0:T(8,128)(2,1)S(1)}, u32[]{:S(2)}, u32[]{:S(2)}) %collective-permute-start.14) | collective-permute-done | bytes 131104 | tf_op jit(solution)/shard_map/ppermute | solution.py:467
  162.5 3.1 %collective-permute-start.15 = (bf16[256,256]{1,0:T(8,128)(2,1)S(1)}, bf16[256,256]{1,0:T(8,128)(2,1)S(1)}, u32[]{:S(2)}, u32[]{:S(2)}) collective-permute-start(bf16[256,256]{1,0:T(8,128)(2,1)S(1)} %get-tuple-element.56), channel_id=1, source_target_pairs={{0,0},{1,1},{2,2},{3,3},{4,32},{5,33},{6,34},{7,35},{8,64},{9,65},... | collective-permute-start | bytes 393224 | tf_op jit(solution)/shard_map/ppermute | solution.py:469
  167.1 9.1 %collective-permute-done.15 = bf16[256,256]{1,0:T(8,128)(2,1)S(1)} collective-permute-done((bf16[256,256]{1,0:T(8,128)(2,1)S(1)}, bf16[256,256]{1,0:T(8,128)(2,1)S(1)}, u32[]{:S(2)}, u32[]{:S(2)}) %collective-permute-start.15) | collective-permute-done | bytes 131104 | tf_op jit(solution)/shard_map/ppermute | solution.py:469
  (33 shorter events, 20.4 us)
Async XLA Ops:
  0.6 17.6 %collective-permute-start = (bf16[256,256]{1,0:T(8,128)(2,1)}, bf16[256,256]{1,0:T(8,128)(2,1)S(1)}, u32[]{:S(2)}, u32[]{:S(2)}) collective-permute-start(bf16[256,256]{1,0:T(8,128)(2,1)} %param.6), channel_id=1, source_target_pairs={{0,0},{1,1},{2,2},{3,3},{4,32},{5,33},{6,34},{7,35},{8,64},{9,65},... | collective-permute-start | bytes 393224 | tf_op jit(solution)/shard_map/ppermute | solution.py:443
  10.3 7.9 %collective-permute-start.1 = (bf16[512,128]{1,0:T(8,128)(2,1)S(1)}, bf16[512,128]{1,0:T(8,128)(2,1)S(1)}, u32[]{:S(2)}, u32[]{:S(2)}) collective-permute-start(bf16[512,128]{1,0:T(8,128)(2,1)S(1)} %get-tuple-element.31), channel_id=1, source_target_pairs={{0,1},{1,2},{2,3},{3,0},{4,5},{5,6},{6,7},{7,4},{8,9},{9,10},{10,1... | collective-permute-start | bytes 393224 | tf_op jit(solution)/shard_map/ppermute | solution.py:445
  11.7 6.6 %collective-permute-start.2 = (bf16[512,128]{1,0:T(8,128)(2,1)S(1)}, bf16[512,128]{1,0:T(8,128)(2,1)S(1)}, u32[]{:S(2)}, u32[]{:S(2)}) collective-permute-start(bf16[512,128]{1,0:T(8,128)(2,1)S(1)} %get-tuple-element.32), channel_id=1, source_target_pairs={{0,3},{1,0},{2,1},{3,2},{4,7},{5,4},{6,5},{7,6},{8,11},{9,8},{10,9... | collective-permute-start | bytes 393224 | tf_op jit(solution)/shard_map/ppermute | solution.py:445
  19.3 30.5 %all-to-all-start = ((bf16[8,256,256]{2,1,0:T(8,128)(2,1)}), bf16[8,256,256]{2,1,0:T(8,128)(2,1)S(1)}, u32[]{:S(2)}, u32[]{:S(2)}) async-start(bf16[8,256,256]{2,1,0:T(8,128)(2,1)} %broadcast_in_dim.9), calls=%async_computation | async-start | bytes 2097152 | tf_op jit(solution)/shard_map/all_to_all | solution.py:46
  22.9 5.4 %collective-permute-start.3 = (bf16[512,128]{1,0:T(8,128)(2,1)S(1)}, bf16[512,128]{1,0:T(8,128)(2,1)S(1)}, u32[]{:S(2)}, u32[]{:S(2)}) collective-permute-start(bf16[512,128]{1,0:T(8,128)(2,1)S(1)} %get-tuple-element.36), channel_id=1, source_target_pairs={{0,2},{1,3},{2,0},{3,1},{4,6},{5,7},{6,4},{7,5},{8,10},{9,11},{10,... | collective-permute-start | bytes 393224 | tf_op jit(solution)/shard_map/ppermute | solution.py:445
  28.9 8.6 %collective-permute-start.6 = (bf16[4,256,128]{2,1,0:T(8,128)(2,1)S(1)}, bf16[4,256,128]{2,1,0:T(8,128)(2,1)S(1)}, u32[]{:S(2)}, u32[]{:S(2)}) collective-permute-start(bf16[4,256,128]{2,1,0:T(8,128)(2,1)S(1)} %get-tuple-element.38.refs_0_), channel_id=1, source_target_pairs={{0,192},{64,0},{128,64},{192,128},{1,193},{65,1},{129,65},{193,129... | collective-permute-start | bytes 786440 | tf_op jit(solution)/shard_map/ppermute | solution.py:451
  30.4 13.5 %collective-permute-start.5 = (bf16[4,256,128]{2,1,0:T(8,128)(2,1)S(1)}, bf16[4,256,128]{2,1,0:T(8,128)(2,1)S(1)}, u32[]{:S(2)}, u32[]{:S(2)}) collective-permute-start(bf16[4,256,128]{2,1,0:T(8,128)(2,1)S(1)} %get-tuple-element.38.refs_0_), channel_id=1, source_target_pairs={{0,128},{64,192},{128,0},{192,64},{1,129},{65,193},{129,1},{193,65... | collective-permute-start | bytes 786440 | tf_op jit(solution)/shard_map/ppermute | solution.py:451
  34.0 12.8 %collective-permute-start.4 = (bf16[4,256,128]{2,1,0:T(8,128)(2,1)S(1)}, bf16[4,256,128]{2,1,0:T(8,128)(2,1)S(1)}, u32[]{:S(2)}, u32[]{:S(2)}) collective-permute-start(bf16[4,256,128]{2,1,0:T(8,128)(2,1)S(1)} %get-tuple-element.38.refs_0_), channel_id=1, source_target_pairs={{0,64},{64,128},{128,192},{192,0},{1,65},{65,129},{129,193},{193,1... | collective-permute-start | bytes 786440 | tf_op jit(solution)/shard_map/ppermute | solution.py:451
  35.9 10.8 %collective-permute-start.7 = (bf16[4,256,128]{2,1,0:T(8,128)(2,1)S(1)}, bf16[4,256,128]{2,1,0:T(8,128)(2,1)S(1)}, u32[]{:S(2)}, u32[]{:S(2)}) collective-permute-start(bf16[4,256,128]{2,1,0:T(8,128)(2,1)S(1)} %get-tuple-element.38.refs_0_), channel_id=1, source_target_pairs={{0,32},{32,0},{1,33},{33,1},{2,34},{34,2},{3,35},{35,3},{4,36},{36... | collective-permute-start | bytes 786440 | tf_op jit(solution)/shard_map/ppermute | solution.py:452
  37.5 9.2 %collective-permute-start.10 = (bf16[4,256,128]{2,1,0:T(8,128)(2,1)S(1)}, bf16[4,256,128]{2,1,0:T(8,128)(2,1)S(1)}, u32[]{:S(2)}, u32[]{:S(2)}) collective-permute-start(bf16[4,256,128]{2,1,0:T(8,128)(2,1)S(1)} %collective-permute-done.6.refs_3_), channel_id=1, source_target_pairs={{0,32},{32,0},{1,33},{33,1},{2,34},{34,2},{3,35},{35,3},{4,36},{36... | collective-permute-start | bytes 786440 | tf_op jit(solution)/shard_map/ppermute | solution.py:452
  43.9 4.0 %collective-permute-start.9 = (bf16[4,256,128]{2,1,0:T(8,128)(2,1)S(1)}, bf16[4,256,128]{2,1,0:T(8,128)(2,1)S(1)}, u32[]{:S(2)}, u32[]{:S(2)}) collective-permute-start(bf16[4,256,128]{2,1,0:T(8,128)(2,1)S(1)} %collective-permute-done.5.refs_2_), channel_id=1, source_target_pairs={{0,32},{32,0},{1,33},{33,1},{2,34},{34,2},{3,35},{35,3},{4,36},{36... | collective-permute-start | bytes 786440 | tf_op jit(solution)/shard_map/ppermute | solution.py:452
  46.7 1.5 collective-permute-start.8
  85.5 34.5 %all-to-all-start.2 = ((bf16[8,256,256]{2,1,0:T(8,128)(2,1)}), bf16[8,256,256]{2,1,0:T(8,128)(2,1)S(1)}, u32[]{:S(2)}, u32[]{:S(2)}) async-start(bf16[8,256,256]{2,1,0:T(8,128)(2,1)} %first_partial.1), calls=%async_computation.2 | async-start | bytes 2097152 | tf_op jit(solution)/shard_map/all_to_all | solution.py:458
  92.6 20.7 %copy-start = (bf16[8,4,256,128]{3,2,1,0:T(8,128)(2,1)S(1)}, bf16[8,4,256,128]{3,2,1,0:T(8,128)(2,1)}, u32[]{:S(2)}) copy-start(bf16[8,4,256,128]{3,2,1,0:T(8,128)(2,1)} %get-tuple-element.46.acts_ref.acts_hbm) | copy-start | bytes 6291460
  106.9 5.0 %collective-permute-start.11 = (bf16[144,256]{1,0:T(8,128)(2,1)}, bf16[144,256]{1,0:T(8,128)(2,1)S(1)}, u32[]{:S(2)}, u32[]{:S(2)}) collective-permute-start(bf16[144,256]{1,0:T(8,128)(2,1)} %get-tuple-element.43), channel_id=1, source_target_pairs={{0,1},{1,2},{2,3},{3,0},{4,5},{5,6},{6,7},{7,4},{8,9},{9,10},{10,1... | collective-permute-start | bytes 221192 | tf_op jit(solution)/shard_map/ppermute | solution.py:462
  107.9 5.2 %collective-permute-start.12 = (bf16[144,256]{1,0:T(8,128)(2,1)}, bf16[144,256]{1,0:T(8,128)(2,1)S(1)}, u32[]{:S(2)}, u32[]{:S(2)}) collective-permute-start(bf16[144,256]{1,0:T(8,128)(2,1)} %get-tuple-element.44), channel_id=1, source_target_pairs={{0,2},{1,3},{2,0},{3,1},{4,6},{5,7},{6,4},{7,5},{8,10},{9,11},{10,... | collective-permute-start | bytes 221192 | tf_op jit(solution)/shard_map/ppermute | solution.py:462
  109.6 3.7 %collective-permute-start.13 = (bf16[144,256]{1,0:T(8,128)(2,1)}, bf16[144,256]{1,0:T(8,128)(2,1)S(1)}, u32[]{:S(2)}, u32[]{:S(2)}) collective-permute-start(bf16[144,256]{1,0:T(8,128)(2,1)} %get-tuple-element.45), channel_id=1, source_target_pairs={{0,3},{1,0},{2,1},{3,2},{4,7},{5,4},{6,5},{7,6},{8,11},{9,8},{10,9... | collective-permute-start | bytes 221192 | tf_op jit(solution)/shard_map/ppermute | solution.py:462
  116.3 49.3 %copy-start.1 = (f32[128,1024]{1,0:T(8,128)S(1)}, f32[128,1024]{1,0:T(8,128)}, u32[]{:S(2)}) copy-start(f32[128,1024]{1,0:T(8,128)} %get-tuple-element.52) | copy-start | bytes 1572868
  120.0 41.1 %all-to-all-start.3 = ((bf16[8,272,256]{2,1,0:T(8,128)(2,1)}), bf16[8,272,256]{2,1,0:T(8,128)(2,1)S(1)}, u32[]{:S(2)}, u32[]{:S(2)}) async-start(bf16[8,272,256]{2,1,0:T(8,128)(2,1)} %second_partial.1), calls=%async_computation.3 | async-start | bytes 2228224 | tf_op jit(solution)/shard_map/all_to_all | solution.py:465
  124.3 36.8 %collective-permute-start.14 = (bf16[256,256]{1,0:T(8,128)(2,1)S(1)}, bf16[256,256]{1,0:T(8,128)(2,1)S(1)}, u32[]{:S(2)}, u32[]{:S(2)}) collective-permute-start(bf16[256,256]{1,0:T(8,128)(2,1)S(1)} %get-tuple-element.49), channel_id=1, source_target_pairs={{0,0},{1,1},{2,2},{3,3},{4,32},{5,33},{6,34},{7,35},{8,64},{9,65},... | collective-permute-start | bytes 393224 | tf_op jit(solution)/shard_map/ppermute | solution.py:467
  162.5 13.7 %collective-permute-start.15 = (bf16[256,256]{1,0:T(8,128)(2,1)S(1)}, bf16[256,256]{1,0:T(8,128)(2,1)S(1)}, u32[]{:S(2)}, u32[]{:S(2)}) collective-permute-start(bf16[256,256]{1,0:T(8,128)(2,1)S(1)} %get-tuple-element.56), channel_id=1, source_target_pairs={{0,0},{1,1},{2,2},{3,3},{4,32},{5,33},{6,34},{7,35},{8,64},{9,65},... | collective-permute-start | bytes 393224 | tf_op jit(solution)/shard_map/ppermute | solution.py:469

commit v9 on v8

--- a/solution.py
+++ b/solution.py
@@ -34,6 +34,12 @@
     for y in range(4)
 ]
 SWAP = [(device(*d), device(d[2], d[3], d[0], d[1], d[4])) for d in EVERY]
+HOME = [
+    (b * 32 + z * 4 + y, (z - b) % 8 * 32 + b * 4 + y)
+    for b in range(8)
+    for z in range(8)
+    for y in range(4)
+]
 FLIP = [(0, 1), (1, 0)]
 
 
@@ -171,38 +177,34 @@
     )(place, cot_all, *own, *swapped)
 
 
-def first_body(place, weight_ref, acts_hbm, out_ref, acts_ref, work, sems):
-    loads = [
-        pltpu.make_async_copy(acts_hbm.at[group], acts_ref.at[group], sems.at[8 + group])
-        for group in range(8)
-    ]
-    for load in loads:
-        load.start()
+def first_body(place, weight_ref, *refs):
+    own, swapped = refs[:4], refs[4:8]
+    out_ref, work, sems = refs[8:]
+    x, c = place[0], place[1]
     weight_t = weight_of(weight_ref).T
     sends = []
-    for group in range(8):
-        loads[group].wait()
-        work[group] = dot_minor(weight_t, wide(acts_ref.at[group])).astype(BF16)
-        sends.append(pltpu.make_async_copy(work.at[group], out_ref.at[group], sems.at[group]))
-        sends[-1].start()
+    for d in range(4):
+        at = ((x - d) & 3) * 2
+        for i, (slab, group) in enumerate(((own[d], at + c), (swapped[d], at + 1 - c))):
+            n = d * 2 + i
+            work[n] = dot_minor(weight_t, wide(slab)).astype(BF16)
+            to = (group + 2 * x + c) & 7
+            sends.append(pltpu.make_async_copy(work.at[n], out_ref.at[to], sems.at[n]))
+            sends[-1].start()
     for send in sends:
         send.wait()
 
 
-def first_partial(place, near_w, acts):
+def first_partial(place, near_w, own, swapped):
     return call(
         first_body,
-        [VMEM, HBM],
+        [VMEM] * 9,
         HBM,
         pltpu.HBM((8, 256, 256), BF16),
-        scratch=[
-            pltpu.VMEM((8, 4, 256, 128), BF16),
-            pltpu.VMEM((8, 256, 256), BF16),
-            pltpu.SemaphoreType.DMA((16,)),
-        ],
+        scratch=[pltpu.VMEM((8, 256, 256), BF16), pltpu.SemaphoreType.DMA((8,))],
         limit=12,
         name="first_partial",
-    )(place, near_w, in_hbm(acts))
+    )(place, near_w, *own, *swapped)
 
 
 def as_rows(value):
@@ -233,7 +235,8 @@
     for group in range(8):
         work[group, :256, :] = dot_minor(update_t, wide(acts_ref.at[group])).astype(BF16)
         work[group, 256:, :] = tail
-        sends.append(pltpu.make_async_copy(work.at[group], out_ref.at[group], sems.at[group]))
+        to = (group + 2 * place[0] + place[1]) & 7
+        sends.append(pltpu.make_async_copy(work.at[group], out_ref.at[to], sems.at[group]))
         sends[-1].start()
     for send in sends:
         send.wait()
@@ -256,21 +259,19 @@
     )(place, *update_parts, acts)
 
 
-def first_add_body(place, parts_ref, total_ref, out_ref):
+def first_add_body(place, parts_ref, total_ref):
     total = parts_ref[0].astype(F32)
     for i in range(1, 8):
         total = total + parts_ref[i].astype(F32)
     total_ref[...] = total
-    out_ref[...] = total.astype(BF16)
 
 
 def first_add(place, parts):
-    shape = (256, 256)
     return call(
         first_add_body,
         [VMEM],
-        [VMEM] * 2,
-        [SHAPE(shape, F32), SHAPE(shape, BF16)],
+        VMEM,
+        SHAPE((256, 256), F32),
         limit=8,
         name="first_add",
     )(place, parts)
@@ -278,6 +279,7 @@
 
 def second_add_body(place, total_ref, parts_ref, out_ref, spread_ref):
     total = total_ref[...]
+    out_ref[0] = total.astype(BF16)
     own = jnp.zeros((1, 1), F32)
     for h in range(4):
         squares = from_rows(parts_ref[2 * h, 256:, :]) + from_rows(parts_ref[2 * h + 1, 256:, :])
@@ -286,7 +288,7 @@
         rate = LEARN_RATE / spread
         change = parts_ref[2 * h, :256, :].astype(F32) + parts_ref[2 * h + 1, :256, :].astype(F32)
         total = total - rate * change
-    out_ref[...] = total.astype(BF16)
+    out_ref[1] = total.astype(BF16)
     spread_ref[...] = jnp.broadcast_to(own, (8, 128))
 
 
@@ -295,7 +297,7 @@
         second_add_body,
         [VMEM] * 2,
         [VMEM] * 2,
-        [SHAPE((256, 256), BF16), SHAPE((8, 128), F32)],
+        [SHAPE((2, 256, 256), BF16), SHAPE((8, 128), F32)],
         limit=8,
         name="second_add",
     )(place, total, parts)
@@ -343,7 +345,6 @@
     sent1,
     sent2,
     sent3,
-    pieces_buf,
     left_buf,
     right_buf,
     grad_ref,
@@ -358,19 +359,13 @@
 ):
     load_left = pltpu.make_async_copy(left_old_ref, left_buf, sems.at[0])
     load_right = pltpu.make_async_copy(right_old_ref, right_buf, sems.at[1])
-    loads = [
-        pltpu.make_async_copy(pieces_ref.at[s], pieces_buf.at[s], sems.at[9 + s]) for s in range(8)
-    ]
-    for load in loads:
-        load.start()
     load_left.start()
     load_right.start()
     first = pl.multiple_of((place[3] * 4 + place[4]) * 128, 128)
     own = pl.ds(first, 128)
     for zl in range(2):
         for y in range(4):
-            loads[zl * 4 + y].wait()
-            piece = pieces_buf[zl * 4 + y]
+            piece = pieces_ref[zl * 4 + y]
             grad_ref[pl.ds(y * 256, 256), pl.ds(zl * 512, 512)] = piece
             grad_t_ref[pl.ds(zl * 512, 512), pl.ds(y * 256, 256)] = piece.T
     load_left.wait()
@@ -422,18 +417,17 @@
     rows = pltpu.HBM((128, BLOCK), F32)
     return call(
         solver_body,
-        [HBM] * 3,
+        [VMEM, HBM, HBM],
         [HBM] * 7,
         [rows, rows, rows, *[pltpu.HBM((144, 256), BF16)] * 4],
         scratch=[
-            pltpu.VMEM((8, 256, 512), BF16),
             *[pltpu.VMEM(square, kind) for kind in (F32, F32, BF16, BF16, F32, BF16, BF16)],
             pltpu.VMEM((128, BLOCK), F32),
             pltpu.VMEM((128, BLOCK), F32),
             pltpu.VMEM((4, 144, 256), BF16),
-            pltpu.SemaphoreType.DMA((17,)),
+            pltpu.SemaphoreType.DMA((9,)),
         ],
-        limit=28,
+        limit=27,
         name="solve",
     )(place, pieces, left_old, right_old)
 
@@ -443,30 +437,28 @@
     cot_turned = lax.ppermute(cotangent, AXES, SWAP)
     packed = pack(place, activations, weight)
     crossed = [lax.ppermute(packed[d], "y", shift(d)) for d in range(1, 4)]
-    cot_turned, crossed[0], crossed[2] = lax.optimization_barrier(
-        (cot_turned, crossed[0], crossed[2])
-    )
+    cot_turned, *crossed = lax.optimization_barrier((cot_turned, *crossed))
     cot_all = copies_to(cot_turned, ZAX, 8)
     slab, near_w = unpack(place, [packed[0], *crossed])
     own = [slab] + [lax.ppermute(slab, "x", shift(d)) for d in range(1, 4)]
     swapped = [lax.ppermute(part, "c", FLIP) for part in own]
+    first = first_partial(place, near_w, own, swapped)
+    cot_all, first = lax.optimization_barrier((cot_all, first))
     copies, acts = grad_piece(place, cot_all, own, swapped)
 
     pieces = lax.all_to_all(copies, SOLVER, 0, 0, tiled=True)
-    pieces, near_w = lax.optimization_barrier((pieces, near_w))
-    first = first_partial(place, near_w, acts)
+    pieces, first = lax.optimization_barrier((pieces, first))
     first_parts = lax.all_to_all(first, ZAX, 0, 0, tiled=True)
     new_left, new_right, update, *sent = solve(
-        place, in_hbm(pieces), in_hbm(left_old[0, 0]), in_hbm(right_old[0, 0])
+        place, pieces, in_hbm(left_old[0, 0]), in_hbm(right_old[0, 0])
     )
     update_parts = [in_hbm(sent[0])] + [lax.ppermute(sent[d], "y", shift(d)) for d in range(1, 4)]
     second = second_partial(place, update_parts, acts)
     second, first_parts = lax.optimization_barrier((second, first_parts))
     arrived = lax.all_to_all(second, ZAX, 0, 0, tiled=True)
-    first_total, first_sum = first_add(place, first_parts)
-    first_out = lax.ppermute(first_sum, AXES, SWAP)
-    second_sum, spread = second_add(place, first_total, arrived)
-    second_out = lax.ppermute(second_sum, AXES, SWAP)
+    outs, spread = second_add(place, first_add(place, first_parts), arrived)
+    outs = lax.ppermute(outs, AXES, HOME)
+    first_out, second_out = outs[0], outs[1]
     direction = update / spread[0, 0]
     return (first_out, new_left[None, None], new_right[None, None], direction, second_out)
 

time: 181 us -> 175 us (0.967); the launches traced: 178 us -> 174 us
  starting transfers between devices: 60.5 us -> 38.7 us
  waiting for transfers between devices: 55.1 us -> 76.3 us
  Pallas kernels: 28.9 us -> 25.5 us
    all_to_all x1, waiting for transfers between devices: 0.01 us -> 28.2 us  [body(): arrived = lax.all_to_all(second, ZAX, 0, 0, tiled=True)]
    ppermute x2 -> x1, waiting for transfers between devices: 36.2 us -> 17.1 us  [body(): outs = lax.ppermute(outs, AXES, HOME)]
    ppermute x2 -> x1, starting transfers between devices: 12.8 us -> 1.92 us  [body(): outs = lax.ppermute(outs, AXES, HOME)]
    all_to_all x1, waiting for transfers between devices: 1.57 us -> 8.96 us  [copies_to(): return lax.all_to_all(copies, axis, split_axis=0, concat_axis=0, tiled=True)]
    ppermute x3, waiting for transfers between devices: 1.78 us -> 9.16 us  [body(): own = [slab] + [lax.ppermute(slab, 'x', shift(d)) for d in range(1, 4)]]
    ppermute x4, starting transfers between devices: 9.03 us -> 4.32 us  [body(): swapped = [lax.ppermute(part, 'c', FLIP) for part in own]]
    ppermute x3, starting transfers between devices: 7.06 us -> 2.75 us  [body(): own = [slab] + [lax.ppermute(slab, 'x', shift(d)) for d in range(1, 4)]]
    pallas_call x4, Pallas kernels: 20.6 us -> 17.2 us  [the longest x1 13.6 us: solve(): call(solver_body, [VMEM, HBM, HBM], [HBM] * 7, [rows, rows, rows, *[pltpu...]
  transfers between devices with their start and end apart: 19 -> 18, of which waited for: 12 -> 12; matrix products, arithmetic and copies ran while one was open for 1% -> 1% of each run, Pallas kernels for 11% -> 12%
where the time goes in v9:
time: 175 us; the launch traced here: 174 us
  waiting for transfers between devices  76.3 us (44%)
  starting transfers between devices  38.7 us (22%)
  blocking collectives  29.1 us (17%)
  Pallas kernels  25.5 us (15%)
  local copies, waits for them, and re-layouts  2.4 us (1%)
    all_to_all x1, blocking collectives, body(): pieces = lax.all_to_all(copies, SOLVER, 0, 0, tiled=True)  29.1 us
    all_to_all x1, waiting for transfers between devices, body(): arrived = lax.all_to_all(second, ZAX, 0, 0, tiled=True)  28.2 us
    ppermute x1, waiting for transfers between devices, body(): outs = lax.ppermute(outs, AXES, HOME)  17.1 us
    pallas_call x1, Pallas kernels, solve(): call(solver_body, [VMEM, HBM, HBM], [HBM] * 7, [rows, rows, rows, *[pltpu...  13.6 us
    ppermute x3, waiting for transfers between devices, body(): own = [slab] + [lax.ppermute(slab, 'x', shift(d)) for d in range(1, 4)]  9.16 us
    all_to_all x1, waiting for transfers between devices, copies_to(): return lax.all_to_all(copies, axis, split_axis=0, concat_axis=0, tiled=True)  8.96 us
    ppermute x1, starting transfers between devices, body(): cot_turned = lax.ppermute(cotangent, AXES, SWAP)  7.96 us
    all_to_all x1, starting transfers between devices, copies_to(): return lax.all_to_all(copies, axis, split_axis=0, concat_axis=0, tiled=True)  5.65 us
  transfers between devices with their start and end apart: 18, of which 12 were waited for; matrix products, arithmetic and copies ran while one was open for 1% of the time, Pallas kernels for 12%

profile of v9, /device:TPU:7, one launch (start us, length us, event | category | flops | bytes accessed | tf_op | source)
XLA Modules:
  0.0 174.2 jit_solution(5718491659305477508)
XLA Ops:
  0.6 8.0 %collective-permute-start = (bf16[256,256]{1,0:T(8,128)(2,1)}, bf16[256,256]{1,0:T(8,128)(2,1)S(1)}, u32[]{:S(2)}, u32[]{:S(2)}) collective-permute-start(bf16[256,256]{1,0:T(8,128)(2,1)} %param.6), channel_id=1, source_target_pairs={{0,0},{1,1},{2,2},{3,3},{4,32},{5,33},{6,34},{7,35},{8,64},{9,65},... | collective-permute-start | bytes 393224 | tf_op jit(solution)/shard_map/ppermute | solution.py:437
  8.7 1.6 pack.1
  11.7 2.6 %collective-permute-start.2 = (bf16[512,128]{1,0:T(8,128)(2,1)S(1)}, bf16[512,128]{1,0:T(8,128)(2,1)S(1)}, u32[]{:S(2)}, u32[]{:S(2)}) collective-permute-start(bf16[512,128]{1,0:T(8,128)(2,1)S(1)} %get-tuple-element.33), channel_id=1, source_target_pairs={{0,2},{1,3},{2,0},{3,1},{4,6},{5,7},{6,4},{7,5},{8,10},{9,11},{10,... | collective-permute-start | bytes 393224 | tf_op jit(solution)/shard_map/ppermute | solution.py:439
  15.4 2.9 %collective-permute-done = bf16[256,256]{1,0:T(8,128)(2,1)S(1)} collective-permute-done((bf16[256,256]{1,0:T(8,128)(2,1)}, bf16[256,256]{1,0:T(8,128)(2,1)S(1)}, u32[]{:S(2)}, u32[]{:S(2)}) %collective-permute-start) | collective-permute-done | bytes 131104 | tf_op jit(solution)/shard_map/ppermute | solution.py:437
  18.3 1.6 collective-permute-done.2.refs_2_
  20.9 5.6 %all-to-all-start = ((bf16[8,256,256]{2,1,0:T(8,128)(2,1)}), bf16[8,256,256]{2,1,0:T(8,128)(2,1)S(1)}, u32[]{:S(2)}, u32[]{:S(2)}) async-start(bf16[8,256,256]{2,1,0:T(8,128)(2,1)} %broadcast_in_dim.9), calls=%async_computation | async-start | bytes 2097152 | tf_op jit(solution)/shard_map/all_to_all | solution.py:52
  28.1 1.8 %collective-permute-start.4 = (bf16[4,256,128]{2,1,0:T(8,128)(2,1)S(1)}, bf16[4,256,128]{2,1,0:T(8,128)(2,1)S(1)}, u32[]{:S(2)}, u32[]{:S(2)}) collective-permute-start(bf16[4,256,128]{2,1,0:T(8,128)(2,1)S(1)} %get-tuple-element.41.refs_0_), channel_id=1, source_target_pairs={{0,64},{64,128},{128,192},{192,0},{1,65},{65,129},{129,193},{193,1... | collective-permute-start | bytes 786440 | tf_op jit(solution)/shard_map/ppermute | solution.py:443
  29.9 1.8 %collective-permute-start.7 = (bf16[4,256,128]{2,1,0:T(8,128)(2,1)S(1)}, bf16[4,256,128]{2,1,0:T(8,128)(2,1)S(1)}, u32[]{:S(2)}, u32[]{:S(2)}) collective-permute-start(bf16[4,256,128]{2,1,0:T(8,128)(2,1)S(1)} %get-tuple-element.41.refs_0_), channel_id=1, source_target_pairs={{0,32},{32,0},{1,33},{33,1},{2,34},{34,2},{3,35},{35,3},{4,36},{36... | collective-permute-start | bytes 786440 | tf_op jit(solution)/shard_map/ppermute | solution.py:444
  31.7 9.2 %collective-permute-done.6.refs_3_ = bf16[4,256,128]{2,1,0:T(8,128)(2,1)S(1)} collective-permute-done((bf16[4,256,128]{2,1,0:T(8,128)(2,1)S(1)}, bf16[4,256,128]{2,1,0:T(8,128)(2,1)S(1)}, u32[]{:S(2)}, u32[]{:S(2)}) %collective-permute-start.6) | collective-permute-done | bytes 262176 | tf_op jit(solution)/shard_map/ppermute | solution.py:443
  40.9 1.9 %collective-permute-start.10 = (bf16[4,256,128]{2,1,0:T(8,128)(2,1)S(1)}, bf16[4,256,128]{2,1,0:T(8,128)(2,1)S(1)}, u32[]{:S(2)}, u32[]{:S(2)}) collective-permute-start(bf16[4,256,128]{2,1,0:T(8,128)(2,1)S(1)} %collective-permute-done.6.refs_3_), channel_id=1, source_target_pairs={{0,32},{32,0},{1,33},{33,1},{2,34},{34,2},{3,35},{35,3},{4,36},{36... | collective-permute-start | bytes 786440 | tf_op jit(solution)/shard_map/ppermute | solution.py:444
  44.7 2.1 %first_partial.1 = bf16[8,256,256]{2,1,0:T(8,128)(2,1)} custom-call(s32[5]{0:T(128)S(1)} %stack.23.place, bf16[4,256,128]{2,1,0:T(8,128)(2,1)S(1)} %get-tuple-element.40.weight_ref, bf16[4,256,128]{2,1,0:T(8,128)(2,1)S(1)} %get-tuple-element.41.refs_0_, bf16[4,256,128]{2,1,0:T(8,128)(2,1)S(1)} %collective-permute-done.4.refs_1_, ...), custom_call_target="tpu_custom_call" | custom-call | tf_op jit(solution)/shard_map/first_partial/pallas_call | solution.py:199
  46.8 9.0 %all-to-all-done.cot_ref = bf16[8,256,256]{2,1,0:T(8,128)(2,1)S(1)} async-done(((bf16[8,256,256]{2,1,0:T(8,128)(2,1)}), bf16[8,256,256]{2,1,0:T(8,128)(2,1)S(1)}, u32[]{:S(2)}, u32[]{:S(2)}) %all-to-all-start) | async-done | bytes 1048608 | tf_op jit(solution)/shard_map/all_to_all | solution.py:52
  55.7 3.1 %grad_piece.1 = (bf16[8,256,512]{2,1,0:T(8,128)(2,1)}, bf16[8,4,256,128]{3,2,1,0:T(8,128)(2,1)}) custom-call(s32[5]{0:T(128)S(1)} %stack.23.place, bf16[8,256,256]{2,1,0:T(8,128)(2,1)S(1)} %all-to-all-done.cot_ref, bf16[4,256,128]{2,1,0:T(8,128)(2,1)S(1)} %get-tuple-element.41.refs_0_, bf16[4,256,128]{2,1,0:T(8,128)(2,1)S(1)} %collective-permute-done.4.refs_1_, ...), custom_call_target="tpu_custom_call" | custom-call | tf_op jit(solution)/shard_map/grad_piece/pallas_call | solution.py:169
  58.9 29.1 %all_to_all.20.pieces_ref = bf16[8,256,512]{2,1,0:T(8,128)(2,1)S(1)} all-to-all(bf16[8,256,512]{2,1,0:T(8,128)(2,1)} %get-tuple-element.43), channel_id=1, replica_groups=mesh['x'=4,'c'=2,'zh'=4,'zl'=2,'y'=4] {'zl','y'}, dimensions={0} | all-to-all | bytes 4194304 | tf_op jit(solution)/shard_map/all_to_all | solution.py:449
  87.9 3.7 %all-to-all-start.2 = ((bf16[8,256,256]{2,1,0:T(8,128)(2,1)}), bf16[8,256,256]{2,1,0:T(8,128)(2,1)S(1)}, u32[]{:S(2)}, u32[]{:S(2)}) async-start(bf16[8,256,256]{2,1,0:T(8,128)(2,1)} %first_partial.1), calls=%async_computation.2 | async-start | bytes 2097152 | tf_op jit(solution)/shard_map/all_to_all | solution.py:451
  91.7 13.6 %solve.1 = (f32[128,1024]{1,0:T(8,128)}, f32[128,1024]{1,0:T(8,128)}, f32[128,1024]{1,0:T(8,128)}, bf16[144,256]{1,0:T(8,128)(2,1)}, bf16[144,256]{1,0:T(8,128)(...) custom-call(s32[5]{0:T(128)S(1)} %stack.23.place, bf16[8,256,512]{2,1,0:T(8,128)(2,1)S(1)} %all_to_all.20.pieces_ref, ...), custom_call_target="tpu_custom_call" | custom-call | tf_op jit(solution)/shard_map/solve/pallas_call | solution.py:418
  105.5 2.4 %collective-permute-start.12 = (bf16[144,256]{1,0:T(8,128)(2,1)}, bf16[144,256]{1,0:T(8,128)(2,1)S(1)}, u32[]{:S(2)}, u32[]{:S(2)}) collective-permute-start(bf16[144,256]{1,0:T(8,128)(2,1)} %get-tuple-element.48), channel_id=1, source_target_pairs={{0,2},{1,3},{2,0},{3,1},{4,6},{5,7},{6,4},{7,5},{8,10},{9,11},{10,... | collective-permute-start | bytes 221192 | tf_op jit(solution)/shard_map/ppermute | solution.py:455
  109.0 2.1 %collective-permute-done.11.u1 = bf16[144,256]{1,0:T(8,128)(2,1)S(1)} collective-permute-done((bf16[144,256]{1,0:T(8,128)(2,1)}, bf16[144,256]{1,0:T(8,128)(2,1)S(1)}, u32[]{:S(2)}, u32[]{:S(2)}) %collective-permute-start.11) | collective-permute-done | bytes 73760 | tf_op jit(solution)/shard_map/ppermute | solution.py:455
  111.7 3.0 %second_partial.1 = bf16[8,272,256]{2,1,0:T(8,128)(2,1)} custom-call(s32[5]{0:T(128)S(1)} %stack.23.place, bf16[144,256]{1,0:T(8,128)(2,1)} %get-tuple-element.46.own_hbm, bf16[144,256]{1,0:T(8,128)(2,1)S(1)} %collective-permute-done.11.u1, bf16[144,256]{1,0:T(8,128)(2,1)S(1)} %collective-permute-done.12.u2, ...), custom_call_target="tpu_custom_call" | custom-call | tf_op jit(solution)/shard_map/second_partial/pallas_call | solution.py:246
  114.7 4.5 %all-to-all-done.2.parts_ref = bf16[8,256,256]{2,1,0:T(8,128)(2,1)S(1)} async-done(((bf16[8,256,256]{2,1,0:T(8,128)(2,1)}), bf16[8,256,256]{2,1,0:T(8,128)(2,1)S(1)}, u32[]{:S(2)}, u32[]{:S(2)}) %all-to-all-start.2) | async-done | bytes 1048608 | tf_op jit(solution)/shard_map/all_to_all | solution.py:451
  119.2 3.6 %all-to-all-start.3 = ((bf16[8,272,256]{2,1,0:T(8,128)(2,1)}), bf16[8,272,256]{2,1,0:T(8,128)(2,1)S(1)}, u32[]{:S(2)}, u32[]{:S(2)}) async-start(bf16[8,272,256]{2,1,0:T(8,128)(2,1)} %second_partial.1), calls=%async_computation.3 | async-start | bytes 2228224 | tf_op jit(solution)/shard_map/all_to_all | solution.py:458
  123.4 28.2 %all-to-all-done.3.parts_ref = bf16[8,272,256]{2,1,0:T(8,128)(2,1)S(1)} async-done(((bf16[8,272,256]{2,1,0:T(8,128)(2,1)}), bf16[8,272,256]{2,1,0:T(8,128)(2,1)S(1)}, u32[]{:S(2)}, u32[]{:S(2)}) %all-to-all-start.3) | async-done | bytes 1114144 | tf_op jit(solution)/shard_map/all_to_all | solution.py:458
  152.5 1.9 %collective-permute-start.14 = (bf16[2,256,256]{2,1,0:T(8,128)(2,1)S(1)}, bf16[2,256,256]{2,1,0:T(8,128)(2,1)S(1)}, u32[]{:S(2)}, u32[]{:S(2)}) collective-permute-start(bf16[2,256,256]{2,1,0:T(8,128)(2,1)S(1)} %get-tuple-element.54), channel_id=1, source_target_pairs={{0,0},{1,1},{2,2},{3,3},{4,32},{5,33},{6,34},{7,35},{8,64},{9,65},... | collective-permute-start | bytes 786440 | tf_op jit(solution)/shard_map/ppermute | solution.py:460
  156.4 17.1 %collective-permute-done.14 = bf16[2,256,256]{2,1,0:T(8,128)(2,1)S(1)} collective-permute-done((bf16[2,256,256]{2,1,0:T(8,128)(2,1)S(1)}, bf16[2,256,256]{2,1,0:T(8,128)(2,1)S(1)}, u32[]{:S(2)}, u32[]{:S(2)}) %collective-permute-start.14) | collective-permute-done | bytes 262176 | tf_op jit(solution)/shard_map/ppermute | solution.py:460
  (30 shorter events, 13.1 us)
Async XLA Ops:
  0.6 17.6 %collective-permute-start = (bf16[256,256]{1,0:T(8,128)(2,1)}, bf16[256,256]{1,0:T(8,128)(2,1)S(1)}, u32[]{:S(2)}, u32[]{:S(2)}) collective-permute-start(bf16[256,256]{1,0:T(8,128)(2,1)} %param.6), channel_id=1, source_target_pairs={{0,0},{1,1},{2,2},{3,3},{4,32},{5,33},{6,34},{7,35},{8,64},{9,65},... | collective-permute-start | bytes 393224 | tf_op jit(solution)/shard_map/ppermute | solution.py:437
  10.3 7.9 %collective-permute-start.1 = (bf16[512,128]{1,0:T(8,128)(2,1)S(1)}, bf16[512,128]{1,0:T(8,128)(2,1)S(1)}, u32[]{:S(2)}, u32[]{:S(2)}) collective-permute-start(bf16[512,128]{1,0:T(8,128)(2,1)S(1)} %get-tuple-element.32), channel_id=1, source_target_pairs={{0,1},{1,2},{2,3},{3,0},{4,5},{5,6},{6,7},{7,4},{8,9},{9,10},{10,1... | collective-permute-start | bytes 393224 | tf_op jit(solution)/shard_map/ppermute | solution.py:439
  11.7 8.1 %collective-permute-start.2 = (bf16[512,128]{1,0:T(8,128)(2,1)S(1)}, bf16[512,128]{1,0:T(8,128)(2,1)S(1)}, u32[]{:S(2)}, u32[]{:S(2)}) collective-permute-start(bf16[512,128]{1,0:T(8,128)(2,1)S(1)} %get-tuple-element.33), channel_id=1, source_target_pairs={{0,2},{1,3},{2,0},{3,1},{4,6},{5,7},{6,4},{7,5},{8,10},{9,11},{10,... | collective-permute-start | bytes 393224 | tf_op jit(solution)/shard_map/ppermute | solution.py:439
  14.3 5.5 %collective-permute-start.3 = (bf16[512,128]{1,0:T(8,128)(2,1)S(1)}, bf16[512,128]{1,0:T(8,128)(2,1)S(1)}, u32[]{:S(2)}, u32[]{:S(2)}) collective-permute-start(bf16[512,128]{1,0:T(8,128)(2,1)S(1)} %get-tuple-element.34), channel_id=1, source_target_pairs={{0,3},{1,0},{2,1},{3,2},{4,7},{5,4},{6,5},{7,6},{8,11},{9,8},{10,9... | collective-permute-start | bytes 393224 | tf_op jit(solution)/shard_map/ppermute | solution.py:439
  20.9 34.8 %all-to-all-start = ((bf16[8,256,256]{2,1,0:T(8,128)(2,1)}), bf16[8,256,256]{2,1,0:T(8,128)(2,1)S(1)}, u32[]{:S(2)}, u32[]{:S(2)}) async-start(bf16[8,256,256]{2,1,0:T(8,128)(2,1)} %broadcast_in_dim.9), calls=%async_computation | async-start | bytes 2097152 | tf_op jit(solution)/shard_map/all_to_all | solution.py:52
  27.1 13.7 %collective-permute-start.6 = (bf16[4,256,128]{2,1,0:T(8,128)(2,1)S(1)}, bf16[4,256,128]{2,1,0:T(8,128)(2,1)S(1)}, u32[]{:S(2)}, u32[]{:S(2)}) collective-permute-start(bf16[4,256,128]{2,1,0:T(8,128)(2,1)S(1)} %get-tuple-element.41.refs_0_), channel_id=1, source_target_pairs={{0,192},{64,0},{128,64},{192,128},{1,193},{65,1},{129,65},{193,129... | collective-permute-start | bytes 786440 | tf_op jit(solution)/shard_map/ppermute | solution.py:443
  27.2 15.5 %collective-permute-start.5 = (bf16[4,256,128]{2,1,0:T(8,128)(2,1)S(1)}, bf16[4,256,128]{2,1,0:T(8,128)(2,1)S(1)}, u32[]{:S(2)}, u32[]{:S(2)}) collective-permute-start(bf16[4,256,128]{2,1,0:T(8,128)(2,1)S(1)} %get-tuple-element.41.refs_0_), channel_id=1, source_target_pairs={{0,128},{64,192},{128,0},{192,64},{1,129},{65,193},{129,1},{193,65... | collective-permute-start | bytes 786440 | tf_op jit(solution)/shard_map/ppermute | solution.py:443
  28.1 14.7 %collective-permute-start.4 = (bf16[4,256,128]{2,1,0:T(8,128)(2,1)S(1)}, bf16[4,256,128]{2,1,0:T(8,128)(2,1)S(1)}, u32[]{:S(2)}, u32[]{:S(2)}) collective-permute-start(bf16[4,256,128]{2,1,0:T(8,128)(2,1)S(1)} %get-tuple-element.41.refs_0_), channel_id=1, source_target_pairs={{0,64},{64,128},{128,192},{192,0},{1,65},{65,129},{129,193},{193,1... | collective-permute-start | bytes 786440 | tf_op jit(solution)/shard_map/ppermute | solution.py:443
  29.9 13.5 %collective-permute-start.7 = (bf16[4,256,128]{2,1,0:T(8,128)(2,1)S(1)}, bf16[4,256,128]{2,1,0:T(8,128)(2,1)S(1)}, u32[]{:S(2)}, u32[]{:S(2)}) collective-permute-start(bf16[4,256,128]{2,1,0:T(8,128)(2,1)S(1)} %get-tuple-element.41.refs_0_), channel_id=1, source_target_pairs={{0,32},{32,0},{1,33},{33,1},{2,34},{34,2},{3,35},{35,3},{4,36},{36... | collective-permute-start | bytes 786440 | tf_op jit(solution)/shard_map/ppermute | solution.py:444
  40.9 3.1 %collective-permute-start.10 = (bf16[4,256,128]{2,1,0:T(8,128)(2,1)S(1)}, bf16[4,256,128]{2,1,0:T(8,128)(2,1)S(1)}, u32[]{:S(2)}, u32[]{:S(2)}) collective-permute-start(bf16[4,256,128]{2,1,0:T(8,128)(2,1)S(1)} %collective-permute-done.6.refs_3_), channel_id=1, source_target_pairs={{0,32},{32,0},{1,33},{33,1},{2,34},{34,2},{3,35},{35,3},{4,36},{36... | collective-permute-start | bytes 786440 | tf_op jit(solution)/shard_map/ppermute | solution.py:444
  42.8 1.5 collective-permute-start.9
  42.8 1.9 %collective-permute-start.8 = (bf16[4,256,128]{2,1,0:T(8,128)(2,1)S(1)}, bf16[4,256,128]{2,1,0:T(8,128)(2,1)S(1)}, u32[]{:S(2)}, u32[]{:S(2)}) collective-permute-start(bf16[4,256,128]{2,1,0:T(8,128)(2,1)S(1)} %collective-permute-done.4.refs_1_), channel_id=1, source_target_pairs={{0,32},{32,0},{1,33},{33,1},{2,34},{34,2},{3,35},{35,3},{4,36},{36... | collective-permute-start | bytes 786440 | tf_op jit(solution)/shard_map/ppermute | solution.py:444
  87.9 31.3 %all-to-all-start.2 = ((bf16[8,256,256]{2,1,0:T(8,128)(2,1)}), bf16[8,256,256]{2,1,0:T(8,128)(2,1)S(1)}, u32[]{:S(2)}, u32[]{:S(2)}) async-start(bf16[8,256,256]{2,1,0:T(8,128)(2,1)} %first_partial.1), calls=%async_computation.2 | async-start | bytes 2097152 | tf_op jit(solution)/shard_map/all_to_all | solution.py:451
  91.7 20.0 %copy-start = (bf16[8,4,256,128]{3,2,1,0:T(8,128)(2,1)S(1)}, bf16[8,4,256,128]{3,2,1,0:T(8,128)(2,1)}, u32[]{:S(2)}) copy-start(bf16[8,4,256,128]{3,2,1,0:T(8,128)(2,1)} %get-tuple-element.50.acts_ref) | copy-start | bytes 6291460
  105.3 5.8 %collective-permute-start.11 = (bf16[144,256]{1,0:T(8,128)(2,1)}, bf16[144,256]{1,0:T(8,128)(2,1)S(1)}, u32[]{:S(2)}, u32[]{:S(2)}) collective-permute-start(bf16[144,256]{1,0:T(8,128)(2,1)} %get-tuple-element.47), channel_id=1, source_target_pairs={{0,1},{1,2},{2,3},{3,0},{4,5},{5,6},{6,7},{7,4},{8,9},{9,10},{10,1... | collective-permute-start | bytes 221192 | tf_op jit(solution)/shard_map/ppermute | solution.py:455
  105.5 5.7 %collective-permute-start.12 = (bf16[144,256]{1,0:T(8,128)(2,1)}, bf16[144,256]{1,0:T(8,128)(2,1)S(1)}, u32[]{:S(2)}, u32[]{:S(2)}) collective-permute-start(bf16[144,256]{1,0:T(8,128)(2,1)} %get-tuple-element.48), channel_id=1, source_target_pairs={{0,2},{1,3},{2,0},{3,1},{4,6},{5,7},{6,4},{7,5},{8,10},{9,11},{10,... | collective-permute-start | bytes 221192 | tf_op jit(solution)/shard_map/ppermute | solution.py:455
  107.9 3.8 %collective-permute-start.13 = (bf16[144,256]{1,0:T(8,128)(2,1)}, bf16[144,256]{1,0:T(8,128)(2,1)S(1)}, u32[]{:S(2)}, u32[]{:S(2)}) collective-permute-start(bf16[144,256]{1,0:T(8,128)(2,1)} %get-tuple-element.49), channel_id=1, source_target_pairs={{0,3},{1,0},{2,1},{3,2},{4,7},{5,4},{6,5},{7,6},{8,11},{9,8},{10,9... | collective-permute-start | bytes 221192 | tf_op jit(solution)/shard_map/ppermute | solution.py:455
  114.7 40.2 %copy-start.1 = (f32[128,1024]{1,0:T(8,128)S(1)}, f32[128,1024]{1,0:T(8,128)}, u32[]{:S(2)}) copy-start(f32[128,1024]{1,0:T(8,128)} %get-tuple-element.57) | copy-start | bytes 1572868
  119.2 32.4 %all-to-all-start.3 = ((bf16[8,272,256]{2,1,0:T(8,128)(2,1)}), bf16[8,272,256]{2,1,0:T(8,128)(2,1)S(1)}, u32[]{:S(2)}, u32[]{:S(2)}) async-start(bf16[8,272,256]{2,1,0:T(8,128)(2,1)} %second_partial.1), calls=%async_computation.3 | async-start | bytes 2228224 | tf_op jit(solution)/shard_map/all_to_all | solution.py:458
  152.5 21.0 %collective-permute-start.14 = (bf16[2,256,256]{2,1,0:T(8,128)(2,1)S(1)}, bf16[2,256,256]{2,1,0:T(8,128)(2,1)S(1)}, u32[]{:S(2)}, u32[]{:S(2)}) collective-permute-start(bf16[2,256,256]{2,1,0:T(8,128)(2,1)S(1)} %get-tuple-element.54), channel_id=1, source_target_pairs={{0,0},{1,1},{2,2},{3,3},{4,32},{5,33},{6,34},{7,35},{8,64},{9,65},... | collective-permute-start | bytes 786440 | tf_op jit(solution)/shard_map/ppermute | solution.py:460

commit v10 on v7

--- a/solution.py
+++ b/solution.py
@@ -137,7 +137,7 @@
 
 def grad_body(place, cot_ref, *refs):
     own, swapped = refs[:4], refs[4:8]
-    copies_ref, acts_ref, piece_ref, sems = refs[8:]
+    piece_ref, kept_ref, acts_ref, sems = refs[8:]
     x, c = place[0], place[1]
     sends = []
     for d in range(4):
@@ -152,9 +152,8 @@
         total = total + dot(cot_ref[at + c], wide(own[d]))
         total = total + dot(cot_ref[at + 1 - c], wide(swapped[d]))
     piece_ref[...] = total.astype(BF16)
-    for s in range(8):
-        sends.append(pltpu.make_async_copy(piece_ref, copies_ref.at[s], sems.at[8 + s]))
-        sends[-1].start()
+    sends.append(pltpu.make_async_copy(piece_ref, kept_ref, sems.at[8]))
+    sends[-1].start()
     for send in sends:
         send.wait()
 
@@ -163,35 +162,45 @@
     return call(
         grad_body,
         [VMEM] * 9,
-        [HBM, HBM],
-        [pltpu.HBM((8, 256, 512), BF16), pltpu.HBM((8, 4, 256, 128), BF16)],
-        scratch=[pltpu.VMEM((256, 512), BF16), pltpu.SemaphoreType.DMA((16,))],
+        [VMEM, HBM, HBM],
+        [
+            SHAPE((256, 512), BF16),
+            pltpu.HBM((256, 512), BF16),
+            pltpu.HBM((8, 4, 256, 128), BF16),
+        ],
+        scratch=[pltpu.SemaphoreType.DMA((9,))],
         limit=10,
         name="grad_piece",
     )(place, cot_all, *own, *swapped)
 
 
-def first_body(place, weight_ref, acts_ref, out_ref, work, sems):
+def first_body(place, weight_ref, *refs):
+    own, swapped = refs[:4], refs[4:8]
+    out_ref, work, sems = refs[8:]
+    x, c = place[0], place[1]
     weight_t = weight_of(weight_ref).T
     sends = []
-    for group in range(8):
-        work[group] = dot_minor(weight_t, wide(acts_ref.at[group])).astype(BF16)
-        sends.append(pltpu.make_async_copy(work.at[group], out_ref.at[group], sems.at[group]))
-        sends[-1].start()
+    for d in range(4):
+        at = ((x - d) & 3) * 2
+        for i, (slab, group) in enumerate(((own[d], at + c), (swapped[d], at + 1 - c))):
+            n = d * 2 + i
+            work[n] = dot_minor(weight_t, wide(slab)).astype(BF16)
+            sends.append(pltpu.make_async_copy(work.at[n], out_ref.at[group], sems.at[n]))
+            sends[-1].start()
     for send in sends:
         send.wait()
 
 
-def first_partial(place, near_w, acts):
+def first_partial(place, near_w, own, swapped):
     return call(
         first_body,
-        [VMEM] * 2,
+        [VMEM] * 9,
         HBM,
         pltpu.HBM((8, 256, 256), BF16),
         scratch=[pltpu.VMEM((8, 256, 256), BF16), pltpu.SemaphoreType.DMA((8,))],
         limit=12,
         name="first_partial",
-    )(place, near_w, acts)
+    )(place, near_w, *own, *swapped)
 
 
 def as_rows(value):
@@ -207,38 +216,80 @@
     return jnp.sum(rows.astype(F32), axis=0, keepdims=True)[:, :1]
 
 
-def second_body(place, u0, u1, u2, u3, acts_ref, out_ref, squares_ref, update_ref, work, sems):
+def order_body(place, *refs):
+    for d in range(4):
+        refs[4][(place[4] - d) & 3] = refs[d][...]
+
+
+def in_order(place, parts):
+    shape = SHAPE((4, 144, 256), BF16)
+    return call(order_body, [VMEM] * 4, VMEM, shape, limit=8, name="in_order")(place, *parts)
+
+
+def second_body(
+    place,
+    near_u,
+    far_u,
+    acts_hbm,
+    far_hbm,
+    swap_hbm,
+    out_ref,
+    spread_ref,
+    near_ref,
+    far_ref,
+    swap_ref,
+    work,
+    sems,
+):
+    c, zl = place[1], place[3]
+    loads = [
+        pltpu.make_async_copy(acts_hbm.at[2 * i + zl], near_ref.at[i], sems.at[i])
+        for i in range(4)
+    ]
+    loads.append(pltpu.make_async_copy(far_hbm, far_ref, sems.at[4]))
+    loads.append(pltpu.make_async_copy(swap_hbm, swap_ref, sems.at[5]))
+    for load in loads:
+        load.start()
     squares = jnp.zeros((1, 1), F32)
-    for d, piece in enumerate((u0, u1, u2, u3)):
-        update_ref[(place[4] - d) & 3] = piece[:128, :]
-        squares = squares + from_rows(piece[128:, :])
-    squares_ref[...] = jnp.broadcast_to(squares, (8, 128))
-    tail = as_rows(squares)
-    update_t = update_ref[...].reshape(512, 256).T
+    for q in range(4):
+        squares = squares + from_rows(near_u[q, 128:, :]) + from_rows(far_u[q, 128:, :])
+    spread = jnp.sqrt(squares / (BLOCK * BLOCK) + EPSILON)
+    spread_ref[...] = jnp.broadcast_to(spread, (8, 128))
+    rate = LEARN_RATE / spread
+    near_t = jnp.concatenate([near_u[q, :128, :] for q in range(4)], axis=0).T
+    far_t = jnp.concatenate([far_u[q, :128, :] for q in range(4)], axis=0).T
+    for load in loads:
+        load.wait()
     sends = []
-    for group in range(8):
-        work[group, :256, :] = dot_minor(update_t, wide(acts_ref.at[group])).astype(BF16)
-        work[group, 256:, :] = tail
-        sends.append(pltpu.make_async_copy(work.at[group], out_ref.at[group], sems.at[group]))
-        sends[-1].start()
+    for i in range(2):
+        for j in range(2):
+            at = (c * 2 if i == 0 else 2 - c * 2) + j
+            total = dot_minor(near_t, wide(near_ref.at[at]))
+            total = total + dot_minor(far_t, wide((far_ref, swap_ref)[i].at[j]))
+            n = i * 2 + j
+            work[n] = (rate * total).astype(BF16)
+            sends.append(pltpu.make_async_copy(work.at[n], out_ref.at[at], sems.at[6 + n]))
+            sends[-1].start()
     for send in sends:
         send.wait()
 
 
-def second_partial(place, update_parts, acts):
+def second_partial(place, near_u, far_u, acts, far, far_swapped):
     return call(
         second_body,
-        [VMEM] * 5,
+        [VMEM, VMEM, HBM, HBM, HBM],
         [HBM, VMEM],
-        [pltpu.HBM((8, 272, 256), BF16), SHAPE((8, 128), F32)],
+        [pltpu.HBM((4, 256, 256), BF16), SHAPE((8, 128), F32)],
         scratch=[
-            pltpu.VMEM((4, 128, 256), BF16),
-            pltpu.VMEM((8, 272, 256), BF16),
-            pltpu.SemaphoreType.DMA((8,)),
+            pltpu.VMEM((4, 4, 256, 128), BF16),
+            pltpu.VMEM((2, 4, 256, 128), BF16),
+            pltpu.VMEM((2, 4, 256, 128), BF16),
+            pltpu.VMEM((4, 256, 256), BF16),
+            pltpu.SemaphoreType.DMA((10,)),
         ],
-        limit=12,
+        limit=14,
         name="second_partial",
-    )(place, *update_parts, acts)
+    )(place, near_u, far_u, in_hbm(acts), in_hbm(far), in_hbm(far_swapped))
 
 
 def first_add_body(place, parts_ref, total_ref, out_ref):
@@ -262,13 +313,10 @@
 
 
 def second_add_body(place, total_ref, parts_ref, out_ref):
-    total = total_ref[...]
-    for h in range(4):
-        squares = from_rows(parts_ref[2 * h, 256:, :]) + from_rows(parts_ref[2 * h + 1, 256:, :])
-        rate = LEARN_RATE / jnp.sqrt(squares / (BLOCK * BLOCK) + EPSILON)
-        change = parts_ref[2 * h, :256, :].astype(F32) + parts_ref[2 * h + 1, :256, :].astype(F32)
-        total = total - rate * change
-    out_ref[...] = total.astype(BF16)
+    change = parts_ref[0].astype(F32)
+    for i in range(1, 4):
+        change = change + parts_ref[i].astype(F32)
+    out_ref[...] = (total_ref[...] - change).astype(BF16)
 
 
 def second_add(place, total, parts):
@@ -314,7 +362,14 @@
 
 def solver_body(
     place,
-    pieces_ref,
+    near0,
+    near1,
+    near2,
+    near3,
+    far0,
+    far1,
+    far2,
+    far3,
     left_old_ref,
     right_old_ref,
     new_left_ref,
@@ -324,6 +379,7 @@
     sent1,
     sent2,
     sent3,
+    pieces_ref,
     left_buf,
     right_buf,
     grad_ref,
@@ -338,10 +394,20 @@
 ):
     load_left = pltpu.make_async_copy(left_old_ref, left_buf, sems.at[0])
     load_right = pltpu.make_async_copy(right_old_ref, right_buf, sems.at[1])
+    load_own = pltpu.make_async_copy(
+        near0, pieces_ref.at[place[3] * 4 + place[4]], sems.at[9]
+    )
+    load_own.start()
     load_left.start()
     load_right.start()
     first = pl.multiple_of((place[3] * 4 + place[4]) * 128, 128)
     own = pl.ds(first, 128)
+    for d, (near, far) in enumerate(((near0, far0), (near1, far1), (near2, far2), (near3, far3))):
+        at = (place[4] - d) & 3
+        if d > 0:
+            pieces_ref[place[3] * 4 + at] = near[...]
+        pieces_ref[4 - place[3] * 4 + at] = far[...]
+    load_own.wait()
     for zl in range(2):
         for y in range(4):
             piece = pieces_ref[zl * 4 + y]
@@ -396,19 +462,20 @@
     rows = pltpu.HBM((128, BLOCK), F32)
     return call(
         solver_body,
-        [VMEM, HBM, HBM],
+        [HBM, *[VMEM] * 7, HBM, HBM],
         [HBM] * 7,
         [rows, rows, rows, *[pltpu.HBM((144, 256), BF16)] * 4],
         scratch=[
+            pltpu.VMEM((8, 256, 512), BF16),
             *[pltpu.VMEM(square, kind) for kind in (F32, F32, BF16, BF16, F32, BF16, BF16)],
             pltpu.VMEM((128, BLOCK), F32),
             pltpu.VMEM((128, BLOCK), F32),
             pltpu.VMEM((4, 144, 256), BF16),
-            pltpu.SemaphoreType.DMA((9,)),
+            pltpu.SemaphoreType.DMA((10,)),
         ],
-        limit=27,
+        limit=28,
         name="solve",
-    )(place, pieces, left_old, right_old)
+    )(place, *pieces, left_old, right_old)
 
 
 def body(activations, cotangent, weight, left_old, right_old):
@@ -416,31 +483,43 @@
     cot_turned = lax.ppermute(cotangent, AXES, SWAP)
     packed = pack(place, activations, weight)
     crossed = [lax.ppermute(packed[d], "y", shift(d)) for d in range(1, 4)]
-    cot_turned, crossed[0], crossed[2] = lax.optimization_barrier(
-        (cot_turned, crossed[0], crossed[2])
-    )
+    cot_turned, *crossed = lax.optimization_barrier((cot_turned, *crossed))
     cot_all = copies_to(cot_turned, ZAX, 8)
     slab, near_w = unpack(place, [packed[0], *crossed])
     own = [slab] + [lax.ppermute(slab, "x", shift(d)) for d in range(1, 4)]
     swapped = [lax.ppermute(part, "c", FLIP) for part in own]
-    copies, acts = grad_piece(place, cot_all, own, swapped)
-
-    pieces = lax.all_to_all(copies, SOLVER, 0, 0, tiled=True)
-    first = first_partial(place, near_w, acts)
-    pieces, first = lax.optimization_barrier((pieces, first))
+    first = first_partial(place, near_w, own, swapped)
+    cot_all, first = lax.optimization_barrier((cot_all, first))
+    piece, kept, acts = grad_piece(place, cot_all, own, swapped)
+
+    beside = lax.ppermute(piece, "zl", FLIP)
+    pieces = [in_hbm(kept)] + [lax.ppermute(piece, "y", shift(d)) for d in range(1, 4)]
+    pieces += [beside, lax.ppermute(beside, "y", shift(1)), lax.ppermute(pieces[2], "zl", FLIP)]
+    pieces += [lax.ppermute(beside, "y", shift(3))]
+    first, *pieces[1:] = lax.optimization_barrier((first, *pieces[1:]))
     first_parts = lax.all_to_all(first, ZAX, 0, 0, tiled=True)
+    halves = acts.reshape(2, 2, 2, 4, 256, 128)
+    away = lax.dynamic_index_in_dim(halves, place[1], 0, keepdims=False)
+    away = lax.dynamic_index_in_dim(away, 1 - place[3], 1, keepdims=False)
+    away, *pieces = lax.optimization_barrier((away, *pieces))
+    far = lax.ppermute(away, "zl", FLIP)
     new_left, new_right, update, *sent = solve(
         place, pieces, in_hbm(left_old[0, 0]), in_hbm(right_old[0, 0])
     )
-    update_parts = [sent[0]] + [lax.ppermute(sent[d], "y", shift(d)) for d in range(1, 4)]
-    second, squares = second_partial(place, update_parts, acts)
-    second, first_parts = lax.optimization_barrier((second, first_parts))
-    arrived = lax.all_to_all(second, ZAX, 0, 0, tiled=True)
+    far, *sent = lax.optimization_barrier((far, *sent))
+    near_u = in_order(
+        place, [sent[0]] + [lax.ppermute(sent[d], "y", shift(d)) for d in range(1, 4)]
+    )
+    far_u = lax.ppermute(near_u, "zl", FLIP)
+    far_swapped = lax.ppermute(far, "c", FLIP)
     first_total, first_sum = first_add(place, first_parts)
+    acts, first_sum = lax.optimization_barrier((acts, first_sum))
     first_out = lax.ppermute(first_sum, AXES, SWAP)
+
+    second, spread = second_partial(place, near_u, far_u, acts, far, far_swapped)
+    arrived = lax.all_to_all(second, "zh", 0, 0, tiled=True)
     second_out = lax.ppermute(second_add(place, first_total, arrived), AXES, SWAP)
-    total = squares[0, 0] + lax.ppermute(squares, "zl", FLIP)[0, 0]
-    direction = update / jnp.sqrt(total / (BLOCK * BLOCK) + EPSILON)
+    direction = update / spread[0, 0]
     return (first_out, new_left[None, None], new_right[None, None], direction, second_out)
 
 

time: 176 us -> 182 us (1.034)
  the two profiles are of different devices: /device:TPU:7 before, /device:TPU:14 now
where the time goes in v10:
time: 182 us; the launch traced here: 181 us
  waiting for transfers between devices  93.7 us (51%)
  starting transfers between devices  54.6 us (30%)
  Pallas kernels  25.9 us (14%)
  local copies, waits for them, and re-layouts  4.93 us (3%)
    ppermute x1, waiting for transfers between devices, body(): far = lax.ppermute(away, 'zl', FLIP)  19.7 us
    all_to_all x1, waiting for transfers between devices, body(): arrived = lax.all_to_all(second, 'zh', 0, 0, tiled=True)  15.1 us
    pallas_call x1, Pallas kernels, solve(): call(solver_body, [HBM, *[VMEM] * 7, HBM, HBM], [HBM] * 7, [rows, rows, r...  13.7 us
    ppermute x3, waiting for transfers between devices, body(): own = [slab] + [lax.ppermute(slab, 'x', shift(d)) for d in range(1, 4)]  10.7 us
    all_to_all x1, waiting for transfers between devices, copies_to(): return lax.all_to_all(copies, axis, split_axis=0, concat_axis=0, tiled=True)  9.1 us
    ppermute x1, starting transfers between devices, body(): cot_turned = lax.ppermute(cotangent, AXES, SWAP)  8.12 us
    ppermute x1, waiting for transfers between devices, body(): far_u = lax.ppermute(near_u, 'zl', FLIP)  7.84 us
    ppermute x1, waiting for transfers between devices, body(): lax.ppermute(second_add(place, first_total, arrived), AXES, SWAP)  7.64 us
  transfers between devices with their start and end apart: 29, of which 20 were waited for; matrix products, arithmetic and copies ran while one was open for 2% of the time, Pallas kernels for 11%

profile of v10, /device:TPU:14, one launch (start us, length us, event | category | flops | bytes accessed | tf_op | source)
XLA Modules:
  0.0 181.5 jit_solution(11878956332175845935)
XLA Ops:
  0.6 8.1 %collective-permute-start = (bf16[256,256]{1,0:T(8,128)(2,1)}, bf16[256,256]{1,0:T(8,128)(2,1)S(1)}, u32[]{:S(2)}, u32[]{:S(2)}) collective-permute-start(bf16[256,256]{1,0:T(8,128)(2,1)} %param.6), channel_id=1, source_target_pairs={{0,0},{1,1},{2,2},{3,3},{4,32},{5,33},{6,34},{7,35},{8,64},{9,65},... | collective-permute-start | bytes 393224 | tf_op jit(solution)/shard_map/ppermute | solution.py:483
  13.1 2.4 %collective-permute-start.3 = (bf16[512,128]{1,0:T(8,128)(2,1)S(1)}, bf16[512,128]{1,0:T(8,128)(2,1)S(1)}, u32[]{:S(2)}, u32[]{:S(2)}) collective-permute-start(bf16[512,128]{1,0:T(8,128)(2,1)S(1)} %get-tuple-element.57), channel_id=1, source_target_pairs={{0,3},{1,0},{2,1},{3,2},{4,7},{5,4},{6,5},{7,6},{8,11},{9,8},{10,9... | collective-permute-start | bytes 393224 | tf_op jit(solution)/shard_map/ppermute | solution.py:485
  15.5 2.1 %collective-permute-done = bf16[256,256]{1,0:T(8,128)(2,1)S(1)} collective-permute-done((bf16[256,256]{1,0:T(8,128)(2,1)}, bf16[256,256]{1,0:T(8,128)(2,1)S(1)}, u32[]{:S(2)}, u32[]{:S(2)}) %collective-permute-start) | collective-permute-done | bytes 131104 | tf_op jit(solution)/shard_map/ppermute | solution.py:483
  17.5 2.3 %collective-permute-done.2.refs_2_ = bf16[512,128]{1,0:T(8,128)(2,1)S(1)} collective-permute-done((bf16[512,128]{1,0:T(8,128)(2,1)S(1)}, bf16[512,128]{1,0:T(8,128)(2,1)S(1)}, u32[]{:S(2)}, u32[]{:S(2)}) %collective-permute-start.2) | collective-permute-done | bytes 131104 | tf_op jit(solution)/shard_map/ppermute | solution.py:485
  21.6 4.9 %all-to-all-start = ((bf16[8,256,256]{2,1,0:T(8,128)(2,1)}), bf16[8,256,256]{2,1,0:T(8,128)(2,1)S(1)}, u32[]{:S(2)}, u32[]{:S(2)}) async-start(bf16[8,256,256]{2,1,0:T(8,128)(2,1)} %broadcast_in_dim.9), calls=%async_computation | async-start | bytes 2097152 | tf_op jit(solution)/shard_map/all_to_all | solution.py:46
  30.7 10.6 %collective-permute-done.6.refs_3_ = bf16[4,256,128]{2,1,0:T(8,128)(2,1)S(1)} collective-permute-done((bf16[4,256,128]{2,1,0:T(8,128)(2,1)S(1)}, bf16[4,256,128]{2,1,0:T(8,128)(2,1)S(1)}, u32[]{:S(2)}, u32[]{:S(2)}) %collective-permute-start.6) | collective-permute-done | bytes 262176 | tf_op jit(solution)/shard_map/ppermute | solution.py:489
  43.6 2.1 %first_partial.1 = bf16[8,256,256]{2,1,0:T(8,128)(2,1)} custom-call(s32[5]{0:T(128)S(1)} %stack.23.place, bf16[4,256,128]{2,1,0:T(8,128)(2,1)S(1)} %get-tuple-element.63.weight_ref, bf16[4,256,128]{2,1,0:T(8,128)(2,1)S(1)} %get-tuple-element.64.refs_0_, bf16[4,256,128]{2,1,0:T(8,128)(2,1)S(1)} %collective-permute-done.4.refs_1_, ...), custom_call_target="tpu_custom_call" | custom-call | tf_op jit(solution)/shard_map/first_partial/pallas_call | solution.py:195
  45.6 9.1 %all-to-all-done.cot_ref = bf16[8,256,256]{2,1,0:T(8,128)(2,1)S(1)} async-done(((bf16[8,256,256]{2,1,0:T(8,128)(2,1)}), bf16[8,256,256]{2,1,0:T(8,128)(2,1)S(1)}, u32[]{:S(2)}, u32[]{:S(2)}) %all-to-all-start) | async-done | bytes 1048608 | tf_op jit(solution)/shard_map/all_to_all | solution.py:46
  54.7 2.5 %grad_piece.1 = (bf16[256,512]{1,0:T(8,128)(2,1)S(1)}, bf16[256,512]{1,0:T(8,128)(2,1)}, bf16[8,4,256,128]{3,2,1,0:T(8,128)(2,1)}) custom-call(s32[5]{0:T(128)S(1)} %stack.23.place, bf16[8,256,256]{2,1,0:T(8,128)(2,1)S(1)} %all-to-all-done.cot_ref, bf16[4,256,128]{2,1,0:T(8,128)(2,1)S(1)} %get-tuple-element.64.refs_0_, ...), custom_call_target="tpu_custom_call" | custom-call | tf_op jit(solution)/shard_map/grad_piece/pallas_call | solution.py:162
  57.9 2.3 %collective-permute-start.12 = (bf16[256,512]{1,0:T(8,128)(2,1)S(1)}, bf16[256,512]{1,0:T(8,128)(2,1)S(1)}, u32[]{:S(2)}, u32[]{:S(2)}) collective-permute-start(bf16[256,512]{1,0:T(8,128)(2,1)S(1)} %get-tuple-element.68), channel_id=1, source_target_pairs={{0,2},{1,3},{2,0},{3,1},{4,6},{5,7},{6,4},{7,5},{8,10},{9,11},{10,... | collective-permute-start | bytes 786440 | tf_op jit(solution)/shard_map/ppermute | solution.py:496
  62.2 3.3 %collective-permute-done.14.far0 = bf16[256,512]{1,0:T(8,128)(2,1)S(1)} collective-permute-done((bf16[256,512]{1,0:T(8,128)(2,1)S(1)}, bf16[256,512]{1,0:T(8,128)(2,1)S(1)}, u32[]{:S(2)}, u32[]{:S(2)}) %collective-permute-start.14) | collective-permute-done | bytes 262176 | tf_op jit(solution)/shard_map/ppermute | solution.py:495
  70.1 2.8 %collective-permute-done.13.near3 = bf16[256,512]{1,0:T(8,128)(2,1)S(1)} collective-permute-done((bf16[256,512]{1,0:T(8,128)(2,1)S(1)}, bf16[256,512]{1,0:T(8,128)(2,1)S(1)}, u32[]{:S(2)}, u32[]{:S(2)}) %collective-permute-start.13) | collective-permute-done | bytes 262176 | tf_op jit(solution)/shard_map/ppermute | solution.py:496
  74.3 4.2 %collective-permute-done.17.far3 = bf16[256,512]{1,0:T(8,128)(2,1)S(1)} collective-permute-done((bf16[256,512]{1,0:T(8,128)(2,1)S(1)}, bf16[256,512]{1,0:T(8,128)(2,1)S(1)}, u32[]{:S(2)}, u32[]{:S(2)}) %collective-permute-start.17) | collective-permute-done | bytes 262176 | tf_op jit(solution)/shard_map/ppermute | solution.py:498
  78.4 3.6 %all-to-all-start.1 = ((bf16[8,256,256]{2,1,0:T(8,128)(2,1)}), bf16[8,256,256]{2,1,0:T(8,128)(2,1)S(1)}, u32[]{:S(2)}, u32[]{:S(2)}) async-start(bf16[8,256,256]{2,1,0:T(8,128)(2,1)} %first_partial.1), calls=%async_computation.1 | async-start | bytes 2097152 | tf_op jit(solution)/shard_map/all_to_all | solution.py:500
  83.1 2.0 %collective-permute-start.19 = (bf16[2,4,256,128]{3,2,1,0:T(8,128)(2,1)S(1)}, bf16[2,4,256,128]{3,2,1,0:T(8,128)(2,1)S(1)}, u32[]{:S(2)}, u32[]{:S(2)}) collective-permute-start(bf16[2,4,256,128]{3,2,1,0:T(8,128)(2,1)S(1)} %dynamic-slice_bitcast_fusion), channel_id=1, source_target_pairs={{0,4},{4,0},{1,5},{5,1},{2,6},{6,2},{3,7},{7,3},{8,12},{12,8},{9,1... | collective-permute-start | bytes 1572872 | tf_op jit(solution)/shard_map/ppermute | solution.py:505
  85.1 13.7 %solve.1 = (f32[128,1024]{1,0:T(8,128)}, f32[128,1024]{1,0:T(8,128)}, f32[128,1024]{1,0:T(8,128)}, bf16[144,256]{1,0:T(8,128)(2,1)}, bf16[144,256]{1,0:T(8,128)(...) custom-call(s32[5]{0:T(128)S(1)} %stack.23.place, bf16[256,512]{1,0:T(8,128)(2,1)} %get-tuple-element.80.near0, ...), custom_call_target="tpu_custom_call" | custom-call | tf_op jit(solution)/shard_map/solve/pallas_call | solution.py:463
  98.7 19.7 %collective-permute-done.19.far_hbm = bf16[2,4,256,128]{3,2,1,0:T(8,128)(2,1)S(1)} collective-permute-done((bf16[2,4,256,128]{3,2,1,0:T(8,128)(2,1)S(1)}, bf16[2,4,256,128]{3,2,1,0:T(8,128)(2,1)S(1)}, u32[]{:S(2)}, u32[]{:S(2)}) %collective-permute-start.19) | collective-permute-done | bytes 524320 | tf_op jit(solution)/shard_map/ppermute | solution.py:505
  123.4 3.3 %collective-permute-done.21.refs_2_ = bf16[144,256]{1,0:T(8,128)(2,1)S(1)} collective-permute-done((bf16[144,256]{1,0:T(8,128)(2,1)}, bf16[144,256]{1,0:T(8,128)(2,1)S(1)}, u32[]{:S(2)}, u32[]{:S(2)}) %collective-permute-start.21) | collective-permute-done | bytes 73760 | tf_op jit(solution)/shard_map/ppermute | solution.py:511
  130.2 7.8 %collective-permute-done.23.far_u = bf16[4,144,256]{2,1,0:T(8,128)(2,1)S(1)} collective-permute-done((bf16[4,144,256]{2,1,0:T(8,128)(2,1)S(1)}, bf16[4,144,256]{2,1,0:T(8,128)(2,1)S(1)}, u32[]{:S(2)}, u32[]{:S(2)}) %collective-permute-start.23) | collective-permute-done | bytes 294944 | tf_op jit(solution)/shard_map/ppermute | solution.py:513
  138.0 3.6 %second_partial.1 = (bf16[4,256,256]{2,1,0:T(8,128)(2,1)}, f32[8,128]{1,0:T(8,128)S(1)}) custom-call(s32[5]{0:T(128)S(1)} %stack.23.place, bf16[4,144,256]{2,1,0:T(8,128)(2,1)S(1)} %in_order.1.near_u, bf16[4,144,256]{2,1,0:T(8,128)(2,1)S(1)} %collective-permute-done.23.far_u, bf16[8,4,256,128]{3,2,1,0:T(8,128)(2,1)} %get-tuple-element.100.acts_hbm, ...), custom_call_target="tpu_custom_call" | custom-call | tf_op jit(solution)/shard_map/second_partial/pallas_call | solution.py:278
  141.6 5.7 %all-to-all-start.2 = ((bf16[4,256,256]{2,1,0:T(8,128)(2,1)}), bf16[4,256,256]{2,1,0:T(8,128)(2,1)S(1)}, u32[]{:S(2)}, u32[]{:S(2)}) async-start(bf16[4,256,256]{2,1,0:T(8,128)(2,1)} %get-tuple-element.104), calls=%async_computation.2 | async-start | bytes 1048576 | tf_op jit(solution)/shard_map/all_to_all | solution.py:520
  147.4 5.4 %collective-permute-start.18 = (bf16[256,256]{1,0:T(8,128)(2,1)S(1)}, bf16[256,256]{1,0:T(8,128)(2,1)S(1)}, u32[]{:S(2)}, u32[]{:S(2)}) collective-permute-start(bf16[256,256]{1,0:T(8,128)(2,1)S(1)} %get-tuple-element.71), channel_id=1, source_target_pairs={{0,0},{1,1},{2,2},{3,3},{4,32},{5,33},{6,34},{7,35},{8,64},{9,65},... | collective-permute-start | bytes 393224 | tf_op jit(solution)/shard_map/ppermute | solution.py:517
  153.3 15.1 %all-to-all-done.2.parts_ref = bf16[4,256,256]{2,1,0:T(8,128)(2,1)S(1)} async-done(((bf16[4,256,256]{2,1,0:T(8,128)(2,1)}), bf16[4,256,256]{2,1,0:T(8,128)(2,1)S(1)}, u32[]{:S(2)}, u32[]{:S(2)}) %all-to-all-start.2) | async-done | bytes 524320 | tf_op jit(solution)/shard_map/all_to_all | solution.py:520
  172.5 7.6 %collective-permute-done.25 = bf16[256,256]{1,0:T(8,128)(2,1)S(1)} collective-permute-done((bf16[256,256]{1,0:T(8,128)(2,1)S(1)}, bf16[256,256]{1,0:T(8,128)(2,1)S(1)}, u32[]{:S(2)}, u32[]{:S(2)}) %collective-permute-start.25) | collective-permute-done | bytes 131104 | tf_op jit(solution)/shard_map/ppermute | solution.py:521
  (56 shorter events, 36.4 us)
Async XLA Ops:
  0.6 16.9 %collective-permute-start = (bf16[256,256]{1,0:T(8,128)(2,1)}, bf16[256,256]{1,0:T(8,128)(2,1)S(1)}, u32[]{:S(2)}, u32[]{:S(2)}) collective-permute-start(bf16[256,256]{1,0:T(8,128)(2,1)} %param.6), channel_id=1, source_target_pairs={{0,0},{1,1},{2,2},{3,3},{4,32},{5,33},{6,34},{7,35},{8,64},{9,65},... | collective-permute-start | bytes 393224 | tf_op jit(solution)/shard_map/ppermute | solution.py:483
  10.5 7.1 %collective-permute-start.1 = (bf16[512,128]{1,0:T(8,128)(2,1)S(1)}, bf16[512,128]{1,0:T(8,128)(2,1)S(1)}, u32[]{:S(2)}, u32[]{:S(2)}) collective-permute-start(bf16[512,128]{1,0:T(8,128)(2,1)S(1)} %get-tuple-element.55), channel_id=1, source_target_pairs={{0,1},{1,2},{2,3},{3,0},{4,5},{5,6},{6,7},{7,4},{8,9},{9,10},{10,1... | collective-permute-start | bytes 393224 | tf_op jit(solution)/shard_map/ppermute | solution.py:485
  12.1 7.8 %collective-permute-start.2 = (bf16[512,128]{1,0:T(8,128)(2,1)S(1)}, bf16[512,128]{1,0:T(8,128)(2,1)S(1)}, u32[]{:S(2)}, u32[]{:S(2)}) collective-permute-start(bf16[512,128]{1,0:T(8,128)(2,1)S(1)} %get-tuple-element.56), channel_id=1, source_target_pairs={{0,2},{1,3},{2,0},{3,1},{4,6},{5,7},{6,4},{7,5},{8,10},{9,11},{10,... | collective-permute-start | bytes 393224 | tf_op jit(solution)/shard_map/ppermute | solution.py:485
  13.1 7.5 %collective-permute-start.3 = (bf16[512,128]{1,0:T(8,128)(2,1)S(1)}, bf16[512,128]{1,0:T(8,128)(2,1)S(1)}, u32[]{:S(2)}, u32[]{:S(2)}) collective-permute-start(bf16[512,128]{1,0:T(8,128)(2,1)S(1)} %get-tuple-element.57), channel_id=1, source_target_pairs={{0,3},{1,0},{2,1},{3,2},{4,7},{5,4},{6,5},{7,6},{8,11},{9,8},{10,9... | collective-permute-start | bytes 393224 | tf_op jit(solution)/shard_map/ppermute | solution.py:485
  21.6 33.2 %all-to-all-start = ((bf16[8,256,256]{2,1,0:T(8,128)(2,1)}), bf16[8,256,256]{2,1,0:T(8,128)(2,1)S(1)}, u32[]{:S(2)}, u32[]{:S(2)}) async-start(bf16[8,256,256]{2,1,0:T(8,128)(2,1)} %broadcast_in_dim.9), calls=%async_computation | async-start | bytes 2097152 | tf_op jit(solution)/shard_map/all_to_all | solution.py:46
  27.1 14.2 %collective-permute-start.6 = (bf16[4,256,128]{2,1,0:T(8,128)(2,1)S(1)}, bf16[4,256,128]{2,1,0:T(8,128)(2,1)S(1)}, u32[]{:S(2)}, u32[]{:S(2)}) collective-permute-start(bf16[4,256,128]{2,1,0:T(8,128)(2,1)S(1)} %get-tuple-element.64.refs_0_), channel_id=1, source_target_pairs={{0,192},{64,0},{128,64},{192,128},{1,193},{65,1},{129,65},{193,129... | collective-permute-start | bytes 786440 | tf_op jit(solution)/shard_map/ppermute | solution.py:489
  27.6 13.7 %collective-permute-start.5 = (bf16[4,256,128]{2,1,0:T(8,128)(2,1)S(1)}, bf16[4,256,128]{2,1,0:T(8,128)(2,1)S(1)}, u32[]{:S(2)}, u32[]{:S(2)}) collective-permute-start(bf16[4,256,128]{2,1,0:T(8,128)(2,1)S(1)} %get-tuple-element.64.refs_0_), channel_id=1, source_target_pairs={{0,128},{64,192},{128,0},{192,64},{1,129},{65,193},{129,1},{193,65... | collective-permute-start | bytes 786440 | tf_op jit(solution)/shard_map/ppermute | solution.py:489
  29.2 12.7 %collective-permute-start.4 = (bf16[4,256,128]{2,1,0:T(8,128)(2,1)S(1)}, bf16[4,256,128]{2,1,0:T(8,128)(2,1)S(1)}, u32[]{:S(2)}, u32[]{:S(2)}) collective-permute-start(bf16[4,256,128]{2,1,0:T(8,128)(2,1)S(1)} %get-tuple-element.64.refs_0_), channel_id=1, source_target_pairs={{0,64},{64,128},{128,192},{192,0},{1,65},{65,129},{129,193},{193,1... | collective-permute-start | bytes 786440 | tf_op jit(solution)/shard_map/ppermute | solution.py:489
  30.7 11.3 %collective-permute-start.7 = (bf16[4,256,128]{2,1,0:T(8,128)(2,1)S(1)}, bf16[4,256,128]{2,1,0:T(8,128)(2,1)S(1)}, u32[]{:S(2)}, u32[]{:S(2)}) collective-permute-start(bf16[4,256,128]{2,1,0:T(8,128)(2,1)S(1)} %get-tuple-element.64.refs_0_), channel_id=1, source_target_pairs={{0,32},{32,0},{1,33},{33,1},{2,34},{34,2},{3,35},{35,3},{4,36},{36... | collective-permute-start | bytes 786440 | tf_op jit(solution)/shard_map/ppermute | solution.py:490
  57.3 8.3 %collective-permute-start.14 = (bf16[256,512]{1,0:T(8,128)(2,1)S(1)}, bf16[256,512]{1,0:T(8,128)(2,1)S(1)}, u32[]{:S(2)}, u32[]{:S(2)}) collective-permute-start(bf16[256,512]{1,0:T(8,128)(2,1)S(1)} %get-tuple-element.68), channel_id=1, source_target_pairs={{0,4},{4,0},{1,5},{5,1},{2,6},{6,2},{3,7},{7,3},{8,12},{12,8},{9,1... | collective-permute-start | bytes 786440 | tf_op jit(solution)/shard_map/ppermute | solution.py:495
  57.9 10.8 %collective-permute-start.12 = (bf16[256,512]{1,0:T(8,128)(2,1)S(1)}, bf16[256,512]{1,0:T(8,128)(2,1)S(1)}, u32[]{:S(2)}, u32[]{:S(2)}) collective-permute-start(bf16[256,512]{1,0:T(8,128)(2,1)S(1)} %get-tuple-element.68), channel_id=1, source_target_pairs={{0,2},{1,3},{2,0},{3,1},{4,6},{5,7},{6,4},{7,5},{8,10},{9,11},{10,... | collective-permute-start | bytes 786440 | tf_op jit(solution)/shard_map/ppermute | solution.py:496
  60.2 12.7 %collective-permute-start.13 = (bf16[256,512]{1,0:T(8,128)(2,1)S(1)}, bf16[256,512]{1,0:T(8,128)(2,1)S(1)}, u32[]{:S(2)}, u32[]{:S(2)}) collective-permute-start(bf16[256,512]{1,0:T(8,128)(2,1)S(1)} %get-tuple-element.68), channel_id=1, source_target_pairs={{0,3},{1,0},{2,1},{3,2},{4,7},{5,4},{6,5},{7,6},{8,11},{9,8},{10,9... | collective-permute-start | bytes 786440 | tf_op jit(solution)/shard_map/ppermute | solution.py:496
  61.4 12.9 %collective-permute-start.11 = (bf16[256,512]{1,0:T(8,128)(2,1)S(1)}, bf16[256,512]{1,0:T(8,128)(2,1)S(1)}, u32[]{:S(2)}, u32[]{:S(2)}) collective-permute-start(bf16[256,512]{1,0:T(8,128)(2,1)S(1)} %get-tuple-element.68), channel_id=1, source_target_pairs={{0,1},{1,2},{2,3},{3,0},{4,5},{5,6},{6,7},{7,4},{8,9},{9,10},{10,1... | collective-permute-start | bytes 786440 | tf_op jit(solution)/shard_map/ppermute | solution.py:496
  65.6 12.8 %collective-permute-start.17 = (bf16[256,512]{1,0:T(8,128)(2,1)S(1)}, bf16[256,512]{1,0:T(8,128)(2,1)S(1)}, u32[]{:S(2)}, u32[]{:S(2)}) collective-permute-start(bf16[256,512]{1,0:T(8,128)(2,1)S(1)} %collective-permute-done.14.far0), channel_id=1, source_target_pairs={{0,3},{1,0},{2,1},{3,2},{4,7},{5,4},{6,5},{7,6},{8,11},{9,8},{10,9... | collective-permute-start | bytes 786440 | tf_op jit(solution)/shard_map/ppermute | solution.py:498
  66.8 11.6 %collective-permute-start.15 = (bf16[256,512]{1,0:T(8,128)(2,1)S(1)}, bf16[256,512]{1,0:T(8,128)(2,1)S(1)}, u32[]{:S(2)}, u32[]{:S(2)}) collective-permute-start(bf16[256,512]{1,0:T(8,128)(2,1)S(1)} %collective-permute-done.14.far0), channel_id=1, source_target_pairs={{0,1},{1,2},{2,3},{3,0},{4,5},{5,6},{6,7},{7,4},{8,9},{9,10},{10,1... | collective-permute-start | bytes 786440 | tf_op jit(solution)/shard_map/ppermute | solution.py:497
  68.7 9.7 %collective-permute-start.16 = (bf16[256,512]{1,0:T(8,128)(2,1)S(1)}, bf16[256,512]{1,0:T(8,128)(2,1)S(1)}, u32[]{:S(2)}, u32[]{:S(2)}) collective-permute-start(bf16[256,512]{1,0:T(8,128)(2,1)S(1)} %collective-permute-done.12.near2), channel_id=1, source_target_pairs={{0,4},{4,0},{1,5},{5,1},{2,6},{6,2},{3,7},{7,3},{8,12},{12,8},{9,1... | collective-permute-start | bytes 786440 | tf_op jit(solution)/shard_map/ppermute | solution.py:497
  78.4 51.1 %all-to-all-start.1 = ((bf16[8,256,256]{2,1,0:T(8,128)(2,1)}), bf16[8,256,256]{2,1,0:T(8,128)(2,1)S(1)}, u32[]{:S(2)}, u32[]{:S(2)}) async-start(bf16[8,256,256]{2,1,0:T(8,128)(2,1)} %first_partial.1), calls=%async_computation.1 | async-start | bytes 2097152 | tf_op jit(solution)/shard_map/all_to_all | solution.py:500
  83.1 35.3 %collective-permute-start.19 = (bf16[2,4,256,128]{3,2,1,0:T(8,128)(2,1)S(1)}, bf16[2,4,256,128]{3,2,1,0:T(8,128)(2,1)S(1)}, u32[]{:S(2)}, u32[]{:S(2)}) collective-permute-start(bf16[2,4,256,128]{3,2,1,0:T(8,128)(2,1)S(1)} %dynamic-slice_bitcast_fusion), channel_id=1, source_target_pairs={{0,4},{4,0},{1,5},{5,1},{2,6},{6,2},{3,7},{7,3},{8,12},{12,8},{9,1... | collective-permute-start | bytes 1572872 | tf_op jit(solution)/shard_map/ppermute | solution.py:505
  118.4 19.6 %collective-permute-start.24 = (bf16[2,4,256,128]{3,2,1,0:T(8,128)(2,1)S(1)}, bf16[2,4,256,128]{3,2,1,0:T(8,128)(2,1)}, u32[]{:S(2)}, u32[]{:S(2)}) collective-permute-start(bf16[2,4,256,128]{3,2,1,0:T(8,128)(2,1)S(1)} %collective-permute-done.19.far_hbm), channel_id=1, source_target_pairs={{0,32},{32,0},{1,33},{33,1},{2,34},{34,2},{3,35},{35,3},{4,36},{36... | collective-permute-start | bytes 1572872 | tf_op jit(solution)/shard_map/ppermute | solution.py:514
  119.8 6.8 %collective-permute-start.21 = (bf16[144,256]{1,0:T(8,128)(2,1)}, bf16[144,256]{1,0:T(8,128)(2,1)S(1)}, u32[]{:S(2)}, u32[]{:S(2)}) collective-permute-start(bf16[144,256]{1,0:T(8,128)(2,1)} %get-tuple-element.98), channel_id=1, source_target_pairs={{0,2},{1,3},{2,0},{3,1},{4,6},{5,7},{6,4},{7,5},{8,10},{9,11},{10,... | collective-permute-start | bytes 221192 | tf_op jit(solution)/shard_map/ppermute | solution.py:511
  129.0 9.0 %collective-permute-start.23 = (bf16[4,144,256]{2,1,0:T(8,128)(2,1)S(1)}, bf16[4,144,256]{2,1,0:T(8,128)(2,1)S(1)}, u32[]{:S(2)}, u32[]{:S(2)}) collective-permute-start(bf16[4,144,256]{2,1,0:T(8,128)(2,1)S(1)} %in_order.1.near_u), channel_id=1, source_target_pairs={{0,4},{4,0},{1,5},{5,1},{2,6},{6,2},{3,7},{7,3},{8,12},{12,8},{9,1... | collective-permute-start | bytes 884744 | tf_op jit(solution)/shard_map/ppermute | solution.py:513
  141.6 26.8 %all-to-all-start.2 = ((bf16[4,256,256]{2,1,0:T(8,128)(2,1)}), bf16[4,256,256]{2,1,0:T(8,128)(2,1)S(1)}, u32[]{:S(2)}, u32[]{:S(2)}) async-start(bf16[4,256,256]{2,1,0:T(8,128)(2,1)} %get-tuple-element.104), calls=%async_computation.2 | async-start | bytes 1048576 | tf_op jit(solution)/shard_map/all_to_all | solution.py:520
  147.4 25.2 %collective-permute-start.18 = (bf16[256,256]{1,0:T(8,128)(2,1)S(1)}, bf16[256,256]{1,0:T(8,128)(2,1)S(1)}, u32[]{:S(2)}, u32[]{:S(2)}) collective-permute-start(bf16[256,256]{1,0:T(8,128)(2,1)S(1)} %get-tuple-element.71), channel_id=1, source_target_pairs={{0,0},{1,1},{2,2},{3,3},{4,32},{5,33},{6,34},{7,35},{8,64},{9,65},... | collective-permute-start | bytes 393224 | tf_op jit(solution)/shard_map/ppermute | solution.py:517
  169.1 11.1 %collective-permute-start.25 = (bf16[256,256]{1,0:T(8,128)(2,1)S(1)}, bf16[256,256]{1,0:T(8,128)(2,1)S(1)}, u32[]{:S(2)}, u32[]{:S(2)}) collective-permute-start(bf16[256,256]{1,0:T(8,128)(2,1)S(1)} %second_add.1), channel_id=1, source_target_pairs={{0,0},{1,1},{2,2},{3,3},{4,32},{5,33},{6,34},{7,35},{8,64},{9,65},... | collective-permute-start | bytes 393224 | tf_op jit(solution)/shard_map/ppermute | solution.py:521
  (8 other events, 79.1 us)

commit v11 on v9

--- a/solution.py
+++ b/solution.py
@@ -143,7 +143,7 @@
 
 def grad_body(place, cot_ref, *refs):
     own, swapped = refs[:4], refs[4:8]
-    copies_ref, acts_ref, piece_ref, sems = refs[8:]
+    piece_ref, kept_ref, acts_ref, sems = refs[8:]
     x, c = place[0], place[1]
     sends = []
     for d in range(4):
@@ -158,9 +158,8 @@
         total = total + dot(cot_ref[at + c], wide(own[d]))
         total = total + dot(cot_ref[at + 1 - c], wide(swapped[d]))
     piece_ref[...] = total.astype(BF16)
-    for s in range(8):
-        sends.append(pltpu.make_async_copy(piece_ref, copies_ref.at[s], sems.at[8 + s]))
-        sends[-1].start()
+    sends.append(pltpu.make_async_copy(piece_ref, kept_ref, sems.at[8]))
+    sends[-1].start()
     for send in sends:
         send.wait()
 
@@ -169,9 +168,13 @@
     return call(
         grad_body,
         [VMEM] * 9,
-        [HBM, HBM],
-        [pltpu.HBM((8, 256, 512), BF16), pltpu.HBM((8, 4, 256, 128), BF16)],
-        scratch=[pltpu.VMEM((256, 512), BF16), pltpu.SemaphoreType.DMA((16,))],
+        [VMEM, HBM, HBM],
+        [
+            SHAPE((256, 512), BF16),
+            pltpu.HBM((256, 512), BF16),
+            pltpu.HBM((8, 4, 256, 128), BF16),
+        ],
+        scratch=[pltpu.SemaphoreType.DMA((9,))],
         limit=10,
         name="grad_piece",
     )(place, cot_all, *own, *swapped)
@@ -335,7 +338,14 @@
 
 def solver_body(
     place,
-    pieces_ref,
+    near0,
+    near1,
+    near2,
+    near3,
+    far0,
+    far1,
+    far2,
+    far3,
     left_old_ref,
     right_old_ref,
     new_left_ref,
@@ -345,6 +355,7 @@
     sent1,
     sent2,
     sent3,
+    pieces_ref,
     left_buf,
     right_buf,
     grad_ref,
@@ -359,10 +370,20 @@
 ):
     load_left = pltpu.make_async_copy(left_old_ref, left_buf, sems.at[0])
     load_right = pltpu.make_async_copy(right_old_ref, right_buf, sems.at[1])
+    load_own = pltpu.make_async_copy(
+        near0, pieces_ref.at[place[3] * 4 + place[4]], sems.at[9]
+    )
+    load_own.start()
     load_left.start()
     load_right.start()
     first = pl.multiple_of((place[3] * 4 + place[4]) * 128, 128)
     own = pl.ds(first, 128)
+    for d, (near, far) in enumerate(((near0, far0), (near1, far1), (near2, far2), (near3, far3))):
+        at = (place[4] - d) & 3
+        if d > 0:
+            pieces_ref[place[3] * 4 + at] = near[...]
+        pieces_ref[4 - place[3] * 4 + at] = far[...]
+    load_own.wait()
     for zl in range(2):
         for y in range(4):
             piece = pieces_ref[zl * 4 + y]
@@ -417,19 +438,20 @@
     rows = pltpu.HBM((128, BLOCK), F32)
     return call(
         solver_body,
-        [VMEM, HBM, HBM],
+        [HBM, *[VMEM] * 7, HBM, HBM],
         [HBM] * 7,
         [rows, rows, rows, *[pltpu.HBM((144, 256), BF16)] * 4],
         scratch=[
+            pltpu.VMEM((8, 256, 512), BF16),
             *[pltpu.VMEM(square, kind) for kind in (F32, F32, BF16, BF16, F32, BF16, BF16)],
             pltpu.VMEM((128, BLOCK), F32),
             pltpu.VMEM((128, BLOCK), F32),
             pltpu.VMEM((4, 144, 256), BF16),
-            pltpu.SemaphoreType.DMA((9,)),
+            pltpu.SemaphoreType.DMA((10,)),
         ],
-        limit=27,
+        limit=28,
         name="solve",
-    )(place, pieces, left_old, right_old)
+    )(place, *pieces, left_old, right_old)
 
 
 def body(activations, cotangent, weight, left_old, right_old):
@@ -444,10 +466,13 @@
     swapped = [lax.ppermute(part, "c", FLIP) for part in own]
     first = first_partial(place, near_w, own, swapped)
     cot_all, first = lax.optimization_barrier((cot_all, first))
-    copies, acts = grad_piece(place, cot_all, own, swapped)
-
-    pieces = lax.all_to_all(copies, SOLVER, 0, 0, tiled=True)
-    pieces, first = lax.optimization_barrier((pieces, first))
+    piece, kept, acts = grad_piece(place, cot_all, own, swapped)
+
+    beside = lax.ppermute(piece, "zl", FLIP)
+    pieces = [in_hbm(kept)] + [lax.ppermute(piece, "y", shift(d)) for d in range(1, 4)]
+    pieces += [beside, lax.ppermute(beside, "y", shift(1)), lax.ppermute(pieces[2], "zl", FLIP)]
+    pieces += [lax.ppermute(beside, "y", shift(3))]
+    first, *pieces[1:] = lax.optimization_barrier((first, *pieces[1:]))
     first_parts = lax.all_to_all(first, ZAX, 0, 0, tiled=True)
     new_left, new_right, update, *sent = solve(
         place, pieces, in_hbm(left_old[0, 0]), in_hbm(right_old[0, 0])

time: 175 us -> 171 us (0.977); the launches traced: 174 us -> 168 us
  blocking collectives: 29.1 us -> 0 us
  waiting for transfers between devices: 76.3 us -> 93.4 us
  starting transfers between devices: 38.7 us -> 45.3 us
    all_to_all x1 -> x0, blocking collectives: 29.1 us -> none  [body(): pieces = lax.all_to_all(copies, SOLVER, 0, 0, tiled=True)]
    ppermute x0 -> x7, waiting for transfers between devices: none -> 14.7 us  [the longest x3 5.26 us: body(): lax.ppermute(piece, 'y', shift(d))]
    ppermute x0 -> x7, starting transfers between devices: none -> 6.3 us  [the longest x3 3.53 us: body(): lax.ppermute(piece, 'y', shift(d))]
  transfers between devices with their start and end apart: 18 -> 25, of which waited for: 12 -> 18; matrix products, arithmetic and copies ran while one was open for 1% -> 1% of each run, Pallas kernels for 12% -> 13%
where the time goes in v11:
time: 171 us; the launch traced here: 168 us
  waiting for transfers between devices  93.4 us (55%)
  starting transfers between devices  45.3 us (26%)
  Pallas kernels  25 us (15%)
  local copies, waits for them, and re-layouts  2.37 us (1%)
    all_to_all x1, waiting for transfers between devices, body(): arrived = lax.all_to_all(second, ZAX, 0, 0, tiled=True)  29.9 us
    ppermute x1, waiting for transfers between devices, body(): outs = lax.ppermute(outs, AXES, HOME)  16.7 us
    pallas_call x1, Pallas kernels, solve(): call(solver_body, [HBM, *[VMEM] * 7, HBM, HBM], [HBM] * 7, [rows, rows, r...  13.7 us
    ppermute x3, waiting for transfers between devices, body(): own = [slab] + [lax.ppermute(slab, 'x', shift(d)) for d in range(1, 4)]  9.16 us
    all_to_all x1, waiting for transfers between devices, copies_to(): return lax.all_to_all(copies, axis, split_axis=0, concat_axis=0, tiled=True)  8.99 us
    ppermute x1, starting transfers between devices, body(): cot_turned = lax.ppermute(cotangent, AXES, SWAP)  7.96 us
    all_to_all x1, starting transfers between devices, copies_to(): return lax.all_to_all(copies, axis, split_axis=0, concat_axis=0, tiled=True)  5.65 us
    ppermute x3, waiting for transfers between devices, body(): lax.ppermute(piece, 'y', shift(d))  5.26 us
  transfers between devices with their start and end apart: 25, of which 18 were waited for; matrix products, arithmetic and copies ran while one was open for 1% of the time, Pallas kernels for 13%

profile of v11, /device:TPU:7, one launch (start us, length us, event | category | flops | bytes accessed | tf_op | source)
XLA Modules:
  0.0 168.4 jit_solution(2696184871280276514)
XLA Ops:
  0.6 8.0 %collective-permute-start = (bf16[256,256]{1,0:T(8,128)(2,1)}, bf16[256,256]{1,0:T(8,128)(2,1)S(1)}, u32[]{:S(2)}, u32[]{:S(2)}) collective-permute-start(bf16[256,256]{1,0:T(8,128)(2,1)} %param.6), channel_id=1, source_target_pairs={{0,0},{1,1},{2,2},{3,3},{4,32},{5,33},{6,34},{7,35},{8,64},{9,65},... | collective-permute-start | bytes 393224 | tf_op jit(solution)/shard_map/ppermute | solution.py:459
  11.7 2.6 %collective-permute-start.2 = (bf16[512,128]{1,0:T(8,128)(2,1)S(1)}, bf16[512,128]{1,0:T(8,128)(2,1)S(1)}, u32[]{:S(2)}, u32[]{:S(2)}) collective-permute-start(bf16[512,128]{1,0:T(8,128)(2,1)S(1)} %get-tuple-element.40), channel_id=1, source_target_pairs={{0,2},{1,3},{2,0},{3,1},{4,6},{5,7},{6,4},{7,5},{8,10},{9,11},{10,... | collective-permute-start | bytes 393224 | tf_op jit(solution)/shard_map/ppermute | solution.py:461
  15.4 2.9 %collective-permute-done = bf16[256,256]{1,0:T(8,128)(2,1)S(1)} collective-permute-done((bf16[256,256]{1,0:T(8,128)(2,1)}, bf16[256,256]{1,0:T(8,128)(2,1)S(1)}, u32[]{:S(2)}, u32[]{:S(2)}) %collective-permute-start) | collective-permute-done | bytes 131104 | tf_op jit(solution)/shard_map/ppermute | solution.py:459
  20.9 5.6 %all-to-all-start = ((bf16[8,256,256]{2,1,0:T(8,128)(2,1)}), bf16[8,256,256]{2,1,0:T(8,128)(2,1)S(1)}, u32[]{:S(2)}, u32[]{:S(2)}) async-start(bf16[8,256,256]{2,1,0:T(8,128)(2,1)} %broadcast_in_dim.9), calls=%async_computation | async-start | bytes 2097152 | tf_op jit(solution)/shard_map/all_to_all | solution.py:52
  31.7 9.2 %collective-permute-done.6.refs_3_ = bf16[4,256,128]{2,1,0:T(8,128)(2,1)S(1)} collective-permute-done((bf16[4,256,128]{2,1,0:T(8,128)(2,1)S(1)}, bf16[4,256,128]{2,1,0:T(8,128)(2,1)S(1)}, u32[]{:S(2)}, u32[]{:S(2)}) %collective-permute-start.6) | collective-permute-done | bytes 262176 | tf_op jit(solution)/shard_map/ppermute | solution.py:465
  40.8 1.9 %collective-permute-start.10 = (bf16[4,256,128]{2,1,0:T(8,128)(2,1)S(1)}, bf16[4,256,128]{2,1,0:T(8,128)(2,1)S(1)}, u32[]{:S(2)}, u32[]{:S(2)}) collective-permute-start(bf16[4,256,128]{2,1,0:T(8,128)(2,1)S(1)} %collective-permute-done.6.refs_3_), channel_id=1, source_target_pairs={{0,32},{32,0},{1,33},{33,1},{2,34},{34,2},{3,35},{35,3},{4,36},{36... | collective-permute-start | bytes 786440 | tf_op jit(solution)/shard_map/ppermute | solution.py:466
  44.7 2.1 %first_partial.1 = bf16[8,256,256]{2,1,0:T(8,128)(2,1)} custom-call(s32[5]{0:T(128)S(1)} %stack.23.place, bf16[4,256,128]{2,1,0:T(8,128)(2,1)S(1)} %get-tuple-element.47.weight_ref, bf16[4,256,128]{2,1,0:T(8,128)(2,1)S(1)} %get-tuple-element.48.refs_0_, bf16[4,256,128]{2,1,0:T(8,128)(2,1)S(1)} %collective-permute-done.4.refs_1_, ...), custom_call_target="tpu_custom_call" | custom-call | tf_op jit(solution)/shard_map/first_partial/pallas_call | solution.py:202
  46.7 9.0 %all-to-all-done.cot_ref = bf16[8,256,256]{2,1,0:T(8,128)(2,1)S(1)} async-done(((bf16[8,256,256]{2,1,0:T(8,128)(2,1)}), bf16[8,256,256]{2,1,0:T(8,128)(2,1)S(1)}, u32[]{:S(2)}, u32[]{:S(2)}) %all-to-all-start) | async-done | bytes 1048608 | tf_op jit(solution)/shard_map/all_to_all | solution.py:52
  55.7 2.5 %grad_piece.1 = (bf16[256,512]{1,0:T(8,128)(2,1)S(1)}, bf16[256,512]{1,0:T(8,128)(2,1)}, bf16[8,4,256,128]{3,2,1,0:T(8,128)(2,1)}) custom-call(s32[5]{0:T(128)S(1)} %stack.23.place, bf16[8,256,256]{2,1,0:T(8,128)(2,1)S(1)} %all-to-all-done.cot_ref, bf16[4,256,128]{2,1,0:T(8,128)(2,1)S(1)} %get-tuple-element.48.refs_0_, ...), custom_call_target="tpu_custom_call" | custom-call | tf_op jit(solution)/shard_map/grad_piece/pallas_call | solution.py:168
  58.4 2.1 %collective-permute-start.12 = (bf16[256,512]{1,0:T(8,128)(2,1)S(1)}, bf16[256,512]{1,0:T(8,128)(2,1)S(1)}, u32[]{:S(2)}, u32[]{:S(2)}) collective-permute-start(bf16[256,512]{1,0:T(8,128)(2,1)S(1)} %get-tuple-element.52), channel_id=1, source_target_pairs={{0,2},{1,3},{2,0},{3,1},{4,6},{5,7},{6,4},{7,5},{8,10},{9,11},{10,... | collective-permute-start | bytes 786440 | tf_op jit(solution)/shard_map/ppermute | solution.py:472
  61.9 3.9 %collective-permute-done.14.far0 = bf16[256,512]{1,0:T(8,128)(2,1)S(1)} collective-permute-done((bf16[256,512]{1,0:T(8,128)(2,1)S(1)}, bf16[256,512]{1,0:T(8,128)(2,1)S(1)}, u32[]{:S(2)}, u32[]{:S(2)}) %collective-permute-start.14) | collective-permute-done | bytes 262176 | tf_op jit(solution)/shard_map/ppermute | solution.py:471
  65.7 2.0 %collective-permute-start.17 = (bf16[256,512]{1,0:T(8,128)(2,1)S(1)}, bf16[256,512]{1,0:T(8,128)(2,1)S(1)}, u32[]{:S(2)}, u32[]{:S(2)}) collective-permute-start(bf16[256,512]{1,0:T(8,128)(2,1)S(1)} %collective-permute-done.14.far0), channel_id=1, source_target_pairs={{0,3},{1,0},{2,1},{3,2},{4,7},{5,4},{6,5},{7,6},{8,11},{9,8},{10,9... | collective-permute-start | bytes 786440 | tf_op jit(solution)/shard_map/ppermute | solution.py:474
  68.4 3.9 %collective-permute-done.13.near3 = bf16[256,512]{1,0:T(8,128)(2,1)S(1)} collective-permute-done((bf16[256,512]{1,0:T(8,128)(2,1)S(1)}, bf16[256,512]{1,0:T(8,128)(2,1)S(1)}, u32[]{:S(2)}, u32[]{:S(2)}) %collective-permute-start.13) | collective-permute-done | bytes 262176 | tf_op jit(solution)/shard_map/ppermute | solution.py:472
  73.7 4.3 %collective-permute-done.17.far3 = bf16[256,512]{1,0:T(8,128)(2,1)S(1)} collective-permute-done((bf16[256,512]{1,0:T(8,128)(2,1)S(1)}, bf16[256,512]{1,0:T(8,128)(2,1)S(1)}, u32[]{:S(2)}, u32[]{:S(2)}) %collective-permute-start.17) | collective-permute-done | bytes 262176 | tf_op jit(solution)/shard_map/ppermute | solution.py:474
  79.3 3.6 %all-to-all-start.1 = ((bf16[8,256,256]{2,1,0:T(8,128)(2,1)}), bf16[8,256,256]{2,1,0:T(8,128)(2,1)S(1)}, u32[]{:S(2)}, u32[]{:S(2)}) async-start(bf16[8,256,256]{2,1,0:T(8,128)(2,1)} %first_partial.1), calls=%async_computation.1 | async-start | bytes 2097152 | tf_op jit(solution)/shard_map/all_to_all | solution.py:476
  82.9 13.7 %solve.1 = (f32[128,1024]{1,0:T(8,128)}, f32[128,1024]{1,0:T(8,128)}, f32[128,1024]{1,0:T(8,128)}, bf16[144,256]{1,0:T(8,128)(2,1)}, bf16[144,256]{1,0:T(8,128)(...) custom-call(s32[5]{0:T(128)S(1)} %stack.23.place, bf16[256,512]{1,0:T(8,128)(2,1)} %get-tuple-element.50.near0, ...), custom_call_target="tpu_custom_call" | custom-call | tf_op jit(solution)/shard_map/solve/pallas_call | solution.py:439
  97.3 2.6 %collective-permute-start.19 = (bf16[144,256]{1,0:T(8,128)(2,1)}, bf16[144,256]{1,0:T(8,128)(2,1)S(1)}, u32[]{:S(2)}, u32[]{:S(2)}) collective-permute-start(bf16[144,256]{1,0:T(8,128)(2,1)} %get-tuple-element.62), channel_id=1, source_target_pairs={{0,2},{1,3},{2,0},{3,1},{4,6},{5,7},{6,4},{7,5},{8,10},{9,11},{10,... | collective-permute-start | bytes 221192 | tf_op jit(solution)/shard_map/ppermute | solution.py:480
  101.6 1.9 %collective-permute-done.19.u2 = bf16[144,256]{1,0:T(8,128)(2,1)S(1)} collective-permute-done((bf16[144,256]{1,0:T(8,128)(2,1)}, bf16[144,256]{1,0:T(8,128)(2,1)S(1)}, u32[]{:S(2)}, u32[]{:S(2)}) %collective-permute-start.19) | collective-permute-done | bytes 73760 | tf_op jit(solution)/shard_map/ppermute | solution.py:480
  104.3 3.0 %second_partial.1 = bf16[8,272,256]{2,1,0:T(8,128)(2,1)} custom-call(s32[5]{0:T(128)S(1)} %stack.23.place, bf16[144,256]{1,0:T(8,128)(2,1)} %get-tuple-element.60.own_hbm, bf16[144,256]{1,0:T(8,128)(2,1)S(1)} %collective-permute-done.18.u1, bf16[144,256]{1,0:T(8,128)(2,1)S(1)} %collective-permute-done.19.u2, ...), custom_call_target="tpu_custom_call" | custom-call | tf_op jit(solution)/shard_map/second_partial/pallas_call | solution.py:249
  107.3 4.7 %all-to-all-done.1.parts_ref = bf16[8,256,256]{2,1,0:T(8,128)(2,1)S(1)} async-done(((bf16[8,256,256]{2,1,0:T(8,128)(2,1)}), bf16[8,256,256]{2,1,0:T(8,128)(2,1)S(1)}, u32[]{:S(2)}, u32[]{:S(2)}) %all-to-all-start.1) | async-done | bytes 1048608 | tf_op jit(solution)/shard_map/all_to_all | solution.py:476
  112.0 3.6 %all-to-all-start.2 = ((bf16[8,272,256]{2,1,0:T(8,128)(2,1)}), bf16[8,272,256]{2,1,0:T(8,128)(2,1)S(1)}, u32[]{:S(2)}, u32[]{:S(2)}) async-start(bf16[8,272,256]{2,1,0:T(8,128)(2,1)} %second_partial.1), calls=%async_computation.2 | async-start | bytes 2228224 | tf_op jit(solution)/shard_map/all_to_all | solution.py:483
  116.3 29.9 %all-to-all-done.2.parts_ref = bf16[8,272,256]{2,1,0:T(8,128)(2,1)S(1)} async-done(((bf16[8,272,256]{2,1,0:T(8,128)(2,1)}), bf16[8,272,256]{2,1,0:T(8,128)(2,1)S(1)}, u32[]{:S(2)}, u32[]{:S(2)}) %all-to-all-start.2) | async-done | bytes 1114144 | tf_op jit(solution)/shard_map/all_to_all | solution.py:483
  147.0 1.9 %collective-permute-start.21 = (bf16[2,256,256]{2,1,0:T(8,128)(2,1)S(1)}, bf16[2,256,256]{2,1,0:T(8,128)(2,1)S(1)}, u32[]{:S(2)}, u32[]{:S(2)}) collective-permute-start(bf16[2,256,256]{2,1,0:T(8,128)(2,1)S(1)} %get-tuple-element.68), channel_id=1, source_target_pairs={{0,0},{1,1},{2,2},{3,3},{4,32},{5,33},{6,34},{7,35},{8,64},{9,65},... | collective-permute-start | bytes 786440 | tf_op jit(solution)/shard_map/ppermute | solution.py:485
  151.0 16.7 %collective-permute-done.21 = bf16[2,256,256]{2,1,0:T(8,128)(2,1)S(1)} collective-permute-done((bf16[2,256,256]{2,1,0:T(8,128)(2,1)S(1)}, bf16[2,256,256]{2,1,0:T(8,128)(2,1)S(1)}, u32[]{:S(2)}, u32[]{:S(2)}) %collective-permute-start.21) | collective-permute-done | bytes 262176 | tf_op jit(solution)/shard_map/ppermute | solution.py:485
  (43 shorter events, 26.2 us)
Async XLA Ops:
  0.6 17.6 %collective-permute-start = (bf16[256,256]{1,0:T(8,128)(2,1)}, bf16[256,256]{1,0:T(8,128)(2,1)S(1)}, u32[]{:S(2)}, u32[]{:S(2)}) collective-permute-start(bf16[256,256]{1,0:T(8,128)(2,1)} %param.6), channel_id=1, source_target_pairs={{0,0},{1,1},{2,2},{3,3},{4,32},{5,33},{6,34},{7,35},{8,64},{9,65},... | collective-permute-start | bytes 393224 | tf_op jit(solution)/shard_map/ppermute | solution.py:459
  10.3 7.9 %collective-permute-start.1 = (bf16[512,128]{1,0:T(8,128)(2,1)S(1)}, bf16[512,128]{1,0:T(8,128)(2,1)S(1)}, u32[]{:S(2)}, u32[]{:S(2)}) collective-permute-start(bf16[512,128]{1,0:T(8,128)(2,1)S(1)} %get-tuple-element.39), channel_id=1, source_target_pairs={{0,1},{1,2},{2,3},{3,0},{4,5},{5,6},{6,7},{7,4},{8,9},{9,10},{10,1... | collective-permute-start | bytes 393224 | tf_op jit(solution)/shard_map/ppermute | solution.py:461
  11.7 8.1 %collective-permute-start.2 = (bf16[512,128]{1,0:T(8,128)(2,1)S(1)}, bf16[512,128]{1,0:T(8,128)(2,1)S(1)}, u32[]{:S(2)}, u32[]{:S(2)}) collective-permute-start(bf16[512,128]{1,0:T(8,128)(2,1)S(1)} %get-tuple-element.40), channel_id=1, source_target_pairs={{0,2},{1,3},{2,0},{3,1},{4,6},{5,7},{6,4},{7,5},{8,10},{9,11},{10,... | collective-permute-start | bytes 393224 | tf_op jit(solution)/shard_map/ppermute | solution.py:461
  14.3 5.5 %collective-permute-start.3 = (bf16[512,128]{1,0:T(8,128)(2,1)S(1)}, bf16[512,128]{1,0:T(8,128)(2,1)S(1)}, u32[]{:S(2)}, u32[]{:S(2)}) collective-permute-start(bf16[512,128]{1,0:T(8,128)(2,1)S(1)} %get-tuple-element.41), channel_id=1, source_target_pairs={{0,3},{1,0},{2,1},{3,2},{4,7},{5,4},{6,5},{7,6},{8,11},{9,8},{10,9... | collective-permute-start | bytes 393224 | tf_op jit(solution)/shard_map/ppermute | solution.py:461
  20.9 34.8 %all-to-all-start = ((bf16[8,256,256]{2,1,0:T(8,128)(2,1)}), bf16[8,256,256]{2,1,0:T(8,128)(2,1)S(1)}, u32[]{:S(2)}, u32[]{:S(2)}) async-start(bf16[8,256,256]{2,1,0:T(8,128)(2,1)} %broadcast_in_dim.9), calls=%async_computation | async-start | bytes 2097152 | tf_op jit(solution)/shard_map/all_to_all | solution.py:52
  27.1 13.7 %collective-permute-start.6 = (bf16[4,256,128]{2,1,0:T(8,128)(2,1)S(1)}, bf16[4,256,128]{2,1,0:T(8,128)(2,1)S(1)}, u32[]{:S(2)}, u32[]{:S(2)}) collective-permute-start(bf16[4,256,128]{2,1,0:T(8,128)(2,1)S(1)} %get-tuple-element.48.refs_0_), channel_id=1, source_target_pairs={{0,192},{64,0},{128,64},{192,128},{1,193},{65,1},{129,65},{193,129... | collective-permute-start | bytes 786440 | tf_op jit(solution)/shard_map/ppermute | solution.py:465
  27.2 15.5 %collective-permute-start.5 = (bf16[4,256,128]{2,1,0:T(8,128)(2,1)S(1)}, bf16[4,256,128]{2,1,0:T(8,128)(2,1)S(1)}, u32[]{:S(2)}, u32[]{:S(2)}) collective-permute-start(bf16[4,256,128]{2,1,0:T(8,128)(2,1)S(1)} %get-tuple-element.48.refs_0_), channel_id=1, source_target_pairs={{0,128},{64,192},{128,0},{192,64},{1,129},{65,193},{129,1},{193,65... | collective-permute-start | bytes 786440 | tf_op jit(solution)/shard_map/ppermute | solution.py:465
  28.0 14.7 %collective-permute-start.4 = (bf16[4,256,128]{2,1,0:T(8,128)(2,1)S(1)}, bf16[4,256,128]{2,1,0:T(8,128)(2,1)S(1)}, u32[]{:S(2)}, u32[]{:S(2)}) collective-permute-start(bf16[4,256,128]{2,1,0:T(8,128)(2,1)S(1)} %get-tuple-element.48.refs_0_), channel_id=1, source_target_pairs={{0,64},{64,128},{128,192},{192,0},{1,65},{65,129},{129,193},{193,1... | collective-permute-start | bytes 786440 | tf_op jit(solution)/shard_map/ppermute | solution.py:465
  29.9 13.5 %collective-permute-start.7 = (bf16[4,256,128]{2,1,0:T(8,128)(2,1)S(1)}, bf16[4,256,128]{2,1,0:T(8,128)(2,1)S(1)}, u32[]{:S(2)}, u32[]{:S(2)}) collective-permute-start(bf16[4,256,128]{2,1,0:T(8,128)(2,1)S(1)} %get-tuple-element.48.refs_0_), channel_id=1, source_target_pairs={{0,32},{32,0},{1,33},{33,1},{2,34},{34,2},{3,35},{35,3},{4,36},{36... | collective-permute-start | bytes 786440 | tf_op jit(solution)/shard_map/ppermute | solution.py:466
  40.8 3.1 %collective-permute-start.10 = (bf16[4,256,128]{2,1,0:T(8,128)(2,1)S(1)}, bf16[4,256,128]{2,1,0:T(8,128)(2,1)S(1)}, u32[]{:S(2)}, u32[]{:S(2)}) collective-permute-start(bf16[4,256,128]{2,1,0:T(8,128)(2,1)S(1)} %collective-permute-done.6.refs_3_), channel_id=1, source_target_pairs={{0,32},{32,0},{1,33},{33,1},{2,34},{34,2},{3,35},{35,3},{4,36},{36... | collective-permute-start | bytes 786440 | tf_op jit(solution)/shard_map/ppermute | solution.py:466
  42.8 1.9 %collective-permute-start.8 = (bf16[4,256,128]{2,1,0:T(8,128)(2,1)S(1)}, bf16[4,256,128]{2,1,0:T(8,128)(2,1)S(1)}, u32[]{:S(2)}, u32[]{:S(2)}) collective-permute-start(bf16[4,256,128]{2,1,0:T(8,128)(2,1)S(1)} %collective-permute-done.4.refs_1_), channel_id=1, source_target_pairs={{0,32},{32,0},{1,33},{33,1},{2,34},{34,2},{3,35},{35,3},{4,36},{36... | collective-permute-start | bytes 786440 | tf_op jit(solution)/shard_map/ppermute | solution.py:466
  58.3 7.5 %collective-permute-start.14 = (bf16[256,512]{1,0:T(8,128)(2,1)S(1)}, bf16[256,512]{1,0:T(8,128)(2,1)S(1)}, u32[]{:S(2)}, u32[]{:S(2)}) collective-permute-start(bf16[256,512]{1,0:T(8,128)(2,1)S(1)} %get-tuple-element.52), channel_id=1, source_target_pairs={{0,4},{4,0},{1,5},{5,1},{2,6},{6,2},{3,7},{7,3},{8,12},{12,8},{9,1... | collective-permute-start | bytes 786440 | tf_op jit(solution)/shard_map/ppermute | solution.py:471
  58.4 9.4 %collective-permute-start.12 = (bf16[256,512]{1,0:T(8,128)(2,1)S(1)}, bf16[256,512]{1,0:T(8,128)(2,1)S(1)}, u32[]{:S(2)}, u32[]{:S(2)}) collective-permute-start(bf16[256,512]{1,0:T(8,128)(2,1)S(1)} %get-tuple-element.52), channel_id=1, source_target_pairs={{0,2},{1,3},{2,0},{3,1},{4,6},{5,7},{6,4},{7,5},{8,10},{9,11},{10,... | collective-permute-start | bytes 786440 | tf_op jit(solution)/shard_map/ppermute | solution.py:472
  60.4 11.9 %collective-permute-start.13 = (bf16[256,512]{1,0:T(8,128)(2,1)S(1)}, bf16[256,512]{1,0:T(8,128)(2,1)S(1)}, u32[]{:S(2)}, u32[]{:S(2)}) collective-permute-start(bf16[256,512]{1,0:T(8,128)(2,1)S(1)} %get-tuple-element.52), channel_id=1, source_target_pairs={{0,3},{1,0},{2,1},{3,2},{4,7},{5,4},{6,5},{7,6},{8,11},{9,8},{10,9... | collective-permute-start | bytes 786440 | tf_op jit(solution)/shard_map/ppermute | solution.py:472
  61.4 12.3 %collective-permute-start.11 = (bf16[256,512]{1,0:T(8,128)(2,1)S(1)}, bf16[256,512]{1,0:T(8,128)(2,1)S(1)}, u32[]{:S(2)}, u32[]{:S(2)}) collective-permute-start(bf16[256,512]{1,0:T(8,128)(2,1)S(1)} %get-tuple-element.52), channel_id=1, source_target_pairs={{0,1},{1,2},{2,3},{3,0},{4,5},{5,6},{6,7},{7,4},{8,9},{9,10},{10,1... | collective-permute-start | bytes 786440 | tf_op jit(solution)/shard_map/ppermute | solution.py:472
  65.7 12.2 %collective-permute-start.17 = (bf16[256,512]{1,0:T(8,128)(2,1)S(1)}, bf16[256,512]{1,0:T(8,128)(2,1)S(1)}, u32[]{:S(2)}, u32[]{:S(2)}) collective-permute-start(bf16[256,512]{1,0:T(8,128)(2,1)S(1)} %collective-permute-done.14.far0), channel_id=1, source_target_pairs={{0,3},{1,0},{2,1},{3,2},{4,7},{5,4},{6,5},{7,6},{8,11},{9,8},{10,9... | collective-permute-start | bytes 786440 | tf_op jit(solution)/shard_map/ppermute | solution.py:474
  67.7 11.6 %collective-permute-start.15 = (bf16[256,512]{1,0:T(8,128)(2,1)S(1)}, bf16[256,512]{1,0:T(8,128)(2,1)S(1)}, u32[]{:S(2)}, u32[]{:S(2)}) collective-permute-start(bf16[256,512]{1,0:T(8,128)(2,1)S(1)} %collective-permute-done.14.far0), channel_id=1, source_target_pairs={{0,1},{1,2},{2,3},{3,0},{4,5},{5,6},{6,7},{7,4},{8,9},{9,10},{10,1... | collective-permute-start | bytes 786440 | tf_op jit(solution)/shard_map/ppermute | solution.py:473
  67.7 11.6 %collective-permute-start.16 = (bf16[256,512]{1,0:T(8,128)(2,1)S(1)}, bf16[256,512]{1,0:T(8,128)(2,1)S(1)}, u32[]{:S(2)}, u32[]{:S(2)}) collective-permute-start(bf16[256,512]{1,0:T(8,128)(2,1)S(1)} %collective-permute-done.12.near2), channel_id=1, source_target_pairs={{0,4},{4,0},{1,5},{5,1},{2,6},{6,2},{3,7},{7,3},{8,12},{12,8},{9,1... | collective-permute-start | bytes 786440 | tf_op jit(solution)/shard_map/ppermute | solution.py:473
  79.3 32.7 %all-to-all-start.1 = ((bf16[8,256,256]{2,1,0:T(8,128)(2,1)}), bf16[8,256,256]{2,1,0:T(8,128)(2,1)S(1)}, u32[]{:S(2)}, u32[]{:S(2)}) async-start(bf16[8,256,256]{2,1,0:T(8,128)(2,1)} %first_partial.1), calls=%async_computation.1 | async-start | bytes 2097152 | tf_op jit(solution)/shard_map/all_to_all | solution.py:476
  96.6 5.0 %collective-permute-start.18 = (bf16[144,256]{1,0:T(8,128)(2,1)}, bf16[144,256]{1,0:T(8,128)(2,1)S(1)}, u32[]{:S(2)}, u32[]{:S(2)}) collective-permute-start(bf16[144,256]{1,0:T(8,128)(2,1)} %get-tuple-element.61), channel_id=1, source_target_pairs={{0,1},{1,2},{2,3},{3,0},{4,5},{5,6},{6,7},{7,4},{8,9},{9,10},{10,1... | collective-permute-start | bytes 221192 | tf_op jit(solution)/shard_map/ppermute | solution.py:480
  97.3 6.2 %collective-permute-start.19 = (bf16[144,256]{1,0:T(8,128)(2,1)}, bf16[144,256]{1,0:T(8,128)(2,1)S(1)}, u32[]{:S(2)}, u32[]{:S(2)}) collective-permute-start(bf16[144,256]{1,0:T(8,128)(2,1)} %get-tuple-element.62), channel_id=1, source_target_pairs={{0,2},{1,3},{2,0},{3,1},{4,6},{5,7},{6,4},{7,5},{8,10},{9,11},{10,... | collective-permute-start | bytes 221192 | tf_op jit(solution)/shard_map/ppermute | solution.py:480
  100.0 4.4 %collective-permute-start.20 = (bf16[144,256]{1,0:T(8,128)(2,1)}, bf16[144,256]{1,0:T(8,128)(2,1)S(1)}, u32[]{:S(2)}, u32[]{:S(2)}) collective-permute-start(bf16[144,256]{1,0:T(8,128)(2,1)} %get-tuple-element.63), channel_id=1, source_target_pairs={{0,3},{1,0},{2,1},{3,2},{4,7},{5,4},{6,5},{7,6},{8,11},{9,8},{10,9... | collective-permute-start | bytes 221192 | tf_op jit(solution)/shard_map/ppermute | solution.py:480
  112.0 34.2 %all-to-all-start.2 = ((bf16[8,272,256]{2,1,0:T(8,128)(2,1)}), bf16[8,272,256]{2,1,0:T(8,128)(2,1)S(1)}, u32[]{:S(2)}, u32[]{:S(2)}) async-start(bf16[8,272,256]{2,1,0:T(8,128)(2,1)} %second_partial.1), calls=%async_computation.2 | async-start | bytes 2228224 | tf_op jit(solution)/shard_map/all_to_all | solution.py:483
  147.0 20.6 %collective-permute-start.21 = (bf16[2,256,256]{2,1,0:T(8,128)(2,1)S(1)}, bf16[2,256,256]{2,1,0:T(8,128)(2,1)S(1)}, u32[]{:S(2)}, u32[]{:S(2)}) collective-permute-start(bf16[2,256,256]{2,1,0:T(8,128)(2,1)S(1)} %get-tuple-element.68), channel_id=1, source_target_pairs={{0,0},{1,1},{2,2},{3,3},{4,32},{5,33},{6,34},{7,35},{8,64},{9,65},... | collective-permute-start | bytes 786440 | tf_op jit(solution)/shard_map/ppermute | solution.py:485
  (3 other events, 65.1 us)

commit v12 on v11

--- a/solution.py
+++ b/solution.py
@@ -459,7 +459,9 @@
     cot_turned = lax.ppermute(cotangent, AXES, SWAP)
     packed = pack(place, activations, weight)
     crossed = [lax.ppermute(packed[d], "y", shift(d)) for d in range(1, 4)]
-    cot_turned, *crossed = lax.optimization_barrier((cot_turned, *crossed))
+    cot_turned, crossed[0], crossed[2] = lax.optimization_barrier(
+        (cot_turned, crossed[0], crossed[2])
+    )
     cot_all = copies_to(cot_turned, ZAX, 8)
     slab, near_w = unpack(place, [packed[0], *crossed])
     own = [slab] + [lax.ppermute(slab, "x", shift(d)) for d in range(1, 4)]

time: 171 us -> 171 us (level)
  the two profiles are of different devices: /device:TPU:7 before, /device:TPU:23 now
where the time goes in v12:
time: 171 us; the launch traced here: 170 us
  waiting for transfers between devices  93 us (54%)
  starting transfers between devices  47.7 us (28%)
  Pallas kernels  25 us (15%)
  local copies, waits for them, and re-layouts  2.38 us (1%)
    all_to_all x1, waiting for transfers between devices, body(): arrived = lax.all_to_all(second, ZAX, 0, 0, tiled=True)  29.9 us
    ppermute x1, waiting for transfers between devices, body(): outs = lax.ppermute(outs, AXES, HOME)  20.8 us
    pallas_call x1, Pallas kernels, solve(): call(solver_body, [HBM, *[VMEM] * 7, HBM, HBM], [HBM] * 7, [rows, rows, r...  13.7 us
    ppermute x3, waiting for transfers between devices, body(): lax.ppermute(piece, 'y', shift(d))  9.16 us
    ppermute x4, starting transfers between devices, body(): swapped = [lax.ppermute(part, 'c', FLIP) for part in own]  9.03 us
    ppermute x1, starting transfers between devices, body(): cot_turned = lax.ppermute(cotangent, AXES, SWAP)  7.96 us
    ppermute x3, starting transfers between devices, body(): own = [slab] + [lax.ppermute(slab, 'x', shift(d)) for d in range(1, 4)]  7.06 us
    ppermute x1, waiting for transfers between devices, body(): cot_turned = lax.ppermute(cotangent, AXES, SWAP)  6.4 us
  transfers between devices with their start and end apart: 25, of which 17 were waited for; matrix products, arithmetic and copies ran while one was open for 1% of the time, Pallas kernels for 13%

profile of v12, /device:TPU:23, one launch (start us, length us, event | category | flops | bytes accessed | tf_op | source)
XLA Modules:
  0.0 170.3 jit_solution(16352381352649484832)
XLA Ops:
  0.6 8.0 %collective-permute-start = (bf16[256,256]{1,0:T(8,128)(2,1)}, bf16[256,256]{1,0:T(8,128)(2,1)S(1)}, u32[]{:S(2)}, u32[]{:S(2)}) collective-permute-start(bf16[256,256]{1,0:T(8,128)(2,1)} %param.6), channel_id=1, source_target_pairs={{0,0},{1,1},{2,2},{3,3},{4,32},{5,33},{6,34},{7,35},{8,64},{9,65},... | collective-permute-start | bytes 393224 | tf_op jit(solution)/shard_map/ppermute | solution.py:459
  11.8 6.4 %collective-permute-done = bf16[256,256]{1,0:T(8,128)(2,1)S(1)} collective-permute-done((bf16[256,256]{1,0:T(8,128)(2,1)}, bf16[256,256]{1,0:T(8,128)(2,1)S(1)}, u32[]{:S(2)}, u32[]{:S(2)}) %collective-permute-start) | collective-permute-done | bytes 131104 | tf_op jit(solution)/shard_map/ppermute | solution.py:459
  19.3 3.6 %all-to-all-start = ((bf16[8,256,256]{2,1,0:T(8,128)(2,1)}), bf16[8,256,256]{2,1,0:T(8,128)(2,1)S(1)}, u32[]{:S(2)}, u32[]{:S(2)}) async-start(bf16[8,256,256]{2,1,0:T(8,128)(2,1)} %broadcast_in_dim.9), calls=%async_computation | async-start | bytes 2097152 | tf_op jit(solution)/shard_map/all_to_all | solution.py:52
  23.0 5.3 %collective-permute-done.3.refs_2_ = bf16[512,128]{1,0:T(8,128)(2,1)S(1)} collective-permute-done((bf16[512,128]{1,0:T(8,128)(2,1)S(1)}, bf16[512,128]{1,0:T(8,128)(2,1)S(1)}, u32[]{:S(2)}, u32[]{:S(2)}) %collective-permute-start.3) | collective-permute-done | bytes 131104 | tf_op jit(solution)/shard_map/ppermute | solution.py:461
  30.4 3.5 %collective-permute-start.5 = (bf16[4,256,128]{2,1,0:T(8,128)(2,1)S(1)}, bf16[4,256,128]{2,1,0:T(8,128)(2,1)S(1)}, u32[]{:S(2)}, u32[]{:S(2)}) collective-permute-start(bf16[4,256,128]{2,1,0:T(8,128)(2,1)S(1)} %get-tuple-element.46.refs_0_), channel_id=1, source_target_pairs={{0,128},{64,192},{128,0},{192,64},{1,129},{65,193},{129,1},{193,65... | collective-permute-start | bytes 786440 | tf_op jit(solution)/shard_map/ppermute | solution.py:467
  34.0 2.0 %collective-permute-start.4 = (bf16[4,256,128]{2,1,0:T(8,128)(2,1)S(1)}, bf16[4,256,128]{2,1,0:T(8,128)(2,1)S(1)}, u32[]{:S(2)}, u32[]{:S(2)}) collective-permute-start(bf16[4,256,128]{2,1,0:T(8,128)(2,1)S(1)} %get-tuple-element.46.refs_0_), channel_id=1, source_target_pairs={{0,64},{64,128},{128,192},{192,0},{1,65},{65,129},{129,193},{193,1... | collective-permute-start | bytes 786440 | tf_op jit(solution)/shard_map/ppermute | solution.py:467
  37.5 4.6 %collective-permute-start.10 = (bf16[4,256,128]{2,1,0:T(8,128)(2,1)S(1)}, bf16[4,256,128]{2,1,0:T(8,128)(2,1)S(1)}, u32[]{:S(2)}, u32[]{:S(2)}) collective-permute-start(bf16[4,256,128]{2,1,0:T(8,128)(2,1)S(1)} %collective-permute-done.6.refs_3_), channel_id=1, source_target_pairs={{0,32},{32,0},{1,33},{33,1},{2,34},{34,2},{3,35},{35,3},{4,36},{36... | collective-permute-start | bytes 786440 | tf_op jit(solution)/shard_map/ppermute | solution.py:468
  43.9 2.8 %collective-permute-start.9 = (bf16[4,256,128]{2,1,0:T(8,128)(2,1)S(1)}, bf16[4,256,128]{2,1,0:T(8,128)(2,1)S(1)}, u32[]{:S(2)}, u32[]{:S(2)}) collective-permute-start(bf16[4,256,128]{2,1,0:T(8,128)(2,1)S(1)} %collective-permute-done.5.refs_2_), channel_id=1, source_target_pairs={{0,32},{32,0},{1,33},{33,1},{2,34},{34,2},{3,35},{35,3},{4,36},{36... | collective-permute-start | bytes 786440 | tf_op jit(solution)/shard_map/ppermute | solution.py:468
  48.3 2.1 %first_partial.1 = bf16[8,256,256]{2,1,0:T(8,128)(2,1)} custom-call(s32[5]{0:T(128)S(1)} %stack.23.place, bf16[4,256,128]{2,1,0:T(8,128)(2,1)S(1)} %get-tuple-element.45.weight_ref, bf16[4,256,128]{2,1,0:T(8,128)(2,1)S(1)} %get-tuple-element.46.refs_0_, bf16[4,256,128]{2,1,0:T(8,128)(2,1)S(1)} %collective-permute-done.4.refs_1_, ...), custom_call_target="tpu_custom_call" | custom-call | tf_op jit(solution)/shard_map/first_partial/pallas_call | solution.py:202
  50.4 2.5 %grad_piece.1 = (bf16[256,512]{1,0:T(8,128)(2,1)S(1)}, bf16[256,512]{1,0:T(8,128)(2,1)}, bf16[8,4,256,128]{3,2,1,0:T(8,128)(2,1)}) custom-call(s32[5]{0:T(128)S(1)} %stack.23.place, bf16[8,256,256]{2,1,0:T(8,128)(2,1)S(1)} %all-to-all-done.cot_ref, bf16[4,256,128]{2,1,0:T(8,128)(2,1)S(1)} %get-tuple-element.46.refs_0_, ...), custom_call_target="tpu_custom_call" | custom-call | tf_op jit(solution)/shard_map/grad_piece/pallas_call | solution.py:168
  54.2 2.1 %collective-permute-start.13 = (bf16[256,512]{1,0:T(8,128)(2,1)S(1)}, bf16[256,512]{1,0:T(8,128)(2,1)S(1)}, u32[]{:S(2)}, u32[]{:S(2)}) collective-permute-start(bf16[256,512]{1,0:T(8,128)(2,1)S(1)} %get-tuple-element.50), channel_id=1, source_target_pairs={{0,3},{1,0},{2,1},{3,2},{4,7},{5,4},{6,5},{7,6},{8,11},{9,8},{10,9... | collective-permute-start | bytes 786440 | tf_op jit(solution)/shard_map/ppermute | solution.py:474
  56.3 2.3 %collective-permute-done.14.far0 = bf16[256,512]{1,0:T(8,128)(2,1)S(1)} collective-permute-done((bf16[256,512]{1,0:T(8,128)(2,1)S(1)}, bf16[256,512]{1,0:T(8,128)(2,1)S(1)}, u32[]{:S(2)}, u32[]{:S(2)}) %collective-permute-start.14) | collective-permute-done | bytes 262176 | tf_op jit(solution)/shard_map/ppermute | solution.py:473
  62.1 5.3 %collective-permute-done.13.near3 = bf16[256,512]{1,0:T(8,128)(2,1)S(1)} collective-permute-done((bf16[256,512]{1,0:T(8,128)(2,1)S(1)}, bf16[256,512]{1,0:T(8,128)(2,1)S(1)}, u32[]{:S(2)}, u32[]{:S(2)}) %collective-permute-start.13) | collective-permute-done | bytes 262176 | tf_op jit(solution)/shard_map/ppermute | solution.py:474
  67.4 2.0 %collective-permute-done.11.near1 = bf16[256,512]{1,0:T(8,128)(2,1)S(1)} collective-permute-done((bf16[256,512]{1,0:T(8,128)(2,1)S(1)}, bf16[256,512]{1,0:T(8,128)(2,1)S(1)}, u32[]{:S(2)}, u32[]{:S(2)}) %collective-permute-start.11) | collective-permute-done | bytes 262176 | tf_op jit(solution)/shard_map/ppermute | solution.py:474
  69.5 3.6 %collective-permute-done.17.far3 = bf16[256,512]{1,0:T(8,128)(2,1)S(1)} collective-permute-done((bf16[256,512]{1,0:T(8,128)(2,1)S(1)}, bf16[256,512]{1,0:T(8,128)(2,1)S(1)}, u32[]{:S(2)}, u32[]{:S(2)}) %collective-permute-start.17) | collective-permute-done | bytes 262176 | tf_op jit(solution)/shard_map/ppermute | solution.py:476
  73.1 2.0 %collective-permute-done.15.far1 = bf16[256,512]{1,0:T(8,128)(2,1)S(1)} collective-permute-done((bf16[256,512]{1,0:T(8,128)(2,1)S(1)}, bf16[256,512]{1,0:T(8,128)(2,1)S(1)}, u32[]{:S(2)}, u32[]{:S(2)}) %collective-permute-start.15) | collective-permute-done | bytes 262176 | tf_op jit(solution)/shard_map/ppermute | solution.py:475
  75.1 5.5 %all-to-all-start.1 = ((bf16[8,256,256]{2,1,0:T(8,128)(2,1)}), bf16[8,256,256]{2,1,0:T(8,128)(2,1)S(1)}, u32[]{:S(2)}, u32[]{:S(2)}) async-start(bf16[8,256,256]{2,1,0:T(8,128)(2,1)} %first_partial.1), calls=%async_computation.1 | async-start | bytes 2097152 | tf_op jit(solution)/shard_map/all_to_all | solution.py:478
  80.6 13.7 %solve.1 = (f32[128,1024]{1,0:T(8,128)}, f32[128,1024]{1,0:T(8,128)}, f32[128,1024]{1,0:T(8,128)}, bf16[144,256]{1,0:T(8,128)(2,1)}, bf16[144,256]{1,0:T(8,128)(...) custom-call(s32[5]{0:T(128)S(1)} %stack.23.place, bf16[256,512]{1,0:T(8,128)(2,1)} %get-tuple-element.48.near0, ...), custom_call_target="tpu_custom_call" | custom-call | tf_op jit(solution)/shard_map/solve/pallas_call | solution.py:439
  98.1 2.5 %collective-permute-done.19.u2 = bf16[144,256]{1,0:T(8,128)(2,1)S(1)} collective-permute-done((bf16[144,256]{1,0:T(8,128)(2,1)}, bf16[144,256]{1,0:T(8,128)(2,1)S(1)}, u32[]{:S(2)}, u32[]{:S(2)}) %collective-permute-start.19) | collective-permute-done | bytes 73760 | tf_op jit(solution)/shard_map/ppermute | solution.py:482
  100.7 3.0 %second_partial.1 = bf16[8,272,256]{2,1,0:T(8,128)(2,1)} custom-call(s32[5]{0:T(128)S(1)} %stack.23.place, bf16[144,256]{1,0:T(8,128)(2,1)} %get-tuple-element.58.own_hbm, bf16[144,256]{1,0:T(8,128)(2,1)S(1)} %collective-permute-done.18.u1, bf16[144,256]{1,0:T(8,128)(2,1)S(1)} %collective-permute-done.19.u2, ...), custom_call_target="tpu_custom_call" | custom-call | tf_op jit(solution)/shard_map/second_partial/pallas_call | solution.py:249
  103.7 6.1 %all-to-all-done.1.parts_ref = bf16[8,256,256]{2,1,0:T(8,128)(2,1)S(1)} async-done(((bf16[8,256,256]{2,1,0:T(8,128)(2,1)}), bf16[8,256,256]{2,1,0:T(8,128)(2,1)S(1)}, u32[]{:S(2)}, u32[]{:S(2)}) %all-to-all-start.1) | async-done | bytes 1048608 | tf_op jit(solution)/shard_map/all_to_all | solution.py:478
  109.8 3.6 %all-to-all-start.2 = ((bf16[8,272,256]{2,1,0:T(8,128)(2,1)}), bf16[8,272,256]{2,1,0:T(8,128)(2,1)S(1)}, u32[]{:S(2)}, u32[]{:S(2)}) async-start(bf16[8,272,256]{2,1,0:T(8,128)(2,1)} %second_partial.1), calls=%async_computation.2 | async-start | bytes 2228224 | tf_op jit(solution)/shard_map/all_to_all | solution.py:485
  114.1 29.9 %all-to-all-done.2.parts_ref = bf16[8,272,256]{2,1,0:T(8,128)(2,1)S(1)} async-done(((bf16[8,272,256]{2,1,0:T(8,128)(2,1)}), bf16[8,272,256]{2,1,0:T(8,128)(2,1)S(1)}, u32[]{:S(2)}, u32[]{:S(2)}) %all-to-all-start.2) | async-done | bytes 1114144 | tf_op jit(solution)/shard_map/all_to_all | solution.py:485
  148.8 20.8 %collective-permute-done.21 = bf16[2,256,256]{2,1,0:T(8,128)(2,1)S(1)} collective-permute-done((bf16[2,256,256]{2,1,0:T(8,128)(2,1)S(1)}, bf16[2,256,256]{2,1,0:T(8,128)(2,1)S(1)}, u32[]{:S(2)}, u32[]{:S(2)}) %collective-permute-start.21) | collective-permute-done | bytes 262176 | tf_op jit(solution)/shard_map/ppermute | solution.py:487
  (43 shorter events, 26.3 us)
Async XLA Ops:
  0.6 17.6 %collective-permute-start = (bf16[256,256]{1,0:T(8,128)(2,1)}, bf16[256,256]{1,0:T(8,128)(2,1)S(1)}, u32[]{:S(2)}, u32[]{:S(2)}) collective-permute-start(bf16[256,256]{1,0:T(8,128)(2,1)} %param.6), channel_id=1, source_target_pairs={{0,0},{1,1},{2,2},{3,3},{4,32},{5,33},{6,34},{7,35},{8,64},{9,65},... | collective-permute-start | bytes 393224 | tf_op jit(solution)/shard_map/ppermute | solution.py:459
  10.3 7.9 %collective-permute-start.1 = (bf16[512,128]{1,0:T(8,128)(2,1)S(1)}, bf16[512,128]{1,0:T(8,128)(2,1)S(1)}, u32[]{:S(2)}, u32[]{:S(2)}) collective-permute-start(bf16[512,128]{1,0:T(8,128)(2,1)S(1)} %get-tuple-element.38), channel_id=1, source_target_pairs={{0,1},{1,2},{2,3},{3,0},{4,5},{5,6},{6,7},{7,4},{8,9},{9,10},{10,1... | collective-permute-start | bytes 393224 | tf_op jit(solution)/shard_map/ppermute | solution.py:461
  11.4 6.9 %collective-permute-start.2 = (bf16[512,128]{1,0:T(8,128)(2,1)S(1)}, bf16[512,128]{1,0:T(8,128)(2,1)S(1)}, u32[]{:S(2)}, u32[]{:S(2)}) collective-permute-start(bf16[512,128]{1,0:T(8,128)(2,1)S(1)} %get-tuple-element.39), channel_id=1, source_target_pairs={{0,3},{1,0},{2,1},{3,2},{4,7},{5,4},{6,5},{7,6},{8,11},{9,8},{10,9... | collective-permute-start | bytes 393224 | tf_op jit(solution)/shard_map/ppermute | solution.py:461
  19.3 31.0 %all-to-all-start = ((bf16[8,256,256]{2,1,0:T(8,128)(2,1)}), bf16[8,256,256]{2,1,0:T(8,128)(2,1)S(1)}, u32[]{:S(2)}, u32[]{:S(2)}) async-start(bf16[8,256,256]{2,1,0:T(8,128)(2,1)} %broadcast_in_dim.9), calls=%async_computation | async-start | bytes 2097152 | tf_op jit(solution)/shard_map/all_to_all | solution.py:52
  22.9 5.4 %collective-permute-start.3 = (bf16[512,128]{1,0:T(8,128)(2,1)S(1)}, bf16[512,128]{1,0:T(8,128)(2,1)S(1)}, u32[]{:S(2)}, u32[]{:S(2)}) collective-permute-start(bf16[512,128]{1,0:T(8,128)(2,1)S(1)} %get-tuple-element.43), channel_id=1, source_target_pairs={{0,2},{1,3},{2,0},{3,1},{4,6},{5,7},{6,4},{7,5},{8,10},{9,11},{10,... | collective-permute-start | bytes 393224 | tf_op jit(solution)/shard_map/ppermute | solution.py:461
  28.9 8.6 %collective-permute-start.6 = (bf16[4,256,128]{2,1,0:T(8,128)(2,1)S(1)}, bf16[4,256,128]{2,1,0:T(8,128)(2,1)S(1)}, u32[]{:S(2)}, u32[]{:S(2)}) collective-permute-start(bf16[4,256,128]{2,1,0:T(8,128)(2,1)S(1)} %get-tuple-element.46.refs_0_), channel_id=1, source_target_pairs={{0,192},{64,0},{128,64},{192,128},{1,193},{65,1},{129,65},{193,129... | collective-permute-start | bytes 786440 | tf_op jit(solution)/shard_map/ppermute | solution.py:467
  30.4 13.5 %collective-permute-start.5 = (bf16[4,256,128]{2,1,0:T(8,128)(2,1)S(1)}, bf16[4,256,128]{2,1,0:T(8,128)(2,1)S(1)}, u32[]{:S(2)}, u32[]{:S(2)}) collective-permute-start(bf16[4,256,128]{2,1,0:T(8,128)(2,1)S(1)} %get-tuple-element.46.refs_0_), channel_id=1, source_target_pairs={{0,128},{64,192},{128,0},{192,64},{1,129},{65,193},{129,1},{193,65... | collective-permute-start | bytes 786440 | tf_op jit(solution)/shard_map/ppermute | solution.py:467
  34.0 12.8 %collective-permute-start.4 = (bf16[4,256,128]{2,1,0:T(8,128)(2,1)S(1)}, bf16[4,256,128]{2,1,0:T(8,128)(2,1)S(1)}, u32[]{:S(2)}, u32[]{:S(2)}) collective-permute-start(bf16[4,256,128]{2,1,0:T(8,128)(2,1)S(1)} %get-tuple-element.46.refs_0_), channel_id=1, source_target_pairs={{0,64},{64,128},{128,192},{192,0},{1,65},{65,129},{129,193},{193,1... | collective-permute-start | bytes 786440 | tf_op jit(solution)/shard_map/ppermute | solution.py:467
  35.9 10.8 %collective-permute-start.7 = (bf16[4,256,128]{2,1,0:T(8,128)(2,1)S(1)}, bf16[4,256,128]{2,1,0:T(8,128)(2,1)S(1)}, u32[]{:S(2)}, u32[]{:S(2)}) collective-permute-start(bf16[4,256,128]{2,1,0:T(8,128)(2,1)S(1)} %get-tuple-element.46.refs_0_), channel_id=1, source_target_pairs={{0,32},{32,0},{1,33},{33,1},{2,34},{34,2},{3,35},{35,3},{4,36},{36... | collective-permute-start | bytes 786440 | tf_op jit(solution)/shard_map/ppermute | solution.py:468
  37.5 9.2 %collective-permute-start.10 = (bf16[4,256,128]{2,1,0:T(8,128)(2,1)S(1)}, bf16[4,256,128]{2,1,0:T(8,128)(2,1)S(1)}, u32[]{:S(2)}, u32[]{:S(2)}) collective-permute-start(bf16[4,256,128]{2,1,0:T(8,128)(2,1)S(1)} %collective-permute-done.6.refs_3_), channel_id=1, source_target_pairs={{0,32},{32,0},{1,33},{33,1},{2,34},{34,2},{3,35},{35,3},{4,36},{36... | collective-permute-start | bytes 786440 | tf_op jit(solution)/shard_map/ppermute | solution.py:468
  43.9 4.0 %collective-permute-start.9 = (bf16[4,256,128]{2,1,0:T(8,128)(2,1)S(1)}, bf16[4,256,128]{2,1,0:T(8,128)(2,1)S(1)}, u32[]{:S(2)}, u32[]{:S(2)}) collective-permute-start(bf16[4,256,128]{2,1,0:T(8,128)(2,1)S(1)} %collective-permute-done.5.refs_2_), channel_id=1, source_target_pairs={{0,32},{32,0},{1,33},{33,1},{2,34},{34,2},{3,35},{35,3},{4,36},{36... | collective-permute-start | bytes 786440 | tf_op jit(solution)/shard_map/ppermute | solution.py:468
  52.9 5.7 %collective-permute-start.14 = (bf16[256,512]{1,0:T(8,128)(2,1)S(1)}, bf16[256,512]{1,0:T(8,128)(2,1)S(1)}, u32[]{:S(2)}, u32[]{:S(2)}) collective-permute-start(bf16[256,512]{1,0:T(8,128)(2,1)S(1)} %get-tuple-element.50), channel_id=1, source_target_pairs={{0,4},{4,0},{1,5},{5,1},{2,6},{6,2},{3,7},{7,3},{8,12},{12,8},{9,1... | collective-permute-start | bytes 786440 | tf_op jit(solution)/shard_map/ppermute | solution.py:473
  54.1 7.8 %collective-permute-start.12 = (bf16[256,512]{1,0:T(8,128)(2,1)S(1)}, bf16[256,512]{1,0:T(8,128)(2,1)S(1)}, u32[]{:S(2)}, u32[]{:S(2)}) collective-permute-start(bf16[256,512]{1,0:T(8,128)(2,1)S(1)} %get-tuple-element.50), channel_id=1, source_target_pairs={{0,2},{1,3},{2,0},{3,1},{4,6},{5,7},{6,4},{7,5},{8,10},{9,11},{10,... | collective-permute-start | bytes 786440 | tf_op jit(solution)/shard_map/ppermute | solution.py:474
  54.2 13.3 %collective-permute-start.13 = (bf16[256,512]{1,0:T(8,128)(2,1)S(1)}, bf16[256,512]{1,0:T(8,128)(2,1)S(1)}, u32[]{:S(2)}, u32[]{:S(2)}) collective-permute-start(bf16[256,512]{1,0:T(8,128)(2,1)S(1)} %get-tuple-element.50), channel_id=1, source_target_pairs={{0,3},{1,0},{2,1},{3,2},{4,7},{5,4},{6,5},{7,6},{8,11},{9,8},{10,9... | collective-permute-start | bytes 786440 | tf_op jit(solution)/shard_map/ppermute | solution.py:474
  56.3 13.2 %collective-permute-start.11 = (bf16[256,512]{1,0:T(8,128)(2,1)S(1)}, bf16[256,512]{1,0:T(8,128)(2,1)S(1)}, u32[]{:S(2)}, u32[]{:S(2)}) collective-permute-start(bf16[256,512]{1,0:T(8,128)(2,1)S(1)} %get-tuple-element.50), channel_id=1, source_target_pairs={{0,1},{1,2},{2,3},{3,0},{4,5},{5,6},{6,7},{7,4},{8,9},{9,10},{10,1... | collective-permute-start | bytes 786440 | tf_op jit(solution)/shard_map/ppermute | solution.py:474
  58.6 14.4 %collective-permute-start.17 = (bf16[256,512]{1,0:T(8,128)(2,1)S(1)}, bf16[256,512]{1,0:T(8,128)(2,1)S(1)}, u32[]{:S(2)}, u32[]{:S(2)}) collective-permute-start(bf16[256,512]{1,0:T(8,128)(2,1)S(1)} %collective-permute-done.14.far0), channel_id=1, source_target_pairs={{0,3},{1,0},{2,1},{3,2},{4,7},{5,4},{6,5},{7,6},{8,11},{9,8},{10,9... | collective-permute-start | bytes 786440 | tf_op jit(solution)/shard_map/ppermute | solution.py:476
  58.8 16.3 %collective-permute-start.15 = (bf16[256,512]{1,0:T(8,128)(2,1)S(1)}, bf16[256,512]{1,0:T(8,128)(2,1)S(1)}, u32[]{:S(2)}, u32[]{:S(2)}) collective-permute-start(bf16[256,512]{1,0:T(8,128)(2,1)S(1)} %collective-permute-done.14.far0), channel_id=1, source_target_pairs={{0,1},{1,2},{2,3},{3,0},{4,5},{5,6},{6,7},{7,4},{8,9},{9,10},{10,1... | collective-permute-start | bytes 786440 | tf_op jit(solution)/shard_map/ppermute | solution.py:475
  61.9 13.2 %collective-permute-start.16 = (bf16[256,512]{1,0:T(8,128)(2,1)S(1)}, bf16[256,512]{1,0:T(8,128)(2,1)S(1)}, u32[]{:S(2)}, u32[]{:S(2)}) collective-permute-start(bf16[256,512]{1,0:T(8,128)(2,1)S(1)} %collective-permute-done.12.near2), channel_id=1, source_target_pairs={{0,4},{4,0},{1,5},{5,1},{2,6},{6,2},{3,7},{7,3},{8,12},{12,8},{9,1... | collective-permute-start | bytes 786440 | tf_op jit(solution)/shard_map/ppermute | solution.py:475
  75.1 34.7 %all-to-all-start.1 = ((bf16[8,256,256]{2,1,0:T(8,128)(2,1)}), bf16[8,256,256]{2,1,0:T(8,128)(2,1)S(1)}, u32[]{:S(2)}, u32[]{:S(2)}) async-start(bf16[8,256,256]{2,1,0:T(8,128)(2,1)} %first_partial.1), calls=%async_computation.1 | async-start | bytes 2097152 | tf_op jit(solution)/shard_map/all_to_all | solution.py:478
  94.3 3.8 %collective-permute-start.18 = (bf16[144,256]{1,0:T(8,128)(2,1)}, bf16[144,256]{1,0:T(8,128)(2,1)S(1)}, u32[]{:S(2)}, u32[]{:S(2)}) collective-permute-start(bf16[144,256]{1,0:T(8,128)(2,1)} %get-tuple-element.59), channel_id=1, source_target_pairs={{0,1},{1,2},{2,3},{3,0},{4,5},{5,6},{6,7},{7,4},{8,9},{9,10},{10,1... | collective-permute-start | bytes 221192 | tf_op jit(solution)/shard_map/ppermute | solution.py:482
  95.4 5.2 %collective-permute-start.19 = (bf16[144,256]{1,0:T(8,128)(2,1)}, bf16[144,256]{1,0:T(8,128)(2,1)S(1)}, u32[]{:S(2)}, u32[]{:S(2)}) collective-permute-start(bf16[144,256]{1,0:T(8,128)(2,1)} %get-tuple-element.60), channel_id=1, source_target_pairs={{0,2},{1,3},{2,0},{3,1},{4,6},{5,7},{6,4},{7,5},{8,10},{9,11},{10,... | collective-permute-start | bytes 221192 | tf_op jit(solution)/shard_map/ppermute | solution.py:482
  95.7 4.9 %collective-permute-start.20 = (bf16[144,256]{1,0:T(8,128)(2,1)}, bf16[144,256]{1,0:T(8,128)(2,1)S(1)}, u32[]{:S(2)}, u32[]{:S(2)}) collective-permute-start(bf16[144,256]{1,0:T(8,128)(2,1)} %get-tuple-element.61), channel_id=1, source_target_pairs={{0,3},{1,0},{2,1},{3,2},{4,7},{5,4},{6,5},{7,6},{8,11},{9,8},{10,9... | collective-permute-start | bytes 221192 | tf_op jit(solution)/shard_map/ppermute | solution.py:482
  109.8 34.2 %all-to-all-start.2 = ((bf16[8,272,256]{2,1,0:T(8,128)(2,1)}), bf16[8,272,256]{2,1,0:T(8,128)(2,1)S(1)}, u32[]{:S(2)}, u32[]{:S(2)}) async-start(bf16[8,272,256]{2,1,0:T(8,128)(2,1)} %second_partial.1), calls=%async_computation.2 | async-start | bytes 2228224 | tf_op jit(solution)/shard_map/all_to_all | solution.py:485
  144.8 24.8 %collective-permute-start.21 = (bf16[2,256,256]{2,1,0:T(8,128)(2,1)S(1)}, bf16[2,256,256]{2,1,0:T(8,128)(2,1)S(1)}, u32[]{:S(2)}, u32[]{:S(2)}) collective-permute-start(bf16[2,256,256]{2,1,0:T(8,128)(2,1)S(1)} %get-tuple-element.66), channel_id=1, source_target_pairs={{0,0},{1,1},{2,2},{3,3},{4,32},{5,33},{6,34},{7,35},{8,64},{9,65},... | collective-permute-start | bytes 786440 | tf_op jit(solution)/shard_map/ppermute | solution.py:487
  (3 other events, 65.2 us)
